TPU v7x, 512 devices: a whole 4x4x16 slice. The times are simulated.
512 devices in a mesh: dp: 32 (over z, y_hi), seq: 16 (over y_lo, x, core).
Axes of the slice: x: 4, y: 4 (y_hi: 2, y_lo: 2; y = y_hi * 2 + y_lo), z: 16, core: 2. Of those that a mesh axis runs over, the one named last changes fastest.
Arguments:
- sequence_in: bfloat16 [32, 8192, 768], P('dp', 'seq'), may hold values from -6 to 6
- output_grad: bfloat16 [32, 8192, 768], P('dp', 'seq'), may hold values from -6 to 6
- skip_mask: int32 [32, 2], P('dp'), may hold values 0 or 1
- in_gain: float32 [2, 768], replicated, may hold values from 0.25 to 1.75
- input_shift_vec: float32 [2, 768], replicated, may hold values from -3 to 3
- mid_gain: float32 [2, 384], replicated, may hold values from 0.25 to 1.75
- mid_offset: float32 [2, 384], replicated, may hold values from -3 to 3
- conv_weight: bfloat16 [2, 3, 768, 384], P(None, None, 'seq'), may hold values from -0.21875 to 0.21875
- point_weight: bfloat16 [384, 2, 768], P('seq'), may hold values from -0.3125 to 0.3125
Outputs:
- point_grad: float32 [384, 2, 768], P('seq')
- input_grad: bfloat16 [32, 8192, 768], P('dp', 'seq')
Inputs may be any that keep to these rules, and one draw needn't show every extreme that they name: skip_mask[s, b] = 1 means that sample s passes block b unchanged in this step.
All inputs are finite; a program needn't handle non-finite values.
Results may differ from a plain program's by a relative error of at most 0.009.
Values may be sent and summed in bfloat16 or wider, within the bound.
No kernel may reach another device: no remote copies, remote signals or barrier semaphores. Data moves between devices by JAX's collectives and lax.ppermute only.
A program may use at most 64 MiB of HBM per device.

v0:
```python
import math

import jax
import jax.numpy as jnp
from jax import lax
from jax.sharding import PartitionSpec as P

FIRST_DILATION = 1024
SECOND_DILATION = 2048


def passed_along(value, axis, by):
    peers = lax.axis_size(axis)
    pairs = [(i, i + by) for i in range(peers) if 0 <= i + by < peers]
    return lax.ppermute(value, axis, pairs)


def gelu_tanh(values):
    return jax.nn.gelu(values, approximate=True)


def contract_last(left, right):
    return lax.dot_general(
        left, right, (((1,), (1,)), ((), ())), preferred_element_type=jnp.float32
    )


def neighbours(source, shards_away):
    earlier = passed_along(source, "seq", shards_away)
    later = passed_along(source, "seq", -shards_away)
    return (earlier, later)


def forward_local(
    state, earlier, activated, later, weight, gain_vec, offset_vec, projection, kept_flag
):
    conv_out = jnp.dot(earlier, weight[0], preferred_element_type=jnp.float32)
    conv_out = conv_out + jnp.dot(activated, weight[1], preferred_element_type=jnp.float32)
    conv_out = conv_out + jnp.dot(later, weight[2], preferred_element_type=jnp.float32)
    middle = conv_out * gain_vec + offset_vec
    hidden_act = gelu_tanh(middle).astype(jnp.bfloat16)
    branch = jnp.dot(hidden_act, projection, preferred_element_type=jnp.float32)
    result = (state.astype(jnp.float32) + kept_flag * branch).astype(jnp.bfloat16)
    return (middle, hidden_act, result)


def backward_first(gradient, middle, projection, gain_vec, kept_flag):
    branch_grad = (kept_flag * gradient.astype(jnp.float32)).astype(jnp.bfloat16)
    hidden_grad = contract_last(branch_grad, projection)
    middle_grad = jax.vjp(gelu_tanh, middle)[1](hidden_grad)[0]
    conv_grad = (middle_grad * gain_vec).astype(jnp.bfloat16)
    return (conv_grad, branch_grad)


def backward_second(gradient, earlier, conv_grad, later, weight, normed, gain_vec):
    act_grad = (
        contract_last(later, weight[0])
        + contract_last(conv_grad, weight[1])
        + contract_last(earlier, weight[2])
    )
    normed_grad = jax.vjp(gelu_tanh, normed)[1](act_grad)[0] * gain_vec
    return (gradient.astype(jnp.float32) + normed_grad).astype(jnp.bfloat16)


def grad_rows(hidden_act, branch_grad):
    return lax.dot_general(
        hidden_act, branch_grad, (((0,), (0,)), ((), ())), preferred_element_type=jnp.float32
    )


def shards(
    sequence_in,
    output_grad,
    skip_mask,
    in_gain,
    input_shift_vec,
    mid_gain,
    mid_offset,
    conv_weight,
    point_weight,
):
    position_list = sequence_in.shape[1]
    channels = sequence_in.shape[2]
    point_full = lax.all_gather(point_weight, "seq", axis=0, tiled=True)
    neighbour_reach = (FIRST_DILATION // position_list, SECOND_DILATION // position_list)
    state = sequence_in.reshape(-1, channels)
    total_rows = state.shape[0]
    saved = []
    kept_weights = []
    for block_index in range(2):
        kept_flag = (1 - skip_mask[0, block_index]).astype(jnp.float32)
        normed = state.astype(jnp.float32) * in_gain[block_index] + input_shift_vec[block_index]
        activated = gelu_tanh(normed).astype(jnp.bfloat16)
        earlier, later = neighbours(
            activated.reshape(sequence_in.shape), neighbour_reach[block_index]
        )
        earlier = earlier.reshape(total_rows, channels)
        later = later.reshape(total_rows, channels)
        weight = lax.all_gather(conv_weight[block_index], "seq", axis=1, tiled=True)
        kept_weights.append(weight)
        operands = (
            state,
            earlier,
            activated,
            later,
            weight,
            mid_gain[block_index],
            mid_offset[block_index],
            point_full[:, block_index, :],
            kept_flag,
        )
        middle, hidden_act, state = forward_local(*operands)
        saved.append((normed, middle, hidden_act, kept_flag))
    gradient = output_grad.reshape(-1, channels)
    hidden_saved = [None, None]
    branch_saved = [None, None]
    for block_index in (1, 0):
        normed, middle, hidden_act, kept_flag = saved[block_index]
        projection = point_full[:, block_index, :]
        first_operands = (gradient, middle, projection, mid_gain[block_index], kept_flag)
        conv_grad, branch_grad = backward_first(*first_operands)
        hidden_saved[block_index] = hidden_act
        branch_saved[block_index] = branch_grad
        earlier, later = neighbours(
            conv_grad.reshape(sequence_in.shape[0], position_list, -1), neighbour_reach[block_index]
        )
        earlier = earlier.reshape(total_rows, -1)
        later = later.reshape(total_rows, -1)
        weight = lax.all_gather(conv_weight[block_index], "seq", axis=1, tiled=True)
        second_operands = (
            gradient,
            earlier,
            conv_grad,
            later,
            weight,
            normed,
            in_gain[block_index],
        )
        gradient = backward_second(*second_operands)
    first_term = grad_rows(hidden_saved[0], branch_saved[0])
    second_term = grad_rows(hidden_saved[1], branch_saved[1])
    shared_part = lax.psum_scatter(
        jnp.stack([first_term, second_term], axis=1), "seq", scatter_dimension=0, tiled=True
    )
    summed = lax.psum(shared_part, "dp")
    sample_count = sequence_in.shape[0] * lax.axis_size("dp")
    full_length = position_list * lax.axis_size("seq")
    point_grad = summed * (1.0 / math.sqrt(sample_count * full_length))
    return (point_grad, gradient.reshape(sequence_in.shape))


def solution(mesh):
    return jax.shard_map(
        shards,
        mesh=mesh,
        in_specs=(
            P("dp", "seq", None),
            P("dp", "seq", None),
            P("dp", None),
            P(),
            P(),
            P(),
            P(),
            P(None, None, "seq", None),
            P("seq", None, None),
        ),
        out_specs=(P("seq", None, None), P("dp", "seq", None)),
        check_vma=False,
    )
```

profile of v0, /device:TPU:6, one launch (start us, length us, event | category | flops | bytes accessed | tf_op | source)
XLA Modules:
  0.0 578.6 jit_solution(11100754376341167043)
XLA Ops:
  7.2 1.7 fusion.103
  8.9 0.0 all-gather.6.cloned.1.call-start
  9.0 1.5 copy.12
  10.5 0.0 all-gather.10.cloned.1.call-start
  10.6 0.7 all-gather.10.cloned.1.call-update
  11.3 0.8 slice_reduce_fusion.2
  12.1 1.8 fusion.15
  13.9 2.7 collective-permute-start.1
  16.6 5.2 collective-permute-start
  21.9 0.6 fusion.104
  23.2 38.9 %all-gather.8.cloned.1.call-done = bf16[1,3,768,384]{3,2,1,0:T(8,128)(2,1)} async-done(((bf16[1,3,48,384]{3,2,1,0:T(8,128)(2,1)}), bf16[1,3,768,384]{3,2,1,0:T(8,128)(2,1)}) %all-gather.8.cloned.1.call-update) | async-done | bytes 1769488 | tf_op jit(solution)/shard_map/all_gather | solution.py:99
  62.0 1.8 fusion.70
  63.8 0.6 fusion.68
  64.4 2.7 fusion.44
  67.1 40.6 %all-gather.6.cloned.1.call-done = bf16[384,2,768]{2,0,1:T(8,128)(2,1)} async-done(((bf16[24,2,768]{2,0,1:T(8,128)(2,1)}), bf16[384,2,768]{2,0,1:T(8,128)(2,1)}) %all-gather.6.cloned.1.call-update) | async-done | bytes 1179664 | tf_op jit(solution)/shard_map/all_gather | solution.py:84
  107.7 2.0 fusion.4
  109.7 0.6 fusion.102
  110.3 4.0 collective-permute-start.3
  114.3 4.3 collective-permute-start.2
  119.2 37.4 %all-gather.10.cloned.1.call-done = bf16[1,3,768,384]{3,2,1,0:T(8,128)(2,1)} async-done(((bf16[1,3,48,384]{3,2,1,0:T(8,128)(2,1)}), bf16[1,3,768,384]{3,2,1,0:T(8,128)(2,1)}) %all-gather.10.cloned.1.call-update) | async-done | bytes 1769488 | tf_op jit(solution)/shard_map/all_gather | solution.py:99
  156.6 2.0 fusion.88
  158.6 1.7 fusion.65
  160.4 1.9 fusion.41
  162.3 0.9 fusion.60
  163.2 7.6 %collective-permute-start.4 = (bf16[1,512,384]{2,1,0:T(8,128)(2,1)S(1)}, bf16[1,512,384]{2,1,0:T(8,128)(2,1)S(1)}, u32[]{:S(2)}, u32[]{:S(2)}) collective-permute-start(bf16[1,512,384]{2,1,0:T(8,128)(2,1)S(1)} %bitcast.136), channel_id=1, source_target_pairs={{4,0},{5,1},{6,2},{7,3},{8,4},{9,5},{10,6},{11,7},{12,8},{13,9},{1... | collective-permute-start | bytes 1179656 | tf_op jit(solution)/shard_map/ppermute | solution.py:15
  170.8 1.9 collective-permute-start.5
  172.7 0.6 fusion.87
  173.3 0.7 convolution_bitcast_fusion
  174.1 6.2 %collective-permute-done.4 = bf16[1,512,384]{2,1,0:T(8,128)(2,1)S(1)} collective-permute-done((bf16[1,512,384]{2,1,0:T(8,128)(2,1)S(1)}, bf16[1,512,384]{2,1,0:T(8,128)(2,1)S(1)}, u32[]{:S(2)}, u32[]{:S(2)}) %collective-permute-start.4) | collective-permute-done | bytes 393248 | tf_op jit(solution)/shard_map/ppermute | solution.py:15
  180.3 0.6 fusion.86
  180.9 7.1 %collective-permute-done.5 = bf16[1,512,384]{2,1,0:T(8,128)(2,1)S(1)} collective-permute-done((bf16[1,512,384]{2,1,0:T(8,128)(2,1)S(1)}, bf16[1,512,384]{2,1,0:T(8,128)(2,1)S(1)}, u32[]{:S(2)}, u32[]{:S(2)}) %collective-permute-start.5) | collective-permute-done | bytes 393248 | tf_op jit(solution)/shard_map/ppermute | solution.py:15
  188.0 1.6 fusion.22
  189.7 0.7 convolution_bitcast_fusion.1
  190.4 0.2 copy-done.9
  190.5 1.6 pad_maximum_fusion
  192.1 0.0 all-reduce.2.cloned.1.call-start
  192.2 1.1 copy-done.10
  193.2 2.8 fusion.52
  196.0 1.9 collective-permute-start.6
  197.9 6.2 %collective-permute-start.7 = (bf16[1,512,384]{2,1,0:T(8,128)(2,1)}, bf16[1,512,384]{2,1,0:T(8,128)(2,1)}, u32[]{:S(2)}, u32[]{:S(2)}) collective-permute-start(bf16[1,512,384]{2,1,0:T(8,128)(2,1)} %bitcast.24), channel_id=1, source_target_pairs={{0,2},{1,3},{2,4},{3,5},{4,6},{5,7},{6,8},{7,9},{8,10},{9,11},{10,... | collective-permute-start | bytes 1179656 | tf_op jit(solution)/shard_map/ppermute | solution.py:15
  204.2 1.6 fusion.84
  205.8 4.9 collective-permute-done.6
  210.7 1.7 fusion.83
  212.4 49.9 %reduce-scatter.2.cloned.1.call-done = f32[24,2,768]{2,0,1:T(8,128)} async-done(((f32[384,2,768]{2,0,1:T(8,128)}), f32[24,2,768]{2,0,1:T(8,128)}) %reduce-scatter.2.cloned.1.call-update) | async-done | bytes 147472 | tf_op jit(solution)/shard_map/reduce_scatter | solution.py:142
  262.4 4.5 fusion.77
  266.8 303.5 %all-reduce.2.cloned.1.call-done = f32[24,2,768]{2,0,1:T(8,128)} async-done(((f32[24,2,768]{2,0,1:T(8,128)}), f32[24,2,768]{2,0,1:T(8,128)}) %all-reduce.2.cloned.1.call-update) | async-done | bytes 147472 | tf_op jit(solution)/shard_map/psum | solution.py:145
  570.4 0.9 broadcast_multiply_fusion
  571.3 0.7 copy.13
  (32 shorter events, 0.2 us)
Async XLA Ops:
  7.2 14.7 %copy-start.6 = (s32[1,2]{1,0:T(1,128)S(1)}, s32[1,2]{1,0:T(1,128)}, u32[]{:S(2)}) copy-start(s32[1,2]{1,0:T(1,128)} %param.11) | copy-start | bytes 28
  7.2 15.9 %copy-start.5 = (f32[2,384]{1,0:T(2,128)S(1)}, f32[2,384]{1,0:T(2,128)}, u32[]{:S(2)}) copy-start(f32[2,384]{1,0:T(2,128)} %param.14) | copy-start | bytes 9220
  7.2 15.9 %copy-start.4 = (f32[2,384]{1,0:T(2,128)S(1)}, f32[2,384]{1,0:T(2,128)}, u32[]{:S(2)}) copy-start(f32[2,384]{1,0:T(2,128)} %param.15) | copy-start | bytes 9220
  7.2 54.8 %all-gather.8.cloned.1.call-start = ((), (), s32[]{:S(2)}) async-start(), calls=%async_computation.4 | async-start | bytes 1880064 | tf_op jit(solution)/shard_map/all_gather | solution.py:99
  8.9 98.8 %all-gather.6.cloned.1.call-start = ((), (), s32[]{:S(2)}) async-start(), calls=%async_computation.1 | async-start | bytes 1253376 | tf_op jit(solution)/shard_map/all_gather | solution.py:84
  10.5 146.1 %all-gather.10.cloned.1.call-start = ((), (), s32[]{:S(2)}) async-start(), calls=%async_computation.5 | async-start | bytes 1880064 | tf_op jit(solution)/shard_map/all_gather | solution.py:99
  11.3 251.1 %reduce-scatter.2.cloned.1.call-start = ((), (), s32[]{:S(2)}) async-start(), calls=%async_computation.2 | async-start | bytes 2506752 | tf_op jit(solution)/shard_map/reduce_scatter | solution.py:142
  13.9 49.9 %collective-permute-start.1 = (bf16[1,512,768]{2,1,0:T(8,128)(2,1)S(1)}, bf16[1,512,768]{2,1,0:T(8,128)(2,1)S(1)}, u32[]{:S(2)}, u32[]{:S(2)}) collective-permute-start(bf16[1,512,768]{2,1,0:T(8,128)(2,1)S(1)} %fusion.15), channel_id=1, source_target_pairs={{2,0},{3,1},{4,2},{5,3},{6,4},{7,5},{8,6},{9,7},{10,8},{11,9},{12,... | collective-permute-start | bytes 2359304 | tf_op jit(solution)/shard_map/ppermute | solution.py:15
  16.6 47.7 %collective-permute-start = (bf16[1,512,768]{2,1,0:T(8,128)(2,1)S(1)}, bf16[1,512,768]{2,1,0:T(8,128)(2,1)}, u32[]{:S(2)}, u32[]{:S(2)}) collective-permute-start(bf16[1,512,768]{2,1,0:T(8,128)(2,1)S(1)} %fusion.15), channel_id=1, source_target_pairs={{0,2},{1,3},{2,4},{3,5},{4,6},{5,7},{6,8},{7,9},{8,10},{9,11},{10,... | collective-permute-start | bytes 2359304 | tf_op jit(solution)/shard_map/ppermute | solution.py:15
  62.0 1.8 copy-start
  64.4 43.3 %copy-start.2 = (bf16[1,512,768]{2,1,0:T(8,128)(2,1)S(1)}, bf16[1,512,768]{2,1,0:T(8,128)(2,1)}, u32[]{:S(2)}) copy-start(bf16[1,512,768]{2,1,0:T(8,128)(2,1)} %param.9) | copy-start | bytes 2359300
  110.3 48.3 %collective-permute-start.3 = (bf16[1,512,768]{2,1,0:T(8,128)(2,1)S(1)}, bf16[1,512,768]{2,1,0:T(8,128)(2,1)}, u32[]{:S(2)}, u32[]{:S(2)}) collective-permute-start(bf16[1,512,768]{2,1,0:T(8,128)(2,1)S(1)} %fusion.102), channel_id=1, source_target_pairs={{4,0},{5,1},{6,2},{7,3},{8,4},{9,5},{10,6},{11,7},{12,8},{13,9},{1... | collective-permute-start | bytes 2359304 | tf_op jit(solution)/shard_map/ppermute | solution.py:15
  114.3 46.0 %collective-permute-start.2 = (bf16[1,512,768]{2,1,0:T(8,128)(2,1)S(1)}, bf16[1,512,768]{2,1,0:T(8,128)(2,1)}, u32[]{:S(2)}, u32[]{:S(2)}) collective-permute-start(bf16[1,512,768]{2,1,0:T(8,128)(2,1)S(1)} %fusion.102), channel_id=1, source_target_pairs={{0,4},{1,5},{2,6},{3,7},{4,8},{5,9},{6,10},{7,11},{8,12},{9,13},{1... | collective-permute-start | bytes 2359304 | tf_op jit(solution)/shard_map/ppermute | solution.py:15
  156.6 2.0 copy-start.1
  160.3 1.9 copy-start.7
  160.4 1.9 copy-start.8
  163.2 17.1 %collective-permute-start.4 = (bf16[1,512,384]{2,1,0:T(8,128)(2,1)S(1)}, bf16[1,512,384]{2,1,0:T(8,128)(2,1)S(1)}, u32[]{:S(2)}, u32[]{:S(2)}) collective-permute-start(bf16[1,512,384]{2,1,0:T(8,128)(2,1)S(1)} %bitcast.136), channel_id=1, source_target_pairs={{4,0},{5,1},{6,2},{7,3},{8,4},{9,5},{10,6},{11,7},{12,8},{13,9},{1... | collective-permute-start | bytes 1179656 | tf_op jit(solution)/shard_map/ppermute | solution.py:15
  170.8 17.2 %collective-permute-start.5 = (bf16[1,512,384]{2,1,0:T(8,128)(2,1)S(1)}, bf16[1,512,384]{2,1,0:T(8,128)(2,1)S(1)}, u32[]{:S(2)}, u32[]{:S(2)}) collective-permute-start(bf16[1,512,384]{2,1,0:T(8,128)(2,1)S(1)} %bitcast.137), channel_id=1, source_target_pairs={{0,4},{1,5},{2,6},{3,7},{4,8},{5,9},{6,10},{7,11},{8,12},{9,13},{1... | collective-permute-start | bytes 1179656 | tf_op jit(solution)/shard_map/ppermute | solution.py:15
  180.9 8.8 %copy-start.3 = (f32[512,384]{1,0:T(8,128)S(1)}, f32[512,384]{1,0:T(8,128)}, u32[]{:S(2)}) copy-start(f32[512,384]{1,0:T(8,128)} %fusion.44) | copy-start | bytes 2359300
  189.7 0.9 copy-start.9
  192.1 1.1 copy-start.10
  192.1 378.2 %all-reduce.2.cloned.1.call-start = ((), (), s32[]{:S(2)}) async-start(), calls=%async_computation.3 | async-start | bytes 294912 | tf_op jit(solution)/shard_map/psum | solution.py:145
  196.0 14.6 %collective-permute-start.6 = (bf16[1,512,384]{2,1,0:T(8,128)(2,1)}, bf16[1,512,384]{2,1,0:T(8,128)(2,1)S(1)}, u32[]{:S(2)}, u32[]{:S(2)}) collective-permute-start(bf16[1,512,384]{2,1,0:T(8,128)(2,1)} %bitcast.24), channel_id=1, source_target_pairs={{2,0},{3,1},{4,2},{5,3},{6,4},{7,5},{8,6},{9,7},{10,8},{11,9},{12,... | collective-permute-start | bytes 1179656 | tf_op jit(solution)/shard_map/ppermute | solution.py:15
  197.9 64.4 %collective-permute-start.7 = (bf16[1,512,384]{2,1,0:T(8,128)(2,1)}, bf16[1,512,384]{2,1,0:T(8,128)(2,1)}, u32[]{:S(2)}, u32[]{:S(2)}) collective-permute-start(bf16[1,512,384]{2,1,0:T(8,128)(2,1)} %bitcast.24), channel_id=1, source_target_pairs={{0,2},{1,3},{2,4},{3,5},{4,6},{5,7},{6,8},{7,9},{8,10},{9,11},{10,... | collective-permute-start | bytes 1179656 | tf_op jit(solution)/shard_map/ppermute | solution.py:15
Sparse Core Ops, SparseCore 0:
  10.7 51.2 all-gather.7
  64.1 43.5 all-gather.5
  110.4 46.2 all-gather.9
  192.3 70.0 reduce-scatter.1
  265.1 305.2 all-reduce.1
where the time goes:
time: 579 us
  waiting for transfers between devices  489 us (84%)
  starting transfers between devices  34.1 us (6%)
  matrix products  28.3 us (5%)
  between operations  15.3 us (3%)
  local copies, waits for them, and re-layouts  6.63 us (1%)
    psum x1, waiting for transfers between devices, shards(): summed = lax.psum(shared_part, 'dp')  304 us
    all_gather x2, waiting for transfers between devices, shards(): weight = lax.all_gather(conv_weight[block_index], 'seq', axis=1, tiled=True)  76.3 us
    reduce_scatter x1, waiting for transfers between devices, shards(): lax.psum_scatter(jnp.stack([first_term, second_term], axis=1), 'seq', sca...  49.9 us
    all_gather x1, waiting for transfers between devices, shards(): point_full = lax.all_gather(point_weight, 'seq', axis=0, tiled=True)  40.6 us
    ppermute x8, starting transfers between devices, passed_along(): return lax.ppermute(value, axis, pairs)  33.9 us
    ppermute x8, waiting for transfers between devices, passed_along(): return lax.ppermute(value, axis, pairs)  18.2 us
    dot_general x8, matrix products, contract_last(): lax.dot_general(left, right, (((1,), (1,)), ((), ())), preferred_element_...  14.3 us
  transfers between devices with their start and end apart: 13, of which 8 were waited for; matrix products, arithmetic and copies ran while one was open for 5% of the time, Pallas kernels for 0%

commit v1 on v0

--- a/solution.py
+++ b/solution.py
@@ -13,6 +13,18 @@
     peers = lax.axis_size(axis)
     pairs = [(i, i + by) for i in range(peers) if 0 <= i + by < peers]
     return lax.ppermute(value, axis, pairs)
+
+
+def gathered(value, axis):
+    peers = lax.axis_size(axis)
+    copies = jnp.broadcast_to(value[None], (peers,) + value.shape)
+    return lax.all_to_all(copies, axis, 0, 0, tiled=True)
+
+
+def summed_over(value, axis):
+    peers = lax.axis_size(axis)
+    pieces = value.reshape((peers, -1) + value.shape[1:])
+    return lax.all_to_all(pieces, axis, 0, 0, tiled=True).sum(axis=0)
 
 
 def gelu_tanh(values):
@@ -81,12 +93,15 @@
 ):
     position_list = sequence_in.shape[1]
     channels = sequence_in.shape[2]
-    point_full = lax.all_gather(point_weight, "seq", axis=0, tiled=True)
+    point_full = gathered(point_weight, "seq").reshape(-1, *point_weight.shape[1:])
+    conv_parts = gathered(conv_weight, "seq")
+    conv_full = jnp.moveaxis(conv_parts, 0, 2).reshape(
+        conv_weight.shape[0], conv_weight.shape[1], -1, conv_weight.shape[3]
+    )
     neighbour_reach = (FIRST_DILATION // position_list, SECOND_DILATION // position_list)
     state = sequence_in.reshape(-1, channels)
     total_rows = state.shape[0]
     saved = []
-    kept_weights = []
     for block_index in range(2):
         kept_flag = (1 - skip_mask[0, block_index]).astype(jnp.float32)
         normed = state.astype(jnp.float32) * in_gain[block_index] + input_shift_vec[block_index]
@@ -96,8 +111,7 @@
         )
         earlier = earlier.reshape(total_rows, channels)
         later = later.reshape(total_rows, channels)
-        weight = lax.all_gather(conv_weight[block_index], "seq", axis=1, tiled=True)
-        kept_weights.append(weight)
+        weight = conv_full[block_index]
         operands = (
             state,
             earlier,
@@ -126,7 +140,7 @@
         )
         earlier = earlier.reshape(total_rows, -1)
         later = later.reshape(total_rows, -1)
-        weight = lax.all_gather(conv_weight[block_index], "seq", axis=1, tiled=True)
+        weight = conv_full[block_index]
         second_operands = (
             gradient,
             earlier,
@@ -139,10 +153,10 @@
         gradient = backward_second(*second_operands)
     first_term = grad_rows(hidden_saved[0], branch_saved[0])
     second_term = grad_rows(hidden_saved[1], branch_saved[1])
-    shared_part = lax.psum_scatter(
-        jnp.stack([first_term, second_term], axis=1), "seq", scatter_dimension=0, tiled=True
-    )
-    summed = lax.psum(shared_part, "dp")
+    shared_part = summed_over(jnp.stack([first_term, second_term], axis=1), "seq")
+    dp_size = lax.axis_size("dp")
+    own_piece = summed_over(shared_part.reshape(dp_size, -1), "dp")
+    summed = gathered(own_piece, "dp").reshape(shared_part.shape)
     sample_count = sequence_in.shape[0] * lax.axis_size("dp")
     full_length = position_list * lax.axis_size("seq")
     point_grad = summed * (1.0 / math.sqrt(sample_count * full_length))

time: 579 us -> 269 us (0.46)
  waiting for transfers between devices: 489 us -> 96.4 us
  blocking collectives: 0 us -> 61.8 us
  starting transfers between devices: 34.1 us -> 62.7 us
  between operations: 15.3 us -> 2.55 us
    psum x1 -> x0, waiting for transfers between devices: 304 us -> none  [shards(): summed = lax.psum(shared_part, 'dp')]
    all_gather x3 -> x0, waiting for transfers between devices: 117 us -> none  [the longest x2 76.3 us: shards(): weight = lax.all_gather(conv_weight[block_index], 'seq', axis=1, tiled=True)]
    all_to_all x0 -> x2, blocking collectives: none -> 61.8 us  [the longest x1 37 us: summed_over(): return lax.all_to_all(pieces, axis, 0, 0, tiled=True).sum(axis=0)]
    reduce_scatter x1 -> x0, waiting for transfers between devices: 49.9 us -> none  [shards(): lax.psum_scatter(jnp.stack([first_term, second_term], axis=1), 'seq', sca...]
    all_to_all x0 -> x3, waiting for transfers between devices: none -> 48.5 us  [the longest x2 43.2 us: gathered(): return lax.all_to_all(copies, axis, 0, 0, tiled=True)]
    ppermute x8, waiting for transfers between devices: 18.2 us -> 47.8 us  [passed_along(): return lax.ppermute(value, axis, pairs)]
    all_to_all x0 -> x3, starting transfers between devices: none -> 29.5 us  [the longest x2 15 us: gathered(): return lax.all_to_all(copies, axis, 0, 0, tiled=True)]
  transfers between devices with their start and end apart: 13 -> 11, of which waited for: 8 -> 7; matrix products, arithmetic and copies ran while one was open for 5% -> 10% of each run, Pallas kernels for 0% -> 0%
where the time goes in v1:
time: 269 us; the launch traced here: 268 us
  waiting for transfers between devices  96.4 us (36%)
  starting transfers between devices  62.7 us (23%)
  blocking collectives  61.8 us (23%)
  matrix products  26.3 us (10%)
  local copies, waits for them, and re-layouts  11.9 us (4%)
  other arithmetic  6.56 us (2%)
    ppermute x8, waiting for transfers between devices, passed_along(): return lax.ppermute(value, axis, pairs)  47.8 us
    all_to_all x2, waiting for transfers between devices, gathered(): return lax.all_to_all(copies, axis, 0, 0, tiled=True)  43.2 us
    all_to_all x1, blocking collectives, summed_over(): return lax.all_to_all(pieces, axis, 0, 0, tiled=True).sum(axis=0)  37 us
    ppermute x8, starting transfers between devices, passed_along(): return lax.ppermute(value, axis, pairs)  33.2 us
    all_to_all x1, blocking collectives, gathered(): return lax.all_to_all(copies, axis, 0, 0, tiled=True)  24.8 us
    dot_general x8, matrix products, contract_last(): lax.dot_general(left, right, (((1,), (1,)), ((), ())), preferred_element_...  15.7 us
    all_to_all x2, starting transfers between devices, gathered(): return lax.all_to_all(copies, axis, 0, 0, tiled=True)  15 us
    all_to_all x1, starting transfers between devices, summed_over(): return lax.all_to_all(pieces, axis, 0, 0, tiled=True).sum(axis=0)  14.6 us
  transfers between devices with their start and end apart: 11, of which 7 were waited for; matrix products, arithmetic and copies ran while one was open for 10% of the time, Pallas kernels for 0%

profile of v1, /device:TPU:6, one launch (start us, length us, event | category | flops | bytes accessed | tf_op | source)
XLA Modules:
  0.0 268.3 jit_solution(1305230478503203726)
XLA Ops:
  0.6 0.9 copy.28
  1.6 24.8 %all_to_all.25 = bf16[16,24,2,768]{3,1,2,0:T(8,128)(2,1)} all-to-all(bf16[16,24,2,768]{3,1,2,0:T(8,128)(2,1)S(1)} %broadcast_in_dim.7), channel_id=1, replica_groups=mesh['dp'=32,'seq'=16] {'seq'}, dimensions={0} | all-to-all | bytes 2359296 | tf_op jit(solution)/shard_map/all_to_all | solution.py:21
  26.4 2.1 broadcast_in_dim.6
  28.5 5.6 %all-to-all-start = ((bf16[16,2,3,48,384]{4,3,2,1,0:T(8,128)(2,1)}), bf16[16,2,3,48,384]{4,3,2,1,0:T(8,128)(2,1)S(1)}, u32[]{:S(2)}, u32[]{:S(2)}) async-start(bf16[16,2,3,48,384]{4,3,2,1,0:T(8,128)(2,1)} %broadcast_in_dim.6), calls=%async_computation | async-start | bytes 7077888 | tf_op jit(solution)/shard_map/all_to_all | solution.py:21
  34.1 0.9 slice_reduce_fusion.2
  35.0 2.7 fusion.13
  37.7 2.7 %collective-permute-start.1 = (bf16[1,512,768]{2,1,0:T(8,128)(2,1)}, bf16[1,512,768]{2,1,0:T(8,128)(2,1)}, u32[]{:S(2)}, u32[]{:S(2)}) collective-permute-start(bf16[1,512,768]{2,1,0:T(8,128)(2,1)} %fusion.13), channel_id=1, source_target_pairs={{2,0},{3,1},{4,2},{5,3},{6,4},{7,5},{8,6},{9,7},{10,8},{11,9},{12,... | collective-permute-start | bytes 2359304 | tf_op jit(solution)/shard_map/ppermute | solution.py:15
  40.4 5.2 %collective-permute-start = (bf16[1,512,768]{2,1,0:T(8,128)(2,1)}, bf16[1,512,768]{2,1,0:T(8,128)(2,1)}, u32[]{:S(2)}, u32[]{:S(2)}) collective-permute-start(bf16[1,512,768]{2,1,0:T(8,128)(2,1)} %fusion.13), channel_id=1, source_target_pairs={{0,2},{1,3},{2,4},{3,5},{4,6},{5,7},{6,8},{7,9},{8,10},{9,11},{10,... | collective-permute-start | bytes 2359304 | tf_op jit(solution)/shard_map/ppermute | solution.py:15
  47.5 1.1 copy.29
  48.6 31.0 %all-to-all-done = bf16[16,2,3,48,384]{4,3,2,1,0:T(8,128)(2,1)S(1)} async-done(((bf16[16,2,3,48,384]{4,3,2,1,0:T(8,128)(2,1)}), bf16[16,2,3,48,384]{4,3,2,1,0:T(8,128)(2,1)S(1)}, u32[]{:S(2)}, u32[]{:S(2)}) %all-to-all-start) | async-done | bytes 3538976 | tf_op jit(solution)/shard_map/all_to_all | solution.py:21
  80.1 2.3 fusion.75
  82.4 13.7 %collective-permute-done.1 = bf16[1,512,768]{2,1,0:T(8,128)(2,1)} collective-permute-done((bf16[1,512,768]{2,1,0:T(8,128)(2,1)}, bf16[1,512,768]{2,1,0:T(8,128)(2,1)}, u32[]{:S(2)}, u32[]{:S(2)}) %collective-permute-start.1) | collective-permute-done | bytes 786464 | tf_op jit(solution)/shard_map/ppermute | solution.py:15
  96.0 1.7 fusion.73
  97.8 1.9 fusion.42
  99.7 0.7 fusion.2
  100.6 0.6 fusion.102
  101.2 5.3 %collective-permute-start.3 = (bf16[1,512,768]{2,1,0:T(8,128)(2,1)S(1)}, bf16[1,512,768]{2,1,0:T(8,128)(2,1)S(1)}, u32[]{:S(2)}, u32[]{:S(2)}) collective-permute-start(bf16[1,512,768]{2,1,0:T(8,128)(2,1)S(1)} %fusion.102), channel_id=1, source_target_pairs={{4,0},{5,1},{6,2},{7,3},{8,4},{9,5},{10,6},{11,7},{12,8},{13,9},{1... | collective-permute-start | bytes 2359304 | tf_op jit(solution)/shard_map/ppermute | solution.py:15
  106.6 2.9 %collective-permute-start.2 = (bf16[1,512,768]{2,1,0:T(8,128)(2,1)S(1)}, bf16[1,512,768]{2,1,0:T(8,128)(2,1)S(1)}, u32[]{:S(2)}, u32[]{:S(2)}) collective-permute-start(bf16[1,512,768]{2,1,0:T(8,128)(2,1)S(1)} %fusion.102), channel_id=1, source_target_pairs={{0,4},{1,5},{2,6},{3,7},{4,8},{5,9},{6,10},{7,11},{8,12},{9,13},{1... | collective-permute-start | bytes 2359304 | tf_op jit(solution)/shard_map/ppermute | solution.py:15
  110.1 0.8 fusion.101
  111.0 15.0 %collective-permute-done.3 = bf16[1,512,768]{2,1,0:T(8,128)(2,1)S(1)} collective-permute-done((bf16[1,512,768]{2,1,0:T(8,128)(2,1)S(1)}, bf16[1,512,768]{2,1,0:T(8,128)(2,1)S(1)}, u32[]{:S(2)}, u32[]{:S(2)}) %collective-permute-start.3) | collective-permute-done | bytes 786464 | tf_op jit(solution)/shard_map/ppermute | solution.py:15
  126.5 13.5 %collective-permute-done.2 = bf16[1,512,768]{2,1,0:T(8,128)(2,1)S(1)} collective-permute-done((bf16[1,512,768]{2,1,0:T(8,128)(2,1)S(1)}, bf16[1,512,768]{2,1,0:T(8,128)(2,1)S(1)}, u32[]{:S(2)}, u32[]{:S(2)}) %collective-permute-start.2) | collective-permute-done | bytes 786464 | tf_op jit(solution)/shard_map/ppermute | solution.py:15
  140.0 1.6 fusion.66
  141.6 0.9 fusion.58
  142.5 1.9 collective-permute-start.4
  144.5 7.0 %collective-permute-start.5 = (bf16[1,512,384]{2,1,0:T(8,128)(2,1)S(1)}, bf16[1,512,384]{2,1,0:T(8,128)(2,1)}, u32[]{:S(2)}, u32[]{:S(2)}) collective-permute-start(bf16[1,512,384]{2,1,0:T(8,128)(2,1)S(1)} %bitcast.154), channel_id=1, source_target_pairs={{0,4},{1,5},{2,6},{3,7},{4,8},{5,9},{6,10},{7,11},{8,12},{9,13},{1... | collective-permute-start | bytes 1179656 | tf_op jit(solution)/shard_map/ppermute | solution.py:15
  151.5 1.2 copy.33
  153.8 5.7 %collective-permute-done.4 = bf16[1,512,384]{2,1,0:T(8,128)(2,1)} collective-permute-done((bf16[1,512,384]{2,1,0:T(8,128)(2,1)S(1)}, bf16[1,512,384]{2,1,0:T(8,128)(2,1)}, u32[]{:S(2)}, u32[]{:S(2)}) %collective-permute-start.4) | collective-permute-done | bytes 393248 | tf_op jit(solution)/shard_map/ppermute | solution.py:15
  159.5 1.6 fusion.99
  161.1 2.7 %fusion.21 = bf16[512,768]{1,0:T(8,128)(2,1)S(1)} fusion(bf16[1,512,768]{2,1,0:T(8,128)(2,1)S(1)} %copy-done.14, f32[512,768]{1,0:T(8,128)S(1)} %fusion.99, f32[512,768]{1,0:T(8,128)S(1)} %fusion.105, bf16[512,768]{1,0:T(8,128)(2,1)S(1)} %copy-done.18, f32[768]{0:T(1024)S(1)} %get-tuple-element.5, f32[768]{0:T(1024)S(1)} %get-tuple-element.20, ...), kind=kOutput, calls=%fused_computation.33 | convolution fusion | flops 312999936 | bytes 6494208 | tf_op jit(solution)/shard_map/dot_general | solution.py:35
  163.8 0.7 fusion.85
  165.2 37.0 %all_to_all.26 = f32[16,24,2,768]{3,1,2,0:T(8,128)S(1)} all-to-all(f32[16,24,2,768]{3,1,2,0:T(8,128)S(1)} %copy.34), channel_id=1, replica_groups=mesh['dp'=32,'seq'=16] {'seq'}, dimensions={0} | all-to-all | bytes 4718592 | tf_op jit(solution)/shard_map/all_to_all | solution.py:27
  202.2 0.8 reduce_sum.18
  203.0 1.0 copy.36
  204.0 0.9 reshape_reshape.4
  204.9 14.6 %all-to-all-start.3 = ((f32[32,1,1152]{2,1,0:T(1,128)}), f32[32,1,1152]{2,1,0:T(1,128)}, u32[]{:S(2)}, u32[]{:S(2)}) async-start(f32[32,1,1152]{2,1,0:T(1,128)} %reshape_reshape.4), calls=%async_computation.3 | async-start | bytes 294912 | tf_op jit(solution)/shard_map/all_to_all | solution.py:27
  219.4 3.1 %fusion.50 = bf16[512,384]{1,0:T(8,128)(2,1)} fusion(f32[512,384]{1,0:T(8,128)} %copy-done.19, bf16[512,768]{1,0:T(8,128)(2,1)} %copy-done.30, f32[]{:T(128)} %bitcast.7, bf16[384,2,768]{2,0,1:T(8,128)(2,1)S(1)} %bitcast.151, f32[384]{0:T(512)S(1)} %copy-done.23), kind=kOutput, calls=%fused_computation.72 | convolution fusion | flops 307298304 | bytes 2557956 | tf_op jit(solution)/shard_map/dot_general | solution.py:35
  222.6 2.3 collective-permute-start.6
  224.9 5.8 %collective-permute-start.7 = (bf16[1,512,384]{2,1,0:T(8,128)(2,1)}, bf16[1,512,384]{2,1,0:T(8,128)(2,1)}, u32[]{:S(2)}, u32[]{:S(2)}) collective-permute-start(bf16[1,512,384]{2,1,0:T(8,128)(2,1)} %bitcast.29), channel_id=1, source_target_pairs={{0,2},{1,3},{2,4},{3,5},{4,6},{5,7},{6,8},{7,9},{8,10},{9,11},{10,... | collective-permute-start | bytes 1179656 | tf_op jit(solution)/shard_map/ppermute | solution.py:15
  230.7 1.6 fusion.106
  232.3 5.4 %all-to-all-done.3 = f32[32,1,1152]{2,1,0:T(1,128)} async-done(((f32[32,1,1152]{2,1,0:T(1,128)}), f32[32,1,1152]{2,1,0:T(1,128)}, u32[]{:S(2)}, u32[]{:S(2)}) %all-to-all-start.3) | async-done | bytes 147488 | tf_op jit(solution)/shard_map/all_to_all | solution.py:27
  237.7 1.0 reduce_sum.19
  238.7 0.7 broadcast_in_dim.8
  239.4 9.4 %all-to-all-start.4 = ((f32[32,1,1152]{2,1,0:T(1,128)}), f32[32,1,1152]{2,1,0:T(1,128)}, u32[]{:S(2)}, u32[]{:S(2)}) async-start(f32[32,1,1152]{2,1,0:T(1,128)} %broadcast_in_dim.8), calls=%async_computation.4 | async-start | bytes 294912 | tf_op jit(solution)/shard_map/all_to_all | solution.py:21
  248.8 1.7 fusion.93
  250.5 3.5 %fusion.78 = bf16[1,512,768]{2,1,0:T(8,128)(2,1)} fusion(f32[768]{0:T(1024)S(1)} %get-tuple-element.4, f32[768]{0:T(1024)S(1)} %get-tuple-element.21, bf16[1,512,768]{2,1,0:T(8,128)(2,1)S(1)} %copy-done.16, f32[512,768]{1,0:T(8,128)S(1)} %fusion.93, f32[512,768]{1,0:T(8,128)S(1)} %fusion.106, bf16[512,768]{1,0:T(8,128)(2,1)S(1)} %copy-done.31, ...), kind=kOutput, calls=%fused_computation.101 | convolution fusion | flops 312999936 | bytes 6494208 | tf_op jit(solution)/shard_map/dot_general | solution.py:35
  254.1 12.1 %all-to-all-done.4 = f32[32,1,1152]{2,1,0:T(1,128)} async-done(((f32[32,1,1152]{2,1,0:T(1,128)}), f32[32,1,1152]{2,1,0:T(1,128)}, u32[]{:S(2)}, u32[]{:S(2)}) %all-to-all-start.4) | async-done | bytes 147488 | tf_op jit(solution)/shard_map/all_to_all | solution.py:21
  266.2 1.3 multiply_reduce_fusion
  267.5 0.8 mul.355
  (77 shorter events, 4.2 us)
Async XLA Ops:
  1.5 24.9 %copy-start.21 = (bf16[2,3,48,384]{3,2,1,0:T(8,128)(2,1)S(1)}, bf16[2,3,48,384]{3,2,1,0:T(8,128)(2,1)}, u32[]{:S(2)}) copy-start(bf16[2,3,48,384]{3,2,1,0:T(8,128)(2,1)} %param.16) | copy-start | bytes 663556
  28.5 51.2 %all-to-all-start = ((bf16[16,2,3,48,384]{4,3,2,1,0:T(8,128)(2,1)}), bf16[16,2,3,48,384]{4,3,2,1,0:T(8,128)(2,1)S(1)}, u32[]{:S(2)}, u32[]{:S(2)}) async-start(bf16[16,2,3,48,384]{4,3,2,1,0:T(8,128)(2,1)} %broadcast_in_dim.6), calls=%async_computation | async-start | bytes 7077888 | tf_op jit(solution)/shard_map/all_to_all | solution.py:21
  34.1 11.5 %copy-start.29 = (s32[1,2]{1,0:T(1,128)S(1)}, s32[1,2]{1,0:T(1,128)}, u32[]{:S(2)}) copy-start(s32[1,2]{1,0:T(1,128)} %param.11) | copy-start | bytes 28
  34.1 12.8 %copy-start.25 = (f32[2,384]{1,0:T(2,128)S(1)}, f32[2,384]{1,0:T(2,128)}, u32[]{:S(2)}) copy-start(f32[2,384]{1,0:T(2,128)} %param.15) | copy-start | bytes 9220
  34.1 12.8 %copy-start.26 = (f32[2,384]{1,0:T(2,128)S(1)}, f32[2,384]{1,0:T(2,128)}, u32[]{:S(2)}) copy-start(f32[2,384]{1,0:T(2,128)} %param.14) | copy-start | bytes 9220
  34.1 13.4 %copy-start.4 = (bf16[16,24,2,768]{3,1,2,0:T(8,128)(2,1)S(1)}, bf16[16,24,2,768]{3,1,2,0:T(8,128)(2,1)}, u32[]{:S(2)}) copy-start(bf16[16,24,2,768]{3,1,2,0:T(8,128)(2,1)} %all_to_all.25) | copy-start | bytes 3538948
  37.7 58.4 %collective-permute-start.1 = (bf16[1,512,768]{2,1,0:T(8,128)(2,1)}, bf16[1,512,768]{2,1,0:T(8,128)(2,1)}, u32[]{:S(2)}, u32[]{:S(2)}) collective-permute-start(bf16[1,512,768]{2,1,0:T(8,128)(2,1)} %fusion.13), channel_id=1, source_target_pairs={{2,0},{3,1},{4,2},{5,3},{6,4},{7,5},{8,6},{9,7},{10,8},{11,9},{12,... | collective-permute-start | bytes 2359304 | tf_op jit(solution)/shard_map/ppermute | solution.py:15
  40.4 57.4 %collective-permute-start = (bf16[1,512,768]{2,1,0:T(8,128)(2,1)}, bf16[1,512,768]{2,1,0:T(8,128)(2,1)}, u32[]{:S(2)}, u32[]{:S(2)}) collective-permute-start(bf16[1,512,768]{2,1,0:T(8,128)(2,1)} %fusion.13), channel_id=1, source_target_pairs={{0,2},{1,3},{2,4},{3,5},{4,6},{5,7},{6,8},{7,9},{8,10},{9,11},{10,... | collective-permute-start | bytes 2359304 | tf_op jit(solution)/shard_map/ppermute | solution.py:15
  80.0 17.7 %copy-start.2 = (bf16[1,1,16,48,384]{4,3,1,0,2:T(8,128)(2,1)}, bf16[1,1,16,48,384]{4,3,1,0,2:T(8,128)(2,1)S(1)}, u32[]{:S(2)}) copy-start(bf16[1,1,16,48,384]{4,3,1,0,2:T(8,128)(2,1)S(1)} %get-tuple-element.14) | copy-start | bytes 1769476
  80.0 17.7 %copy-start.9 = (bf16[1,1,16,48,384]{4,3,1,0,2:T(8,128)(2,1)}, bf16[1,1,16,48,384]{4,3,1,0,2:T(8,128)(2,1)S(1)}, u32[]{:S(2)}) copy-start(bf16[1,1,16,48,384]{4,3,1,0,2:T(8,128)(2,1)S(1)} %get-tuple-element.13) | copy-start | bytes 1769476
  80.1 17.7 %copy-start = (bf16[1,1,16,48,384]{4,3,1,0,2:T(8,128)(2,1)}, bf16[1,1,16,48,384]{4,3,1,0,2:T(8,128)(2,1)S(1)}, u32[]{:S(2)}) copy-start(bf16[1,1,16,48,384]{4,3,1,0,2:T(8,128)(2,1)S(1)} %get-tuple-element.15) | copy-start | bytes 1769476
  80.1 30.1 %copy-start.7 = (bf16[1,1,16,48,384]{4,3,1,0,2:T(8,128)(2,1)}, bf16[1,1,16,48,384]{4,3,1,0,2:T(8,128)(2,1)S(1)}, u32[]{:S(2)}) copy-start(bf16[1,1,16,48,384]{4,3,1,0,2:T(8,128)(2,1)S(1)} %get-tuple-element.12) | copy-start | bytes 1769476
  80.1 45.9 %copy-start.11 = (bf16[1,1,16,48,384]{4,3,1,0,2:T(8,128)(2,1)}, bf16[1,1,16,48,384]{4,3,1,0,2:T(8,128)(2,1)S(1)}, u32[]{:S(2)}) copy-start(bf16[1,1,16,48,384]{4,3,1,0,2:T(8,128)(2,1)S(1)} %get-tuple-element.11) | copy-start | bytes 1769476
  80.1 59.9 %copy-start.5 = (bf16[1,1,16,48,384]{4,3,1,0,2:T(8,128)(2,1)}, bf16[1,1,16,48,384]{4,3,1,0,2:T(8,128)(2,1)S(1)}, u32[]{:S(2)}) copy-start(bf16[1,1,16,48,384]{4,3,1,0,2:T(8,128)(2,1)S(1)} %get-tuple-element.10) | copy-start | bytes 1769476
  82.4 15.4 %copy-start.22 = (f32[384]{0:T(512)S(1)}, f32[384]{0:T(512)}, u32[]{:S(2)}) copy-start(f32[384]{0:T(512)} %get-tuple-element.22) | copy-start | bytes 4612
  82.4 15.4 %copy-start.24 = (f32[384]{0:T(512)S(1)}, f32[384]{0:T(512)}, u32[]{:S(2)}) copy-start(f32[384]{0:T(512)} %get-tuple-element.9) | copy-start | bytes 4612
  97.8 1.9 copy-start.13
  97.8 1.9 copy-start.15
  99.7 0.9 copy-start.19
  100.6 10.4 %copy-start.17 = (bf16[512,768]{1,0:T(8,128)(2,1)}, bf16[512,768]{1,0:T(8,128)(2,1)S(1)}, u32[]{:S(2)}) copy-start(bf16[512,768]{1,0:T(8,128)(2,1)S(1)} %fusion.2) | copy-start | bytes 2359300
  101.2 24.7 %collective-permute-start.3 = (bf16[1,512,768]{2,1,0:T(8,128)(2,1)S(1)}, bf16[1,512,768]{2,1,0:T(8,128)(2,1)S(1)}, u32[]{:S(2)}, u32[]{:S(2)}) collective-permute-start(bf16[1,512,768]{2,1,0:T(8,128)(2,1)S(1)} %fusion.102), channel_id=1, source_target_pairs={{4,0},{5,1},{6,2},{7,3},{8,4},{9,5},{10,6},{11,7},{12,8},{13,9},{1... | collective-permute-start | bytes 2359304 | tf_op jit(solution)/shard_map/ppermute | solution.py:15
  106.6 33.4 %collective-permute-start.2 = (bf16[1,512,768]{2,1,0:T(8,128)(2,1)S(1)}, bf16[1,512,768]{2,1,0:T(8,128)(2,1)S(1)}, u32[]{:S(2)}, u32[]{:S(2)}) collective-permute-start(bf16[1,512,768]{2,1,0:T(8,128)(2,1)S(1)} %fusion.102), channel_id=1, source_target_pairs={{0,4},{1,5},{2,6},{3,7},{4,8},{5,9},{6,10},{7,11},{8,12},{9,13},{1... | collective-permute-start | bytes 2359304 | tf_op jit(solution)/shard_map/ppermute | solution.py:15
  110.9 29.1 %copy-start.27 = (f32[384]{0:T(512)S(1)}, f32[384]{0:T(512)}, u32[]{:S(2)}) copy-start(f32[384]{0:T(512)} %get-tuple-element.23) | copy-start | bytes 4612
  111.0 29.1 %copy-start.28 = (f32[384]{0:T(512)S(1)}, f32[384]{0:T(512)}, u32[]{:S(2)}) copy-start(f32[384]{0:T(512)} %get-tuple-element.8) | copy-start | bytes 4612
  140.0 1.6 copy-start.14
  141.6 11.0 %copy-start.8 = (bf16[1,1,16,48,384]{4,3,1,0,2:T(8,128)(2,1)S(1)}, bf16[1,1,16,48,384]{4,3,1,0,2:T(8,128)(2,1)}, u32[]{:S(2)}) copy-start(bf16[1,1,16,48,384]{4,3,1,0,2:T(8,128)(2,1)} %copy-done.7) | copy-start | bytes 1769476
  142.5 16.9 %collective-permute-start.4 = (bf16[1,512,384]{2,1,0:T(8,128)(2,1)S(1)}, bf16[1,512,384]{2,1,0:T(8,128)(2,1)}, u32[]{:S(2)}, u32[]{:S(2)}) collective-permute-start(bf16[1,512,384]{2,1,0:T(8,128)(2,1)S(1)} %bitcast.153), channel_id=1, source_target_pairs={{4,0},{5,1},{6,2},{7,3},{8,4},{9,5},{10,6},{11,7},{12,8},{13,9},{1... | collective-permute-start | bytes 1179656 | tf_op jit(solution)/shard_map/ppermute | solution.py:15
  144.5 16.6 %collective-permute-start.5 = (bf16[1,512,384]{2,1,0:T(8,128)(2,1)S(1)}, bf16[1,512,384]{2,1,0:T(8,128)(2,1)}, u32[]{:S(2)}, u32[]{:S(2)}) collective-permute-start(bf16[1,512,384]{2,1,0:T(8,128)(2,1)S(1)} %bitcast.154), channel_id=1, source_target_pairs={{0,4},{1,5},{2,6},{3,7},{4,8},{5,9},{6,10},{7,11},{8,12},{9,13},{1... | collective-permute-start | bytes 1179656 | tf_op jit(solution)/shard_map/ppermute | solution.py:15
  153.2 6.2 %copy-start.6 = (bf16[1,1,16,48,384]{4,3,1,0,2:T(8,128)(2,1)S(1)}, bf16[1,1,16,48,384]{4,3,1,0,2:T(8,128)(2,1)}, u32[]{:S(2)}) copy-start(bf16[1,1,16,48,384]{4,3,1,0,2:T(8,128)(2,1)} %copy-done.5) | copy-start | bytes 1769476
  153.7 7.4 %copy-start.12 = (bf16[1,1,16,48,384]{4,3,1,0,2:T(8,128)(2,1)S(1)}, bf16[1,1,16,48,384]{4,3,1,0,2:T(8,128)(2,1)}, u32[]{:S(2)}) copy-start(bf16[1,1,16,48,384]{4,3,1,0,2:T(8,128)(2,1)} %copy-done.11) | copy-start | bytes 1769476
  153.7 7.4 %copy-start.18 = (bf16[512,768]{1,0:T(8,128)(2,1)S(1)}, bf16[512,768]{1,0:T(8,128)(2,1)}, u32[]{:S(2)}) copy-start(bf16[512,768]{1,0:T(8,128)(2,1)} %copy-done.17) | copy-start | bytes 2359300
  161.1 2.7 %copy-start.20 = (f32[512,384]{1,0:T(8,128)S(1)}, f32[512,384]{1,0:T(8,128)}, u32[]{:S(2)}) copy-start(f32[512,384]{1,0:T(8,128)} %copy-done.19) | copy-start | bytes 2359300
  163.8 0.9 copy-start.30
  202.2 17.2 %copy-start.23 = (f32[384]{0:T(512)S(1)}, f32[384]{0:T(512)}, u32[]{:S(2)}) copy-start(f32[384]{0:T(512)} %get-tuple-element.22) | copy-start | bytes 4612
  204.9 32.8 %all-to-all-start.3 = ((f32[32,1,1152]{2,1,0:T(1,128)}), f32[32,1,1152]{2,1,0:T(1,128)}, u32[]{:S(2)}, u32[]{:S(2)}) async-start(f32[32,1,1152]{2,1,0:T(1,128)} %reshape_reshape.4), calls=%async_computation.3 | async-start | bytes 294912 | tf_op jit(solution)/shard_map/all_to_all | solution.py:27
  219.4 11.2 %copy-start.3 = (bf16[1,1,16,48,384]{4,3,1,0,2:T(8,128)(2,1)S(1)}, bf16[1,1,16,48,384]{4,3,1,0,2:T(8,128)(2,1)}, u32[]{:S(2)}) copy-start(bf16[1,1,16,48,384]{4,3,1,0,2:T(8,128)(2,1)} %copy-done.2) | copy-start | bytes 1769476
  222.6 26.3 %copy-start.1 = (bf16[1,1,16,48,384]{4,3,1,0,2:T(8,128)(2,1)S(1)}, bf16[1,1,16,48,384]{4,3,1,0,2:T(8,128)(2,1)}, u32[]{:S(2)}) copy-start(bf16[1,1,16,48,384]{4,3,1,0,2:T(8,128)(2,1)} %copy-done) | copy-start | bytes 1769476
  222.6 26.2 %collective-permute-start.6 = (bf16[1,512,384]{2,1,0:T(8,128)(2,1)}, bf16[1,512,384]{2,1,0:T(8,128)(2,1)}, u32[]{:S(2)}, u32[]{:S(2)}) collective-permute-start(bf16[1,512,384]{2,1,0:T(8,128)(2,1)} %bitcast.29), channel_id=1, source_target_pairs={{2,0},{3,1},{4,2},{5,3},{6,4},{7,5},{8,6},{9,7},{10,8},{11,9},{12,... | collective-permute-start | bytes 1179656 | tf_op jit(solution)/shard_map/ppermute | solution.py:15
  224.9 25.6 %collective-permute-start.7 = (bf16[1,512,384]{2,1,0:T(8,128)(2,1)}, bf16[1,512,384]{2,1,0:T(8,128)(2,1)}, u32[]{:S(2)}, u32[]{:S(2)}) collective-permute-start(bf16[1,512,384]{2,1,0:T(8,128)(2,1)} %bitcast.29), channel_id=1, source_target_pairs={{0,2},{1,3},{2,4},{3,5},{4,6},{5,7},{6,8},{7,9},{8,10},{9,11},{10,... | collective-permute-start | bytes 1179656 | tf_op jit(solution)/shard_map/ppermute | solution.py:15
  232.3 18.2 %copy-start.10 = (bf16[1,1,16,48,384]{4,3,1,0,2:T(8,128)(2,1)S(1)}, bf16[1,1,16,48,384]{4,3,1,0,2:T(8,128)(2,1)}, u32[]{:S(2)}) copy-start(bf16[1,1,16,48,384]{4,3,1,0,2:T(8,128)(2,1)} %copy-done.9) | copy-start | bytes 1769476
  232.3 18.2 %copy-start.16 = (bf16[1,512,768]{2,1,0:T(8,128)(2,1)S(1)}, bf16[1,512,768]{2,1,0:T(8,128)(2,1)}, u32[]{:S(2)}) copy-start(bf16[1,512,768]{2,1,0:T(8,128)(2,1)} %param.9) | copy-start | bytes 2359300
  239.4 26.8 %all-to-all-start.4 = ((f32[32,1,1152]{2,1,0:T(1,128)}), f32[32,1,1152]{2,1,0:T(1,128)}, u32[]{:S(2)}, u32[]{:S(2)}) async-start(f32[32,1,1152]{2,1,0:T(1,128)} %broadcast_in_dim.8), calls=%async_computation.4 | async-start | bytes 294912 | tf_op jit(solution)/shard_map/all_to_all | solution.py:21
  248.8 1.7 copy-start.31

commit v2 on v1

--- a/solution.py
+++ b/solution.py
@@ -21,10 +21,18 @@
     return lax.all_to_all(copies, axis, 0, 0, tiled=True)
 
 
-def summed_over(value, axis):
+def summed_over(value, axis, sent_as=jnp.float32):
     peers = lax.axis_size(axis)
-    pieces = value.reshape((peers, -1) + value.shape[1:])
-    return lax.all_to_all(pieces, axis, 0, 0, tiled=True).sum(axis=0)
+    pieces = value.reshape((peers, -1) + value.shape[1:]).astype(sent_as)
+    arrived = lax.all_to_all(pieces, axis, 0, 0, tiled=True)
+    return arrived.astype(jnp.float32).sum(axis=0)
+
+
+def reduced_term(term):
+    shared_part = summed_over(term, "seq", jnp.bfloat16)
+    dp_size = lax.axis_size("dp")
+    own_piece = summed_over(shared_part.reshape(dp_size, -1), "dp")
+    return gathered(own_piece, "dp").reshape(shared_part.shape)
 
 
 def gelu_tanh(values):
@@ -93,11 +101,16 @@
 ):
     position_list = sequence_in.shape[1]
     channels = sequence_in.shape[2]
-    point_full = gathered(point_weight, "seq").reshape(-1, *point_weight.shape[1:])
-    conv_parts = gathered(conv_weight, "seq")
-    conv_full = jnp.moveaxis(conv_parts, 0, 2).reshape(
-        conv_weight.shape[0], conv_weight.shape[1], -1, conv_weight.shape[3]
-    )
+    def conv_gathered(shard):
+        return jnp.moveaxis(gathered(shard, "seq"), 0, 1).reshape(
+            conv_weight.shape[1], -1, conv_weight.shape[3]
+        )
+
+    first_conv = conv_gathered(conv_weight[0])
+    point_shard, first_conv = lax.optimization_barrier((point_weight, first_conv))
+    point_full = gathered(point_shard, "seq").reshape(-1, *point_weight.shape[1:])
+    second_shard, point_full = lax.optimization_barrier((conv_weight[1], point_full))
+    conv_full = [first_conv, conv_gathered(second_shard)]
     neighbour_reach = (FIRST_DILATION // position_list, SECOND_DILATION // position_list)
     state = sequence_in.reshape(-1, channels)
     total_rows = state.shape[0]
@@ -126,15 +139,13 @@
         middle, hidden_act, state = forward_local(*operands)
         saved.append((normed, middle, hidden_act, kept_flag))
     gradient = output_grad.reshape(-1, channels)
-    hidden_saved = [None, None]
-    branch_saved = [None, None]
+    reduced_terms = [None, None]
     for block_index in (1, 0):
         normed, middle, hidden_act, kept_flag = saved[block_index]
         projection = point_full[:, block_index, :]
         first_operands = (gradient, middle, projection, mid_gain[block_index], kept_flag)
         conv_grad, branch_grad = backward_first(*first_operands)
-        hidden_saved[block_index] = hidden_act
-        branch_saved[block_index] = branch_grad
+        reduced_terms[block_index] = reduced_term(grad_rows(hidden_act, branch_grad))
         earlier, later = neighbours(
             conv_grad.reshape(sequence_in.shape[0], position_list, -1), neighbour_reach[block_index]
         )
@@ -151,12 +162,7 @@
             in_gain[block_index],
         )
         gradient = backward_second(*second_operands)
-    first_term = grad_rows(hidden_saved[0], branch_saved[0])
-    second_term = grad_rows(hidden_saved[1], branch_saved[1])
-    shared_part = summed_over(jnp.stack([first_term, second_term], axis=1), "seq")
-    dp_size = lax.axis_size("dp")
-    own_piece = summed_over(shared_part.reshape(dp_size, -1), "dp")
-    summed = gathered(own_piece, "dp").reshape(shared_part.shape)
+    summed = jnp.stack([reduced_terms[0], reduced_terms[1]], axis=1)
     sample_count = sequence_in.shape[0] * lax.axis_size("dp")
     full_length = position_list * lax.axis_size("seq")
     point_grad = summed * (1.0 / math.sqrt(sample_count * full_length))

time: 269 us -> 272 us (1.011)
  blocking collectives: 61.8 us -> 30.2 us
  starting transfers between devices: 62.7 us -> 89 us
  matrix products: 26.3 us -> 36.7 us
    all_to_all x1 -> x0, blocking collectives: 37 us -> none  [summed_over(): return lax.all_to_all(pieces, axis, 0, 0, tiled=True).sum(axis=0)]
    all_to_all x1 -> x4, waiting for transfers between devices: 5.37 us -> 29.2 us  [summed_over(): arrived = lax.all_to_all(pieces, axis, 0, 0, tiled=True)]
    all_to_all x1 -> x4, starting transfers between devices: 14.6 us -> 36.2 us  [summed_over(): arrived = lax.all_to_all(pieces, axis, 0, 0, tiled=True)]
    all_to_all x2 -> x4, waiting for transfers between devices: 43.2 us -> 26 us  [gathered(): return lax.all_to_all(copies, axis, 0, 0, tiled=True)]
    ppermute x8, waiting for transfers between devices: 47.8 us -> 39.5 us  [passed_along(): return lax.ppermute(value, axis, pairs)]
    dot_general x8, matrix products: 15.7 us -> 21.2 us  [contract_last(): lax.dot_general(left, right, (((1,), (1,)), ((), ())), preferred_element_...]
    all_to_all x1, blocking collectives: 24.8 us -> 30.2 us  [gathered(): return lax.all_to_all(copies, axis, 0, 0, tiled=True)]
    all_to_all x2 -> x4, starting transfers between devices: 15 us -> 19.9 us  [gathered(): return lax.all_to_all(copies, axis, 0, 0, tiled=True)]
  transfers between devices with their start and end apart: 11 -> 16, of which waited for: 7 -> 10; matrix products, arithmetic and copies ran while one was open for 10% -> 17% of each run, Pallas kernels for 0% -> 0%
where the time goes in v2:
time: 272 us; the launch traced here: 270 us
  waiting for transfers between devices  94.6 us (35%)
  starting transfers between devices  89 us (33%)
  matrix products  36.7 us (13%)
  blocking collectives  30.2 us (11%)
  local copies, waits for them, and re-layouts  12.3 us (5%)
  other arithmetic  4.88 us (2%)
    ppermute x8, waiting for transfers between devices, passed_along(): return lax.ppermute(value, axis, pairs)  39.5 us
    all_to_all x4, starting transfers between devices, summed_over(): arrived = lax.all_to_all(pieces, axis, 0, 0, tiled=True)  36.2 us
    ppermute x8, starting transfers between devices, passed_along(): return lax.ppermute(value, axis, pairs)  32.8 us
    all_to_all x1, blocking collectives, gathered(): return lax.all_to_all(copies, axis, 0, 0, tiled=True)  30.2 us
    all_to_all x4, waiting for transfers between devices, summed_over(): arrived = lax.all_to_all(pieces, axis, 0, 0, tiled=True)  29.2 us
    all_to_all x4, waiting for transfers between devices, gathered(): return lax.all_to_all(copies, axis, 0, 0, tiled=True)  26 us
    dot_general x8, matrix products, contract_last(): lax.dot_general(left, right, (((1,), (1,)), ((), ())), preferred_element_...  21.2 us
    all_to_all x4, starting transfers between devices, gathered(): return lax.all_to_all(copies, axis, 0, 0, tiled=True)  19.9 us
  transfers between devices with their start and end apart: 16, of which 10 were waited for; matrix products, arithmetic and copies ran while one was open for 17% of the time, Pallas kernels for 0%

profile of v2, /device:TPU:6, one launch (start us, length us, event | category | flops | bytes accessed | tf_op | source)
XLA Modules:
  0.0 270.2 jit_solution(12178221628080654745)
XLA Ops:
  0.6 1.0 slice_bitcast_fusion.1
  1.8 30.2 %all_to_all.45 = bf16[16,3,48,384]{3,2,1,0:T(8,128)(2,1)S(1)} all-to-all(bf16[16,3,48,384]{3,2,1,0:T(8,128)(2,1)S(1)} %broadcast_in_dim.13), channel_id=1, replica_groups=mesh['dp'=32,'seq'=16] {'seq'}, dimensions={0} | all-to-all | bytes 3538944 | tf_op jit(solution)/shard_map/all_to_all | solution.py:21
  32.9 1.1 broadcast_in_dim.14
  34.0 5.9 %all-to-all-start.1 = ((bf16[16,24,2,768]{3,1,2,0:T(8,128)(2,1)}), bf16[16,24,2,768]{3,1,2,0:T(8,128)(2,1)S(1)}, u32[]{:S(2)}, u32[]{:S(2)}) async-start(bf16[16,24,2,768]{3,1,2,0:T(8,128)(2,1)} %broadcast_in_dim.14), calls=%async_computation.1 | async-start | bytes 2359296 | tf_op jit(solution)/shard_map/all_to_all | solution.py:21
  39.9 2.7 fusion.13
  42.6 2.7 %collective-permute-start.1 = (bf16[1,512,768]{2,1,0:T(8,128)(2,1)}, bf16[1,512,768]{2,1,0:T(8,128)(2,1)}, u32[]{:S(2)}, u32[]{:S(2)}) collective-permute-start(bf16[1,512,768]{2,1,0:T(8,128)(2,1)} %fusion.13), channel_id=1, source_target_pairs={{2,0},{3,1},{4,2},{5,3},{6,4},{7,5},{8,6},{9,7},{10,8},{11,9},{12,... | collective-permute-start | bytes 2359304 | tf_op jit(solution)/shard_map/ppermute | solution.py:15
  45.4 5.2 %collective-permute-start = (bf16[1,512,768]{2,1,0:T(8,128)(2,1)}, bf16[1,512,768]{2,1,0:T(8,128)(2,1)}, u32[]{:S(2)}, u32[]{:S(2)}) collective-permute-start(bf16[1,512,768]{2,1,0:T(8,128)(2,1)} %fusion.13), channel_id=1, source_target_pairs={{0,2},{1,3},{2,4},{3,5},{4,6},{5,7},{6,8},{7,9},{8,10},{9,11},{10,... | collective-permute-start | bytes 2359304 | tf_op jit(solution)/shard_map/ppermute | solution.py:15
  52.5 2.6 fusion.75
  55.1 1.1 copy.23
  56.3 1.4 broadcast_in_dim.15
  57.6 6.3 %all-to-all-start.2 = ((bf16[16,3,48,384]{3,2,1,0:T(8,128)(2,1)}), bf16[16,3,48,384]{3,2,1,0:T(8,128)(2,1)S(1)}, u32[]{:S(2)}, u32[]{:S(2)}) async-start(bf16[16,3,48,384]{3,2,1,0:T(8,128)(2,1)} %broadcast_in_dim.15), calls=%async_computation.2 | async-start | bytes 3538944 | tf_op jit(solution)/shard_map/all_to_all | solution.py:21
  64.0 9.5 %collective-permute-done.1 = bf16[1,512,768]{2,1,0:T(8,128)(2,1)} collective-permute-done((bf16[1,512,768]{2,1,0:T(8,128)(2,1)}, bf16[1,512,768]{2,1,0:T(8,128)(2,1)}, u32[]{:S(2)}, u32[]{:S(2)}) %collective-permute-start.1) | collective-permute-done | bytes 786464 | tf_op jit(solution)/shard_map/ppermute | solution.py:15
  73.4 1.7 fusion.73
  75.2 1.9 fusion.42
  78.0 1.5 fusion.120
  79.5 2.6 collective-permute-start.3
  82.8 5.7 %collective-permute-start.2 = (bf16[1,512,768]{2,1,0:T(8,128)(2,1)}, bf16[1,512,768]{2,1,0:T(8,128)(2,1)}, u32[]{:S(2)}, u32[]{:S(2)}) collective-permute-start(bf16[1,512,768]{2,1,0:T(8,128)(2,1)} %fusion.120), channel_id=1, source_target_pairs={{0,4},{1,5},{2,6},{3,7},{4,8},{5,9},{6,10},{7,11},{8,12},{9,13},{1... | collective-permute-start | bytes 2359304 | tf_op jit(solution)/shard_map/ppermute | solution.py:15
  88.4 2.7 %all-to-all-done.2 = bf16[16,3,48,384]{3,2,1,0:T(8,128)(2,1)S(1)} async-done(((bf16[16,3,48,384]{3,2,1,0:T(8,128)(2,1)}), bf16[16,3,48,384]{3,2,1,0:T(8,128)(2,1)S(1)}, u32[]{:S(2)}, u32[]{:S(2)}) %all-to-all-start.2) | async-done | bytes 1769504 | tf_op jit(solution)/shard_map/all_to_all | solution.py:21
  91.4 19.6 %collective-permute-done.3 = bf16[1,512,768]{2,1,0:T(8,128)(2,1)} collective-permute-done((bf16[1,512,768]{2,1,0:T(8,128)(2,1)}, bf16[1,512,768]{2,1,0:T(8,128)(2,1)}, u32[]{:S(2)}, u32[]{:S(2)}) %collective-permute-start.3) | collective-permute-done | bytes 786464 | tf_op jit(solution)/shard_map/ppermute | solution.py:15
  110.9 1.7 fusion.68
  113.5 10.4 %collective-permute-done.2 = bf16[1,512,768]{2,1,0:T(8,128)(2,1)} collective-permute-done((bf16[1,512,768]{2,1,0:T(8,128)(2,1)}, bf16[1,512,768]{2,1,0:T(8,128)(2,1)}, u32[]{:S(2)}, u32[]{:S(2)}) %collective-permute-start.2) | collective-permute-done | bytes 786464 | tf_op jit(solution)/shard_map/ppermute | solution.py:15
  123.9 2.1 fusion.66
  126.1 1.7 fusion.58
  127.8 1.9 collective-permute-start.4
  129.7 2.8 %fusion.123 = f32[512,768]{1,0:T(8,128)} fusion(bf16[512,384]{1,0:T(8,128)(2,1)} %fusion.58, bf16[768,384]{1,0:T(8,128)(2,1)S(1)} %bitcast.157), kind=kOutput, calls=%fused_computation.147 | convolution fusion | flops 301989888 | bytes 2555904 | tf_op jit(solution)/shard_map/dot_general | solution.py:43
  132.5 6.8 %collective-permute-start.5 = (bf16[1,512,384]{2,1,0:T(8,128)(2,1)}, bf16[1,512,384]{2,1,0:T(8,128)(2,1)}, u32[]{:S(2)}, u32[]{:S(2)}) collective-permute-start(bf16[1,512,384]{2,1,0:T(8,128)(2,1)} %bitcast.25), channel_id=1, source_target_pairs={{0,4},{1,5},{2,6},{3,7},{4,8},{5,9},{6,10},{7,11},{8,12},{9,13},{1... | collective-permute-start | bytes 1179656 | tf_op jit(solution)/shard_map/ppermute | solution.py:15
  139.5 2.5 convolution_convert_fusion
  142.0 6.2 %all-to-all-start.6 = ((bf16[16,24,768]{2,1,0:T(8,128)(2,1)}), bf16[16,24,768]{2,1,0:T(8,128)(2,1)S(1)}, u32[]{:S(2)}, u32[]{:S(2)}) async-start(bf16[16,24,768]{2,1,0:T(8,128)(2,1)} %convolution_convert_fusion), calls=%async_computation.6 | async-start | bytes 1179648 | tf_op jit(solution)/shard_map/all_to_all | solution.py:27
  148.3 1.7 fusion.117
  150.1 3.0 %fusion.21 = bf16[512,768]{1,0:T(8,128)(2,1)S(1)} fusion(bf16[1,512,768]{2,1,0:T(8,128)(2,1)} %param.10, f32[512,768]{1,0:T(8,128)S(1)} %fusion.117, f32[512,768]{1,0:T(8,128)S(1)} %copy-done.5, bf16[512,768]{1,0:T(8,128)(2,1)S(1)} %copy-done.11, f32[768]{0:T(1024)S(1)} %get-tuple-element.17, f32[768]{0:T(1024)S(1)} %get-tuple-element.31, ...), kind=kOutput, calls=%fused_computation.32 | convolution fusion | flops 312999936 | bytes 6494208 | tf_op jit(solution)/shard_map/dot_general | solution.py:43
  153.9 1.5 convolution_convert_fusion.1
  155.5 2.9 %all-to-all-done.6 = bf16[16,24,768]{2,1,0:T(8,128)(2,1)S(1)} async-done(((bf16[16,24,768]{2,1,0:T(8,128)(2,1)}), bf16[16,24,768]{2,1,0:T(8,128)(2,1)S(1)}, u32[]{:S(2)}, u32[]{:S(2)}) %all-to-all-start.6) | async-done | bytes 589856 | tf_op jit(solution)/shard_map/all_to_all | solution.py:27
  158.4 4.9 %all-to-all-start.3 = ((bf16[16,24,768]{2,1,0:T(8,128)(2,1)}), bf16[16,24,768]{2,1,0:T(8,128)(2,1)S(1)}, u32[]{:S(2)}, u32[]{:S(2)}) async-start(bf16[16,24,768]{2,1,0:T(8,128)(2,1)} %bitcast.28), calls=%async_computation.3 | async-start | bytes 1179648 | tf_op jit(solution)/shard_map/all_to_all | solution.py:27
  164.1 7.9 %all-to-all-done.3 = bf16[16,24,768]{2,1,0:T(8,128)(2,1)S(1)} async-done(((bf16[16,24,768]{2,1,0:T(8,128)(2,1)}), bf16[16,24,768]{2,1,0:T(8,128)(2,1)S(1)}, u32[]{:S(2)}, u32[]{:S(2)}) %all-to-all-start.3) | async-done | bytes 589856 | tf_op jit(solution)/shard_map/all_to_all | solution.py:27
  172.0 15.0 %all-to-all-start.7 = ((f32[32,1,576]{2,1,0:T(1,128)}), f32[32,1,576]{2,1,0:T(1,128)S(1)}, u32[]{:S(2)}, u32[]{:S(2)}) async-start(f32[32,1,576]{2,1,0:T(1,128)} %reshape_reshape.7), calls=%async_computation.7 | async-start | bytes 163840 | tf_op jit(solution)/shard_map/all_to_all | solution.py:27
  187.1 3.2 %fusion.50 = bf16[512,384]{1,0:T(8,128)(2,1)} fusion(f32[512,384]{1,0:T(8,128)} %copy-done.12, bf16[512,768]{1,0:T(8,128)(2,1)} %copy-done.26, f32[]{:T(128)} %bitcast.9, bf16[384,2,768]{2,0,1:T(8,128)(2,1)} %bitcast.160, f32[384]{0:T(512)S(1)} %copy-done.16), kind=kOutput, calls=%fused_computation.74 | convolution fusion | flops 307298304 | bytes 2557952 | tf_op jit(solution)/shard_map/dot_general | solution.py:43
  190.3 2.3 collective-permute-start.6
  192.6 5.7 %collective-permute-start.7 = (bf16[1,512,384]{2,1,0:T(8,128)(2,1)}, bf16[1,512,384]{2,1,0:T(8,128)(2,1)}, u32[]{:S(2)}, u32[]{:S(2)}) collective-permute-start(bf16[1,512,384]{2,1,0:T(8,128)(2,1)} %bitcast.32), channel_id=1, source_target_pairs={{0,2},{1,3},{2,4},{3,5},{4,6},{5,7},{6,8},{7,9},{8,10},{9,11},{10,... | collective-permute-start | bytes 1179656 | tf_op jit(solution)/shard_map/ppermute | solution.py:15
  199.1 4.6 %all-to-all-done.7 = f32[32,1,576]{2,1,0:T(1,128)S(1)} async-done(((f32[32,1,576]{2,1,0:T(1,128)}), f32[32,1,576]{2,1,0:T(1,128)S(1)}, u32[]{:S(2)}, u32[]{:S(2)}) %all-to-all-start.7) | async-done | bytes 73760 | tf_op jit(solution)/shard_map/all_to_all | solution.py:27
  203.7 10.0 %all-to-all-start.4 = ((f32[32,1,576]{2,1,0:T(1,128)}), f32[32,1,576]{2,1,0:T(1,128)S(1)}, u32[]{:S(2)}, u32[]{:S(2)}) async-start(f32[32,1,576]{2,1,0:T(1,128)} %reshape_reshape.6), calls=%async_computation.4 | async-start | bytes 163840 | tf_op jit(solution)/shard_map/all_to_all | solution.py:27
  213.7 1.6 fusion.96
  215.4 13.9 %all-to-all-done.4 = f32[32,1,576]{2,1,0:T(1,128)S(1)} async-done(((f32[32,1,576]{2,1,0:T(1,128)}), f32[32,1,576]{2,1,0:T(1,128)S(1)}, u32[]{:S(2)}, u32[]{:S(2)}) %all-to-all-start.4) | async-done | bytes 73760 | tf_op jit(solution)/shard_map/all_to_all | solution.py:27
  229.9 3.9 %all-to-all-start.8 = ((f32[32,1,576]{2,1,0:T(1,128)}), f32[32,1,576]{2,1,0:T(1,128)S(1)}, u32[]{:S(2)}, u32[]{:S(2)}) async-start(f32[32,1,576]{2,1,0:T(1,128)} %broadcast_in_dim.17), calls=%async_computation.8 | async-start | bytes 163840 | tf_op jit(solution)/shard_map/all_to_all | solution.py:21
  233.8 2.7 %fusion.99 = f32[512,768]{1,0:T(8,128)} fusion(bf16[3,768,384]{2,1,0:T(8,128)(2,1)S(1)} %bitcast.151, bf16[1,512,384]{2,1,0:T(8,128)(2,1)} %collective-permute-done.6), kind=kOutput, calls=%fused_computation.114 | convolution fusion | flops 301989888 | bytes 2555904 | tf_op jit(solution)/shard_map/dot_general | solution.py:43
  236.6 12.6 %all-to-all-done.8 = f32[32,1,576]{2,1,0:T(1,128)S(1)} async-done(((f32[32,1,576]{2,1,0:T(1,128)}), f32[32,1,576]{2,1,0:T(1,128)S(1)}, u32[]{:S(2)}, u32[]{:S(2)}) %all-to-all-start.8) | async-done | bytes 73760 | tf_op jit(solution)/shard_map/all_to_all | solution.py:21
  249.9 3.9 %all-to-all-start.5 = ((f32[32,1,576]{2,1,0:T(1,128)}), f32[32,1,576]{2,1,0:T(1,128)S(1)}, u32[]{:S(2)}, u32[]{:S(2)}) async-start(f32[32,1,576]{2,1,0:T(1,128)} %broadcast_in_dim.16), calls=%async_computation.5 | async-start | bytes 163840 | tf_op jit(solution)/shard_map/all_to_all | solution.py:21
  253.8 4.5 %fusion.78 = bf16[1,512,768]{2,1,0:T(8,128)(2,1)} fusion(f32[768]{0:T(1024)S(1)} %get-tuple-element.16, f32[768]{0:T(1024)S(1)} %get-tuple-element.32, bf16[1,512,768]{2,1,0:T(8,128)(2,1)} %param.9, f32[512,768]{1,0:T(8,128)} %fusion.99, f32[512,768]{1,0:T(8,128)S(1)} %fusion.96, bf16[512,768]{1,0:T(8,128)(2,1)} %copy-done.26, ...), kind=kOutput, calls=%fused_computation.103 | convolution fusion | flops 312999936 | bytes 6496256 | tf_op jit(solution)/shard_map/dot_general | solution.py:43
  258.5 10.6 %all-to-all-done.5 = f32[32,1,576]{2,1,0:T(1,128)S(1)} async-done(((f32[32,1,576]{2,1,0:T(1,128)}), f32[32,1,576]{2,1,0:T(1,128)S(1)}, u32[]{:S(2)}, u32[]{:S(2)}) %all-to-all-start.5) | async-done | bytes 73760 | tf_op jit(solution)/shard_map/all_to_all | solution.py:21
  (84 shorter events, 9.9 us)
Async XLA Ops:
  32.0 0.9 copy-start.14
  32.9 7.0 %copy-start.18 = (f32[2,768]{1,0:T(2,128)S(1)}, f32[2,768]{1,0:T(2,128)}, u32[]{:S(2)}) copy-start(f32[2,768]{1,0:T(2,128)} %param.13) | copy-start | bytes 18436
  32.9 7.0 %copy-start.19 = (f32[2,768]{1,0:T(2,128)S(1)}, f32[2,768]{1,0:T(2,128)}, u32[]{:S(2)}) copy-start(f32[2,768]{1,0:T(2,128)} %param.12) | copy-start | bytes 18436
  34.0 16.6 %copy-start.24 = (s32[1,2]{1,0:T(1,128)S(1)}, s32[1,2]{1,0:T(1,128)}, u32[]{:S(2)}) copy-start(s32[1,2]{1,0:T(1,128)} %param.11) | copy-start | bytes 28
  34.0 17.9 %copy-start.20 = (f32[2,384]{1,0:T(2,128)S(1)}, f32[2,384]{1,0:T(2,128)}, u32[]{:S(2)}) copy-start(f32[2,384]{1,0:T(2,128)} %param.15) | copy-start | bytes 9220
  34.0 17.9 %copy-start.21 = (f32[2,384]{1,0:T(2,128)S(1)}, f32[2,384]{1,0:T(2,128)}, u32[]{:S(2)}) copy-start(f32[2,384]{1,0:T(2,128)} %param.14) | copy-start | bytes 9220
  34.0 21.1 %all-to-all-start.1 = ((bf16[16,24,2,768]{3,1,2,0:T(8,128)(2,1)}), bf16[16,24,2,768]{3,1,2,0:T(8,128)(2,1)S(1)}, u32[]{:S(2)}, u32[]{:S(2)}) async-start(bf16[16,24,2,768]{3,1,2,0:T(8,128)(2,1)} %broadcast_in_dim.14), calls=%async_computation.1 | async-start | bytes 2359296 | tf_op jit(solution)/shard_map/all_to_all | solution.py:21
  42.6 30.8 %collective-permute-start.1 = (bf16[1,512,768]{2,1,0:T(8,128)(2,1)}, bf16[1,512,768]{2,1,0:T(8,128)(2,1)}, u32[]{:S(2)}, u32[]{:S(2)}) collective-permute-start(bf16[1,512,768]{2,1,0:T(8,128)(2,1)} %fusion.13), channel_id=1, source_target_pairs={{2,0},{3,1},{4,2},{5,3},{6,4},{7,5},{8,6},{9,7},{10,8},{11,9},{12,... | collective-permute-start | bytes 2359304 | tf_op jit(solution)/shard_map/ppermute | solution.py:15
  45.4 29.8 %collective-permute-start = (bf16[1,512,768]{2,1,0:T(8,128)(2,1)}, bf16[1,512,768]{2,1,0:T(8,128)(2,1)}, u32[]{:S(2)}, u32[]{:S(2)}) collective-permute-start(bf16[1,512,768]{2,1,0:T(8,128)(2,1)} %fusion.13), channel_id=1, source_target_pairs={{0,2},{1,3},{2,4},{3,5},{4,6},{5,7},{6,8},{7,9},{8,10},{9,11},{10,... | collective-permute-start | bytes 2359304 | tf_op jit(solution)/shard_map/ppermute | solution.py:15
  57.6 33.5 %all-to-all-start.2 = ((bf16[16,3,48,384]{3,2,1,0:T(8,128)(2,1)}), bf16[16,3,48,384]{3,2,1,0:T(8,128)(2,1)S(1)}, u32[]{:S(2)}, u32[]{:S(2)}) async-start(bf16[16,3,48,384]{3,2,1,0:T(8,128)(2,1)} %broadcast_in_dim.15), calls=%async_computation.2 | async-start | bytes 3538944 | tf_op jit(solution)/shard_map/all_to_all | solution.py:21
  63.9 11.2 %copy-start = (f32[512,384]{1,0:T(8,128)S(1)}, f32[512,384]{1,0:T(8,128)}, u32[]{:S(2)}) copy-start(f32[512,384]{1,0:T(8,128)} %fusion.75) | copy-start | bytes 2359300
  63.9 11.2 %copy-start.15 = (f32[384]{0:T(512)S(1)}, f32[384]{0:T(512)}, u32[]{:S(2)}) copy-start(f32[384]{0:T(512)} %get-tuple-element.33) | copy-start | bytes 4612
  63.9 11.2 %copy-start.17 = (f32[384]{0:T(512)S(1)}, f32[384]{0:T(512)}, u32[]{:S(2)}) copy-start(f32[384]{0:T(512)} %get-tuple-element.21) | copy-start | bytes 4612
  75.2 1.9 copy-start.6
  75.2 1.9 copy-start.8
  77.1 0.9 copy-start.12
  78.0 4.8 %copy-start.9 = (bf16[512,768]{1,0:T(8,128)(2,1)}, bf16[512,768]{1,0:T(8,128)(2,1)S(1)}, u32[]{:S(2)}) copy-start(bf16[512,768]{1,0:T(8,128)(2,1)S(1)} %fusion.2) | copy-start | bytes 2359300
  79.5 31.5 %collective-permute-start.3 = (bf16[1,512,768]{2,1,0:T(8,128)(2,1)}, bf16[1,512,768]{2,1,0:T(8,128)(2,1)}, u32[]{:S(2)}, u32[]{:S(2)}) collective-permute-start(bf16[1,512,768]{2,1,0:T(8,128)(2,1)} %fusion.120), channel_id=1, source_target_pairs={{4,0},{5,1},{6,2},{7,3},{8,4},{9,5},{10,6},{11,7},{12,8},{13,9},{1... | collective-permute-start | bytes 2359304 | tf_op jit(solution)/shard_map/ppermute | solution.py:15
  82.8 41.2 %collective-permute-start.2 = (bf16[1,512,768]{2,1,0:T(8,128)(2,1)}, bf16[1,512,768]{2,1,0:T(8,128)(2,1)}, u32[]{:S(2)}, u32[]{:S(2)}) collective-permute-start(bf16[1,512,768]{2,1,0:T(8,128)(2,1)} %fusion.120), channel_id=1, source_target_pairs={{0,4},{1,5},{2,6},{3,7},{4,8},{5,9},{6,10},{7,11},{8,12},{9,13},{1... | collective-permute-start | bytes 2359304 | tf_op jit(solution)/shard_map/ppermute | solution.py:15
  91.3 22.2 %copy-start.3 = (bf16[1,16,48,384]{3,2,0,1:T(8,128)(2,1)}, bf16[1,16,48,384]{3,2,0,1:T(8,128)(2,1)S(1)}, u32[]{:S(2)}) copy-start(bf16[1,16,48,384]{3,2,0,1:T(8,128)(2,1)S(1)} %get-tuple-element.23) | copy-start | bytes 1769476
  91.3 32.6 %copy-start.1 = (bf16[1,16,48,384]{3,2,0,1:T(8,128)(2,1)}, bf16[1,16,48,384]{3,2,0,1:T(8,128)(2,1)S(1)}, u32[]{:S(2)}) copy-start(bf16[1,16,48,384]{3,2,0,1:T(8,128)(2,1)S(1)} %get-tuple-element.22) | copy-start | bytes 1769476
  91.3 21.3 %copy-start.10 = (bf16[512,768]{1,0:T(8,128)(2,1)S(1)}, bf16[512,768]{1,0:T(8,128)(2,1)}, u32[]{:S(2)}) copy-start(bf16[512,768]{1,0:T(8,128)(2,1)} %copy-done.9) | copy-start | bytes 2359300
  112.7 11.3 %copy-start.22 = (f32[384]{0:T(512)S(1)}, f32[384]{0:T(512)}, u32[]{:S(2)}) copy-start(f32[384]{0:T(512)} %get-tuple-element.34) | copy-start | bytes 4612
  112.7 11.3 %copy-start.23 = (f32[384]{0:T(512)S(1)}, f32[384]{0:T(512)}, u32[]{:S(2)}) copy-start(f32[384]{0:T(512)} %get-tuple-element.20) | copy-start | bytes 4612
  123.9 2.1 copy-start.7
  123.9 2.1 copy-start.25
  127.8 20.5 %collective-permute-start.4 = (bf16[1,512,384]{2,1,0:T(8,128)(2,1)}, bf16[1,512,384]{2,1,0:T(8,128)(2,1)}, u32[]{:S(2)}, u32[]{:S(2)}) collective-permute-start(bf16[1,512,384]{2,1,0:T(8,128)(2,1)} %bitcast.25), channel_id=1, source_target_pairs={{4,0},{5,1},{6,2},{7,3},{8,4},{9,5},{10,6},{11,7},{12,8},{13,9},{1... | collective-permute-start | bytes 1179656 | tf_op jit(solution)/shard_map/ppermute | solution.py:15
  132.5 17.5 %collective-permute-start.5 = (bf16[1,512,384]{2,1,0:T(8,128)(2,1)}, bf16[1,512,384]{2,1,0:T(8,128)(2,1)}, u32[]{:S(2)}, u32[]{:S(2)}) collective-permute-start(bf16[1,512,384]{2,1,0:T(8,128)(2,1)} %bitcast.25), channel_id=1, source_target_pairs={{0,4},{1,5},{2,6},{3,7},{4,8},{5,9},{6,10},{7,11},{8,12},{9,13},{1... | collective-permute-start | bytes 1179656 | tf_op jit(solution)/shard_map/ppermute | solution.py:15
  139.5 8.8 %copy-start.2 = (bf16[1,16,48,384]{3,2,0,1:T(8,128)(2,1)S(1)}, bf16[1,16,48,384]{3,2,0,1:T(8,128)(2,1)}, u32[]{:S(2)}) copy-start(bf16[1,16,48,384]{3,2,0,1:T(8,128)(2,1)} %copy-done.1) | copy-start | bytes 1769476
  142.0 8.0 %copy-start.4 = (bf16[1,16,48,384]{3,2,0,1:T(8,128)(2,1)S(1)}, bf16[1,16,48,384]{3,2,0,1:T(8,128)(2,1)}, u32[]{:S(2)}) copy-start(bf16[1,16,48,384]{3,2,0,1:T(8,128)(2,1)} %copy-done.3) | copy-start | bytes 1769476
  142.0 16.4 %all-to-all-start.6 = ((bf16[16,24,768]{2,1,0:T(8,128)(2,1)}), bf16[16,24,768]{2,1,0:T(8,128)(2,1)S(1)}, u32[]{:S(2)}, u32[]{:S(2)}) async-start(bf16[16,24,768]{2,1,0:T(8,128)(2,1)} %convolution_convert_fusion), calls=%async_computation.6 | async-start | bytes 1179648 | tf_op jit(solution)/shard_map/all_to_all | solution.py:27
  148.2 1.8 copy-start.5
  148.2 1.8 copy-start.11
  150.0 3.9 %copy-start.13 = (f32[512,384]{1,0:T(8,128)S(1)}, f32[512,384]{1,0:T(8,128)}, u32[]{:S(2)}) copy-start(f32[512,384]{1,0:T(8,128)} %copy-done.12) | copy-start | bytes 2359300
  153.0 0.9 copy-start.26
  155.5 31.6 %copy-start.16 = (f32[384]{0:T(512)S(1)}, f32[384]{0:T(512)}, u32[]{:S(2)}) copy-start(f32[384]{0:T(512)} %get-tuple-element.33) | copy-start | bytes 4612
  158.4 13.6 %all-to-all-start.3 = ((bf16[16,24,768]{2,1,0:T(8,128)(2,1)}), bf16[16,24,768]{2,1,0:T(8,128)(2,1)S(1)}, u32[]{:S(2)}, u32[]{:S(2)}) async-start(bf16[16,24,768]{2,1,0:T(8,128)(2,1)} %bitcast.28), calls=%async_computation.3 | async-start | bytes 1179648 | tf_op jit(solution)/shard_map/all_to_all | solution.py:27
  172.0 31.7 %all-to-all-start.7 = ((f32[32,1,576]{2,1,0:T(1,128)}), f32[32,1,576]{2,1,0:T(1,128)S(1)}, u32[]{:S(2)}, u32[]{:S(2)}) async-start(f32[32,1,576]{2,1,0:T(1,128)} %reshape_reshape.7), calls=%async_computation.7 | async-start | bytes 163840 | tf_op jit(solution)/shard_map/all_to_all | solution.py:27
  190.3 43.5 %collective-permute-start.6 = (bf16[1,512,384]{2,1,0:T(8,128)(2,1)}, bf16[1,512,384]{2,1,0:T(8,128)(2,1)}, u32[]{:S(2)}, u32[]{:S(2)}) collective-permute-start(bf16[1,512,384]{2,1,0:T(8,128)(2,1)} %bitcast.32), channel_id=1, source_target_pairs={{2,0},{3,1},{4,2},{5,3},{6,4},{7,5},{8,6},{9,7},{10,8},{11,9},{12,... | collective-permute-start | bytes 1179656 | tf_op jit(solution)/shard_map/ppermute | solution.py:15
  192.6 61.2 %collective-permute-start.7 = (bf16[1,512,384]{2,1,0:T(8,128)(2,1)}, bf16[1,512,384]{2,1,0:T(8,128)(2,1)}, u32[]{:S(2)}, u32[]{:S(2)}) collective-permute-start(bf16[1,512,384]{2,1,0:T(8,128)(2,1)} %bitcast.32), channel_id=1, source_target_pairs={{0,2},{1,3},{2,4},{3,5},{4,6},{5,7},{6,8},{7,9},{8,10},{9,11},{10,... | collective-permute-start | bytes 1179656 | tf_op jit(solution)/shard_map/ppermute | solution.py:15
  203.7 25.6 %all-to-all-start.4 = ((f32[32,1,576]{2,1,0:T(1,128)}), f32[32,1,576]{2,1,0:T(1,128)S(1)}, u32[]{:S(2)}, u32[]{:S(2)}) async-start(f32[32,1,576]{2,1,0:T(1,128)} %reshape_reshape.6), calls=%async_computation.4 | async-start | bytes 163840 | tf_op jit(solution)/shard_map/all_to_all | solution.py:27
  229.9 19.3 %all-to-all-start.8 = ((f32[32,1,576]{2,1,0:T(1,128)}), f32[32,1,576]{2,1,0:T(1,128)S(1)}, u32[]{:S(2)}, u32[]{:S(2)}) async-start(f32[32,1,576]{2,1,0:T(1,128)} %broadcast_in_dim.17), calls=%async_computation.8 | async-start | bytes 163840 | tf_op jit(solution)/shard_map/all_to_all | solution.py:21
  249.9 19.3 %all-to-all-start.5 = ((f32[32,1,576]{2,1,0:T(1,128)}), f32[32,1,576]{2,1,0:T(1,128)S(1)}, u32[]{:S(2)}, u32[]{:S(2)}) async-start(f32[32,1,576]{2,1,0:T(1,128)} %broadcast_in_dim.16), calls=%async_computation.5 | async-start | bytes 163840 | tf_op jit(solution)/shard_map/all_to_all | solution.py:21

commit v3 on v2

--- a/solution.py
+++ b/solution.py
@@ -28,11 +28,10 @@
     return arrived.astype(jnp.float32).sum(axis=0)
 
 
-def reduced_term(term):
-    shared_part = summed_over(term, "seq", jnp.bfloat16)
+def reduced_over_dp(value):
     dp_size = lax.axis_size("dp")
-    own_piece = summed_over(shared_part.reshape(dp_size, -1), "dp")
-    return gathered(own_piece, "dp").reshape(shared_part.shape)
+    own_piece = summed_over(value.reshape(dp_size, -1), "dp")
+    return gathered(own_piece, "dp").reshape(value.shape)
 
 
 def gelu_tanh(values):
@@ -106,10 +105,14 @@
             conv_weight.shape[1], -1, conv_weight.shape[3]
         )
 
-    first_conv = conv_gathered(conv_weight[0])
-    point_shard, first_conv = lax.optimization_barrier((point_weight, first_conv))
-    point_full = gathered(point_shard, "seq").reshape(-1, *point_weight.shape[1:])
-    second_shard, point_full = lax.optimization_barrier((conv_weight[1], point_full))
+    conv_size = conv_weight[0].size
+    joined = jnp.concatenate([conv_weight[0].reshape(-1), point_weight.reshape(-1)])
+    joined_full = gathered(joined, "seq")
+    first_conv = jnp.moveaxis(
+        joined_full[:, :conv_size].reshape((-1,) + conv_weight.shape[1:]), 0, 1
+    ).reshape(conv_weight.shape[1], -1, conv_weight.shape[3])
+    point_full = joined_full[:, conv_size:].reshape(-1, *point_weight.shape[1:])
+    second_shard, first_conv = lax.optimization_barrier((conv_weight[1], first_conv))
     conv_full = [first_conv, conv_gathered(second_shard)]
     neighbour_reach = (FIRST_DILATION // position_list, SECOND_DILATION // position_list)
     state = sequence_in.reshape(-1, channels)
@@ -145,7 +148,9 @@
         projection = point_full[:, block_index, :]
         first_operands = (gradient, middle, projection, mid_gain[block_index], kept_flag)
         conv_grad, branch_grad = backward_first(*first_operands)
-        reduced_terms[block_index] = reduced_term(grad_rows(hidden_act, branch_grad))
+        reduced_terms[block_index] = summed_over(
+            grad_rows(hidden_act, branch_grad), "seq", jnp.bfloat16
+        )
         earlier, later = neighbours(
             conv_grad.reshape(sequence_in.shape[0], position_list, -1), neighbour_reach[block_index]
         )
@@ -162,7 +167,7 @@
             in_gain[block_index],
         )
         gradient = backward_second(*second_operands)
-    summed = jnp.stack([reduced_terms[0], reduced_terms[1]], axis=1)
+    summed = reduced_over_dp(jnp.stack([reduced_terms[0], reduced_terms[1]], axis=1))
     sample_count = sequence_in.shape[0] * lax.axis_size("dp")
     full_length = position_list * lax.axis_size("seq")
     point_grad = summed * (1.0 / math.sqrt(sample_count * full_length))

time: 272 us -> 313 us (1.15)
  other arithmetic: 4.88 us -> 69.5 us
  blocking collectives: 30.2 us -> 0 us
  local copies, waits for them, and re-layouts: 12.3 us -> 39.5 us
  waiting for transfers between devices: 94.6 us -> 81.4 us
  starting transfers between devices: 89 us -> 85.3 us
    broadcast_in_dim x0 -> x1, other arithmetic: none -> 62.7 us  [gathered(): copies = jnp.broadcast_to(value[None], (peers,) + value.shape)]
    all_to_all x1 -> x0, blocking collectives: 30.2 us -> none  [gathered(): return lax.all_to_all(copies, axis, 0, 0, tiled=True)]
    unnamed x55 -> x46, local copies, waits for them, and re-layouts: 2.6 us -> 17.7 us
    all_to_all x4 -> x3, waiting for transfers between devices: 29.2 us -> 15.2 us  [summed_over(): arrived = lax.all_to_all(pieces, axis, 0, 0, tiled=True)]
    all_to_all x4 -> x3, waiting for transfers between devices: 26 us -> 37.6 us  [gathered(): return lax.all_to_all(copies, axis, 0, 0, tiled=True)]
    ppermute x8, waiting for transfers between devices: 39.5 us -> 28.7 us  [passed_along(): return lax.ppermute(value, axis, pairs)]
    all_to_all x4 -> x3, starting transfers between devices: 36.2 us -> 26.8 us  [summed_over(): arrived = lax.all_to_all(pieces, axis, 0, 0, tiled=True)]
    all_to_all x4 -> x3, starting transfers between devices: 19.9 us -> 25.5 us  [gathered(): return lax.all_to_all(copies, axis, 0, 0, tiled=True)]
  transfers between devices with their start and end apart: 16 -> 14, of which waited for: 10 -> 7; matrix products, arithmetic and copies ran while one was open for 17% -> 19% of each run, Pallas kernels for 0% -> 0%
where the time goes in v3:
time: 313 us; the launch traced here: 312 us
  starting transfers between devices  85.3 us (27%)
  waiting for transfers between devices  81.4 us (26%)
  other arithmetic  69.5 us (22%)
  local copies, waits for them, and re-layouts  39.5 us (13%)
  matrix products  33.6 us (11%)
    broadcast_in_dim x1, other arithmetic, gathered(): copies = jnp.broadcast_to(value[None], (peers,) + value.shape)  62.7 us
    all_to_all x3, waiting for transfers between devices, gathered(): return lax.all_to_all(copies, axis, 0, 0, tiled=True)  37.6 us
    ppermute x8, starting transfers between devices, passed_along(): return lax.ppermute(value, axis, pairs)  33 us
    ppermute x8, waiting for transfers between devices, passed_along(): return lax.ppermute(value, axis, pairs)  28.7 us
    all_to_all x3, starting transfers between devices, summed_over(): arrived = lax.all_to_all(pieces, axis, 0, 0, tiled=True)  26.8 us
    all_to_all x3, starting transfers between devices, gathered(): return lax.all_to_all(copies, axis, 0, 0, tiled=True)  25.5 us
    dot_general x8, matrix products, contract_last(): lax.dot_general(left, right, (((1,), (1,)), ((), ())), preferred_element_...  19 us
    unnamed x46, local copies, waits for them, and re-layouts  17.7 us
  transfers between devices with their start and end apart: 14, of which 7 were waited for; matrix products, arithmetic and copies ran while one was open for 19% of the time, Pallas kernels for 0%

profile of v3, /device:TPU:6, one launch (start us, length us, event | category | flops | bytes accessed | tf_op | source)
XLA Modules:
  0.0 311.9 jit_solution(15222120554611286069)
XLA Ops:
  2.6 5.6 %broadcast_in_dim.6 = bf16[16,1,92160]{2,1,0:T(2,128)(2,1)} broadcast(bf16[92160]{0:T(1024)(128)(2,1)S(1)} %pad_maximum_fusion), dimensions={2} | broadcast | bytes 3133440 | tf_op jit(solution)/shard_map/broadcast_in_dim | solution.py:20
  8.7 62.7 %reduce.19 = bf16[16,92160]{1,0:T(8,128)(2,1)S(1)} reduce(bf16[16,1,92160]{2,1,0:T(2,128)(2,1)} %broadcast_in_dim.6, bf16[]{:T(256)} %broadcast.185), dimensions={1}, to_apply=%broadcast_in_dim.6.reduce_sub_computation | reduce | bytes 5898242 | tf_op jit(solution)/shard_map/broadcast_in_dim | solution.py:20
  71.5 3.7 %reshape.146 = bf16[16,2,46080]{2,1,0:T(2,128)(2,1)} reshape(bf16[16,92160]{1,0:T(8,128)(2,1)S(1)} %reduce.19) | data formatting | bytes 5898240
  75.1 9.5 %all-to-all-start = ((bf16[16,2,46080]{2,1,0:T(2,128)(2,1)}), bf16[16,2,46080]{2,1,0:T(2,128)(2,1)S(1)}, u32[]{:S(2)}, u32[]{:S(2)}) async-start(bf16[16,2,46080]{2,1,0:T(2,128)(2,1)} %reshape.146), calls=%async_computation | async-start | bytes 5898240 | tf_op jit(solution)/shard_map/all_to_all | solution.py:21
  84.8 2.7 fusion.13
  87.4 2.7 collective-permute-start.1
  90.2 5.4 %collective-permute-start = (bf16[1,512,768]{2,1,0:T(8,128)(2,1)}, bf16[1,512,768]{2,1,0:T(8,128)(2,1)}, u32[]{:S(2)}, u32[]{:S(2)}) collective-permute-start(bf16[1,512,768]{2,1,0:T(8,128)(2,1)} %fusion.13), channel_id=1, source_target_pairs={{0,2},{1,3},{2,4},{3,5},{4,6},{5,7},{6,8},{7,9},{8,10},{9,11},{10,... | collective-permute-start | bytes 2359304 | tf_op jit(solution)/shard_map/ppermute | solution.py:15
  96.9 25.4 %all-to-all-done = bf16[16,2,46080]{2,1,0:T(2,128)(2,1)S(1)} async-done(((bf16[16,2,46080]{2,1,0:T(2,128)(2,1)}), bf16[16,2,46080]{2,1,0:T(2,128)(2,1)S(1)}, u32[]{:S(2)}, u32[]{:S(2)}) %all-to-all-start) | async-done | bytes 2949152 | tf_op jit(solution)/shard_map/all_to_all | solution.py:21
  122.3 7.3 %reshape.147 = bf16[16,1,92160]{2,1,0:T(2,128)(2,1)} reshape(bf16[16,2,46080]{2,1,0:T(2,128)(2,1)S(1)} %all-to-all-done) | data formatting | bytes 5898240
  129.5 4.4 %copy.43 = bf16[16,1,92160]{2,0,1:T(8,128)(2,1)S(1)} copy(bf16[16,1,92160]{2,1,0:T(2,128)(2,1)} %reshape.147) | data formatting | bytes 5898240
  134.1 1.1 slice.103
  135.6 1.4 broadcast_in_dim.7
  136.9 7.0 %all-to-all-start.1 = ((bf16[16,3,48,384]{3,2,1,0:T(8,128)(2,1)}), bf16[16,3,48,384]{3,2,1,0:T(8,128)(2,1)}, u32[]{:S(2)}, u32[]{:S(2)}) async-start(bf16[16,3,48,384]{3,2,1,0:T(8,128)(2,1)} %broadcast_in_dim.7), calls=%async_computation.1 | async-start | bytes 3538944 | tf_op jit(solution)/shard_map/all_to_all | solution.py:21
  144.0 2.0 reshape.123
  145.9 1.7 fusion.75
  147.7 1.7 fusion.73
  149.4 1.7 fusion.42
  151.1 2.7 fusion.116
  155.8 1.5 fusion.114
  157.3 3.4 %collective-permute-start.3 = (bf16[1,512,768]{2,1,0:T(8,128)(2,1)}, bf16[1,512,768]{2,1,0:T(8,128)(2,1)}, u32[]{:S(2)}, u32[]{:S(2)}) collective-permute-start(bf16[1,512,768]{2,1,0:T(8,128)(2,1)} %fusion.114), channel_id=1, source_target_pairs={{4,0},{5,1},{6,2},{7,3},{8,4},{9,5},{10,6},{11,7},{12,8},{13,9},{1... | collective-permute-start | bytes 2359304 | tf_op jit(solution)/shard_map/ppermute | solution.py:15
  161.3 4.9 %collective-permute-start.2 = (bf16[1,512,768]{2,1,0:T(8,128)(2,1)}, bf16[1,512,768]{2,1,0:T(8,128)(2,1)}, u32[]{:S(2)}, u32[]{:S(2)}) collective-permute-start(bf16[1,512,768]{2,1,0:T(8,128)(2,1)} %fusion.114), channel_id=1, source_target_pairs={{0,4},{1,5},{2,6},{3,7},{4,8},{5,9},{6,10},{7,11},{8,12},{9,13},{1... | collective-permute-start | bytes 2359304 | tf_op jit(solution)/shard_map/ppermute | solution.py:15
  166.2 1.6 fusion.115
  167.8 17.9 %collective-permute-done.3 = bf16[1,512,768]{2,1,0:T(8,128)(2,1)} collective-permute-done((bf16[1,512,768]{2,1,0:T(8,128)(2,1)}, bf16[1,512,768]{2,1,0:T(8,128)(2,1)}, u32[]{:S(2)}, u32[]{:S(2)}) %collective-permute-start.3) | collective-permute-done | bytes 786464 | tf_op jit(solution)/shard_map/ppermute | solution.py:15
  185.7 1.7 fusion.68
  188.2 10.8 %collective-permute-done.2 = bf16[1,512,768]{2,1,0:T(8,128)(2,1)} collective-permute-done((bf16[1,512,768]{2,1,0:T(8,128)(2,1)}, bf16[1,512,768]{2,1,0:T(8,128)(2,1)}, u32[]{:S(2)}, u32[]{:S(2)}) %collective-permute-start.2) | collective-permute-done | bytes 786464 | tf_op jit(solution)/shard_map/ppermute | solution.py:15
  199.0 2.1 fusion.66
  201.1 1.7 fusion.58
  202.8 1.9 collective-permute-start.4
  204.7 2.8 fusion.119
  207.5 6.8 %collective-permute-start.5 = (bf16[1,512,384]{2,1,0:T(8,128)(2,1)}, bf16[1,512,384]{2,1,0:T(8,128)(2,1)}, u32[]{:S(2)}, u32[]{:S(2)}) collective-permute-start(bf16[1,512,384]{2,1,0:T(8,128)(2,1)} %bitcast.23), channel_id=1, source_target_pairs={{0,4},{1,5},{2,6},{3,7},{4,8},{5,9},{6,10},{7,11},{8,12},{9,13},{1... | collective-permute-start | bytes 1179656 | tf_op jit(solution)/shard_map/ppermute | solution.py:15
  215.2 2.6 convolution_convert_fusion
  217.8 6.3 %all-to-all-start.3 = ((bf16[16,24,768]{2,1,0:T(8,128)(2,1)}), bf16[16,24,768]{2,1,0:T(8,128)(2,1)S(1)}, u32[]{:S(2)}, u32[]{:S(2)}) async-start(bf16[16,24,768]{2,1,0:T(8,128)(2,1)} %convolution_convert_fusion), calls=%async_computation.3 | async-start | bytes 1179648 | tf_op jit(solution)/shard_map/all_to_all | solution.py:27
  224.1 1.7 fusion.111
  225.9 3.0 fusion.21
  229.7 1.6 convolution_convert_fusion.1
  231.3 1.7 all-to-all-done.3
  233.0 6.3 %all-to-all-start.2 = ((bf16[16,24,768]{2,1,0:T(8,128)(2,1)}), bf16[16,24,768]{2,1,0:T(8,128)(2,1)S(1)}, u32[]{:S(2)}, u32[]{:S(2)}) async-start(bf16[16,24,768]{2,1,0:T(8,128)(2,1)} %bitcast.26), calls=%async_computation.2 | async-start | bytes 1179648 | tf_op jit(solution)/shard_map/all_to_all | solution.py:27
  240.1 7.9 %all-to-all-done.2 = bf16[16,24,768]{2,1,0:T(8,128)(2,1)S(1)} async-done(((bf16[16,24,768]{2,1,0:T(8,128)(2,1)}), bf16[16,24,768]{2,1,0:T(8,128)(2,1)S(1)}, u32[]{:S(2)}, u32[]{:S(2)}) %all-to-all-start.2) | async-done | bytes 589856 | tf_op jit(solution)/shard_map/all_to_all | solution.py:27
  250.0 14.3 %all-to-all-start.4 = ((f32[32,1,1152]{2,1,0:T(1,128)}), f32[32,1,1152]{2,1,0:T(1,128)}, u32[]{:S(2)}, u32[]{:S(2)}) async-start(f32[32,1,1152]{2,1,0:T(1,128)} %reshape_reshape.4), calls=%async_computation.4 | async-start | bytes 294912 | tf_op jit(solution)/shard_map/all_to_all | solution.py:27
  264.3 3.1 fusion.50
  267.4 2.3 collective-permute-start.6
  269.7 5.7 %collective-permute-start.7 = (bf16[1,512,384]{2,1,0:T(8,128)(2,1)}, bf16[1,512,384]{2,1,0:T(8,128)(2,1)}, u32[]{:S(2)}, u32[]{:S(2)}) collective-permute-start(bf16[1,512,384]{2,1,0:T(8,128)(2,1)} %bitcast.30), channel_id=1, source_target_pairs={{0,2},{1,3},{2,4},{3,5},{4,6},{5,7},{6,8},{7,9},{8,10},{9,11},{10,... | collective-permute-start | bytes 1179656 | tf_op jit(solution)/shard_map/ppermute | solution.py:15
  275.3 1.6 fusion.93
  276.9 5.6 %all-to-all-done.4 = f32[32,1,1152]{2,1,0:T(1,128)} async-done(((f32[32,1,1152]{2,1,0:T(1,128)}), f32[32,1,1152]{2,1,0:T(1,128)}, u32[]{:S(2)}, u32[]{:S(2)}) %all-to-all-start.4) | async-done | bytes 147488 | tf_op jit(solution)/shard_map/all_to_all | solution.py:27
  284.3 8.9 %all-to-all-start.5 = ((f32[32,1,1152]{2,1,0:T(1,128)}), f32[32,1,1152]{2,1,0:T(1,128)S(1)}, u32[]{:S(2)}, u32[]{:S(2)}) async-start(f32[32,1,1152]{2,1,0:T(1,128)} %broadcast_in_dim.8), calls=%async_computation.5 | async-start | bytes 294912 | tf_op jit(solution)/shard_map/all_to_all | solution.py:21
  293.3 1.7 fusion.96
  295.0 3.5 %fusion.78 = bf16[1,512,768]{2,1,0:T(8,128)(2,1)} fusion(f32[768]{0:T(1024)S(1)} %get-tuple-element.8, f32[768]{0:T(1024)S(1)} %get-tuple-element.26, bf16[1,512,768]{2,1,0:T(8,128)(2,1)S(1)} %copy-done.5, f32[512,768]{1,0:T(8,128)S(1)} %fusion.96, f32[512,768]{1,0:T(8,128)S(1)} %fusion.93, bf16[512,768]{1,0:T(8,128)(2,1)S(1)} %copy-done.20, ...), kind=kOutput, calls=%fused_computation.104 | convolution fusion | flops 312999936 | bytes 6496256 | tf_op jit(solution)/shard_map/dot_general | solution.py:42
  298.5 12.2 %all-to-all-done.5 = f32[32,1,1152]{2,1,0:T(1,128)S(1)} async-done(((f32[32,1,1152]{2,1,0:T(1,128)}), f32[32,1,1152]{2,1,0:T(1,128)S(1)}, u32[]{:S(2)}, u32[]{:S(2)}) %all-to-all-start.5) | async-done | bytes 147488 | tf_op jit(solution)/shard_map/all_to_all | solution.py:21
  (73 shorter events, 14.0 us)
Async XLA Ops:
  75.1 9.5 %copy-start.13 = (f32[2,768]{1,0:T(2,128)S(1)}, f32[2,768]{1,0:T(2,128)}, u32[]{:S(2)}) copy-start(f32[2,768]{1,0:T(2,128)} %param.13) | copy-start | bytes 18436
  75.1 9.6 %copy-start.14 = (f32[2,768]{1,0:T(2,128)S(1)}, f32[2,768]{1,0:T(2,128)}, u32[]{:S(2)}) copy-start(f32[2,768]{1,0:T(2,128)} %param.12) | copy-start | bytes 18436
  75.1 47.1 %all-to-all-start = ((bf16[16,2,46080]{2,1,0:T(2,128)(2,1)}), bf16[16,2,46080]{2,1,0:T(2,128)(2,1)S(1)}, u32[]{:S(2)}, u32[]{:S(2)}) async-start(bf16[16,2,46080]{2,1,0:T(2,128)(2,1)} %reshape.146), calls=%async_computation | async-start | bytes 5898240 | tf_op jit(solution)/shard_map/all_to_all | solution.py:21
  84.7 10.9 %copy-start.17 = (s32[1,2]{1,0:T(1,128)S(1)}, s32[1,2]{1,0:T(1,128)}, u32[]{:S(2)}) copy-start(s32[1,2]{1,0:T(1,128)} %param.11) | copy-start | bytes 28
  84.7 12.2 %copy-start.15 = (f32[2,384]{1,0:T(2,128)S(1)}, f32[2,384]{1,0:T(2,128)}, u32[]{:S(2)}) copy-start(f32[2,384]{1,0:T(2,128)} %param.15) | copy-start | bytes 9220
  84.7 12.2 %copy-start.16 = (f32[2,384]{1,0:T(2,128)S(1)}, f32[2,384]{1,0:T(2,128)}, u32[]{:S(2)}) copy-start(f32[2,384]{1,0:T(2,128)} %param.14) | copy-start | bytes 9220
  87.4 60.2 %collective-permute-start.1 = (bf16[1,512,768]{2,1,0:T(8,128)(2,1)}, bf16[1,512,768]{2,1,0:T(8,128)(2,1)}, u32[]{:S(2)}, u32[]{:S(2)}) collective-permute-start(bf16[1,512,768]{2,1,0:T(8,128)(2,1)} %fusion.13), channel_id=1, source_target_pairs={{2,0},{3,1},{4,2},{5,3},{6,4},{7,5},{8,6},{9,7},{10,8},{11,9},{12,... | collective-permute-start | bytes 2359304 | tf_op jit(solution)/shard_map/ppermute | solution.py:15
  90.2 59.2 %collective-permute-start = (bf16[1,512,768]{2,1,0:T(8,128)(2,1)}, bf16[1,512,768]{2,1,0:T(8,128)(2,1)}, u32[]{:S(2)}, u32[]{:S(2)}) collective-permute-start(bf16[1,512,768]{2,1,0:T(8,128)(2,1)} %fusion.13), channel_id=1, source_target_pairs={{0,2},{1,3},{2,4},{3,5},{4,6},{5,7},{6,8},{7,9},{8,10},{9,11},{10,... | collective-permute-start | bytes 2359304 | tf_op jit(solution)/shard_map/ppermute | solution.py:15
  96.9 52.5 %copy-start.11 = (f32[384]{0:T(512)}, f32[384]{0:T(512)S(1)}, u32[]{:S(2)}) copy-start(f32[384]{0:T(512)S(1)} %get-tuple-element.27) | copy-start | bytes 4612
  136.9 29.2 %all-to-all-start.1 = ((bf16[16,3,48,384]{3,2,1,0:T(8,128)(2,1)}), bf16[16,3,48,384]{3,2,1,0:T(8,128)(2,1)}, u32[]{:S(2)}, u32[]{:S(2)}) async-start(bf16[16,3,48,384]{3,2,1,0:T(8,128)(2,1)} %broadcast_in_dim.7), calls=%async_computation.1 | async-start | bytes 3538944 | tf_op jit(solution)/shard_map/all_to_all | solution.py:21
  151.1 2.7 copy-start.9
  151.1 2.7 copy-start.4
  153.8 1.0 copy-start.1
  154.9 0.9 copy-start.6
  157.3 28.4 %collective-permute-start.3 = (bf16[1,512,768]{2,1,0:T(8,128)(2,1)}, bf16[1,512,768]{2,1,0:T(8,128)(2,1)}, u32[]{:S(2)}, u32[]{:S(2)}) collective-permute-start(bf16[1,512,768]{2,1,0:T(8,128)(2,1)} %fusion.114), channel_id=1, source_target_pairs={{4,0},{5,1},{6,2},{7,3},{8,4},{9,5},{10,6},{11,7},{12,8},{13,9},{1... | collective-permute-start | bytes 2359304 | tf_op jit(solution)/shard_map/ppermute | solution.py:15
  161.3 37.7 %collective-permute-start.2 = (bf16[1,512,768]{2,1,0:T(8,128)(2,1)}, bf16[1,512,768]{2,1,0:T(8,128)(2,1)}, u32[]{:S(2)}, u32[]{:S(2)}) collective-permute-start(bf16[1,512,768]{2,1,0:T(8,128)(2,1)} %fusion.114), channel_id=1, source_target_pairs={{0,4},{1,5},{2,6},{3,7},{4,8},{5,9},{6,10},{7,11},{8,12},{9,13},{1... | collective-permute-start | bytes 2359304 | tf_op jit(solution)/shard_map/ppermute | solution.py:15
  167.8 19.6 %copy-start.7 = (bf16[512,768]{1,0:T(8,128)(2,1)S(1)}, bf16[512,768]{1,0:T(8,128)(2,1)}, u32[]{:S(2)}) copy-start(bf16[512,768]{1,0:T(8,128)(2,1)} %copy-done.6) | copy-start | bytes 2359300
  199.0 2.1 copy-start.3
  199.0 2.1 copy-start.18
  202.8 21.3 %collective-permute-start.4 = (bf16[1,512,384]{2,1,0:T(8,128)(2,1)}, bf16[1,512,384]{2,1,0:T(8,128)(2,1)}, u32[]{:S(2)}, u32[]{:S(2)}) collective-permute-start(bf16[1,512,384]{2,1,0:T(8,128)(2,1)} %bitcast.23), channel_id=1, source_target_pairs={{4,0},{5,1},{6,2},{7,3},{8,4},{9,5},{10,6},{11,7},{12,8},{13,9},{1... | collective-permute-start | bytes 1179656 | tf_op jit(solution)/shard_map/ppermute | solution.py:15
  207.5 18.4 %collective-permute-start.5 = (bf16[1,512,384]{2,1,0:T(8,128)(2,1)}, bf16[1,512,384]{2,1,0:T(8,128)(2,1)}, u32[]{:S(2)}, u32[]{:S(2)}) collective-permute-start(bf16[1,512,384]{2,1,0:T(8,128)(2,1)} %bitcast.23), channel_id=1, source_target_pairs={{0,4},{1,5},{2,6},{3,7},{4,8},{5,9},{6,10},{7,11},{8,12},{9,13},{1... | collective-permute-start | bytes 1179656 | tf_op jit(solution)/shard_map/ppermute | solution.py:15
  217.8 15.3 %all-to-all-start.3 = ((bf16[16,24,768]{2,1,0:T(8,128)(2,1)}), bf16[16,24,768]{2,1,0:T(8,128)(2,1)S(1)}, u32[]{:S(2)}, u32[]{:S(2)}) async-start(bf16[16,24,768]{2,1,0:T(8,128)(2,1)} %convolution_convert_fusion), calls=%async_computation.3 | async-start | bytes 1179648 | tf_op jit(solution)/shard_map/all_to_all | solution.py:27
  224.1 1.8 copy-start
  224.1 1.8 copy-start.8
  225.8 3.9 %copy-start.10 = (f32[512,384]{1,0:T(8,128)S(1)}, f32[512,384]{1,0:T(8,128)}, u32[]{:S(2)}) copy-start(f32[512,384]{1,0:T(8,128)} %copy-done.9) | copy-start | bytes 2359300
  228.8 0.9 copy-start.19
  233.0 31.3 %copy-start.12 = (f32[384]{0:T(512)S(1)}, f32[384]{0:T(512)}, u32[]{:S(2)}) copy-start(f32[384]{0:T(512)} %copy-done.11) | copy-start | bytes 4612
  233.0 15.0 %all-to-all-start.2 = ((bf16[16,24,768]{2,1,0:T(8,128)(2,1)}), bf16[16,24,768]{2,1,0:T(8,128)(2,1)S(1)}, u32[]{:S(2)}, u32[]{:S(2)}) async-start(bf16[16,24,768]{2,1,0:T(8,128)(2,1)} %bitcast.26), calls=%async_computation.2 | async-start | bytes 1179648 | tf_op jit(solution)/shard_map/all_to_all | solution.py:27
  239.4 25.0 %copy-start.2 = (bf16[384,1,768]{2,1,0:T(2,128)(2,1)S(1)}, bf16[384,1,768]{2,1,0:T(2,128)(2,1)}, u32[]{:S(2)}) copy-start(bf16[384,1,768]{2,1,0:T(2,128)(2,1)} %copy-done.1) | copy-start | bytes 1769476
  250.0 32.5 %all-to-all-start.4 = ((f32[32,1,1152]{2,1,0:T(1,128)}), f32[32,1,1152]{2,1,0:T(1,128)}, u32[]{:S(2)}, u32[]{:S(2)}) async-start(f32[32,1,1152]{2,1,0:T(1,128)} %reshape_reshape.4), calls=%async_computation.4 | async-start | bytes 294912 | tf_op jit(solution)/shard_map/all_to_all | solution.py:27
  267.4 25.9 %collective-permute-start.6 = (bf16[1,512,384]{2,1,0:T(8,128)(2,1)}, bf16[1,512,384]{2,1,0:T(8,128)(2,1)}, u32[]{:S(2)}, u32[]{:S(2)}) collective-permute-start(bf16[1,512,384]{2,1,0:T(8,128)(2,1)} %bitcast.30), channel_id=1, source_target_pairs={{2,0},{3,1},{4,2},{5,3},{6,4},{7,5},{8,6},{9,7},{10,8},{11,9},{12,... | collective-permute-start | bytes 1179656 | tf_op jit(solution)/shard_map/ppermute | solution.py:15
  269.7 25.3 %collective-permute-start.7 = (bf16[1,512,384]{2,1,0:T(8,128)(2,1)}, bf16[1,512,384]{2,1,0:T(8,128)(2,1)}, u32[]{:S(2)}, u32[]{:S(2)}) collective-permute-start(bf16[1,512,384]{2,1,0:T(8,128)(2,1)} %bitcast.30), channel_id=1, source_target_pairs={{0,2},{1,3},{2,4},{3,5},{4,6},{5,7},{6,8},{7,9},{8,10},{9,11},{10,... | collective-permute-start | bytes 1179656 | tf_op jit(solution)/shard_map/ppermute | solution.py:15
  284.3 26.4 %all-to-all-start.5 = ((f32[32,1,1152]{2,1,0:T(1,128)}), f32[32,1,1152]{2,1,0:T(1,128)S(1)}, u32[]{:S(2)}, u32[]{:S(2)}) async-start(f32[32,1,1152]{2,1,0:T(1,128)} %broadcast_in_dim.8), calls=%async_computation.5 | async-start | bytes 294912 | tf_op jit(solution)/shard_map/all_to_all | solution.py:21
  293.2 1.8 copy-start.5
  293.2 1.7 copy-start.20

commit v4 on v3

--- a/solution.py
+++ b/solution.py
@@ -105,13 +105,16 @@
             conv_weight.shape[1], -1, conv_weight.shape[3]
         )
 
-    conv_size = conv_weight[0].size
-    joined = jnp.concatenate([conv_weight[0].reshape(-1), point_weight.reshape(-1)])
+    lanes = conv_weight.shape[3]
+    conv_rows = conv_weight.shape[1] * conv_weight.shape[2]
+    joined = jnp.concatenate(
+        [conv_weight[0].reshape(conv_rows, lanes), point_weight.reshape(-1, lanes)]
+    )
     joined_full = gathered(joined, "seq")
     first_conv = jnp.moveaxis(
-        joined_full[:, :conv_size].reshape((-1,) + conv_weight.shape[1:]), 0, 1
-    ).reshape(conv_weight.shape[1], -1, conv_weight.shape[3])
-    point_full = joined_full[:, conv_size:].reshape(-1, *point_weight.shape[1:])
+        joined_full[:, :conv_rows].reshape((-1,) + conv_weight.shape[1:]), 0, 1
+    ).reshape(conv_weight.shape[1], -1, lanes)
+    point_full = joined_full[:, conv_rows:].reshape(-1, *point_weight.shape[1:])
     second_shard, first_conv = lax.optimization_barrier((conv_weight[1], first_conv))
     conv_full = [first_conv, conv_gathered(second_shard)]
     neighbour_reach = (FIRST_DILATION // position_list, SECOND_DILATION // position_list)

time: 313 us -> 235 us (0.75)
  other arithmetic: 69.5 us -> 6.8 us
  local copies, waits for them, and re-layouts: 39.5 us -> 21 us
  waiting for transfers between devices: 81.4 us -> 84.7 us
    broadcast_in_dim x1 -> x0, other arithmetic: 62.7 us -> none  [gathered(): copies = jnp.broadcast_to(value[None], (peers,) + value.shape)]
    unnamed x46, local copies, waits for them, and re-layouts: 17.7 us -> 3.64 us
    broadcast_in_dim x4 -> x3, local copies, waits for them, and re-layouts: 8.17 us -> 3.99 us  [gathered(): copies = jnp.broadcast_to(value[None], (peers,) + value.shape)]
  transfers between devices with their start and end apart: 14 -> 14, of which waited for: 7 -> 9; matrix products, arithmetic and copies ran while one was open for 19% -> 20% of each run, Pallas kernels for 0% -> 0%
where the time goes in v4:
time: 235 us; the launch traced here: 234 us
  starting transfers between devices  85 us (36%)
  waiting for transfers between devices  84.7 us (36%)
  matrix products  33.7 us (14%)
  local copies, waits for them, and re-layouts  21 us (9%)
  other arithmetic  6.8 us (3%)
  between operations  2.4 us (1%)
    all_to_all x3, waiting for transfers between devices, gathered(): return lax.all_to_all(copies, axis, 0, 0, tiled=True)  37.8 us
    ppermute x8, starting transfers between devices, passed_along(): return lax.ppermute(value, axis, pairs)  33.3 us
    ppermute x8, waiting for transfers between devices, passed_along(): return lax.ppermute(value, axis, pairs)  31.2 us
    all_to_all x3, starting transfers between devices, summed_over(): arrived = lax.all_to_all(pieces, axis, 0, 0, tiled=True)  26.2 us
    all_to_all x3, starting transfers between devices, gathered(): return lax.all_to_all(copies, axis, 0, 0, tiled=True)  25.5 us
    dot_general x8, matrix products, contract_last(): lax.dot_general(left, right, (((1,), (1,)), ((), ())), preferred_element_...  19.1 us
    all_to_all x3, waiting for transfers between devices, summed_over(): arrived = lax.all_to_all(pieces, axis, 0, 0, tiled=True)  15.7 us
  transfers between devices with their start and end apart: 14, of which 9 were waited for; matrix products, arithmetic and copies ran while one was open for 20% of the time, Pallas kernels for 0%

profile of v4, /device:TPU:6, one launch (start us, length us, event | category | flops | bytes accessed | tf_op | source)
XLA Modules:
  0.0 233.6 jit_solution(5843999175179539312)
XLA Ops:
  2.6 1.8 broadcast_in_dim.6
  4.4 9.5 %all-to-all-start = ((bf16[16,240,384]{2,1,0:T(8,128)(2,1)}), bf16[16,240,384]{2,1,0:T(8,128)(2,1)S(1)}, u32[]{:S(2)}, u32[]{:S(2)}) async-start(bf16[16,240,384]{2,1,0:T(8,128)(2,1)} %broadcast_in_dim.6), calls=%async_computation | async-start | bytes 5898240 | tf_op jit(solution)/shard_map/all_to_all | solution.py:21
  14.1 2.7 %fusion.13 = bf16[1,512,768]{2,1,0:T(8,128)(2,1)} fusion(bf16[1,512,768]{2,1,0:T(8,128)(2,1)} %param.9, f32[768]{0:T(1024)S(1)} %get-tuple-element.8, f32[768]{0:T(1024)S(1)} %get-tuple-element.26), kind=kLoop, calls=%fused_computation.24 | loop fusion | flops 4718592 | bytes 1579008 | tf_op jit(solution)/shard_map/convert_element_type | solution.py:127
  16.7 2.7 %collective-permute-start.1 = (bf16[1,512,768]{2,1,0:T(8,128)(2,1)}, bf16[1,512,768]{2,1,0:T(8,128)(2,1)}, u32[]{:S(2)}, u32[]{:S(2)}) collective-permute-start(bf16[1,512,768]{2,1,0:T(8,128)(2,1)} %fusion.13), channel_id=1, source_target_pairs={{2,0},{3,1},{4,2},{5,3},{6,4},{7,5},{8,6},{9,7},{10,8},{11,9},{12,... | collective-permute-start | bytes 2359304 | tf_op jit(solution)/shard_map/ppermute | solution.py:15
  19.5 5.2 %collective-permute-start = (bf16[1,512,768]{2,1,0:T(8,128)(2,1)}, bf16[1,512,768]{2,1,0:T(8,128)(2,1)}, u32[]{:S(2)}, u32[]{:S(2)}) collective-permute-start(bf16[1,512,768]{2,1,0:T(8,128)(2,1)} %fusion.13), channel_id=1, source_target_pairs={{0,2},{1,3},{2,4},{3,5},{4,6},{5,7},{6,8},{7,9},{8,10},{9,11},{10,... | collective-permute-start | bytes 2359304 | tf_op jit(solution)/shard_map/ppermute | solution.py:15
  26.0 25.6 %all-to-all-done = bf16[16,240,384]{2,1,0:T(8,128)(2,1)S(1)} async-done(((bf16[16,240,384]{2,1,0:T(8,128)(2,1)}), bf16[16,240,384]{2,1,0:T(8,128)(2,1)S(1)}, u32[]{:S(2)}, u32[]{:S(2)}) %all-to-all-start) | async-done | bytes 2949152 | tf_op jit(solution)/shard_map/all_to_all | solution.py:21
  51.7 1.5 copy-done
  53.4 1.4 broadcast_in_dim.7
  54.8 7.0 %all-to-all-start.1 = ((bf16[16,3,48,384]{3,2,1,0:T(8,128)(2,1)}), bf16[16,3,48,384]{3,2,1,0:T(8,128)(2,1)}, u32[]{:S(2)}, u32[]{:S(2)}) async-start(bf16[16,3,48,384]{3,2,1,0:T(8,128)(2,1)} %broadcast_in_dim.7), calls=%async_computation.1 | async-start | bytes 3538944 | tf_op jit(solution)/shard_map/all_to_all | solution.py:21
  61.8 1.3 slice-done
  63.1 1.6 reshape.118
  64.7 1.7 fusion.75
  66.4 2.0 collective-permute-done.1
  68.4 1.7 fusion.73
  70.1 1.8 fusion.42
  72.0 2.7 %fusion.122 = (bf16[384,1,768]{2,1,0:T(2,128)(2,1)}, bf16[384,1,768]{2,1,0:T(2,128)(2,1)S(1)}) fusion(bf16[384,2,768]{2,1,0:T(2,128)(2,1)S(1)} %copy-done.1), kind=kLoop, calls=%fused_computation.147 | loop fusion | bytes 2359296 | tf_op jit(solution)/shard_map/slice | solution.py:151
  76.6 1.5 fusion.120
  78.1 5.8 %collective-permute-start.3 = (bf16[1,512,768]{2,1,0:T(8,128)(2,1)}, bf16[1,512,768]{2,1,0:T(8,128)(2,1)}, u32[]{:S(2)}, u32[]{:S(2)}) collective-permute-start(bf16[1,512,768]{2,1,0:T(8,128)(2,1)} %fusion.120), channel_id=1, source_target_pairs={{4,0},{5,1},{6,2},{7,3},{8,4},{9,5},{10,6},{11,7},{12,8},{13,9},{1... | collective-permute-start | bytes 2359304 | tf_op jit(solution)/shard_map/ppermute | solution.py:15
  84.6 2.9 %collective-permute-start.2 = (bf16[1,512,768]{2,1,0:T(8,128)(2,1)}, bf16[1,512,768]{2,1,0:T(8,128)(2,1)}, u32[]{:S(2)}, u32[]{:S(2)}) collective-permute-start(bf16[1,512,768]{2,1,0:T(8,128)(2,1)} %fusion.120), channel_id=1, source_target_pairs={{0,4},{1,5},{2,6},{3,7},{4,8},{5,9},{6,10},{7,11},{8,12},{9,13},{1... | collective-permute-start | bytes 2359304 | tf_op jit(solution)/shard_map/ppermute | solution.py:15
  87.5 1.6 fusion.121
  89.2 15.5 %collective-permute-done.3 = bf16[1,512,768]{2,1,0:T(8,128)(2,1)} collective-permute-done((bf16[1,512,768]{2,1,0:T(8,128)(2,1)}, bf16[1,512,768]{2,1,0:T(8,128)(2,1)}, u32[]{:S(2)}, u32[]{:S(2)}) %collective-permute-start.3) | collective-permute-done | bytes 786464 | tf_op jit(solution)/shard_map/ppermute | solution.py:15
  104.7 1.7 fusion.68
  107.2 13.6 %collective-permute-done.2 = bf16[1,512,768]{2,1,0:T(8,128)(2,1)} collective-permute-done((bf16[1,512,768]{2,1,0:T(8,128)(2,1)}, bf16[1,512,768]{2,1,0:T(8,128)(2,1)}, u32[]{:S(2)}, u32[]{:S(2)}) %collective-permute-start.2) | collective-permute-done | bytes 786464 | tf_op jit(solution)/shard_map/ppermute | solution.py:15
  120.8 2.1 fusion.66
  122.9 1.7 fusion.58
  124.6 1.9 collective-permute-start.4
  126.5 2.8 %fusion.125 = f32[512,768]{1,0:T(8,128)} fusion(bf16[512,384]{1,0:T(8,128)(2,1)} %fusion.58, bf16[768,384]{1,0:T(8,128)(2,1)S(1)} %bitcast.156), kind=kOutput, calls=%fused_computation.150 | convolution fusion | flops 301989888 | bytes 2555904 | tf_op jit(solution)/shard_map/dot_general | solution.py:42
  129.3 6.8 %collective-permute-start.5 = (bf16[1,512,384]{2,1,0:T(8,128)(2,1)}, bf16[1,512,384]{2,1,0:T(8,128)(2,1)}, u32[]{:S(2)}, u32[]{:S(2)}) collective-permute-start(bf16[1,512,384]{2,1,0:T(8,128)(2,1)} %bitcast.23), channel_id=1, source_target_pairs={{0,4},{1,5},{2,6},{3,7},{4,8},{5,9},{6,10},{7,11},{8,12},{9,13},{1... | collective-permute-start | bytes 1179656 | tf_op jit(solution)/shard_map/ppermute | solution.py:15
  137.0 2.6 %convolution_convert_fusion = bf16[16,24,768]{2,1,0:T(8,128)(2,1)} fusion(bf16[16,24,512]{2,1,0:T(8,128)(2,1)} %bitcast.160, bf16[1,512,768]{2,1,0:T(8,128)(2,1)} %param.10, f32[]{:T(128)} %bitcast.13), kind=kOutput, calls=%fused_computation.50 | convolution fusion | flops 303464448 | bytes 1769476 | tf_op jit(solution)/shard_map/dot_general | solution.py:85
  139.6 6.1 %all-to-all-start.3 = ((bf16[16,24,768]{2,1,0:T(8,128)(2,1)}), bf16[16,24,768]{2,1,0:T(8,128)(2,1)S(1)}, u32[]{:S(2)}, u32[]{:S(2)}) async-start(bf16[16,24,768]{2,1,0:T(8,128)(2,1)} %convolution_convert_fusion), calls=%async_computation.3 | async-start | bytes 1179648 | tf_op jit(solution)/shard_map/all_to_all | solution.py:27
  145.7 1.7 fusion.115
  147.5 3.0 %fusion.21 = bf16[512,768]{1,0:T(8,128)(2,1)S(1)} fusion(bf16[1,512,768]{2,1,0:T(8,128)(2,1)} %param.10, f32[512,768]{1,0:T(8,128)S(1)} %fusion.115, f32[512,768]{1,0:T(8,128)S(1)} %copy-done.2, bf16[512,768]{1,0:T(8,128)(2,1)S(1)} %copy-done.10, f32[768]{0:T(1024)S(1)} %get-tuple-element.9, f32[768]{0:T(1024)S(1)} %get-tuple-element.25, ...), kind=kOutput, calls=%fused_computation.32 | convolution fusion | flops 312999936 | bytes 6494208 | tf_op jit(solution)/shard_map/dot_general | solution.py:42
  151.4 1.5 convolution_convert_fusion.1
  152.9 2.2 all-to-all-done.3
  155.2 5.8 %all-to-all-start.2 = ((bf16[16,24,768]{2,1,0:T(8,128)(2,1)}), bf16[16,24,768]{2,1,0:T(8,128)(2,1)S(1)}, u32[]{:S(2)}, u32[]{:S(2)}) async-start(bf16[16,24,768]{2,1,0:T(8,128)(2,1)} %bitcast.26), calls=%async_computation.2 | async-start | bytes 1179648 | tf_op jit(solution)/shard_map/all_to_all | solution.py:27
  161.7 7.9 %all-to-all-done.2 = bf16[16,24,768]{2,1,0:T(8,128)(2,1)S(1)} async-done(((bf16[16,24,768]{2,1,0:T(8,128)(2,1)}), bf16[16,24,768]{2,1,0:T(8,128)(2,1)S(1)}, u32[]{:S(2)}, u32[]{:S(2)}) %all-to-all-start.2) | async-done | bytes 589856 | tf_op jit(solution)/shard_map/all_to_all | solution.py:27
  169.8 1.0 pad_maximum_fusion.1
  171.7 14.3 %all-to-all-start.4 = ((f32[32,1,1152]{2,1,0:T(1,128)}), f32[32,1,1152]{2,1,0:T(1,128)}, u32[]{:S(2)}, u32[]{:S(2)}) async-start(f32[32,1,1152]{2,1,0:T(1,128)} %reshape_reshape.4), calls=%async_computation.4 | async-start | bytes 294912 | tf_op jit(solution)/shard_map/all_to_all | solution.py:27
  186.0 3.1 %fusion.50 = bf16[512,384]{1,0:T(8,128)(2,1)} fusion(f32[512,384]{1,0:T(8,128)} %copy-done.11, bf16[512,768]{1,0:T(8,128)(2,1)} %copy-done.21, f32[]{:T(128)} %bitcast.11, f32[384]{0:T(512)S(1)} %copy-done.14, bf16[384,1,768]{2,1,0:T(2,128)(2,1)S(1)} %copy-done.4), kind=kOutput, calls=%fused_computation.74 | convolution fusion | flops 307298304 | bytes 2557444 | tf_op jit(solution)/shard_map/dot_general | solution.py:42
  189.1 2.3 collective-permute-start.6
  191.4 5.7 %collective-permute-start.7 = (bf16[1,512,384]{2,1,0:T(8,128)(2,1)}, bf16[1,512,384]{2,1,0:T(8,128)(2,1)}, u32[]{:S(2)}, u32[]{:S(2)}) collective-permute-start(bf16[1,512,384]{2,1,0:T(8,128)(2,1)} %bitcast.30), channel_id=1, source_target_pairs={{0,2},{1,3},{2,4},{3,5},{4,6},{5,7},{6,8},{7,9},{8,10},{9,11},{10,... | collective-permute-start | bytes 1179656 | tf_op jit(solution)/shard_map/ppermute | solution.py:15
  197.1 1.6 fusion.97
  198.7 5.6 %all-to-all-done.4 = f32[32,1,1152]{2,1,0:T(1,128)} async-done(((f32[32,1,1152]{2,1,0:T(1,128)}), f32[32,1,1152]{2,1,0:T(1,128)}, u32[]{:S(2)}, u32[]{:S(2)}) %all-to-all-start.4) | async-done | bytes 147488 | tf_op jit(solution)/shard_map/all_to_all | solution.py:27
  204.2 1.0 reduce_sum.29
  206.0 8.9 %all-to-all-start.5 = ((f32[32,1,1152]{2,1,0:T(1,128)}), f32[32,1,1152]{2,1,0:T(1,128)S(1)}, u32[]{:S(2)}, u32[]{:S(2)}) async-start(f32[32,1,1152]{2,1,0:T(1,128)} %broadcast_in_dim.8), calls=%async_computation.5 | async-start | bytes 294912 | tf_op jit(solution)/shard_map/all_to_all | solution.py:21
  215.0 1.7 fusion.100
  216.7 3.5 %fusion.78 = bf16[1,512,768]{2,1,0:T(8,128)(2,1)} fusion(f32[768]{0:T(1024)S(1)} %get-tuple-element.8, f32[768]{0:T(1024)S(1)} %get-tuple-element.26, bf16[1,512,768]{2,1,0:T(8,128)(2,1)S(1)} %copy-done.7, f32[512,768]{1,0:T(8,128)S(1)} %fusion.100, f32[512,768]{1,0:T(8,128)S(1)} %fusion.97, bf16[512,768]{1,0:T(8,128)(2,1)S(1)} %copy-done.22, ...), kind=kOutput, calls=%fused_computation.103 | convolution fusion | flops 312999936 | bytes 6496256 | tf_op jit(solution)/shard_map/dot_general | solution.py:42
  220.2 12.2 %all-to-all-done.5 = f32[32,1,1152]{2,1,0:T(1,128)S(1)} async-done(((f32[32,1,1152]{2,1,0:T(1,128)}), f32[32,1,1152]{2,1,0:T(1,128)S(1)}, u32[]{:S(2)}, u32[]{:S(2)}) %all-to-all-start.5) | async-done | bytes 147488 | tf_op jit(solution)/shard_map/all_to_all | solution.py:21
  (71 shorter events, 11.3 us)
Async XLA Ops:
  4.4 9.5 %copy-start.15 = (f32[2,768]{1,0:T(2,128)S(1)}, f32[2,768]{1,0:T(2,128)}, u32[]{:S(2)}) copy-start(f32[2,768]{1,0:T(2,128)} %param.13) | copy-start | bytes 18436
  4.4 9.6 %copy-start.16 = (f32[2,768]{1,0:T(2,128)S(1)}, f32[2,768]{1,0:T(2,128)}, u32[]{:S(2)}) copy-start(f32[2,768]{1,0:T(2,128)} %param.12) | copy-start | bytes 18436
  4.4 47.1 %all-to-all-start = ((bf16[16,240,384]{2,1,0:T(8,128)(2,1)}), bf16[16,240,384]{2,1,0:T(8,128)(2,1)S(1)}, u32[]{:S(2)}, u32[]{:S(2)}) async-start(bf16[16,240,384]{2,1,0:T(8,128)(2,1)} %broadcast_in_dim.6), calls=%async_computation | async-start | bytes 5898240 | tf_op jit(solution)/shard_map/all_to_all | solution.py:21
  14.0 10.7 %copy-start.19 = (s32[1,2]{1,0:T(1,128)S(1)}, s32[1,2]{1,0:T(1,128)}, u32[]{:S(2)}) copy-start(s32[1,2]{1,0:T(1,128)} %param.11) | copy-start | bytes 28
  14.0 11.9 %copy-start.17 = (f32[2,384]{1,0:T(2,128)S(1)}, f32[2,384]{1,0:T(2,128)}, u32[]{:S(2)}) copy-start(f32[2,384]{1,0:T(2,128)} %param.15) | copy-start | bytes 9220
  14.0 11.9 %copy-start.18 = (f32[2,384]{1,0:T(2,128)S(1)}, f32[2,384]{1,0:T(2,128)}, u32[]{:S(2)}) copy-start(f32[2,384]{1,0:T(2,128)} %param.14) | copy-start | bytes 9220
  16.7 51.7 %collective-permute-start.1 = (bf16[1,512,768]{2,1,0:T(8,128)(2,1)}, bf16[1,512,768]{2,1,0:T(8,128)(2,1)}, u32[]{:S(2)}, u32[]{:S(2)}) collective-permute-start(bf16[1,512,768]{2,1,0:T(8,128)(2,1)} %fusion.13), channel_id=1, source_target_pairs={{2,0},{3,1},{4,2},{5,3},{6,4},{7,5},{8,6},{9,7},{10,8},{11,9},{12,... | collective-permute-start | bytes 2359304 | tf_op jit(solution)/shard_map/ppermute | solution.py:15
  19.5 50.7 %collective-permute-start = (bf16[1,512,768]{2,1,0:T(8,128)(2,1)}, bf16[1,512,768]{2,1,0:T(8,128)(2,1)}, u32[]{:S(2)}, u32[]{:S(2)}) collective-permute-start(bf16[1,512,768]{2,1,0:T(8,128)(2,1)} %fusion.13), channel_id=1, source_target_pairs={{0,2},{1,3},{2,4},{3,5},{4,6},{5,7},{6,8},{7,9},{8,10},{9,11},{10,... | collective-permute-start | bytes 2359304 | tf_op jit(solution)/shard_map/ppermute | solution.py:15
  26.0 44.2 %copy-start.13 = (f32[384]{0:T(512)}, f32[384]{0:T(512)S(1)}, u32[]{:S(2)}) copy-start(f32[384]{0:T(512)S(1)} %get-tuple-element.27) | copy-start | bytes 4612
  51.6 1.6 copy-start
  54.8 32.7 %all-to-all-start.1 = ((bf16[16,3,48,384]{3,2,1,0:T(8,128)(2,1)}), bf16[16,3,48,384]{3,2,1,0:T(8,128)(2,1)}, u32[]{:S(2)}, u32[]{:S(2)}) async-start(bf16[16,3,48,384]{3,2,1,0:T(8,128)(2,1)} %broadcast_in_dim.7), calls=%async_computation.1 | async-start | bytes 3538944 | tf_op jit(solution)/shard_map/all_to_all | solution.py:21
  61.8 1.3 slice-start
  70.1 1.8 copy-start.1
  72.0 2.7 %copy-start.11 = (f32[512,384]{1,0:T(8,128)}, f32[512,384]{1,0:T(8,128)S(1)}, u32[]{:S(2)}) copy-start(f32[512,384]{1,0:T(8,128)S(1)} %fusion.42) | copy-start | bytes 2359300
  72.0 2.7 %copy-start.6 = (bf16[1,512,768]{2,1,0:T(8,128)(2,1)S(1)}, bf16[1,512,768]{2,1,0:T(8,128)(2,1)}, u32[]{:S(2)}) copy-start(bf16[1,512,768]{2,1,0:T(8,128)(2,1)} %param.9) | copy-start | bytes 2359300
  74.6 1.1 copy-start.3
  75.7 0.9 copy-start.8
  78.1 26.6 %collective-permute-start.3 = (bf16[1,512,768]{2,1,0:T(8,128)(2,1)}, bf16[1,512,768]{2,1,0:T(8,128)(2,1)}, u32[]{:S(2)}, u32[]{:S(2)}) collective-permute-start(bf16[1,512,768]{2,1,0:T(8,128)(2,1)} %fusion.120), channel_id=1, source_target_pairs={{4,0},{5,1},{6,2},{7,3},{8,4},{9,5},{10,6},{11,7},{12,8},{13,9},{1... | collective-permute-start | bytes 2359304 | tf_op jit(solution)/shard_map/ppermute | solution.py:15
  84.6 36.2 %collective-permute-start.2 = (bf16[1,512,768]{2,1,0:T(8,128)(2,1)}, bf16[1,512,768]{2,1,0:T(8,128)(2,1)}, u32[]{:S(2)}, u32[]{:S(2)}) collective-permute-start(bf16[1,512,768]{2,1,0:T(8,128)(2,1)} %fusion.120), channel_id=1, source_target_pairs={{0,4},{1,5},{2,6},{3,7},{4,8},{5,9},{6,10},{7,11},{8,12},{9,13},{1... | collective-permute-start | bytes 2359304 | tf_op jit(solution)/shard_map/ppermute | solution.py:15
  89.2 17.2 %copy-start.9 = (bf16[512,768]{1,0:T(8,128)(2,1)S(1)}, bf16[512,768]{1,0:T(8,128)(2,1)}, u32[]{:S(2)}) copy-start(bf16[512,768]{1,0:T(8,128)(2,1)} %copy-done.8) | copy-start | bytes 2359300
  120.8 2.1 copy-start.5
  120.8 2.1 copy-start.20
  124.6 21.1 %collective-permute-start.4 = (bf16[1,512,384]{2,1,0:T(8,128)(2,1)}, bf16[1,512,384]{2,1,0:T(8,128)(2,1)}, u32[]{:S(2)}, u32[]{:S(2)}) collective-permute-start(bf16[1,512,384]{2,1,0:T(8,128)(2,1)} %bitcast.23), channel_id=1, source_target_pairs={{4,0},{5,1},{6,2},{7,3},{8,4},{9,5},{10,6},{11,7},{12,8},{13,9},{1... | collective-permute-start | bytes 1179656 | tf_op jit(solution)/shard_map/ppermute | solution.py:15
  129.3 18.2 %collective-permute-start.5 = (bf16[1,512,384]{2,1,0:T(8,128)(2,1)}, bf16[1,512,384]{2,1,0:T(8,128)(2,1)}, u32[]{:S(2)}, u32[]{:S(2)}) collective-permute-start(bf16[1,512,384]{2,1,0:T(8,128)(2,1)} %bitcast.23), channel_id=1, source_target_pairs={{0,4},{1,5},{2,6},{3,7},{4,8},{5,9},{6,10},{7,11},{8,12},{9,13},{1... | collective-permute-start | bytes 1179656 | tf_op jit(solution)/shard_map/ppermute | solution.py:15
  139.6 15.6 %all-to-all-start.3 = ((bf16[16,24,768]{2,1,0:T(8,128)(2,1)}), bf16[16,24,768]{2,1,0:T(8,128)(2,1)S(1)}, u32[]{:S(2)}, u32[]{:S(2)}) async-start(bf16[16,24,768]{2,1,0:T(8,128)(2,1)} %convolution_convert_fusion), calls=%async_computation.3 | async-start | bytes 1179648 | tf_op jit(solution)/shard_map/all_to_all | solution.py:27
  145.7 1.8 copy-start.2
  145.7 1.8 copy-start.10
  147.5 3.9 %copy-start.12 = (f32[512,384]{1,0:T(8,128)S(1)}, f32[512,384]{1,0:T(8,128)}, u32[]{:S(2)}) copy-start(f32[512,384]{1,0:T(8,128)} %copy-done.11) | copy-start | bytes 2359300
  150.5 0.9 copy-start.21
  155.1 30.9 %copy-start.14 = (f32[384]{0:T(512)S(1)}, f32[384]{0:T(512)}, u32[]{:S(2)}) copy-start(f32[384]{0:T(512)} %copy-done.13) | copy-start | bytes 4612
  155.2 14.5 %all-to-all-start.2 = ((bf16[16,24,768]{2,1,0:T(8,128)(2,1)}), bf16[16,24,768]{2,1,0:T(8,128)(2,1)S(1)}, u32[]{:S(2)}, u32[]{:S(2)}) async-start(bf16[16,24,768]{2,1,0:T(8,128)(2,1)} %bitcast.26), calls=%async_computation.2 | async-start | bytes 1179648 | tf_op jit(solution)/shard_map/all_to_all | solution.py:27
  161.0 25.0 %copy-start.4 = (bf16[384,1,768]{2,1,0:T(2,128)(2,1)S(1)}, bf16[384,1,768]{2,1,0:T(2,128)(2,1)}, u32[]{:S(2)}) copy-start(bf16[384,1,768]{2,1,0:T(2,128)(2,1)} %copy-done.3) | copy-start | bytes 1769476
  171.7 32.6 %all-to-all-start.4 = ((f32[32,1,1152]{2,1,0:T(1,128)}), f32[32,1,1152]{2,1,0:T(1,128)}, u32[]{:S(2)}, u32[]{:S(2)}) async-start(f32[32,1,1152]{2,1,0:T(1,128)} %reshape_reshape.4), calls=%async_computation.4 | async-start | bytes 294912 | tf_op jit(solution)/shard_map/all_to_all | solution.py:27
  189.1 25.9 %collective-permute-start.6 = (bf16[1,512,384]{2,1,0:T(8,128)(2,1)}, bf16[1,512,384]{2,1,0:T(8,128)(2,1)}, u32[]{:S(2)}, u32[]{:S(2)}) collective-permute-start(bf16[1,512,384]{2,1,0:T(8,128)(2,1)} %bitcast.30), channel_id=1, source_target_pairs={{2,0},{3,1},{4,2},{5,3},{6,4},{7,5},{8,6},{9,7},{10,8},{11,9},{12,... | collective-permute-start | bytes 1179656 | tf_op jit(solution)/shard_map/ppermute | solution.py:15
  191.4 25.3 %collective-permute-start.7 = (bf16[1,512,384]{2,1,0:T(8,128)(2,1)}, bf16[1,512,384]{2,1,0:T(8,128)(2,1)}, u32[]{:S(2)}, u32[]{:S(2)}) collective-permute-start(bf16[1,512,384]{2,1,0:T(8,128)(2,1)} %bitcast.30), channel_id=1, source_target_pairs={{0,2},{1,3},{2,4},{3,5},{4,6},{5,7},{6,8},{7,9},{8,10},{9,11},{10,... | collective-permute-start | bytes 1179656 | tf_op jit(solution)/shard_map/ppermute | solution.py:15
  206.0 26.4 %all-to-all-start.5 = ((f32[32,1,1152]{2,1,0:T(1,128)}), f32[32,1,1152]{2,1,0:T(1,128)S(1)}, u32[]{:S(2)}, u32[]{:S(2)}) async-start(f32[32,1,1152]{2,1,0:T(1,128)} %broadcast_in_dim.8), calls=%async_computation.5 | async-start | bytes 294912 | tf_op jit(solution)/shard_map/all_to_all | solution.py:21
  214.9 1.8 copy-start.7
  215.0 1.7 copy-start.22

commit v5 on v4

--- a/solution.py
+++ b/solution.py
@@ -29,9 +29,13 @@
 
 
 def reduced_over_dp(value):
-    dp_size = lax.axis_size("dp")
-    own_piece = summed_over(value.reshape(dp_size, -1), "dp")
-    return gathered(own_piece, "dp").reshape(value.shape)
+    peers = lax.axis_size("dp")
+    distance = 1
+    while distance < peers:
+        pairs = [(i, i ^ distance) for i in range(peers)]
+        value = value + lax.ppermute(value, "dp", pairs)
+        distance *= 2
+    return value
 
 
 def gelu_tanh(values):

time: 235 us -> 252 us (1.072)
  waiting for transfers between devices: 84.7 us -> 103 us
  starting transfers between devices: 85 us -> 90.2 us
  matrix products: 33.7 us -> 30.1 us
  other arithmetic: 6.8 us -> 3.35 us
    ppermute x0 -> x5, waiting for transfers between devices: none -> 37.1 us  [reduced_over_dp(): value = value + lax.ppermute(value, 'dp', pairs)]
    ppermute x0 -> x5, starting transfers between devices: none -> 27.4 us  [reduced_over_dp(): value = value + lax.ppermute(value, 'dp', pairs)]
    all_to_all x3 -> x2, starting transfers between devices: 26.2 us -> 12.4 us  [summed_over(): arrived = lax.all_to_all(pieces, axis, 0, 0, tiled=True)]
    all_to_all x3 -> x2, waiting for transfers between devices: 37.8 us -> 26.8 us  [gathered(): return lax.all_to_all(copies, axis, 0, 0, tiled=True)]
    all_to_all x3 -> x2, starting transfers between devices: 25.5 us -> 17.4 us  [gathered(): return lax.all_to_all(copies, axis, 0, 0, tiled=True)]
    all_to_all x3 -> x2, waiting for transfers between devices: 15.7 us -> 10.3 us  [summed_over(): arrived = lax.all_to_all(pieces, axis, 0, 0, tiled=True)]
    dot_general x8, matrix products: 19.1 us -> 15.6 us  [contract_last(): lax.dot_general(left, right, (((1,), (1,)), ((), ())), preferred_element_...]
  transfers between devices with their start and end apart: 14 -> 17, of which waited for: 9 -> 10; matrix products, arithmetic and copies ran while one was open for 20% -> 18% of each run, Pallas kernels for 0% -> 0%
where the time goes in v5:
time: 252 us; the launch traced here: 250 us
  waiting for transfers between devices  103 us (41%)
  starting transfers between devices  90.2 us (36%)
  matrix products  30.1 us (12%)
  local copies, waits for them, and re-layouts  21.1 us (8%)
  other arithmetic  3.35 us (1%)
    ppermute x5, waiting for transfers between devices, reduced_over_dp(): value = value + lax.ppermute(value, 'dp', pairs)  37.1 us
    ppermute x8, starting transfers between devices, passed_along(): return lax.ppermute(value, axis, pairs)  33 us
    ppermute x8, waiting for transfers between devices, passed_along(): return lax.ppermute(value, axis, pairs)  29.1 us
    ppermute x5, starting transfers between devices, reduced_over_dp(): value = value + lax.ppermute(value, 'dp', pairs)  27.4 us
    all_to_all x2, waiting for transfers between devices, gathered(): return lax.all_to_all(copies, axis, 0, 0, tiled=True)  26.8 us
    all_to_all x2, starting transfers between devices, gathered(): return lax.all_to_all(copies, axis, 0, 0, tiled=True)  17.4 us
    dot_general x8, matrix products, contract_last(): lax.dot_general(left, right, (((1,), (1,)), ((), ())), preferred_element_...  15.6 us
    all_to_all x2, starting transfers between devices, summed_over(): arrived = lax.all_to_all(pieces, axis, 0, 0, tiled=True)  12.4 us
  transfers between devices with their start and end apart: 17, of which 10 were waited for; matrix products, arithmetic and copies ran while one was open for 18% of the time, Pallas kernels for 0%

profile of v5, /device:TPU:6, one launch (start us, length us, event | category | flops | bytes accessed | tf_op | source)
XLA Modules:
  0.0 250.5 jit_solution(3802401041607056381)
XLA Ops:
  2.6 1.8 broadcast_in_dim.4
  4.4 10.2 %all-to-all-start = ((bf16[16,240,384]{2,1,0:T(8,128)(2,1)}), bf16[16,240,384]{2,1,0:T(8,128)(2,1)}, u32[]{:S(2)}, u32[]{:S(2)}) async-start(bf16[16,240,384]{2,1,0:T(8,128)(2,1)} %broadcast_in_dim.4), calls=%async_computation | async-start | bytes 5898240 | tf_op jit(solution)/shard_map/all_to_all | solution.py:21
  14.8 1.5 fusion.13
  16.3 2.7 %collective-permute-start.1 = (bf16[1,512,768]{2,1,0:T(8,128)(2,1)}, bf16[1,512,768]{2,1,0:T(8,128)(2,1)}, u32[]{:S(2)}, u32[]{:S(2)}) collective-permute-start(bf16[1,512,768]{2,1,0:T(8,128)(2,1)} %fusion.13), channel_id=1, source_target_pairs={{2,0},{3,1},{4,2},{5,3},{6,4},{7,5},{8,6},{9,7},{10,8},{11,9},{12,... | collective-permute-start | bytes 2359304 | tf_op jit(solution)/shard_map/ppermute | solution.py:15
  19.0 5.2 %collective-permute-start = (bf16[1,512,768]{2,1,0:T(8,128)(2,1)}, bf16[1,512,768]{2,1,0:T(8,128)(2,1)}, u32[]{:S(2)}, u32[]{:S(2)}) collective-permute-start(bf16[1,512,768]{2,1,0:T(8,128)(2,1)} %fusion.13), channel_id=1, source_target_pairs={{0,2},{1,3},{2,4},{3,5},{4,6},{5,7},{6,8},{7,9},{8,10},{9,11},{10,... | collective-permute-start | bytes 2359304 | tf_op jit(solution)/shard_map/ppermute | solution.py:15
  25.6 26.7 %all-to-all-done = bf16[16,240,384]{2,1,0:T(8,128)(2,1)} async-done(((bf16[16,240,384]{2,1,0:T(8,128)(2,1)}), bf16[16,240,384]{2,1,0:T(8,128)(2,1)}, u32[]{:S(2)}, u32[]{:S(2)}) %all-to-all-start) | async-done | bytes 2949152 | tf_op jit(solution)/shard_map/all_to_all | solution.py:21
  52.3 1.7 slice.102
  54.1 1.4 broadcast_in_dim.5
  55.5 7.1 %all-to-all-start.1 = ((bf16[16,3,48,384]{3,2,1,0:T(8,128)(2,1)}), bf16[16,3,48,384]{3,2,1,0:T(8,128)(2,1)}, u32[]{:S(2)}, u32[]{:S(2)}) async-start(bf16[16,3,48,384]{3,2,1,0:T(8,128)(2,1)} %broadcast_in_dim.5), calls=%async_computation.1 | async-start | bytes 3538944 | tf_op jit(solution)/shard_map/all_to_all | solution.py:21
  62.6 2.4 slice.103
  65.0 2.9 %reshape.110 = bf16[384,2,768]{2,1,0:T(2,128)(2,1)S(1)} reshape(bf16[16,96,384]{2,1,0:T(8,128)(2,1)} %slice.103) | data formatting | bytes 2359296 | tf_op jit(solution)/shard_map/reshape | solution.py:121
  68.0 1.7 fusion.75
  69.7 1.7 fusion.73
  71.4 1.7 fusion.42
  73.2 2.6 %fusion.123 = (bf16[384,1,768]{2,1,0:T(2,128)(2,1)}, bf16[384,1,768]{2,1,0:T(2,128)(2,1)S(1)}) fusion(bf16[384,2,768]{2,1,0:T(2,128)(2,1)S(1)} %reshape.110), kind=kLoop, calls=%fused_computation.148 | loop fusion | bytes 2359296 | tf_op jit(solution)/shard_map/slice | solution.py:155
  77.8 1.5 fusion.121
  79.3 5.2 %collective-permute-start.3 = (bf16[1,512,768]{2,1,0:T(8,128)(2,1)}, bf16[1,512,768]{2,1,0:T(8,128)(2,1)}, u32[]{:S(2)}, u32[]{:S(2)}) collective-permute-start(bf16[1,512,768]{2,1,0:T(8,128)(2,1)} %fusion.121), channel_id=1, source_target_pairs={{4,0},{5,1},{6,2},{7,3},{8,4},{9,5},{10,6},{11,7},{12,8},{13,9},{1... | collective-permute-start | bytes 2359304 | tf_op jit(solution)/shard_map/ppermute | solution.py:15
  85.2 3.0 %collective-permute-start.2 = (bf16[1,512,768]{2,1,0:T(8,128)(2,1)}, bf16[1,512,768]{2,1,0:T(8,128)(2,1)}, u32[]{:S(2)}, u32[]{:S(2)}) collective-permute-start(bf16[1,512,768]{2,1,0:T(8,128)(2,1)} %fusion.121), channel_id=1, source_target_pairs={{0,4},{1,5},{2,6},{3,7},{4,8},{5,9},{6,10},{7,11},{8,12},{9,13},{1... | collective-permute-start | bytes 2359304 | tf_op jit(solution)/shard_map/ppermute | solution.py:15
  88.2 1.6 fusion.122
  89.9 15.4 %collective-permute-done.3 = bf16[1,512,768]{2,1,0:T(8,128)(2,1)} collective-permute-done((bf16[1,512,768]{2,1,0:T(8,128)(2,1)}, bf16[1,512,768]{2,1,0:T(8,128)(2,1)}, u32[]{:S(2)}, u32[]{:S(2)}) %collective-permute-start.3) | collective-permute-done | bytes 786464 | tf_op jit(solution)/shard_map/ppermute | solution.py:15
  105.3 1.7 fusion.68
  107.8 13.7 %collective-permute-done.2 = bf16[1,512,768]{2,1,0:T(8,128)(2,1)} collective-permute-done((bf16[1,512,768]{2,1,0:T(8,128)(2,1)}, bf16[1,512,768]{2,1,0:T(8,128)(2,1)}, u32[]{:S(2)}, u32[]{:S(2)}) %collective-permute-start.2) | collective-permute-done | bytes 786464 | tf_op jit(solution)/shard_map/ppermute | solution.py:15
  121.5 2.1 fusion.66
  123.6 1.7 fusion.58
  125.3 1.9 collective-permute-start.4
  127.2 2.8 %fusion.126 = f32[512,768]{1,0:T(8,128)} fusion(bf16[512,384]{1,0:T(8,128)(2,1)} %fusion.58, bf16[768,384]{1,0:T(8,128)(2,1)S(1)} %bitcast.158), kind=kOutput, calls=%fused_computation.151 | convolution fusion | flops 301989888 | bytes 2555904 | tf_op jit(solution)/shard_map/dot_general | solution.py:46
  130.0 7.0 %collective-permute-start.5 = (bf16[1,512,384]{2,1,0:T(8,128)(2,1)}, bf16[1,512,384]{2,1,0:T(8,128)(2,1)}, u32[]{:S(2)}, u32[]{:S(2)}) collective-permute-start(bf16[1,512,384]{2,1,0:T(8,128)(2,1)} %bitcast.23), channel_id=1, source_target_pairs={{0,4},{1,5},{2,6},{3,7},{4,8},{5,9},{6,10},{7,11},{8,12},{9,13},{1... | collective-permute-start | bytes 1179656 | tf_op jit(solution)/shard_map/ppermute | solution.py:15
  137.9 2.6 %convolution_convert_fusion = bf16[16,24,768]{2,1,0:T(8,128)(2,1)} fusion(bf16[16,24,512]{2,1,0:T(8,128)(2,1)} %bitcast.171, bf16[1,512,768]{2,1,0:T(8,128)(2,1)} %param.10, f32[]{:T(128)} %bitcast.13), kind=kOutput, calls=%fused_computation.50 | convolution fusion | flops 303464448 | bytes 1769476 | tf_op jit(solution)/shard_map/dot_general | solution.py:89
  140.4 6.1 %all-to-all-start.3 = ((bf16[16,24,768]{2,1,0:T(8,128)(2,1)}), bf16[16,24,768]{2,1,0:T(8,128)(2,1)S(1)}, u32[]{:S(2)}, u32[]{:S(2)}) async-start(bf16[16,24,768]{2,1,0:T(8,128)(2,1)} %convolution_convert_fusion), calls=%async_computation.3 | async-start | bytes 1179648 | tf_op jit(solution)/shard_map/all_to_all | solution.py:27
  146.6 1.7 fusion.115
  148.4 3.0 %fusion.21 = bf16[512,768]{1,0:T(8,128)(2,1)S(1)} fusion(bf16[1,512,768]{2,1,0:T(8,128)(2,1)} %param.10, f32[512,768]{1,0:T(8,128)S(1)} %fusion.115, f32[512,768]{1,0:T(8,128)S(1)} %copy-done, bf16[512,768]{1,0:T(8,128)(2,1)S(1)} %copy-done.8, f32[768]{0:T(1024)S(1)} %get-tuple-element.13, f32[768]{0:T(1024)S(1)} %get-tuple-element.29, ...), kind=kOutput, calls=%fused_computation.32 | convolution fusion | flops 312999936 | bytes 6494208 | tf_op jit(solution)/shard_map/dot_general | solution.py:46
  152.2 1.6 convolution_convert_fusion.1
  153.8 1.7 all-to-all-done.3
  155.5 6.3 %all-to-all-start.2 = ((bf16[16,24,768]{2,1,0:T(8,128)(2,1)}), bf16[16,24,768]{2,1,0:T(8,128)(2,1)S(1)}, u32[]{:S(2)}, u32[]{:S(2)}) async-start(bf16[16,24,768]{2,1,0:T(8,128)(2,1)} %bitcast.167), calls=%async_computation.2 | async-start | bytes 1179648 | tf_op jit(solution)/shard_map/all_to_all | solution.py:27
  161.8 8.6 %all-to-all-done.2 = bf16[16,24,768]{2,1,0:T(8,128)(2,1)S(1)} async-done(((bf16[16,24,768]{2,1,0:T(8,128)(2,1)}), bf16[16,24,768]{2,1,0:T(8,128)(2,1)S(1)}, u32[]{:S(2)}, u32[]{:S(2)}) %all-to-all-start.2) | async-done | bytes 589856 | tf_op jit(solution)/shard_map/all_to_all | solution.py:27
  170.6 1.9 collective-permute-start.6
  172.5 7.9 %collective-permute-done.6 = f32[24,2,768]{2,0,1:T(8,128)S(1)} collective-permute-done((f32[24,2,768]{2,0,1:T(8,128)S(1)}, f32[24,2,768]{2,0,1:T(8,128)S(1)}, u32[]{:S(2)}, u32[]{:S(2)}) %collective-permute-start.6) | collective-permute-done | bytes 147488 | tf_op jit(solution)/shard_map/ppermute | solution.py:36
  180.4 1.9 collective-permute-start.7
  182.3 2.7 %fusion.50 = bf16[512,384]{1,0:T(8,128)(2,1)S(1)} fusion(f32[512,384]{1,0:T(8,128)} %copy-done.9, bf16[512,768]{1,0:T(8,128)(2,1)} %copy-done.19, f32[]{:T(128)} %bitcast.11, f32[384]{0:T(512)S(1)} %copy-done.12, bf16[384,1,768]{2,1,0:T(2,128)(2,1)} %copy-done.1), kind=kOutput, calls=%fused_computation.74 | convolution fusion | flops 307298304 | bytes 2557444 | tf_op jit(solution)/shard_map/dot_general | solution.py:46
  185.0 2.3 collective-permute-start.11
  187.3 5.7 %collective-permute-start.12 = (bf16[1,512,384]{2,1,0:T(8,128)(2,1)S(1)}, bf16[1,512,384]{2,1,0:T(8,128)(2,1)S(1)}, u32[]{:S(2)}, u32[]{:S(2)}) collective-permute-start(bf16[1,512,384]{2,1,0:T(8,128)(2,1)S(1)} %bitcast.170), channel_id=1, source_target_pairs={{0,2},{1,3},{2,4},{3,5},{4,6},{5,7},{6,8},{7,9},{8,10},{9,11},{10,... | collective-permute-start | bytes 1179656 | tf_op jit(solution)/shard_map/ppermute | solution.py:15
  193.0 2.8 %collective-permute-start.8 = (f32[24,2,768]{2,0,1:T(8,128)S(1)}, f32[24,2,768]{2,0,1:T(8,128)S(1)}, u32[]{:S(2)}, u32[]{:S(2)}) collective-permute-start(f32[24,2,768]{2,0,1:T(8,128)S(1)} %fusion.136), channel_id=1, source_target_pairs={{0,64},{16,80},{32,96},{48,112},{64,0},{80,16},{96,32},{112,48},{1... | collective-permute-start | bytes 442376 | tf_op jit(solution)/shard_map/ppermute | solution.py:36
  196.4 7.5 %collective-permute-done.8 = f32[24,2,768]{2,0,1:T(8,128)S(1)} collective-permute-done((f32[24,2,768]{2,0,1:T(8,128)S(1)}, f32[24,2,768]{2,0,1:T(8,128)S(1)}, u32[]{:S(2)}, u32[]{:S(2)}) %collective-permute-start.8) | collective-permute-done | bytes 147488 | tf_op jit(solution)/shard_map/ppermute | solution.py:36
  204.0 6.9 %collective-permute-start.9 = (f32[24,2,768]{2,0,1:T(8,128)S(1)}, f32[24,2,768]{2,0,1:T(8,128)S(1)}, u32[]{:S(2)}, u32[]{:S(2)}) collective-permute-start(f32[24,2,768]{2,0,1:T(8,128)S(1)} %add.185), channel_id=1, source_target_pairs={{0,128},{16,144},{32,160},{48,176},{64,192},{80,208},{96,224},{112... | collective-permute-start | bytes 442376 | tf_op jit(solution)/shard_map/ppermute | solution.py:36
  211.5 11.6 %collective-permute-done.9 = f32[24,2,768]{2,0,1:T(8,128)S(1)} collective-permute-done((f32[24,2,768]{2,0,1:T(8,128)S(1)}, f32[24,2,768]{2,0,1:T(8,128)S(1)}, u32[]{:S(2)}, u32[]{:S(2)}) %collective-permute-start.9) | collective-permute-done | bytes 147488 | tf_op jit(solution)/shard_map/ppermute | solution.py:36
  223.2 13.9 %collective-permute-start.10 = (f32[24,2,768]{2,0,1:T(8,128)S(1)}, f32[24,2,768]{2,0,1:T(8,128)S(1)}, u32[]{:S(2)}, u32[]{:S(2)}) collective-permute-start(f32[24,2,768]{2,0,1:T(8,128)S(1)} %add.186), channel_id=1, source_target_pairs={{0,256},{16,272},{32,288},{48,304},{64,320},{80,336},{96,352},{112... | collective-permute-start | bytes 442376 | tf_op jit(solution)/shard_map/ppermute | solution.py:36
  237.1 2.5 %fusion.78 = bf16[1,512,768]{2,1,0:T(8,128)(2,1)} fusion(f32[768]{0:T(1024)S(1)} %get-tuple-element.12, f32[768]{0:T(1024)S(1)} %get-tuple-element.30, bf16[1,512,768]{2,1,0:T(8,128)(2,1)S(1)} %copy-done.5, f32[512,768]{1,0:T(8,128)S(1)} %fusion.100, f32[512,768]{1,0:T(8,128)S(1)} %fusion.97, bf16[512,768]{1,0:T(8,128)(2,1)S(1)} %copy-done.20, ...), kind=kOutput, calls=%fused_computation.103 | convolution fusion | flops 312999936 | bytes 6496256 | tf_op jit(solution)/shard_map/dot_general | solution.py:46
  239.6 10.1 %collective-permute-done.10 = f32[24,2,768]{2,0,1:T(8,128)S(1)} collective-permute-done((f32[24,2,768]{2,0,1:T(8,128)S(1)}, f32[24,2,768]{2,0,1:T(8,128)S(1)}, u32[]{:S(2)}, u32[]{:S(2)}) %collective-permute-start.10) | collective-permute-done | bytes 147488 | tf_op jit(solution)/shard_map/ppermute | solution.py:36
  (71 shorter events, 9.7 us)
Async XLA Ops:
  4.4 10.2 %copy-start.13 = (f32[2,768]{1,0:T(2,128)S(1)}, f32[2,768]{1,0:T(2,128)}, u32[]{:S(2)}) copy-start(f32[2,768]{1,0:T(2,128)} %param.13) | copy-start | bytes 18436
  4.4 10.2 %copy-start.14 = (f32[2,768]{1,0:T(2,128)S(1)}, f32[2,768]{1,0:T(2,128)}, u32[]{:S(2)}) copy-start(f32[2,768]{1,0:T(2,128)} %param.12) | copy-start | bytes 18436
  4.4 10.3 %copy-start.3 = (bf16[1,512,768]{2,1,0:T(8,128)(2,1)S(1)}, bf16[1,512,768]{2,1,0:T(8,128)(2,1)}, u32[]{:S(2)}) copy-start(bf16[1,512,768]{2,1,0:T(8,128)(2,1)} %param.9) | copy-start | bytes 2359300
  4.4 47.8 %all-to-all-start = ((bf16[16,240,384]{2,1,0:T(8,128)(2,1)}), bf16[16,240,384]{2,1,0:T(8,128)(2,1)}, u32[]{:S(2)}, u32[]{:S(2)}) async-start(bf16[16,240,384]{2,1,0:T(8,128)(2,1)} %broadcast_in_dim.4), calls=%async_computation | async-start | bytes 5898240 | tf_op jit(solution)/shard_map/all_to_all | solution.py:21
  14.7 9.6 %copy-start.17 = (s32[1,2]{1,0:T(1,128)S(1)}, s32[1,2]{1,0:T(1,128)}, u32[]{:S(2)}) copy-start(s32[1,2]{1,0:T(1,128)} %param.11) | copy-start | bytes 28
  14.7 10.8 %copy-start.15 = (f32[2,384]{1,0:T(2,128)S(1)}, f32[2,384]{1,0:T(2,128)}, u32[]{:S(2)}) copy-start(f32[2,384]{1,0:T(2,128)} %param.15) | copy-start | bytes 9220
  14.7 10.8 %copy-start.16 = (f32[2,384]{1,0:T(2,128)S(1)}, f32[2,384]{1,0:T(2,128)}, u32[]{:S(2)}) copy-start(f32[2,384]{1,0:T(2,128)} %param.14) | copy-start | bytes 9220
  16.3 53.4 %collective-permute-start.1 = (bf16[1,512,768]{2,1,0:T(8,128)(2,1)}, bf16[1,512,768]{2,1,0:T(8,128)(2,1)}, u32[]{:S(2)}, u32[]{:S(2)}) collective-permute-start(bf16[1,512,768]{2,1,0:T(8,128)(2,1)} %fusion.13), channel_id=1, source_target_pairs={{2,0},{3,1},{4,2},{5,3},{6,4},{7,5},{8,6},{9,7},{10,8},{11,9},{12,... | collective-permute-start | bytes 2359304 | tf_op jit(solution)/shard_map/ppermute | solution.py:15
  19.0 52.4 %collective-permute-start = (bf16[1,512,768]{2,1,0:T(8,128)(2,1)}, bf16[1,512,768]{2,1,0:T(8,128)(2,1)}, u32[]{:S(2)}, u32[]{:S(2)}) collective-permute-start(bf16[1,512,768]{2,1,0:T(8,128)(2,1)} %fusion.13), channel_id=1, source_target_pairs={{0,2},{1,3},{2,4},{3,5},{4,6},{5,7},{6,8},{7,9},{8,10},{9,11},{10,... | collective-permute-start | bytes 2359304 | tf_op jit(solution)/shard_map/ppermute | solution.py:15
  25.6 45.8 %copy-start.11 = (f32[384]{0:T(512)}, f32[384]{0:T(512)S(1)}, u32[]{:S(2)}) copy-start(f32[384]{0:T(512)S(1)} %get-tuple-element.31) | copy-start | bytes 4612
  55.5 32.7 %all-to-all-start.1 = ((bf16[16,3,48,384]{3,2,1,0:T(8,128)(2,1)}), bf16[16,3,48,384]{3,2,1,0:T(8,128)(2,1)}, u32[]{:S(2)}, u32[]{:S(2)}) async-start(bf16[16,3,48,384]{3,2,1,0:T(8,128)(2,1)} %broadcast_in_dim.5), calls=%async_computation.1 | async-start | bytes 3538944 | tf_op jit(solution)/shard_map/all_to_all | solution.py:21
  73.1 2.7 %copy-start.9 = (f32[512,384]{1,0:T(8,128)}, f32[512,384]{1,0:T(8,128)S(1)}, u32[]{:S(2)}) copy-start(f32[512,384]{1,0:T(8,128)S(1)} %fusion.42) | copy-start | bytes 2359300
  73.2 2.7 %copy-start.4 = (bf16[1,512,768]{2,1,0:T(8,128)(2,1)S(1)}, bf16[1,512,768]{2,1,0:T(8,128)(2,1)}, u32[]{:S(2)}) copy-start(bf16[1,512,768]{2,1,0:T(8,128)(2,1)} %param.9) | copy-start | bytes 2359300
  75.8 1.1 copy-start.1
  76.9 0.9 copy-start.6
  79.3 26.0 %collective-permute-start.3 = (bf16[1,512,768]{2,1,0:T(8,128)(2,1)}, bf16[1,512,768]{2,1,0:T(8,128)(2,1)}, u32[]{:S(2)}, u32[]{:S(2)}) collective-permute-start(bf16[1,512,768]{2,1,0:T(8,128)(2,1)} %fusion.121), channel_id=1, source_target_pairs={{4,0},{5,1},{6,2},{7,3},{8,4},{9,5},{10,6},{11,7},{12,8},{13,9},{1... | collective-permute-start | bytes 2359304 | tf_op jit(solution)/shard_map/ppermute | solution.py:15
  85.2 36.3 %collective-permute-start.2 = (bf16[1,512,768]{2,1,0:T(8,128)(2,1)}, bf16[1,512,768]{2,1,0:T(8,128)(2,1)}, u32[]{:S(2)}, u32[]{:S(2)}) collective-permute-start(bf16[1,512,768]{2,1,0:T(8,128)(2,1)} %fusion.121), channel_id=1, source_target_pairs={{0,4},{1,5},{2,6},{3,7},{4,8},{5,9},{6,10},{7,11},{8,12},{9,13},{1... | collective-permute-start | bytes 2359304 | tf_op jit(solution)/shard_map/ppermute | solution.py:15
  89.8 17.2 %copy-start.7 = (bf16[512,768]{1,0:T(8,128)(2,1)S(1)}, bf16[512,768]{1,0:T(8,128)(2,1)}, u32[]{:S(2)}) copy-start(bf16[512,768]{1,0:T(8,128)(2,1)} %copy-done.6) | copy-start | bytes 2359300
  121.5 2.1 copy-start.2
  121.5 2.1 copy-start.18
  125.3 21.3 %collective-permute-start.4 = (bf16[1,512,384]{2,1,0:T(8,128)(2,1)}, bf16[1,512,384]{2,1,0:T(8,128)(2,1)}, u32[]{:S(2)}, u32[]{:S(2)}) collective-permute-start(bf16[1,512,384]{2,1,0:T(8,128)(2,1)} %bitcast.23), channel_id=1, source_target_pairs={{4,0},{5,1},{6,2},{7,3},{8,4},{9,5},{10,6},{11,7},{12,8},{13,9},{1... | collective-permute-start | bytes 1179656 | tf_op jit(solution)/shard_map/ppermute | solution.py:15
  130.0 18.4 %collective-permute-start.5 = (bf16[1,512,384]{2,1,0:T(8,128)(2,1)}, bf16[1,512,384]{2,1,0:T(8,128)(2,1)}, u32[]{:S(2)}, u32[]{:S(2)}) collective-permute-start(bf16[1,512,384]{2,1,0:T(8,128)(2,1)} %bitcast.23), channel_id=1, source_target_pairs={{0,4},{1,5},{2,6},{3,7},{4,8},{5,9},{6,10},{7,11},{8,12},{9,13},{1... | collective-permute-start | bytes 1179656 | tf_op jit(solution)/shard_map/ppermute | solution.py:15
  140.4 15.0 %all-to-all-start.3 = ((bf16[16,24,768]{2,1,0:T(8,128)(2,1)}), bf16[16,24,768]{2,1,0:T(8,128)(2,1)S(1)}, u32[]{:S(2)}, u32[]{:S(2)}) async-start(bf16[16,24,768]{2,1,0:T(8,128)(2,1)} %convolution_convert_fusion), calls=%async_computation.3 | async-start | bytes 1179648 | tf_op jit(solution)/shard_map/all_to_all | solution.py:27
  146.6 1.8 copy-start
  146.6 1.8 copy-start.8
  148.3 3.9 %copy-start.10 = (f32[512,384]{1,0:T(8,128)S(1)}, f32[512,384]{1,0:T(8,128)}, u32[]{:S(2)}) copy-start(f32[512,384]{1,0:T(8,128)} %copy-done.9) | copy-start | bytes 2359300
  151.3 0.9 copy-start.19
  155.5 26.8 %copy-start.12 = (f32[384]{0:T(512)S(1)}, f32[384]{0:T(512)}, u32[]{:S(2)}) copy-start(f32[384]{0:T(512)} %copy-done.11) | copy-start | bytes 4612
  155.5 15.0 %all-to-all-start.2 = ((bf16[16,24,768]{2,1,0:T(8,128)(2,1)}), bf16[16,24,768]{2,1,0:T(8,128)(2,1)S(1)}, u32[]{:S(2)}, u32[]{:S(2)}) async-start(bf16[16,24,768]{2,1,0:T(8,128)(2,1)} %bitcast.167), calls=%async_computation.2 | async-start | bytes 1179648 | tf_op jit(solution)/shard_map/all_to_all | solution.py:27
  170.6 9.8 %collective-permute-start.6 = (f32[24,2,768]{2,0,1:T(8,128)S(1)}, f32[24,2,768]{2,0,1:T(8,128)S(1)}, u32[]{:S(2)}, u32[]{:S(2)}) collective-permute-start(f32[24,2,768]{2,0,1:T(8,128)S(1)} %pad_maximum_fusion.1), channel_id=1, source_target_pairs={{0,16},{16,0},{32,48},{48,32},{64,80},{80,64},{96,112},{112,96},{1... | collective-permute-start | bytes 442376 | tf_op jit(solution)/shard_map/ppermute | solution.py:36
  180.4 12.6 %collective-permute-start.7 = (f32[24,2,768]{2,0,1:T(8,128)S(1)}, f32[24,2,768]{2,0,1:T(8,128)S(1)}, u32[]{:S(2)}, u32[]{:S(2)}) collective-permute-start(f32[24,2,768]{2,0,1:T(8,128)S(1)} %fusion.119), channel_id=1, source_target_pairs={{0,32},{16,48},{32,0},{48,16},{64,96},{80,112},{96,64},{112,80},{1... | collective-permute-start | bytes 442376 | tf_op jit(solution)/shard_map/ppermute | solution.py:36
  185.0 25.9 %collective-permute-start.11 = (bf16[1,512,384]{2,1,0:T(8,128)(2,1)S(1)}, bf16[1,512,384]{2,1,0:T(8,128)(2,1)S(1)}, u32[]{:S(2)}, u32[]{:S(2)}) collective-permute-start(bf16[1,512,384]{2,1,0:T(8,128)(2,1)S(1)} %bitcast.169), channel_id=1, source_target_pairs={{2,0},{3,1},{4,2},{5,3},{6,4},{7,5},{8,6},{9,7},{10,8},{11,9},{12,... | collective-permute-start | bytes 1179656 | tf_op jit(solution)/shard_map/ppermute | solution.py:15
  187.3 49.8 %collective-permute-start.12 = (bf16[1,512,384]{2,1,0:T(8,128)(2,1)S(1)}, bf16[1,512,384]{2,1,0:T(8,128)(2,1)S(1)}, u32[]{:S(2)}, u32[]{:S(2)}) collective-permute-start(bf16[1,512,384]{2,1,0:T(8,128)(2,1)S(1)} %bitcast.170), channel_id=1, source_target_pairs={{0,2},{1,3},{2,4},{3,5},{4,6},{5,7},{6,8},{7,9},{8,10},{9,11},{10,... | collective-permute-start | bytes 1179656 | tf_op jit(solution)/shard_map/ppermute | solution.py:15
  193.0 10.9 %collective-permute-start.8 = (f32[24,2,768]{2,0,1:T(8,128)S(1)}, f32[24,2,768]{2,0,1:T(8,128)S(1)}, u32[]{:S(2)}, u32[]{:S(2)}) collective-permute-start(f32[24,2,768]{2,0,1:T(8,128)S(1)} %fusion.136), channel_id=1, source_target_pairs={{0,64},{16,80},{32,96},{48,112},{64,0},{80,16},{96,32},{112,48},{1... | collective-permute-start | bytes 442376 | tf_op jit(solution)/shard_map/ppermute | solution.py:36
  203.9 33.1 %copy-start.5 = (bf16[1,512,768]{2,1,0:T(8,128)(2,1)S(1)}, bf16[1,512,768]{2,1,0:T(8,128)(2,1)}, u32[]{:S(2)}) copy-start(bf16[1,512,768]{2,1,0:T(8,128)(2,1)} %param.9) | copy-start | bytes 2359300
  204.0 33.1 %copy-start.20 = (bf16[512,768]{1,0:T(8,128)(2,1)S(1)}, bf16[512,768]{1,0:T(8,128)(2,1)}, u32[]{:S(2)}) copy-start(bf16[512,768]{1,0:T(8,128)(2,1)} %copy-done.19) | copy-start | bytes 2359300
  204.0 19.2 %collective-permute-start.9 = (f32[24,2,768]{2,0,1:T(8,128)S(1)}, f32[24,2,768]{2,0,1:T(8,128)S(1)}, u32[]{:S(2)}, u32[]{:S(2)}) collective-permute-start(f32[24,2,768]{2,0,1:T(8,128)S(1)} %add.185), channel_id=1, source_target_pairs={{0,128},{16,144},{32,160},{48,176},{64,192},{80,208},{96,224},{112... | collective-permute-start | bytes 442376 | tf_op jit(solution)/shard_map/ppermute | solution.py:36
  223.2 26.5 %collective-permute-start.10 = (f32[24,2,768]{2,0,1:T(8,128)S(1)}, f32[24,2,768]{2,0,1:T(8,128)S(1)}, u32[]{:S(2)}, u32[]{:S(2)}) collective-permute-start(f32[24,2,768]{2,0,1:T(8,128)S(1)} %add.186), channel_id=1, source_target_pairs={{0,256},{16,272},{32,288},{48,304},{64,320},{80,336},{96,352},{112... | collective-permute-start | bytes 442376 | tf_op jit(solution)/shard_map/ppermute | solution.py:36

commit v6 on v4

--- a/solution.py
+++ b/solution.py
@@ -87,6 +87,29 @@
     )
 
 
+def strided(block):
+    peers = lax.axis_size("seq")
+    channels = block.shape[-1]
+    rows = block.reshape(-1, peers, channels).swapaxes(0, 1)
+    arrived = lax.all_to_all(rows, "seq", 0, 0, tiled=True)
+    return arrived.reshape(-1, channels)
+
+
+def contiguous(rows):
+    peers = lax.axis_size("seq")
+    channels = rows.shape[-1]
+    pieces = rows.reshape(peers, -1, channels)
+    arrived = lax.all_to_all(pieces, "seq", 0, 0, tiled=True)
+    return arrived.swapaxes(0, 1).reshape(-1, channels)
+
+
+def row_shifted(source, rows_away):
+    padding = jnp.zeros((rows_away, source.shape[1]), source.dtype)
+    earlier = jnp.concatenate([padding, source[: source.shape[0] - rows_away]], axis=0)
+    later = jnp.concatenate([source[rows_away:], padding], axis=0)
+    return (earlier, later)
+
+
 def shards(
     sequence_in,
     output_grad,
@@ -98,13 +121,7 @@
     conv_weight,
     point_weight,
 ):
-    position_list = sequence_in.shape[1]
-    channels = sequence_in.shape[2]
-    def conv_gathered(shard):
-        return jnp.moveaxis(gathered(shard, "seq"), 0, 1).reshape(
-            conv_weight.shape[1], -1, conv_weight.shape[3]
-        )
-
+    peers = lax.axis_size("seq")
     lanes = conv_weight.shape[3]
     conv_rows = conv_weight.shape[1] * conv_weight.shape[2]
     joined = jnp.concatenate(
@@ -116,27 +133,21 @@
     ).reshape(conv_weight.shape[1], -1, lanes)
     point_full = joined_full[:, conv_rows:].reshape(-1, *point_weight.shape[1:])
     second_shard, first_conv = lax.optimization_barrier((conv_weight[1], first_conv))
-    conv_full = [first_conv, conv_gathered(second_shard)]
-    neighbour_reach = (FIRST_DILATION // position_list, SECOND_DILATION // position_list)
-    state = sequence_in.reshape(-1, channels)
-    total_rows = state.shape[0]
+    conv_full = [first_conv, conv_gathered_block(second_shard, conv_weight.shape)]
+    row_reach = (FIRST_DILATION // peers, SECOND_DILATION // peers)
+    state = strided(sequence_in[0])
     saved = []
     for block_index in range(2):
         kept_flag = (1 - skip_mask[0, block_index]).astype(jnp.float32)
         normed = state.astype(jnp.float32) * in_gain[block_index] + input_shift_vec[block_index]
         activated = gelu_tanh(normed).astype(jnp.bfloat16)
-        earlier, later = neighbours(
-            activated.reshape(sequence_in.shape), neighbour_reach[block_index]
-        )
-        earlier = earlier.reshape(total_rows, channels)
-        later = later.reshape(total_rows, channels)
-        weight = conv_full[block_index]
+        earlier, later = row_shifted(activated, row_reach[block_index])
         operands = (
             state,
             earlier,
             activated,
             later,
-            weight,
+            conv_full[block_index],
             mid_gain[block_index],
             mid_offset[block_index],
             point_full[:, block_index, :],
@@ -144,7 +155,7 @@
         )
         middle, hidden_act, state = forward_local(*operands)
         saved.append((normed, middle, hidden_act, kept_flag))
-    gradient = output_grad.reshape(-1, channels)
+    gradient = strided(output_grad[0])
     reduced_terms = [None, None]
     for block_index in (1, 0):
         normed, middle, hidden_act, kept_flag = saved[block_index]
@@ -154,27 +165,26 @@
         reduced_terms[block_index] = summed_over(
             grad_rows(hidden_act, branch_grad), "seq", jnp.bfloat16
         )
-        earlier, later = neighbours(
-            conv_grad.reshape(sequence_in.shape[0], position_list, -1), neighbour_reach[block_index]
-        )
-        earlier = earlier.reshape(total_rows, -1)
-        later = later.reshape(total_rows, -1)
-        weight = conv_full[block_index]
+        earlier, later = row_shifted(conv_grad, row_reach[block_index])
         second_operands = (
             gradient,
             earlier,
             conv_grad,
             later,
-            weight,
+            conv_full[block_index],
             normed,
             in_gain[block_index],
         )
         gradient = backward_second(*second_operands)
     summed = reduced_over_dp(jnp.stack([reduced_terms[0], reduced_terms[1]], axis=1))
     sample_count = sequence_in.shape[0] * lax.axis_size("dp")
-    full_length = position_list * lax.axis_size("seq")
+    full_length = sequence_in.shape[1] * peers
     point_grad = summed * (1.0 / math.sqrt(sample_count * full_length))
-    return (point_grad, gradient.reshape(sequence_in.shape))
+    return (point_grad, contiguous(gradient).reshape(sequence_in.shape))
+
+
+def conv_gathered_block(shard, full_shape):
+    return jnp.moveaxis(gathered(shard, "seq"), 0, 1).reshape(full_shape[1], -1, full_shape[3])
 
 
 def solution(mesh):

time: 235 us -> 239 us (1.017)
  starting transfers between devices: 85 us -> 67.4 us
  waiting for transfers between devices: 84.7 us -> 101 us
  local copies, waits for them, and re-layouts: 21 us -> 29.6 us
  matrix products: 33.7 us -> 27.3 us
    ppermute x8 -> x0, starting transfers between devices: 33.3 us -> none  [passed_along(): return lax.ppermute(value, axis, pairs)]
    ppermute x8 -> x0, waiting for transfers between devices: 31.2 us -> none  [passed_along(): return lax.ppermute(value, axis, pairs)]
    all_to_all x0 -> x3, waiting for transfers between devices: none -> 30.6 us  [the longest x2 20 us: strided(): arrived = lax.all_to_all(rows, 'seq', 0, 0, tiled=True)]
    all_to_all x0 -> x3, starting transfers between devices: none -> 21.6 us  [the longest x2 15.9 us: strided(): arrived = lax.all_to_all(rows, 'seq', 0, 0, tiled=True)]
    all_to_all x3, waiting for transfers between devices: 37.8 us -> 52 us  [gathered(): return lax.all_to_all(copies, axis, 0, 0, tiled=True)]
    all_to_all x3, starting transfers between devices: 25.5 us -> 18 us  [gathered(): return lax.all_to_all(copies, axis, 0, 0, tiled=True)]
    dot_general x8, matrix products: 19.1 us -> 14.5 us  [contract_last(): lax.dot_general(left, right, (((1,), (1,)), ((), ())), preferred_element_...]
    slice x1 -> x6, local copies, waits for them, and re-layouts: 1.6 us -> 5.83 us  [the longest x2 2.3 us: row_shifted(): later = jnp.concatenate([source[rows_away:], padding], axis=0)]
  transfers between devices with their start and end apart: 14 -> 9, of which waited for: 9 -> 9; matrix products, arithmetic and copies ran while one was open for 20% -> 16% of each run, Pallas kernels for 0% -> 0%
where the time goes in v6:
time: 239 us; the launch traced here: 236 us
  waiting for transfers between devices  101 us (42%)
  starting transfers between devices  67.4 us (28%)
  local copies, waits for them, and re-layouts  29.6 us (12%)
  matrix products  27.3 us (11%)
  other arithmetic  8.39 us (4%)
    all_to_all x3, waiting for transfers between devices, gathered(): return lax.all_to_all(copies, axis, 0, 0, tiled=True)  52 us
    all_to_all x3, starting transfers between devices, summed_over(): arrived = lax.all_to_all(pieces, axis, 0, 0, tiled=True)  27.9 us
    all_to_all x2, waiting for transfers between devices, strided(): arrived = lax.all_to_all(rows, 'seq', 0, 0, tiled=True)  20 us
    all_to_all x3, waiting for transfers between devices, summed_over(): arrived = lax.all_to_all(pieces, axis, 0, 0, tiled=True)  18.5 us
    all_to_all x3, starting transfers between devices, gathered(): return lax.all_to_all(copies, axis, 0, 0, tiled=True)  18 us
    all_to_all x2, starting transfers between devices, strided(): arrived = lax.all_to_all(rows, 'seq', 0, 0, tiled=True)  15.9 us
    dot_general x8, matrix products, contract_last(): lax.dot_general(left, right, (((1,), (1,)), ((), ())), preferred_element_...  14.5 us
    all_to_all x1, waiting for transfers between devices, contiguous(): arrived = lax.all_to_all(pieces, 'seq', 0, 0, tiled=True)  10.5 us
  transfers between devices with their start and end apart: 9, of which 9 were waited for; matrix products, arithmetic and copies ran while one was open for 16% of the time, Pallas kernels for 0%

profile of v6, /device:TPU:6, one launch (start us, length us, event | category | flops | bytes accessed | tf_op | source)
XLA Modules:
  0.0 236.0 jit_solution(13600972780583693296)
XLA Ops:
  0.6 2.3 copy.64
  3.0 9.3 %all-to-all-start = ((bf16[16,32,768]{2,1,0:T(8,128)(2,1)}), bf16[16,32,768]{2,1,0:T(8,128)(2,1)S(1)}, u32[]{:S(2)}, u32[]{:S(2)}) async-start(bf16[16,32,768]{2,1,0:T(8,128)(2,1)} %bitcast.98), calls=%async_computation | async-start | bytes 1572864 | tf_op jit(solution)/shard_map/all_to_all | solution.py:94
  12.3 1.1 copy.63
  13.4 9.5 %all-to-all-done = bf16[16,32,768]{2,1,0:T(8,128)(2,1)S(1)} async-done(((bf16[16,32,768]{2,1,0:T(8,128)(2,1)}), bf16[16,32,768]{2,1,0:T(8,128)(2,1)S(1)}, u32[]{:S(2)}, u32[]{:S(2)}) %all-to-all-start) | async-done | bytes 786464 | tf_op jit(solution)/shard_map/all_to_all | solution.py:94
  22.9 6.6 %all-to-all-start.2 = ((bf16[16,32,768]{2,1,0:T(8,128)(2,1)}), bf16[16,32,768]{2,1,0:T(8,128)(2,1)S(1)}, u32[]{:S(2)}, u32[]{:S(2)}) async-start(bf16[16,32,768]{2,1,0:T(8,128)(2,1)} %bitcast.97), calls=%async_computation.2 | async-start | bytes 1572864 | tf_op jit(solution)/shard_map/all_to_all | solution.py:94
  29.6 10.5 %all-to-all-done.2 = bf16[16,32,768]{2,1,0:T(8,128)(2,1)S(1)} async-done(((bf16[16,32,768]{2,1,0:T(8,128)(2,1)}), bf16[16,32,768]{2,1,0:T(8,128)(2,1)S(1)}, u32[]{:S(2)}, u32[]{:S(2)}) %all-to-all-start.2) | async-done | bytes 786464 | tf_op jit(solution)/shard_map/all_to_all | solution.py:94
  40.2 1.9 broadcast_in_dim.6
  42.1 6.9 %all-to-all-start.1 = ((bf16[16,240,384]{2,1,0:T(8,128)(2,1)}), bf16[16,240,384]{2,1,0:T(8,128)(2,1)S(1)}, u32[]{:S(2)}, u32[]{:S(2)}) async-start(bf16[16,240,384]{2,1,0:T(8,128)(2,1)} %broadcast_in_dim.6), calls=%async_computation.1 | async-start | bytes 5898240 | tf_op jit(solution)/shard_map/all_to_all | solution.py:21
  50.9 2.2 multiply_convert_fusion.1
  53.1 1.6 fusion.25
  54.6 1.8 fusion.5
  56.5 1.2 fusion.114
  57.6 28.4 %all-to-all-done.1 = bf16[16,240,384]{2,1,0:T(8,128)(2,1)S(1)} async-done(((bf16[16,240,384]{2,1,0:T(8,128)(2,1)}), bf16[16,240,384]{2,1,0:T(8,128)(2,1)S(1)}, u32[]{:S(2)}, u32[]{:S(2)}) %all-to-all-start.1) | async-done | bytes 2949152 | tf_op jit(solution)/shard_map/all_to_all | solution.py:21
  86.2 1.4 copy-done
  87.8 1.4 broadcast_in_dim.7
  89.2 7.2 %all-to-all-start.3 = ((bf16[16,3,48,384]{3,2,1,0:T(8,128)(2,1)}), bf16[16,3,48,384]{3,2,1,0:T(8,128)(2,1)}, u32[]{:S(2)}, u32[]{:S(2)}) async-start(bf16[16,3,48,384]{3,2,1,0:T(8,128)(2,1)} %broadcast_in_dim.7), calls=%async_computation.3 | async-start | bytes 3538944 | tf_op jit(solution)/shard_map/all_to_all | solution.py:21
  96.4 1.5 fusion.68
  97.9 1.3 slice-done
  99.1 1.6 reshape.68
  100.7 2.0 convolution_add_fusion.3
  104.0 2.7 %fusion.112 = (bf16[384,1,768]{2,1,0:T(2,128)(2,1)}, bf16[384,1,768]{2,1,0:T(2,128)(2,1)S(1)}) fusion(bf16[384,2,768]{2,1,0:T(2,128)(2,1)S(1)} %copy-done.1), kind=kLoop, calls=%fused_computation.147 | loop fusion | bytes 2359296 | tf_op jit(solution)/shard_map/slice | solution.py:162
  106.7 2.1 multiply_convert_fusion
  109.7 1.1 fusion.113
  110.8 6.9 %all-to-all-done.3 = bf16[16,3,48,384]{3,2,1,0:T(8,128)(2,1)} async-done(((bf16[16,3,48,384]{3,2,1,0:T(8,128)(2,1)}), bf16[16,3,48,384]{3,2,1,0:T(8,128)(2,1)}, u32[]{:S(2)}, u32[]{:S(2)}) %all-to-all-start.3) | async-done | bytes 1769504 | tf_op jit(solution)/shard_map/all_to_all | solution.py:21
  117.8 1.7 fusion.111
  121.4 1.5 fusion.63
  124.8 1.8 fusion.119
  126.5 1.2 copy.39
  127.7 2.4 %convolution_convert_fusion = bf16[16,24,768]{2,1,0:T(8,128)(2,1)} fusion(bf16[16,24,512]{2,1,0:T(8,128)(2,1)S(1)} %bitcast.114, bf16[512,768,1]{1,0,2:T(8,128)(2,1)} %bitcast.110), kind=kOutput, calls=%fused_computation.49 | convolution fusion | flops 302284800 | bytes 1769472 | tf_op jit(solution)/shard_map/dot_general | solution.py:85
  130.2 7.2 %all-to-all-start.5 = ((bf16[16,24,768]{2,1,0:T(8,128)(2,1)}), bf16[16,24,768]{2,1,0:T(8,128)(2,1)}, u32[]{:S(2)}, u32[]{:S(2)}) async-start(bf16[16,24,768]{2,1,0:T(8,128)(2,1)} %convolution_convert_fusion), calls=%async_computation.5 | async-start | bytes 1179648 | tf_op jit(solution)/shard_map/all_to_all | solution.py:27
  137.3 1.7 fusion.99
  139.1 3.0 %fusion.17 = bf16[512,768]{1,0:T(8,128)(2,1)S(1)} fusion(f32[512,768]{1,0:T(8,128)S(1)} %fusion.99, f32[512,768]{1,0:T(8,128)S(1)} %copy-done.14, bf16[512,768]{1,0:T(8,128)(2,1)} %get-tuple-element.34, bf16[768,384]{1,0:T(8,128)(2,1)} %bitcast.119, f32[768]{0:T(1024)S(1)} %get-tuple-element.8, f32[768]{0:T(1024)S(1)} %copy-done.31, ...), kind=kOutput, calls=%fused_computation.24 | convolution fusion | flops 312999936 | bytes 6395904 | tf_op jit(solution)/shard_map/dot_general | solution.py:42
  142.2 1.6 convolution_convert_fusion.1
  144.7 1.5 all-to-all-done.5
  146.1 6.4 %all-to-all-start.4 = ((bf16[16,24,768]{2,1,0:T(8,128)(2,1)}), bf16[16,24,768]{2,1,0:T(8,128)(2,1)S(1)}, u32[]{:S(2)}, u32[]{:S(2)}) async-start(bf16[16,24,768]{2,1,0:T(8,128)(2,1)} %bitcast.120), calls=%async_computation.4 | async-start | bytes 1179648 | tf_op jit(solution)/shard_map/all_to_all | solution.py:27
  152.5 1.0 fusion.115
  153.5 1.8 fusion.84
  155.3 1.2 convert_reduce_fusion
  157.2 4.1 %all-to-all-done.4 = bf16[16,24,768]{2,1,0:T(8,128)(2,1)S(1)} async-done(((bf16[16,24,768]{2,1,0:T(8,128)(2,1)}), bf16[16,24,768]{2,1,0:T(8,128)(2,1)S(1)}, u32[]{:S(2)}, u32[]{:S(2)}) %all-to-all-start.4) | async-done | bytes 589856 | tf_op jit(solution)/shard_map/all_to_all | solution.py:27
  161.4 1.0 pad_maximum_fusion.1
  163.3 14.3 %all-to-all-start.6 = ((f32[32,1,1152]{2,1,0:T(1,128)}), f32[32,1,1152]{2,1,0:T(1,128)S(1)}, u32[]{:S(2)}, u32[]{:S(2)}) async-start(f32[32,1,1152]{2,1,0:T(1,128)} %reshape_reshape.8), calls=%async_computation.6 | async-start | bytes 294912 | tf_op jit(solution)/shard_map/all_to_all | solution.py:27
  179.2 3.7 %fusion.1 = bf16[512,768]{1,0:T(8,128)(2,1)} fusion(bf16[512,768]{1,0:T(8,128)(2,1)S(1)} %copy-done.36, bf16[16,32,768]{2,1,0:T(8,128)(2,1)S(1)} %copy-done.4, f32[512,768]{1,0:T(8,128)S(1)} %copy-done.13, f32[512,768]{1,0:T(8,128)S(1)} %fusion.87, f32[512,768]{1,0:T(8,128)} %fusion.84, f32[768]{0:T(1024)S(1)} %get-tuple-element.9, ...), kind=kOutput, calls=%fused_computation.8 | convolution fusion | flops 311427072 | bytes 8019968 | tf_op jit(solution)/shard_map/dot_general | solution.py:42
  182.9 12.9 %all-to-all-done.6 = f32[32,1,1152]{2,1,0:T(1,128)S(1)} async-done(((f32[32,1,1152]{2,1,0:T(1,128)}), f32[32,1,1152]{2,1,0:T(1,128)S(1)}, u32[]{:S(2)}, u32[]{:S(2)}) %all-to-all-start.6) | async-done | bytes 147488 | tf_op jit(solution)/shard_map/all_to_all | solution.py:27
  195.8 5.7 %all-to-all-start.8 = ((bf16[16,32,768]{2,1,0:T(8,128)(2,1)}), bf16[16,32,768]{2,1,0:T(8,128)(2,1)S(1)}, u32[]{:S(2)}, u32[]{:S(2)}) async-start(bf16[16,32,768]{2,1,0:T(8,128)(2,1)} %bitcast.26), calls=%async_computation.8 | async-start | bytes 1572864 | tf_op jit(solution)/shard_map/all_to_all | solution.py:102
  201.6 10.5 %all-to-all-done.8 = bf16[16,32,768]{2,1,0:T(8,128)(2,1)S(1)} async-done(((bf16[16,32,768]{2,1,0:T(8,128)(2,1)}), bf16[16,32,768]{2,1,0:T(8,128)(2,1)S(1)}, u32[]{:S(2)}, u32[]{:S(2)}) %all-to-all-start.8) | async-done | bytes 786464 | tf_op jit(solution)/shard_map/all_to_all | solution.py:102
  212.9 3.9 %all-to-all-start.7 = ((f32[32,1,1152]{2,1,0:T(1,128)}), f32[32,1,1152]{2,1,0:T(1,128)S(1)}, u32[]{:S(2)}, u32[]{:S(2)}) async-start(f32[32,1,1152]{2,1,0:T(1,128)} %broadcast_in_dim.8), calls=%async_computation.7 | async-start | bytes 294912 | tf_op jit(solution)/shard_map/all_to_all | solution.py:21
  216.9 1.3 copy.41
  218.2 16.7 %all-to-all-done.7 = f32[32,1,1152]{2,1,0:T(1,128)S(1)} async-done(((f32[32,1,1152]{2,1,0:T(1,128)}), f32[32,1,1152]{2,1,0:T(1,128)S(1)}, u32[]{:S(2)}, u32[]{:S(2)}) %all-to-all-start.7) | async-done | bytes 147488 | tf_op jit(solution)/shard_map/all_to_all | solution.py:21
  (98 shorter events, 13.3 us)
Async XLA Ops:
  0.6 11.6 %copy-start.19 = (bf16[1,512,768]{2,1,0:T(8,128)(2,1)S(1)}, bf16[1,512,768]{2,1,0:T(8,128)(2,1)}, u32[]{:S(2)}) copy-start(bf16[1,512,768]{2,1,0:T(8,128)(2,1)} %param.10) | copy-start | bytes 2359300
  3.0 19.9 %all-to-all-start = ((bf16[16,32,768]{2,1,0:T(8,128)(2,1)}), bf16[16,32,768]{2,1,0:T(8,128)(2,1)S(1)}, u32[]{:S(2)}, u32[]{:S(2)}) async-start(bf16[16,32,768]{2,1,0:T(8,128)(2,1)} %bitcast.98), calls=%async_computation | async-start | bytes 1572864 | tf_op jit(solution)/shard_map/all_to_all | solution.py:94
  12.3 17.3 %copy-start.27 = (bf16[24,2,768]{2,1,0:T(2,128)(2,1)S(1)}, bf16[24,2,768]{2,1,0:T(2,128)(2,1)}, u32[]{:S(2)}) copy-start(bf16[24,2,768]{2,1,0:T(2,128)(2,1)} %param.17) | copy-start | bytes 221188
  12.3 17.3 %copy-start.26 = (bf16[2,3,48,384]{3,2,1,0:T(8,128)(2,1)S(1)}, bf16[2,3,48,384]{3,2,1,0:T(8,128)(2,1)}, u32[]{:S(2)}) copy-start(bf16[2,3,48,384]{3,2,1,0:T(8,128)(2,1)} %param.16) | copy-start | bytes 663556
  22.9 19.1 %copy-start.2 = (bf16[16,32,768]{2,1,0:T(8,128)(2,1)}, bf16[16,32,768]{2,1,0:T(8,128)(2,1)S(1)}, u32[]{:S(2)}) copy-start(bf16[16,32,768]{2,1,0:T(8,128)(2,1)S(1)} %all-to-all-done) | copy-start | bytes 2359300
  22.9 17.3 %all-to-all-start.2 = ((bf16[16,32,768]{2,1,0:T(8,128)(2,1)}), bf16[16,32,768]{2,1,0:T(8,128)(2,1)S(1)}, u32[]{:S(2)}, u32[]{:S(2)}) async-start(bf16[16,32,768]{2,1,0:T(8,128)(2,1)} %bitcast.97), calls=%async_computation.2 | async-start | bytes 1572864 | tf_op jit(solution)/shard_map/all_to_all | solution.py:94
  40.2 1.9 copy-start.8
  42.0 6.9 %copy-start.34 = (s32[1,2]{1,0:T(1,128)S(1)}, s32[1,2]{1,0:T(1,128)}, u32[]{:S(2)}) copy-start(s32[1,2]{1,0:T(1,128)} %param.11) | copy-start | bytes 28
  42.0 8.7 %copy-start.32 = (f32[2,384]{1,0:T(2,128)S(1)}, f32[2,384]{1,0:T(2,128)}, u32[]{:S(2)}) copy-start(f32[2,384]{1,0:T(2,128)} %param.15) | copy-start | bytes 9220
  42.0 8.8 %copy-start.33 = (f32[2,384]{1,0:T(2,128)S(1)}, f32[2,384]{1,0:T(2,128)}, u32[]{:S(2)}) copy-start(f32[2,384]{1,0:T(2,128)} %param.14) | copy-start | bytes 9220
  42.0 8.8 %copy-start.28 = (f32[2,768]{1,0:T(2,128)S(1)}, f32[2,768]{1,0:T(2,128)}, u32[]{:S(2)}) copy-start(f32[2,768]{1,0:T(2,128)} %param.13) | copy-start | bytes 18436
  42.0 8.8 %copy-start.29 = (f32[2,768]{1,0:T(2,128)S(1)}, f32[2,768]{1,0:T(2,128)}, u32[]{:S(2)}) copy-start(f32[2,768]{1,0:T(2,128)} %param.12) | copy-start | bytes 18436
  42.1 44.0 %all-to-all-start.1 = ((bf16[16,240,384]{2,1,0:T(8,128)(2,1)}), bf16[16,240,384]{2,1,0:T(8,128)(2,1)S(1)}, u32[]{:S(2)}, u32[]{:S(2)}) async-start(bf16[16,240,384]{2,1,0:T(8,128)(2,1)} %broadcast_in_dim.6), calls=%async_computation.1 | async-start | bytes 5898240 | tf_op jit(solution)/shard_map/all_to_all | solution.py:21
  48.9 4.1 %copy-start.3 = (bf16[16,32,768]{2,1,0:T(8,128)(2,1)S(1)}, bf16[16,32,768]{2,1,0:T(8,128)(2,1)}, u32[]{:S(2)}) copy-start(bf16[16,32,768]{2,1,0:T(8,128)(2,1)} %copy-done.2) | copy-start | bytes 2359300
  50.9 55.8 %copy-start.30 = (f32[768]{0:T(1024)}, f32[768]{0:T(1024)S(1)}, u32[]{:S(2)}) copy-start(f32[768]{0:T(1024)S(1)} %get-tuple-element.38) | copy-start | bytes 9220
  86.1 1.6 copy-start
  89.2 7.2 %copy-start.11 = (bf16[448,768]{1,0:T(8,128)(2,1)S(1)}, bf16[448,768]{1,0:T(8,128)(2,1)}, u32[]{:S(2)}) copy-start(bf16[448,768]{1,0:T(8,128)(2,1)} %get-tuple-element.24) | copy-start | bytes 2064388
  89.2 28.5 %all-to-all-start.3 = ((bf16[16,3,48,384]{3,2,1,0:T(8,128)(2,1)}), bf16[16,3,48,384]{3,2,1,0:T(8,128)(2,1)}, u32[]{:S(2)}, u32[]{:S(2)}) async-start(bf16[16,3,48,384]{3,2,1,0:T(8,128)(2,1)} %broadcast_in_dim.7), calls=%async_computation.3 | async-start | bytes 3538944 | tf_op jit(solution)/shard_map/all_to_all | solution.py:21
  97.9 1.3 slice-start
  100.7 2.0 copy-start.10
  102.8 1.3 copy-start.1
  104.0 2.7 %copy-start.20 = (f32[512,384]{1,0:T(8,128)}, f32[512,384]{1,0:T(8,128)S(1)}, u32[]{:S(2)}) copy-start(f32[512,384]{1,0:T(8,128)S(1)} %fusion.39) | copy-start | bytes 2359300
  104.0 2.7 %copy-start.4 = (bf16[16,32,768]{2,1,0:T(8,128)(2,1)S(1)}, bf16[16,32,768]{2,1,0:T(8,128)(2,1)}, u32[]{:S(2)}) copy-start(bf16[16,32,768]{2,1,0:T(8,128)(2,1)} %copy-done.2) | copy-start | bytes 2359300
  106.7 2.1 copy-start.16
  108.8 0.9 copy-start.5
  117.8 1.7 copy-start.12
  119.4 1.9 copy-start.22
  119.4 1.3 copy-start.6
  120.0 1.4 copy-start.23
  121.4 1.6 copy-start.7
  121.4 1.6 copy-start.18
  130.1 8.9 %copy-start.25 = (bf16[384,384]{1,0:T(8,128)(2,1)S(1)}, bf16[384,384]{1,0:T(8,128)(2,1)}, u32[]{:S(2)}) copy-start(bf16[384,384]{1,0:T(8,128)(2,1)} %get-tuple-element.27) | copy-start | bytes 884740
  130.1 8.9 %copy-start.31 = (f32[768]{0:T(1024)S(1)}, f32[768]{0:T(1024)}, u32[]{:S(2)}) copy-start(f32[768]{0:T(1024)} %copy-done.30) | copy-start | bytes 9220
  130.2 16.0 %all-to-all-start.5 = ((bf16[16,24,768]{2,1,0:T(8,128)(2,1)}), bf16[16,24,768]{2,1,0:T(8,128)(2,1)}, u32[]{:S(2)}, u32[]{:S(2)}) async-start(bf16[16,24,768]{2,1,0:T(8,128)(2,1)} %convolution_convert_fusion), calls=%async_computation.5 | async-start | bytes 1179648 | tf_op jit(solution)/shard_map/all_to_all | solution.py:27
  137.3 1.7 copy-start.9
  137.3 1.7 copy-start.14
  139.1 3.0 %copy-start.21 = (f32[512,384]{1,0:T(8,128)S(1)}, f32[512,384]{1,0:T(8,128)}, u32[]{:S(2)}) copy-start(f32[512,384]{1,0:T(8,128)} %copy-done.20) | copy-start | bytes 2359300
  142.1 1.6 copy-start.35
  142.1 1.6 copy-start.17
  146.1 15.1 %all-to-all-start.4 = ((bf16[16,24,768]{2,1,0:T(8,128)(2,1)}), bf16[16,24,768]{2,1,0:T(8,128)(2,1)S(1)}, u32[]{:S(2)}, u32[]{:S(2)}) async-start(bf16[16,24,768]{2,1,0:T(8,128)(2,1)} %bitcast.120), calls=%async_computation.4 | async-start | bytes 1179648 | tf_op jit(solution)/shard_map/all_to_all | solution.py:27
  155.3 22.3 %copy-start.15 = (bf16[448,384]{1,0:T(8,128)(2,1)S(1)}, bf16[448,384]{1,0:T(8,128)(2,1)}, u32[]{:S(2)}) copy-start(bf16[448,384]{1,0:T(8,128)(2,1)} %get-tuple-element.26) | copy-start | bytes 1032196
  162.4 15.8 %copy-start.24 = (bf16[448,384]{1,0:T(8,128)(2,1)S(1)}, bf16[448,384]{1,0:T(8,128)(2,1)}, u32[]{:S(2)}) copy-start(bf16[448,384]{1,0:T(8,128)(2,1)} %get-tuple-element.25) | copy-start | bytes 1032196
  163.3 32.5 %all-to-all-start.6 = ((f32[32,1,1152]{2,1,0:T(1,128)}), f32[32,1,1152]{2,1,0:T(1,128)S(1)}, u32[]{:S(2)}, u32[]{:S(2)}) async-start(f32[32,1,1152]{2,1,0:T(1,128)} %reshape_reshape.8), calls=%async_computation.6 | async-start | bytes 294912 | tf_op jit(solution)/shard_map/all_to_all | solution.py:27
  177.6 1.4 copy-start.13
  177.6 1.6 copy-start.36
  195.8 16.3 %all-to-all-start.8 = ((bf16[16,32,768]{2,1,0:T(8,128)(2,1)}), bf16[16,32,768]{2,1,0:T(8,128)(2,1)S(1)}, u32[]{:S(2)}, u32[]{:S(2)}) async-start(bf16[16,32,768]{2,1,0:T(8,128)(2,1)} %bitcast.26), calls=%async_computation.8 | async-start | bytes 1572864 | tf_op jit(solution)/shard_map/all_to_all | solution.py:102
  212.9 21.9 %all-to-all-start.7 = ((f32[32,1,1152]{2,1,0:T(1,128)}), f32[32,1,1152]{2,1,0:T(1,128)S(1)}, u32[]{:S(2)}, u32[]{:S(2)}) async-start(f32[32,1,1152]{2,1,0:T(1,128)} %broadcast_in_dim.8), calls=%async_computation.7 | async-start | bytes 294912 | tf_op jit(solution)/shard_map/all_to_all | solution.py:21

commit v7 on v6

--- a/solution.py
+++ b/solution.py
@@ -87,20 +87,30 @@
     )
 
 
-def strided(block):
-    peers = lax.axis_size("seq")
-    channels = block.shape[-1]
-    rows = block.reshape(-1, peers, channels).swapaxes(0, 1)
-    arrived = lax.all_to_all(rows, "seq", 0, 0, tiled=True)
-    return arrived.reshape(-1, channels)
-
-
-def contiguous(rows):
-    peers = lax.axis_size("seq")
-    channels = rows.shape[-1]
-    pieces = rows.reshape(peers, -1, channels)
-    arrived = lax.all_to_all(pieces, "seq", 0, 0, tiled=True)
-    return arrived.swapaxes(0, 1).reshape(-1, channels)
+def exchanged(parts, axis):
+    joined = jnp.concatenate(parts, axis=1)
+    arrived = lax.all_to_all(joined, axis, 0, 0, tiled=True)
+    pieces = []
+    offset = 0
+    for part in parts:
+        pieces.append(arrived[:, offset : offset + part.shape[1]])
+        offset += part.shape[1]
+    return pieces
+
+
+def strided_pieces(block, peers):
+    return block.reshape(-1, peers, block.shape[-1]).swapaxes(0, 1)
+
+
+def same_for_all(shard, peers, lanes):
+    flat = shard.reshape(-1, lanes)
+    return jnp.broadcast_to(flat[None], (peers,) + flat.shape)
+
+
+def conv_from_pieces(pieces, block_shape):
+    taps, rows, hidden = block_shape
+    parts = pieces.reshape(-1, taps, rows, hidden)
+    return jnp.moveaxis(parts, 0, 1).reshape(taps, -1, hidden)
 
 
 def row_shifted(source, rows_away):
@@ -122,20 +132,27 @@
     point_weight,
 ):
     peers = lax.axis_size("seq")
-    lanes = conv_weight.shape[3]
-    conv_rows = conv_weight.shape[1] * conv_weight.shape[2]
-    joined = jnp.concatenate(
-        [conv_weight[0].reshape(conv_rows, lanes), point_weight.reshape(-1, lanes)]
-    )
-    joined_full = gathered(joined, "seq")
-    first_conv = jnp.moveaxis(
-        joined_full[:, :conv_rows].reshape((-1,) + conv_weight.shape[1:]), 0, 1
-    ).reshape(conv_weight.shape[1], -1, lanes)
-    point_full = joined_full[:, conv_rows:].reshape(-1, *point_weight.shape[1:])
-    second_shard, first_conv = lax.optimization_barrier((conv_weight[1], first_conv))
-    conv_full = [first_conv, conv_gathered_block(second_shard, conv_weight.shape)]
+    channels = sequence_in.shape[2]
+    block_shape = conv_weight.shape[1:]
+    state_pieces, first_pieces, point_pieces = exchanged(
+        [
+            strided_pieces(sequence_in[0], peers),
+            same_for_all(conv_weight[0], peers, channels),
+            same_for_all(point_weight, peers, channels),
+        ],
+        "seq",
+    )
+    state = state_pieces.reshape(-1, channels)
+    point_full = point_pieces.reshape(-1, *point_weight.shape[1:])
+    grad_in, second_in, state = lax.optimization_barrier((output_grad[0], conv_weight[1], state))
+    grad_pieces, second_pieces = exchanged(
+        [strided_pieces(grad_in, peers), same_for_all(second_in, peers, channels)], "seq"
+    )
+    conv_full = [
+        conv_from_pieces(first_pieces, block_shape),
+        conv_from_pieces(second_pieces, block_shape),
+    ]
     row_reach = (FIRST_DILATION // peers, SECOND_DILATION // peers)
-    state = strided(sequence_in[0])
     saved = []
     for block_index in range(2):
         kept_flag = (1 - skip_mask[0, block_index]).astype(jnp.float32)
@@ -155,16 +172,14 @@
         )
         middle, hidden_act, state = forward_local(*operands)
         saved.append((normed, middle, hidden_act, kept_flag))
-    gradient = strided(output_grad[0])
-    reduced_terms = [None, None]
+    gradient = grad_pieces.reshape(-1, channels)
+    terms = [None, None]
     for block_index in (1, 0):
         normed, middle, hidden_act, kept_flag = saved[block_index]
         projection = point_full[:, block_index, :]
         first_operands = (gradient, middle, projection, mid_gain[block_index], kept_flag)
         conv_grad, branch_grad = backward_first(*first_operands)
-        reduced_terms[block_index] = summed_over(
-            grad_rows(hidden_act, branch_grad), "seq", jnp.bfloat16
-        )
+        terms[block_index] = grad_rows(hidden_act, branch_grad)
         earlier, later = row_shifted(conv_grad, row_reach[block_index])
         second_operands = (
             gradient,
@@ -176,15 +191,21 @@
             in_gain[block_index],
         )
         gradient = backward_second(*second_operands)
-    summed = reduced_over_dp(jnp.stack([reduced_terms[0], reduced_terms[1]], axis=1))
+    term_pieces = [
+        term.astype(jnp.bfloat16).reshape(peers, -1, channels) for term in terms
+    ]
+    first_term, second_term, back_pieces = exchanged(
+        term_pieces + [gradient.reshape(peers, -1, channels)], "seq"
+    )
+    own_terms = [
+        piece.astype(jnp.float32).sum(axis=0) for piece in (first_term, second_term)
+    ]
+    summed = reduced_over_dp(jnp.stack(own_terms, axis=1))
     sample_count = sequence_in.shape[0] * lax.axis_size("dp")
     full_length = sequence_in.shape[1] * peers
     point_grad = summed * (1.0 / math.sqrt(sample_count * full_length))
-    return (point_grad, contiguous(gradient).reshape(sequence_in.shape))
-
-
-def conv_gathered_block(shard, full_shape):
-    return jnp.moveaxis(gathered(shard, "seq"), 0, 1).reshape(full_shape[1], -1, full_shape[3])
+    input_grad = back_pieces.swapaxes(0, 1).reshape(sequence_in.shape)
+    return (point_grad, input_grad)
 
 
 def solution(mesh):

time: 239 us -> 216 us (0.904)
  blocking collectives: 0 us -> 61.9 us
  starting transfers between devices: 67.4 us -> 21.6 us
  waiting for transfers between devices: 101 us -> 69.4 us
  matrix products: 27.3 us -> 14.4 us
  local copies, waits for them, and re-layouts: 29.6 us -> 40.2 us
  other arithmetic: 8.39 us -> 5.42 us
    all_to_all x0 -> x2, blocking collectives: none -> 61.9 us  [the longest x1 31.4 us: summed_over(): arrived = lax.all_to_all(pieces, axis, 0, 0, tiled=True)]
    all_to_all x3 -> x1, waiting for transfers between devices: 52 us -> 16.2 us  [gathered(): return lax.all_to_all(copies, axis, 0, 0, tiled=True)]
    all_to_all x6 -> x2, starting transfers between devices: 49.5 us -> 17.4 us  [exchanged(): arrived = lax.all_to_all(joined, axis, 0, 0, tiled=True)]
    all_to_all x3 -> x1, starting transfers between devices: 18 us -> 4.24 us  [gathered(): return lax.all_to_all(copies, axis, 0, 0, tiled=True)]
    reshape x2 -> x4, local copies, waits for them, and re-layouts: 1.66 us -> 11.4 us  [the longest x2 7.48 us: conv_from_pieces(): parts = pieces.reshape(-1, taps, rows, hidden)]
    slice x4 -> x6, local copies, waits for them, and re-layouts: 1.47 us -> 8.8 us  [the longest x5 7.82 us: exchanged(): pieces.append(arrived[:, offset:offset + part.shape[1]])]
    dot_general x8, matrix products: 14.5 us -> 7.54 us  [contract_last(): lax.dot_general(left, right, (((1,), (1,)), ((), ())), preferred_element_...]
    all_to_all x6 -> x2, waiting for transfers between devices: 49 us -> 53.2 us  [exchanged(): arrived = lax.all_to_all(joined, axis, 0, 0, tiled=True)]
  transfers between devices with their start and end apart: 9 -> 3, of which waited for: 9 -> 3; matrix products, arithmetic and copies ran while one was open for 16% -> 11% of each run, Pallas kernels for 0% -> 0%
where the time goes in v7:
time: 216 us; the launch traced here: 215 us
  waiting for transfers between devices  69.4 us (32%)
  blocking collectives  61.9 us (29%)
  local copies, waits for them, and re-layouts  40.2 us (19%)
  starting transfers between devices  21.6 us (10%)
  matrix products  14.4 us (7%)
  other arithmetic  5.42 us (3%)
  between operations  2.4 us (1%)
    all_to_all x2, waiting for transfers between devices, exchanged(): arrived = lax.all_to_all(joined, axis, 0, 0, tiled=True)  53.2 us
    all_to_all x1, blocking collectives, summed_over(): arrived = lax.all_to_all(pieces, axis, 0, 0, tiled=True)  31.4 us
    all_to_all x1, blocking collectives, exchanged(): arrived = lax.all_to_all(joined, axis, 0, 0, tiled=True)  30.4 us
    all_to_all x2, starting transfers between devices, exchanged(): arrived = lax.all_to_all(joined, axis, 0, 0, tiled=True)  17.4 us
    all_to_all x1, waiting for transfers between devices, gathered(): return lax.all_to_all(copies, axis, 0, 0, tiled=True)  16.2 us
    slice x5, local copies, waits for them, and re-layouts, exchanged(): pieces.append(arrived[:, offset:offset + part.shape[1]])  7.82 us
    dot_general x8, matrix products, contract_last(): lax.dot_general(left, right, (((1,), (1,)), ((), ())), preferred_element_...  7.54 us
    reshape x2, local copies, waits for them, and re-layouts, conv_from_pieces(): parts = pieces.reshape(-1, taps, rows, hidden)  7.48 us
  transfers between devices with their start and end apart: 3, of which 3 were waited for; matrix products, arithmetic and copies ran while one was open for 11% of the time, Pallas kernels for 0%

profile of v7, /device:TPU:6, one launch (start us, length us, event | category | flops | bytes accessed | tf_op | source)
XLA Modules:
  0.0 215.3 jit_solution(6118204971695454752)
XLA Ops:
  0.6 1.0 fusion.98
  1.6 0.9 broadcast_in_dim.16
  2.6 1.4 copy.43
  4.2 2.0 pad_maximum_fusion
  6.1 10.3 %all-to-all-start = ((bf16[16,152,768]{2,1,0:T(8,128)(2,1)}), bf16[16,152,768]{2,1,0:T(8,128)(2,1)}, u32[]{:S(2)}, u32[]{:S(2)}) async-start(bf16[16,152,768]{2,1,0:T(8,128)(2,1)} %pad_maximum_fusion), calls=%async_computation | async-start | bytes 7471104 | tf_op jit(solution)/shard_map/all_to_all | solution.py:92
  16.5 0.6 fusion.99
  18.5 45.6 %all-to-all-done = bf16[16,152,768]{2,1,0:T(8,128)(2,1)} async-done(((bf16[16,152,768]{2,1,0:T(8,128)(2,1)}), bf16[16,152,768]{2,1,0:T(8,128)(2,1)}, u32[]{:S(2)}, u32[]{:S(2)}) %all-to-all-start) | async-done | bytes 3735584 | tf_op jit(solution)/shard_map/all_to_all | solution.py:92
  64.1 1.2 slice.161
  65.3 0.8 broadcast_in_dim.35
  66.3 0.7 copy-done.19
  67.1 1.6 pad_maximum_fusion.1
  68.7 7.1 %all-to-all-start.1 = ((bf16[16,104,768]{2,1,0:T(8,128)(2,1)}), bf16[16,104,768]{2,1,0:T(8,128)(2,1)S(1)}, u32[]{:S(2)}, u32[]{:S(2)}) async-start(bf16[16,104,768]{2,1,0:T(8,128)(2,1)} %pad_maximum_fusion.1), calls=%async_computation.1 | async-start | bytes 5111808 | tf_op jit(solution)/shard_map/all_to_all | solution.py:92
  75.8 2.4 %slice.169 = bf16[16,48,768]{2,1,0:T(8,128)(2,1)} slice(bf16[16,152,768]{2,1,0:T(8,128)(2,1)} %all-to-all-done), slice={[0:16], [104:152], [0:768]} | slice | bytes 2359296 | tf_op jit(solution)/shard_map/slice | solution.py:96
  78.2 3.6 %reshape.69 = bf16[384,2,768]{2,1,0:T(2,128)(2,1)} reshape(bf16[16,48,768]{2,1,0:T(8,128)(2,1)} %slice.169) | data formatting | bytes 2359296 | tf_op jit(solution)/shard_map/reshape | solution.py:146
  81.8 2.9 %slice.163 = bf16[16,72,768]{2,1,0:T(8,128)(2,1)} slice(bf16[16,152,768]{2,1,0:T(8,128)(2,1)} %all-to-all-done), slice={[0:16], [32:104], [0:768]} | slice | bytes 3538944 | tf_op jit(solution)/shard_map/slice | solution.py:96
  84.7 3.8 %reshape.67 = bf16[16,3,48,384]{3,2,1,0:T(8,128)(2,1)} reshape(bf16[16,72,768]{2,1,0:T(8,128)(2,1)} %slice.163) | data formatting | bytes 3538944 | tf_op jit(solution)/shard_map/reshape | solution.py:112
  88.4 0.6 fusion.6
  89.2 1.4 copy-done.1
  91.3 0.6 convolution_add_fusion.3
  91.9 0.6 fusion.32
  92.5 0.7 copy-done
  93.2 2.7 %fusion.93 = (bf16[384,1,768]{2,1,0:T(2,128)(2,1)}, bf16[384,1,768]{2,1,0:T(2,128)(2,1)S(1)}) fusion(bf16[384,2,768]{2,1,0:T(2,128)(2,1)S(1)} %copy-done), kind=kLoop, calls=%fused_computation.130 | loop fusion | bytes 2359296 | tf_op jit(solution)/shard_map/slice | solution.py:179
  95.9 2.1 multiply_convert_fusion
  98.0 1.0 copy-done.4
  98.9 1.2 fusion.94
  100.1 7.6 %all-to-all-done.1 = bf16[16,104,768]{2,1,0:T(8,128)(2,1)S(1)} async-done(((bf16[16,104,768]{2,1,0:T(8,128)(2,1)}), bf16[16,104,768]{2,1,0:T(8,128)(2,1)S(1)}, u32[]{:S(2)}, u32[]{:S(2)}) %all-to-all-start.1) | async-done | bytes 2555936 | tf_op jit(solution)/shard_map/all_to_all | solution.py:92
  107.7 1.3 slice.173
  109.0 3.7 %reshape.70 = bf16[16,3,48,384]{3,2,1,0:T(8,128)(2,1)} reshape(bf16[16,72,768]{2,1,0:T(8,128)(2,1)} %slice.173) | data formatting | bytes 3538944 | tf_op jit(solution)/shard_map/reshape | solution.py:112
  112.7 1.7 fusion.91
  116.1 0.6 fusion.30
  117.4 0.9 fusion.48
  118.4 0.6 fusion.100
  119.0 0.6 fusion.71
  120.2 1.6 fusion.24
  121.8 1.0 fusion.40
  122.8 1.0 copy-done.3
  123.8 0.6 fusion.101
  124.4 0.7 convolution_convert_fusion.1
  125.1 0.6 fusion.68
  125.9 0.6 convolution_convert_fusion
  127.2 1.6 fusion.11
  129.0 30.4 %all_to_all.25 = bf16[16,80,768]{2,1,0:T(8,128)(2,1)S(1)} all-to-all(bf16[16,80,768]{2,1,0:T(8,128)(2,1)S(1)} %pad_maximum_fusion.2), channel_id=1, replica_groups=mesh['dp'=32,'seq'=16] {'seq'}, dimensions={0} | all-to-all | bytes 3932160 | tf_op jit(solution)/shard_map/all_to_all | solution.py:92
  160.0 31.4 %all_to_all.26 = f32[32,1,1152]{2,1,0:T(1,128)S(1)} all-to-all(f32[32,1,1152]{2,1,0:T(1,128)S(1)} %reshape_reshape.4), channel_id=1, replica_groups=mesh['dp'=32,'seq'=16] {'dp'}, dimensions={0} | all-to-all | bytes 294912 | tf_op jit(solution)/shard_map/all_to_all | solution.py:27
  191.6 0.7 broadcast_in_dim.37
  192.3 4.2 %all-to-all-start.4 = ((f32[32,1,1152]{2,1,0:T(1,128)}), f32[32,1,1152]{2,1,0:T(1,128)S(1)}, u32[]{:S(2)}, u32[]{:S(2)}) async-start(f32[32,1,1152]{2,1,0:T(1,128)} %broadcast_in_dim.37), calls=%async_computation.4 | async-start | bytes 294912 | tf_op jit(solution)/shard_map/all_to_all | solution.py:21
  196.6 1.3 copy.23
  198.0 16.2 %all-to-all-done.4 = f32[32,1,1152]{2,1,0:T(1,128)S(1)} async-done(((f32[32,1,1152]{2,1,0:T(1,128)}), f32[32,1,1152]{2,1,0:T(1,128)S(1)}, u32[]{:S(2)}, u32[]{:S(2)}) %all-to-all-start.4) | async-done | bytes 147488 | tf_op jit(solution)/shard_map/all_to_all | solution.py:21
  214.6 0.8 mul.345
  (74 shorter events, 6.7 us)
Async XLA Ops:
  6.1 10.3 %copy-start.24 = (s32[1,2]{1,0:T(1,128)S(1)}, s32[1,2]{1,0:T(1,128)}, u32[]{:S(2)}) copy-start(s32[1,2]{1,0:T(1,128)} %param.11) | copy-start | bytes 28
  6.1 12.2 %copy-start.22 = (f32[2,384]{1,0:T(2,128)S(1)}, f32[2,384]{1,0:T(2,128)}, u32[]{:S(2)}) copy-start(f32[2,384]{1,0:T(2,128)} %param.15) | copy-start | bytes 9220
  6.1 12.2 %copy-start.23 = (f32[2,384]{1,0:T(2,128)S(1)}, f32[2,384]{1,0:T(2,128)}, u32[]{:S(2)}) copy-start(f32[2,384]{1,0:T(2,128)} %param.14) | copy-start | bytes 9220
  6.1 12.3 %copy-start.20 = (f32[2,768]{1,0:T(2,128)S(1)}, f32[2,768]{1,0:T(2,128)}, u32[]{:S(2)}) copy-start(f32[2,768]{1,0:T(2,128)} %param.13) | copy-start | bytes 18436
  6.1 12.3 %copy-start.21 = (f32[2,768]{1,0:T(2,128)S(1)}, f32[2,768]{1,0:T(2,128)}, u32[]{:S(2)}) copy-start(f32[2,768]{1,0:T(2,128)} %param.12) | copy-start | bytes 18436
  6.1 57.9 %all-to-all-start = ((bf16[16,152,768]{2,1,0:T(8,128)(2,1)}), bf16[16,152,768]{2,1,0:T(8,128)(2,1)}, u32[]{:S(2)}, u32[]{:S(2)}) async-start(bf16[16,152,768]{2,1,0:T(8,128)(2,1)} %pad_maximum_fusion), calls=%async_computation | async-start | bytes 7471104 | tf_op jit(solution)/shard_map/all_to_all | solution.py:92
  16.4 49.6 %copy-start.16 = (bf16[1,512,768]{2,1,0:T(8,128)(2,1)S(1)}, bf16[1,512,768]{2,1,0:T(8,128)(2,1)}, u32[]{:S(2)}) copy-start(bf16[1,512,768]{2,1,0:T(8,128)(2,1)} %param.10) | copy-start | bytes 2359300
  65.3 23.2 %copy-start.6 = (bf16[16,32,768]{2,1,0:T(8,128)(2,1)}, bf16[16,32,768]{2,1,0:T(8,128)(2,1)S(1)}, u32[]{:S(2)}) copy-start(bf16[16,32,768]{2,1,0:T(8,128)(2,1)S(1)} %slice.161) | copy-start | bytes 2359300
  66.1 0.9 copy-start.19
  68.7 39.0 %all-to-all-start.1 = ((bf16[16,104,768]{2,1,0:T(8,128)(2,1)}), bf16[16,104,768]{2,1,0:T(8,128)(2,1)S(1)}, u32[]{:S(2)}, u32[]{:S(2)}) async-start(bf16[16,104,768]{2,1,0:T(8,128)(2,1)} %pad_maximum_fusion.1), calls=%async_computation.1 | async-start | bytes 5111808 | tf_op jit(solution)/shard_map/all_to_all | solution.py:92
  89.1 1.5 copy-start.1
  90.7 1.2 copy-start.2
  90.8 1.2 copy-start.9
  91.9 1.3 copy-start
  93.2 2.7 %copy-start.17 = (f32[512,384]{1,0:T(8,128)}, f32[512,384]{1,0:T(8,128)S(1)}, u32[]{:S(2)}) copy-start(f32[512,384]{1,0:T(8,128)S(1)} %fusion.32) | copy-start | bytes 2359300
  93.2 2.7 %copy-start.7 = (bf16[16,32,768]{2,1,0:T(8,128)(2,1)S(1)}, bf16[16,32,768]{2,1,0:T(8,128)(2,1)}, u32[]{:S(2)}) copy-start(bf16[16,32,768]{2,1,0:T(8,128)(2,1)} %copy-done.6) | copy-start | bytes 2359300
  95.9 2.1 copy-start.13
  98.0 1.0 copy-start.4
  112.7 1.7 copy-start.12
  114.4 1.1 copy-start.5
  115.0 1.1 copy-start.11
  116.1 1.3 copy-start.15
  119.0 1.1 copy-start.25
  120.2 1.6 copy-start.14
  120.2 1.6 copy-start.18
  122.8 1.1 copy-start.3
  125.9 1.1 copy-start.8
  125.9 1.3 copy-start.10
  192.3 21.9 %all-to-all-start.4 = ((f32[32,1,1152]{2,1,0:T(1,128)}), f32[32,1,1152]{2,1,0:T(1,128)S(1)}, u32[]{:S(2)}, u32[]{:S(2)}) async-start(f32[32,1,1152]{2,1,0:T(1,128)} %broadcast_in_dim.37), calls=%async_computation.4 | async-start | bytes 294912 | tf_op jit(solution)/shard_map/all_to_all | solution.py:21

commit v8 on v7

--- a/solution.py
+++ b/solution.py
@@ -102,9 +102,18 @@
     return block.reshape(-1, peers, block.shape[-1]).swapaxes(0, 1)
 
 
-def same_for_all(shard, peers, lanes):
-    flat = shard.reshape(-1, lanes)
-    return jnp.broadcast_to(flat[None], (peers,) + flat.shape)
+def half_for_each(shard, peers, lanes):
+    halves = shard.reshape(2, -1, lanes)
+    return jnp.tile(halves, (peers // 2, 1, 1))
+
+
+def whole_from_halves(own_halves, axis):
+    peers = lax.axis_size(axis)
+    partner = lax.ppermute(own_halves, axis, [(i, i ^ 1) for i in range(peers)])
+    first_core = lax.axis_index(axis) % 2 == 0
+    low = jnp.where(first_core, own_halves, partner)
+    high = jnp.where(first_core, partner, own_halves)
+    return jnp.concatenate([low, high], axis=1)
 
 
 def conv_from_pieces(pieces, block_shape):
@@ -134,20 +143,26 @@
     peers = lax.axis_size("seq")
     channels = sequence_in.shape[2]
     block_shape = conv_weight.shape[1:]
-    state_pieces, first_pieces, point_pieces = exchanged(
+    conv_rows = conv_weight[0].size // channels
+    first_weights = jnp.concatenate(
+        [conv_weight[0].reshape(-1, channels), point_weight.reshape(-1, channels)]
+    )
+    state_pieces, first_halves = exchanged(
         [
             strided_pieces(sequence_in[0], peers),
-            same_for_all(conv_weight[0], peers, channels),
-            same_for_all(point_weight, peers, channels),
+            half_for_each(first_weights, peers, channels),
         ],
         "seq",
     )
     state = state_pieces.reshape(-1, channels)
-    point_full = point_pieces.reshape(-1, *point_weight.shape[1:])
     grad_in, second_in, state = lax.optimization_barrier((output_grad[0], conv_weight[1], state))
-    grad_pieces, second_pieces = exchanged(
-        [strided_pieces(grad_in, peers), same_for_all(second_in, peers, channels)], "seq"
-    )
+    grad_pieces, second_halves = exchanged(
+        [strided_pieces(grad_in, peers), half_for_each(second_in, peers, channels)], "seq"
+    )
+    first_whole = whole_from_halves(first_halves, "seq")
+    first_pieces = first_whole[:, :conv_rows]
+    point_full = first_whole[:, conv_rows:].reshape(-1, *point_weight.shape[1:])
+    second_pieces = whole_from_halves(second_halves, "seq")
     conv_full = [
         conv_from_pieces(first_pieces, block_shape),
         conv_from_pieces(second_pieces, block_shape),

time: 216 us -> 192 us (0.89)
  waiting for transfers between devices: 69.4 us -> 16.2 us
  blocking collectives: 61.9 us -> 98.6 us
  starting transfers between devices: 21.6 us -> 14.3 us
  local copies, waits for them, and re-layouts: 40.2 us -> 34.7 us
  other arithmetic: 5.42 us -> 9.68 us
    all_to_all x2 -> x1, waiting for transfers between devices: 53.2 us -> 0.01 us  [exchanged(): arrived = lax.all_to_all(joined, axis, 0, 0, tiled=True)]
    all_to_all x1 -> x2, blocking collectives: 30.4 us -> 65.5 us  [exchanged(): arrived = lax.all_to_all(joined, axis, 0, 0, tiled=True)]
    all_to_all x2 -> x1, starting transfers between devices: 17.4 us -> 5.53 us  [exchanged(): arrived = lax.all_to_all(joined, axis, 0, 0, tiled=True)]
    slice x5 -> x7, local copies, waits for them, and re-layouts: 7.82 us -> 2.83 us  [exchanged(): pieces.append(arrived[:, offset:offset + part.shape[1]])]
    ppermute x0 -> x2, starting transfers between devices: none -> 4.55 us  [whole_from_halves(): partner = lax.ppermute(own_halves, axis, [(i, i ^ 1) for i in range(peers)])]
    reshape x2, local copies, waits for them, and re-layouts: 7.48 us -> 4.54 us  [conv_from_pieces(): parts = pieces.reshape(-1, taps, rows, hidden)]
    select_n x0 -> x2, other arithmetic: none -> 2.72 us  [whole_from_halves(): low = jnp.where(first_core, own_halves, partner)]
    unnamed x52 -> x74, local copies, waits for them, and re-layouts: 6.89 us -> 6.25 us
  transfers between devices with their start and end apart: 3 -> 4, of which waited for: 3 -> 1; matrix products, arithmetic and copies ran while one was open for 11% -> 17% of each run, Pallas kernels for 0% -> 0%
where the time goes in v8:
time: 192 us; the launch traced here: 191 us
  blocking collectives  98.6 us (51%)
  local copies, waits for them, and re-layouts  34.7 us (18%)
  waiting for transfers between devices  16.2 us (8%)
  matrix products  14.4 us (8%)
  starting transfers between devices  14.3 us (7%)
  other arithmetic  9.68 us (5%)
  between operations  2.64 us (1%)
    all_to_all x2, blocking collectives, exchanged(): arrived = lax.all_to_all(joined, axis, 0, 0, tiled=True)  65.5 us
    all_to_all x1, blocking collectives, summed_over(): arrived = lax.all_to_all(pieces, axis, 0, 0, tiled=True)  33.1 us
    all_to_all x1, waiting for transfers between devices, gathered(): return lax.all_to_all(copies, axis, 0, 0, tiled=True)  16.2 us
    dot_general x8, matrix products, contract_last(): lax.dot_general(left, right, (((1,), (1,)), ((), ())), preferred_element_...  7.55 us
    unnamed x74, local copies, waits for them, and re-layouts  6.25 us
    all_to_all x1, starting transfers between devices, exchanged(): arrived = lax.all_to_all(joined, axis, 0, 0, tiled=True)  5.53 us
    ppermute x2, starting transfers between devices, whole_from_halves(): partner = lax.ppermute(own_halves, axis, [(i, i ^ 1) for i in range(peers)])  4.55 us
    reshape x2, local copies, waits for them, and re-layouts, conv_from_pieces(): parts = pieces.reshape(-1, taps, rows, hidden)  4.54 us
  transfers between devices with their start and end apart: 4, of which 1 were waited for; matrix products, arithmetic and copies ran while one was open for 17% of the time, Pallas kernels for 0%

profile of v8, /device:TPU:6, one launch (start us, length us, event | category | flops | bytes accessed | tf_op | source)
XLA Modules:
  0.0 190.6 jit_solution(4433311284284791723)
XLA Ops:
  0.6 1.0 fusion.98
  1.7 0.9 reshape.74
  3.4 36.4 %all_to_all.25 = bf16[16,92,768]{2,1,0:T(8,128)(2,1)S(1)} all-to-all(bf16[16,92,768]{2,1,0:T(8,128)(2,1)S(1)} %pad_maximum_fusion), channel_id=1, replica_groups=mesh['dp'=32,'seq'=16] {'seq'}, dimensions={0} | all-to-all | bytes 4521984 | tf_op jit(solution)/shard_map/all_to_all | solution.py:92
  39.9 2.0 %copy.56 = bf16[16,60,768]{2,0,1:T(8,128)(2,1)} copy(bf16[16,60,768]{2,1,0:T(8,128)(2,1)S(1)} %slice.167) | data formatting | bytes 2949120 | tf_op jit(solution)/shard_map/slice | solution.py:96
  41.9 2.4 %collective-permute-start = (bf16[16,60,768]{2,0,1:T(8,128)(2,1)}, bf16[16,60,768]{2,0,1:T(8,128)(2,1)}, u32[]{:S(2)}, u32[]{:S(2)}) collective-permute-start(bf16[16,60,768]{2,0,1:T(8,128)(2,1)} %copy.56), channel_id=1, source_target_pairs={{0,1},{1,0},{2,3},{3,2},{4,5},{5,4},{6,7},{7,6},{8,9},{9,8},{10,11... | collective-permute-start | bytes 4423688 | tf_op jit(solution)/shard_map/ppermute | solution.py:112
  44.3 0.6 fusion.99
  46.2 0.6 slice_reduce_fusion.4
  47.0 1.6 copy.59
  48.7 1.3 pad_maximum_fusion.3
  50.0 5.5 %all-to-all-start.1 = ((bf16[16,68,768]{2,1,0:T(8,128)(2,1)}), bf16[16,68,768]{2,1,0:T(8,128)(2,1)S(1)}, u32[]{:S(2)}, u32[]{:S(2)}) async-start(bf16[16,68,768]{2,1,0:T(8,128)(2,1)} %pad_maximum_fusion.3), calls=%async_computation.1 | async-start | bytes 3538944 | tf_op jit(solution)/shard_map/all_to_all | solution.py:92
  55.5 0.6 fusion.6
  56.2 1.2 fusion.95
  57.4 1.0 copy-done.2
  58.3 2.4 %broadcast_select_fusion.1 = (bf16[16,60,768]{2,1,0:T(8,128)(2,1)S(1)}, bf16[16,60,768]{2,1,0:T(8,128)(2,1)S(1)}) fusion(pred[]{:T(512)S(6)} %eq.7, bf16[16,60,768]{2,0,1:T(8,128)(2,1)} %collective-permute-done, bf16[16,92,768]{2,1,0:T(8,128)(2,1)S(1)} %copy-done.2), kind=kLoop, calls=%fused_computation.46 | loop fusion | flops 1474560 | bytes 5898241 | tf_op jit(solution)/shard_map/jit(_where)/select_n | solution.py:114
  60.8 1.4 pad_maximum_fusion.2
  62.2 1.4 slice.173
  63.6 3.7 %reshape.78 = bf16[384,2,768]{2,1,0:T(2,128)(2,1)} reshape(bf16[16,48,768]{2,1,0:T(8,128)(2,1)} %slice.173) | data formatting | bytes 2359296 | tf_op jit(solution)/shard_map/reshape | solution.py:164
  67.3 3.7 %reshape.76 = bf16[16,3,48,384]{3,2,1,0:T(8,128)(2,1)} reshape(bf16[16,72,768]{2,1,0:T(8,128)(2,1)} %pad_maximum_fusion.2) | data formatting | bytes 3538944 | tf_op jit(solution)/shard_map/reshape | solution.py:121
  71.0 1.7 fusion.92
  73.3 0.6 convolution_add_fusion.3
  75.2 3.1 %fusion.93 = (bf16[384,1,768]{2,1,0:T(2,128)(2,1)}, bf16[384,1,768]{2,1,0:T(2,128)(2,1)}) fusion(bf16[384,2,768]{2,1,0:T(2,128)(2,1)S(1)} %copy-done.3), kind=kLoop, calls=%fused_computation.135 | loop fusion | bytes 2359296 | tf_op jit(solution)/shard_map/slice | solution.py:194
  78.5 2.2 %collective-permute-start.1 = (bf16[16,36,768]{2,0,1:T(8,128)(2,1)S(1)}, bf16[16,36,768]{2,0,1:T(8,128)(2,1)S(1)}, u32[]{:S(2)}, u32[]{:S(2)}) collective-permute-start(bf16[16,36,768]{2,0,1:T(8,128)(2,1)S(1)} %copy.60), channel_id=1, source_target_pairs={{0,1},{1,0},{2,3},{3,2},{4,5},{5,4},{6,7},{7,6},{8,9},{9,8},{10,11... | collective-permute-start | bytes 2654216 | tf_op jit(solution)/shard_map/ppermute | solution.py:112
  80.8 2.1 %multiply_convert_fusion = (bf16[512,768]{1,0:T(8,128)(2,1)S(1)}, bf16[512,768]{1,0:T(8,128)(2,1)}) fusion(f32[768]{0:T(1024)S(1)} %get-tuple-element.12, f32[768]{0:T(1024)S(1)} %get-tuple-element.45, bf16[384,1,768]{2,1,0:T(2,128)(2,1)S(1)} %copy-done.18, f32[512,384]{1,0:T(8,128)S(1)} %fusion.32, f32[]{:T(128)} %bitcast.10, bf16[512,768]{1,0:T(8,128)(2,1)S(1)} %bitcast.79), kind=kOutput, calls=%fused_computation.42 | convolution fusion | flops 310050816 | bytes 3741700 | tf_op jit(solution)/shard_map/dot_general | solution.py:61
  82.9 1.2 fusion.94
  84.2 1.0 fusion.25
  85.2 1.0 fusion.26
  86.9 0.8 reshape.79
  87.9 0.9 copy-done.17
  89.4 0.6 convolution_add_fusion.1
  90.4 0.6 fusion.30
  91.5 0.9 fusion.48
  92.5 0.6 fusion.100
  93.2 0.6 fusion.71
  94.5 1.6 fusion.24
  96.2 1.0 fusion.40
  97.2 1.0 copy-done.7
  98.2 0.6 fusion.101
  98.8 0.7 convolution_convert_fusion.1
  99.9 0.6 fusion.68
  100.7 0.6 convolution_convert_fusion
  102.0 1.6 fusion.11
  103.8 29.2 %all_to_all.26 = bf16[16,80,768]{2,1,0:T(8,128)(2,1)S(1)} all-to-all(bf16[16,80,768]{2,1,0:T(8,128)(2,1)S(1)} %pad_maximum_fusion.1), channel_id=1, replica_groups=mesh['dp'=32,'seq'=16] {'seq'}, dimensions={0} | all-to-all | bytes 3932160 | tf_op jit(solution)/shard_map/all_to_all | solution.py:92
  133.7 33.1 %all_to_all.27 = f32[32,1,1152]{2,1,0:T(1,128)S(1)} all-to-all(f32[32,1,1152]{2,1,0:T(1,128)S(1)} %reshape_reshape.4), channel_id=1, replica_groups=mesh['dp'=32,'seq'=16] {'dp'}, dimensions={0} | all-to-all | bytes 294912 | tf_op jit(solution)/shard_map/all_to_all | solution.py:27
  166.8 0.7 broadcast_in_dim.2
  167.5 4.2 %all-to-all-start.4 = ((f32[32,1,1152]{2,1,0:T(1,128)}), f32[32,1,1152]{2,1,0:T(1,128)S(1)}, u32[]{:S(2)}, u32[]{:S(2)}) async-start(f32[32,1,1152]{2,1,0:T(1,128)} %broadcast_in_dim.2), calls=%async_computation.4 | async-start | bytes 294912 | tf_op jit(solution)/shard_map/all_to_all | solution.py:21
  171.9 1.3 copy.64
  173.2 16.2 %all-to-all-done.4 = f32[32,1,1152]{2,1,0:T(1,128)S(1)} async-done(((f32[32,1,1152]{2,1,0:T(1,128)}), f32[32,1,1152]{2,1,0:T(1,128)S(1)}, u32[]{:S(2)}, u32[]{:S(2)}) %all-to-all-start.4) | async-done | bytes 147488 | tf_op jit(solution)/shard_map/all_to_all | solution.py:21
  189.8 0.8 mul.345
  (107 shorter events, 9.2 us)
Async XLA Ops:
  0.6 2.1 %copy-start.21 = (bf16[1,512,768]{2,1,0:T(8,128)(2,1)S(1)}, bf16[1,512,768]{2,1,0:T(8,128)(2,1)}, u32[]{:S(2)}) copy-start(bf16[1,512,768]{2,1,0:T(8,128)(2,1)} %param.9) | copy-start | bytes 2359300
  39.7 7.1 %copy-start.1 = (bf16[16,92,768]{2,1,0:T(8,128)(2,1)}, bf16[16,92,768]{2,1,0:T(8,128)(2,1)S(1)}, u32[]{:S(2)}) copy-start(bf16[16,92,768]{2,1,0:T(8,128)(2,1)S(1)} %all_to_all.25) | copy-start | bytes 6782980
  39.8 4.4 %copy-start.35 = (s32[1,2]{1,0:T(1,128)S(1)}, s32[1,2]{1,0:T(1,128)}, u32[]{:S(2)}) copy-start(s32[1,2]{1,0:T(1,128)} %param.11) | copy-start | bytes 28
  39.9 6.3 %copy-start.33 = (f32[2,384]{1,0:T(2,128)S(1)}, f32[2,384]{1,0:T(2,128)}, u32[]{:S(2)}) copy-start(f32[2,384]{1,0:T(2,128)} %param.15) | copy-start | bytes 9220
  39.9 6.9 %copy-start.34 = (f32[2,384]{1,0:T(2,128)S(1)}, f32[2,384]{1,0:T(2,128)}, u32[]{:S(2)}) copy-start(f32[2,384]{1,0:T(2,128)} %param.14) | copy-start | bytes 9220
  39.9 6.9 %copy-start.27 = (f32[2,768]{1,0:T(2,128)S(1)}, f32[2,768]{1,0:T(2,128)}, u32[]{:S(2)}) copy-start(f32[2,768]{1,0:T(2,128)} %param.13) | copy-start | bytes 18436
  39.9 6.9 %copy-start.28 = (f32[2,768]{1,0:T(2,128)S(1)}, f32[2,768]{1,0:T(2,128)}, u32[]{:S(2)}) copy-start(f32[2,768]{1,0:T(2,128)} %param.12) | copy-start | bytes 18436
  41.9 15.5 %collective-permute-start = (bf16[16,60,768]{2,0,1:T(8,128)(2,1)}, bf16[16,60,768]{2,0,1:T(8,128)(2,1)}, u32[]{:S(2)}, u32[]{:S(2)}) collective-permute-start(bf16[16,60,768]{2,0,1:T(8,128)(2,1)} %copy.56), channel_id=1, source_target_pairs={{0,1},{1,0},{2,3},{3,2},{4,5},{5,4},{6,7},{7,6},{8,9},{9,8},{10,11... | collective-permute-start | bytes 4423688 | tf_op jit(solution)/shard_map/ppermute | solution.py:112
  46.9 33.9 %copy-start.29 = (f32[768]{0:T(1024)}, f32[768]{0:T(1024)S(1)}, u32[]{:S(2)}) copy-start(f32[768]{0:T(1024)S(1)} %get-tuple-element.12) | copy-start | bytes 9220
  46.9 33.9 %copy-start.31 = (f32[768]{0:T(1024)}, f32[768]{0:T(1024)S(1)}, u32[]{:S(2)}) copy-start(f32[768]{0:T(1024)S(1)} %get-tuple-element.45) | copy-start | bytes 9220
  46.9 33.8 %copy-start.10 = (bf16[16,32,768]{2,1,0:T(8,128)(2,1)}, bf16[16,32,768]{2,1,0:T(8,128)(2,1)S(1)}, u32[]{:S(2)}) copy-start(bf16[16,32,768]{2,1,0:T(8,128)(2,1)S(1)} %slice.165) | copy-start | bytes 2359300
  50.0 28.3 %all-to-all-start.1 = ((bf16[16,68,768]{2,1,0:T(8,128)(2,1)}), bf16[16,68,768]{2,1,0:T(8,128)(2,1)S(1)}, u32[]{:S(2)}, u32[]{:S(2)}) async-start(bf16[16,68,768]{2,1,0:T(8,128)(2,1)} %pad_maximum_fusion.3), calls=%async_computation.1 | async-start | bytes 3538944 | tf_op jit(solution)/shard_map/all_to_all | solution.py:92
  56.2 2.2 %copy-start.2 = (bf16[16,92,768]{2,1,0:T(8,128)(2,1)S(1)}, bf16[16,92,768]{2,1,0:T(8,128)(2,1)}, u32[]{:S(2)}) copy-start(bf16[16,92,768]{2,1,0:T(8,128)(2,1)} %copy-done.1) | copy-start | bytes 6782980
  71.0 1.7 copy-start.13
  72.7 1.2 copy-start.4
  72.7 1.2 copy-start.6
  72.7 1.3 copy-start.14
  73.3 1.1 copy-start.12
  73.9 1.3 copy-start.3
  75.2 5.6 %copy-start.24 = (f32[512,384]{1,0:T(8,128)}, f32[512,384]{1,0:T(8,128)S(1)}, u32[]{:S(2)}) copy-start(f32[512,384]{1,0:T(8,128)S(1)} %fusion.32) | copy-start | bytes 2359300
  78.3 7.9 %copy-start = (bf16[16,68,768]{2,1,0:T(8,128)(2,1)}, bf16[16,68,768]{2,1,0:T(8,128)(2,1)S(1)}, u32[]{:S(2)}) copy-start(bf16[16,68,768]{2,1,0:T(8,128)(2,1)S(1)} %all-to-all-done.1) | copy-start | bytes 5013508
  78.3 2.5 %copy-start.18 = (bf16[384,1,768]{2,1,0:T(2,128)(2,1)S(1)}, bf16[384,1,768]{2,1,0:T(2,128)(2,1)}, u32[]{:S(2)}) copy-start(bf16[384,1,768]{2,1,0:T(2,128)(2,1)} %get-tuple-element.29) | copy-start | bytes 1769476
  78.5 7.7 %collective-permute-start.1 = (bf16[16,36,768]{2,0,1:T(8,128)(2,1)S(1)}, bf16[16,36,768]{2,0,1:T(8,128)(2,1)S(1)}, u32[]{:S(2)}, u32[]{:S(2)}) collective-permute-start(bf16[16,36,768]{2,0,1:T(8,128)(2,1)S(1)} %copy.60), channel_id=1, source_target_pairs={{0,1},{1,0},{2,3},{3,2},{4,5},{5,4},{6,7},{7,6},{8,9},{9,8},{10,11... | collective-permute-start | bytes 2654216 | tf_op jit(solution)/shard_map/ppermute | solution.py:112
  82.9 1.3 copy-start.8
  87.7 1.1 copy-start.17
  87.9 1.5 copy-start.9
  89.4 1.1 copy-start.16
  89.4 1.1 copy-start.26
  90.0 1.3 copy-start.20
  90.0 1.5 copy-start.23
  93.1 1.1 slice-start
  93.1 1.1 copy-start.30
  93.2 1.1 copy-start.32
  93.2 1.4 copy-start.36
  94.5 1.7 copy-start.19
  94.5 1.7 copy-start.25
  97.2 1.1 copy-start.7
  98.8 1.1 copy-start.5
  99.6 1.2 copy-start.22
  100.7 1.1 copy-start.11
  100.7 1.3 copy-start.15
  167.5 21.9 %all-to-all-start.4 = ((f32[32,1,1152]{2,1,0:T(1,128)}), f32[32,1,1152]{2,1,0:T(1,128)S(1)}, u32[]{:S(2)}, u32[]{:S(2)}) async-start(f32[32,1,1152]{2,1,0:T(1,128)} %broadcast_in_dim.2), calls=%async_computation.4 | async-start | bytes 294912 | tf_op jit(solution)/shard_map/all_to_all | solution.py:21

commit v9 on v8

--- a/solution.py
+++ b/solution.py
@@ -120,6 +120,22 @@
     taps, rows, hidden = block_shape
     parts = pieces.reshape(-1, taps, rows, hidden)
     return jnp.moveaxis(parts, 0, 1).reshape(taps, -1, hidden)
+
+
+def chip_half(term, peers, channels):
+    half = channels // 2
+    first_core = lax.axis_index("seq") % 2 == 0
+    kept = jnp.where(first_core, term[:, :half], term[:, half:])
+    given = jnp.where(first_core, term[:, half:], term[:, :half])
+    partner = lax.ppermute(given, "seq", [(i, i ^ 1) for i in range(peers)])
+    summed = (kept + partner).astype(jnp.bfloat16)
+    return summed.reshape(peers, -1, channels)
+
+
+def chip_sum(piece, peers, channels):
+    half = channels // 2
+    parts = piece.reshape(peers // 2, 2, -1, half).astype(jnp.float32).sum(axis=0)
+    return jnp.moveaxis(parts, 0, 1).reshape(-1, channels)
 
 
 def row_shifted(source, rows_away):
@@ -206,15 +222,11 @@
             in_gain[block_index],
         )
         gradient = backward_second(*second_operands)
-    term_pieces = [
-        term.astype(jnp.bfloat16).reshape(peers, -1, channels) for term in terms
-    ]
+    term_pieces = [chip_half(term, peers, channels) for term in terms]
     first_term, second_term, back_pieces = exchanged(
         term_pieces + [gradient.reshape(peers, -1, channels)], "seq"
     )
-    own_terms = [
-        piece.astype(jnp.float32).sum(axis=0) for piece in (first_term, second_term)
-    ]
+    own_terms = [chip_sum(piece, peers, channels) for piece in (first_term, second_term)]
     summed = reduced_over_dp(jnp.stack(own_terms, axis=1))
     sample_count = sequence_in.shape[0] * lax.axis_size("dp")
     full_length = sequence_in.shape[1] * peers

time: 192 us -> 191 us (level)
  blocking collectives: 98.6 us -> 92.3 us
  starting transfers between devices: 14.3 us -> 19.2 us
    all_to_all x2, blocking collectives: 65.5 us -> 59.3 us  [exchanged(): arrived = lax.all_to_all(joined, axis, 0, 0, tiled=True)]
    ppermute x0 -> x2, starting transfers between devices: none -> 4.67 us  [chip_half(): partner = lax.ppermute(given, 'seq', [(i, i ^ 1) for i in range(peers)])]
  transfers between devices with their start and end apart: 4 -> 6, of which waited for: 1 -> 1; matrix products, arithmetic and copies ran while one was open for 17% -> 18% of each run, Pallas kernels for 0% -> 0%
where the time goes in v9:
time: 191 us; the launch traced here: 190 us
  blocking collectives  92.3 us (48%)
  local copies, waits for them, and re-layouts  34.4 us (18%)
  starting transfers between devices  19.2 us (10%)
  waiting for transfers between devices  16.2 us (8%)
  matrix products  14.3 us (7%)
  other arithmetic  10.8 us (6%)
  between operations  2.8 us (1%)
    all_to_all x2, blocking collectives, exchanged(): arrived = lax.all_to_all(joined, axis, 0, 0, tiled=True)  59.3 us
    all_to_all x1, blocking collectives, summed_over(): arrived = lax.all_to_all(pieces, axis, 0, 0, tiled=True)  32.9 us
    all_to_all x1, waiting for transfers between devices, gathered(): return lax.all_to_all(copies, axis, 0, 0, tiled=True)  16.2 us
    dot_general x8, matrix products, contract_last(): lax.dot_general(left, right, (((1,), (1,)), ((), ())), preferred_element_...  7.52 us
    unnamed x74, local copies, waits for them, and re-layouts  5.53 us
    all_to_all x1, starting transfers between devices, exchanged(): arrived = lax.all_to_all(joined, axis, 0, 0, tiled=True)  5.53 us
    ppermute x2, starting transfers between devices, whole_from_halves(): partner = lax.ppermute(own_halves, axis, [(i, i ^ 1) for i in range(peers)])  4.73 us
    ppermute x2, starting transfers between devices, chip_half(): partner = lax.ppermute(given, 'seq', [(i, i ^ 1) for i in range(peers)])  4.67 us
  transfers between devices with their start and end apart: 6, of which 1 were waited for; matrix products, arithmetic and copies ran while one was open for 18% of the time, Pallas kernels for 0%

profile of v9, /device:TPU:6, one launch (start us, length us, event | category | flops | bytes accessed | tf_op | source)
XLA Modules:
  0.0 190.0 jit_solution(18236160795017059286)
XLA Ops:
  0.6 1.0 fusion.100
  1.7 0.9 reshape.80
  3.4 36.4 %all_to_all.25 = bf16[16,92,768]{2,1,0:T(8,128)(2,1)S(1)} all-to-all(bf16[16,92,768]{2,1,0:T(8,128)(2,1)S(1)} %pad_maximum_fusion), channel_id=1, replica_groups=mesh['dp'=32,'seq'=16] {'seq'}, dimensions={0} | all-to-all | bytes 4521984 | tf_op jit(solution)/shard_map/all_to_all | solution.py:92
  39.9 1.9 %copy.68 = bf16[16,60,768]{2,0,1:T(8,128)(2,1)} copy(bf16[16,60,768]{2,1,0:T(8,128)(2,1)S(1)} %slice.187) | data formatting | bytes 2949120 | tf_op jit(solution)/shard_map/slice | solution.py:96
  41.9 2.4 %collective-permute-start = (bf16[16,60,768]{2,0,1:T(8,128)(2,1)}, bf16[16,60,768]{2,0,1:T(8,128)(2,1)}, u32[]{:S(2)}, u32[]{:S(2)}) collective-permute-start(bf16[16,60,768]{2,0,1:T(8,128)(2,1)} %copy.68), channel_id=1, source_target_pairs={{0,1},{1,0},{2,3},{3,2},{4,5},{5,4},{6,7},{7,6},{8,9},{9,8},{10,11... | collective-permute-start | bytes 4423688 | tf_op jit(solution)/shard_map/ppermute | solution.py:112
  44.2 0.6 fusion.101
  46.1 0.6 slice_reduce_fusion.4
  47.0 1.6 copy.71
  48.7 1.3 pad_maximum_fusion.2
  50.0 5.5 %all-to-all-start.1 = ((bf16[16,68,768]{2,1,0:T(8,128)(2,1)}), bf16[16,68,768]{2,1,0:T(8,128)(2,1)S(1)}, u32[]{:S(2)}, u32[]{:S(2)}) async-start(bf16[16,68,768]{2,1,0:T(8,128)(2,1)} %pad_maximum_fusion.2), calls=%async_computation.1 | async-start | bytes 3538944 | tf_op jit(solution)/shard_map/all_to_all | solution.py:92
  55.5 0.6 fusion.6
  56.2 1.2 fusion.97
  57.3 1.0 copy-done.2
  58.3 2.4 %broadcast_select_fusion.1 = (bf16[16,60,768]{2,1,0:T(8,128)(2,1)S(1)}, bf16[16,60,768]{2,1,0:T(8,128)(2,1)S(1)}) fusion(pred[]{:T(512)S(6)} %eq.11, bf16[16,60,768]{2,0,1:T(8,128)(2,1)} %collective-permute-done, bf16[16,92,768]{2,1,0:T(8,128)(2,1)S(1)} %copy-done.2), kind=kLoop, calls=%fused_computation.45 | loop fusion | flops 1474560 | bytes 5898241 | tf_op jit(solution)/shard_map/jit(_where)/select_n | solution.py:114
  60.8 1.4 pad_maximum_fusion.1
  62.2 1.4 slice.193
  63.6 3.6 %reshape.84 = bf16[384,2,768]{2,1,0:T(2,128)(2,1)} reshape(bf16[16,48,768]{2,1,0:T(8,128)(2,1)} %slice.193) | data formatting | bytes 2359296 | tf_op jit(solution)/shard_map/reshape | solution.py:180
  67.2 3.7 %reshape.82 = bf16[16,3,48,384]{3,2,1,0:T(8,128)(2,1)} reshape(bf16[16,72,768]{2,1,0:T(8,128)(2,1)} %pad_maximum_fusion.1) | data formatting | bytes 3538944 | tf_op jit(solution)/shard_map/reshape | solution.py:121
  71.0 1.7 fusion.94
  75.2 3.1 %fusion.95 = (bf16[384,1,768]{2,1,0:T(2,128)(2,1)}, bf16[384,1,768]{2,1,0:T(2,128)(2,1)}) fusion(bf16[384,2,768]{2,1,0:T(2,128)(2,1)S(1)} %copy-done.3), kind=kLoop, calls=%fused_computation.139 | loop fusion | bytes 2359296 | tf_op jit(solution)/shard_map/slice | solution.py:210
  78.5 2.4 %collective-permute-start.1 = (bf16[16,36,768]{2,0,1:T(8,128)(2,1)S(1)}, bf16[16,36,768]{2,0,1:T(8,128)(2,1)S(1)}, u32[]{:S(2)}, u32[]{:S(2)}) collective-permute-start(bf16[16,36,768]{2,0,1:T(8,128)(2,1)S(1)} %copy.72), channel_id=1, source_target_pairs={{0,1},{1,0},{2,3},{3,2},{4,5},{5,4},{6,7},{7,6},{8,9},{9,8},{10,11... | collective-permute-start | bytes 2654216 | tf_op jit(solution)/shard_map/ppermute | solution.py:112
  81.0 2.1 %multiply_convert_fusion = (bf16[512,768]{1,0:T(8,128)(2,1)S(1)}, bf16[512,768]{1,0:T(8,128)(2,1)}) fusion(f32[768]{0:T(1024)S(1)} %get-tuple-element.10, f32[768]{0:T(1024)S(1)} %get-tuple-element.45, bf16[384,1,768]{2,1,0:T(2,128)(2,1)S(1)} %copy-done.18, f32[512,384]{1,0:T(8,128)S(1)} %fusion.32, f32[]{:T(128)} %bitcast.10, bf16[512,768]{1,0:T(8,128)(2,1)S(1)} %bitcast.79), kind=kOutput, calls=%fused_computation.41 | convolution fusion | flops 310050816 | bytes 3741700 | tf_op jit(solution)/shard_map/dot_general | solution.py:61
  83.1 1.2 fusion.96
  84.4 1.0 fusion.25
  85.4 1.0 fusion.26
  87.1 0.6 reshape.85
  87.9 0.9 copy-done.17
  90.4 0.6 fusion.30
  91.5 0.9 fusion.48
  92.5 0.6 fusion.102
  93.2 0.6 fusion.73
  94.5 1.6 fusion.24
  96.2 1.0 fusion.40
  97.2 1.0 copy-done.7
  98.2 0.6 fusion.103
  98.8 0.7 fusion.57
  99.9 0.6 fusion.70
  101.4 2.4 %collective-permute-start.3 = (f32[384,384]{1,0:T(8,128)S(1)}, f32[384,384]{1,0:T(8,128)S(1)}, u32[]{:S(2)}, u32[]{:S(2)}) collective-permute-start(f32[384,384]{1,0:T(8,128)S(1)} %slice_select_fusion), channel_id=1, source_target_pairs={{0,1},{1,0},{2,3},{3,2},{4,5},{5,4},{6,7},{7,6},{8,9},{9,8},{10,11... | collective-permute-start | bytes 1769480 | tf_op jit(solution)/shard_map/ppermute | solution.py:130
  103.8 0.9 slice_select_fusion.1
  104.7 2.2 %collective-permute-start.2 = (f32[384,384]{1,0:T(8,128)}, f32[384,384]{1,0:T(8,128)S(1)}, u32[]{:S(2)}, u32[]{:S(2)}) collective-permute-start(f32[384,384]{1,0:T(8,128)} %slice_select_fusion.1), channel_id=1, source_target_pairs={{0,1},{1,0},{2,3},{3,2},{4,5},{5,4},{6,7},{7,6},{8,9},{9,8},{10,11... | collective-permute-start | bytes 1769480 | tf_op jit(solution)/shard_map/ppermute | solution.py:130
  106.9 1.6 fusion.11
  109.2 23.0 %all_to_all.26 = bf16[16,56,768]{2,1,0:T(8,128)(2,1)S(1)} all-to-all(bf16[16,56,768]{2,1,0:T(8,128)(2,1)S(1)} %pad_maximum_fusion.4), channel_id=1, replica_groups=mesh['dp'=32,'seq'=16] {'seq'}, dimensions={0} | all-to-all | bytes 2752512 | tf_op jit(solution)/shard_map/all_to_all | solution.py:92
  133.2 32.9 %all_to_all.27 = f32[32,1,1152]{2,1,0:T(1,128)S(1)} all-to-all(f32[32,1,1152]{2,1,0:T(1,128)S(1)} %reshape_reshape.4), channel_id=1, replica_groups=mesh['dp'=32,'seq'=16] {'dp'}, dimensions={0} | all-to-all | bytes 294912 | tf_op jit(solution)/shard_map/all_to_all | solution.py:27
  166.2 0.7 broadcast_in_dim.2
  167.0 4.3 %all-to-all-start.4 = ((f32[32,1,1152]{2,1,0:T(1,128)}), f32[32,1,1152]{2,1,0:T(1,128)S(1)}, u32[]{:S(2)}, u32[]{:S(2)}) async-start(f32[32,1,1152]{2,1,0:T(1,128)} %broadcast_in_dim.2), calls=%async_computation.4 | async-start | bytes 294912 | tf_op jit(solution)/shard_map/all_to_all | solution.py:21
  171.4 1.3 copy.79
  172.7 16.2 %all-to-all-done.4 = f32[32,1,1152]{2,1,0:T(1,128)S(1)} async-done(((f32[32,1,1152]{2,1,0:T(1,128)}), f32[32,1,1152]{2,1,0:T(1,128)S(1)}, u32[]{:S(2)}, u32[]{:S(2)}) %all-to-all-start.4) | async-done | bytes 147488 | tf_op jit(solution)/shard_map/all_to_all | solution.py:21
  189.3 0.8 mul.345
  (124 shorter events, 11.0 us)
Async XLA Ops:
  0.6 2.1 %copy-start.21 = (bf16[1,512,768]{2,1,0:T(8,128)(2,1)S(1)}, bf16[1,512,768]{2,1,0:T(8,128)(2,1)}, u32[]{:S(2)}) copy-start(bf16[1,512,768]{2,1,0:T(8,128)(2,1)} %param.9) | copy-start | bytes 2359300
  39.7 7.1 %copy-start.1 = (bf16[16,92,768]{2,1,0:T(8,128)(2,1)}, bf16[16,92,768]{2,1,0:T(8,128)(2,1)S(1)}, u32[]{:S(2)}) copy-start(bf16[16,92,768]{2,1,0:T(8,128)(2,1)S(1)} %all_to_all.25) | copy-start | bytes 6782980
  39.8 4.4 %copy-start.35 = (s32[1,2]{1,0:T(1,128)S(1)}, s32[1,2]{1,0:T(1,128)}, u32[]{:S(2)}) copy-start(s32[1,2]{1,0:T(1,128)} %param.11) | copy-start | bytes 28
  39.9 6.3 %copy-start.33 = (f32[2,384]{1,0:T(2,128)S(1)}, f32[2,384]{1,0:T(2,128)}, u32[]{:S(2)}) copy-start(f32[2,384]{1,0:T(2,128)} %param.15) | copy-start | bytes 9220
  39.9 6.9 %copy-start.34 = (f32[2,384]{1,0:T(2,128)S(1)}, f32[2,384]{1,0:T(2,128)}, u32[]{:S(2)}) copy-start(f32[2,384]{1,0:T(2,128)} %param.14) | copy-start | bytes 9220
  39.9 6.9 %copy-start.27 = (f32[2,768]{1,0:T(2,128)S(1)}, f32[2,768]{1,0:T(2,128)}, u32[]{:S(2)}) copy-start(f32[2,768]{1,0:T(2,128)} %param.13) | copy-start | bytes 18436
  39.9 6.9 %copy-start.28 = (f32[2,768]{1,0:T(2,128)S(1)}, f32[2,768]{1,0:T(2,128)}, u32[]{:S(2)}) copy-start(f32[2,768]{1,0:T(2,128)} %param.12) | copy-start | bytes 18436
  41.9 15.5 %collective-permute-start = (bf16[16,60,768]{2,0,1:T(8,128)(2,1)}, bf16[16,60,768]{2,0,1:T(8,128)(2,1)}, u32[]{:S(2)}, u32[]{:S(2)}) collective-permute-start(bf16[16,60,768]{2,0,1:T(8,128)(2,1)} %copy.68), channel_id=1, source_target_pairs={{0,1},{1,0},{2,3},{3,2},{4,5},{5,4},{6,7},{7,6},{8,9},{9,8},{10,11... | collective-permute-start | bytes 4423688 | tf_op jit(solution)/shard_map/ppermute | solution.py:112
  46.8 34.1 %copy-start.29 = (f32[768]{0:T(1024)}, f32[768]{0:T(1024)S(1)}, u32[]{:S(2)}) copy-start(f32[768]{0:T(1024)S(1)} %get-tuple-element.10) | copy-start | bytes 9220
  46.9 34.1 %copy-start.31 = (f32[768]{0:T(1024)}, f32[768]{0:T(1024)S(1)}, u32[]{:S(2)}) copy-start(f32[768]{0:T(1024)S(1)} %get-tuple-element.45) | copy-start | bytes 9220
  46.9 34.0 %copy-start.10 = (bf16[16,32,768]{2,1,0:T(8,128)(2,1)}, bf16[16,32,768]{2,1,0:T(8,128)(2,1)S(1)}, u32[]{:S(2)}) copy-start(bf16[16,32,768]{2,1,0:T(8,128)(2,1)S(1)} %slice.185) | copy-start | bytes 2359300
  50.0 28.3 %all-to-all-start.1 = ((bf16[16,68,768]{2,1,0:T(8,128)(2,1)}), bf16[16,68,768]{2,1,0:T(8,128)(2,1)S(1)}, u32[]{:S(2)}, u32[]{:S(2)}) async-start(bf16[16,68,768]{2,1,0:T(8,128)(2,1)} %pad_maximum_fusion.2), calls=%async_computation.1 | async-start | bytes 3538944 | tf_op jit(solution)/shard_map/all_to_all | solution.py:92
  56.2 2.2 %copy-start.2 = (bf16[16,92,768]{2,1,0:T(8,128)(2,1)S(1)}, bf16[16,92,768]{2,1,0:T(8,128)(2,1)}, u32[]{:S(2)}) copy-start(bf16[16,92,768]{2,1,0:T(8,128)(2,1)} %copy-done.1) | copy-start | bytes 6782980
  71.0 1.7 copy-start.13
  72.6 1.2 copy-start.4
  72.7 1.2 copy-start.6
  72.7 1.3 copy-start.14
  73.3 1.1 copy-start.12
  73.9 1.3 copy-start.3
  75.2 5.8 %copy-start.24 = (f32[512,384]{1,0:T(8,128)}, f32[512,384]{1,0:T(8,128)S(1)}, u32[]{:S(2)}) copy-start(f32[512,384]{1,0:T(8,128)S(1)} %fusion.32) | copy-start | bytes 2359300
  78.3 8.1 %copy-start = (bf16[16,68,768]{2,1,0:T(8,128)(2,1)}, bf16[16,68,768]{2,1,0:T(8,128)(2,1)S(1)}, u32[]{:S(2)}) copy-start(bf16[16,68,768]{2,1,0:T(8,128)(2,1)S(1)} %all-to-all-done.1) | copy-start | bytes 5013508
  78.3 2.7 %copy-start.18 = (bf16[384,1,768]{2,1,0:T(2,128)(2,1)S(1)}, bf16[384,1,768]{2,1,0:T(2,128)(2,1)}, u32[]{:S(2)}) copy-start(bf16[384,1,768]{2,1,0:T(2,128)(2,1)} %get-tuple-element.29) | copy-start | bytes 1769476
  78.5 7.9 %collective-permute-start.1 = (bf16[16,36,768]{2,0,1:T(8,128)(2,1)S(1)}, bf16[16,36,768]{2,0,1:T(8,128)(2,1)S(1)}, u32[]{:S(2)}, u32[]{:S(2)}) collective-permute-start(bf16[16,36,768]{2,0,1:T(8,128)(2,1)S(1)} %copy.72), channel_id=1, source_target_pairs={{0,1},{1,0},{2,3},{3,2},{4,5},{5,4},{6,7},{7,6},{8,9},{9,8},{10,11... | collective-permute-start | bytes 2654216 | tf_op jit(solution)/shard_map/ppermute | solution.py:112
  83.1 1.3 copy-start.8
  87.7 1.1 copy-start.17
  87.9 1.5 copy-start.9
  89.4 1.1 copy-start.16
  89.4 1.1 copy-start.26
  90.0 1.3 copy-start.20
  90.0 1.5 copy-start.23
  93.1 1.1 slice-start
  93.1 1.1 copy-start.30
  93.1 1.1 copy-start.32
  93.1 1.4 copy-start.36
  94.5 1.6 copy-start.19
  94.5 1.6 copy-start.25
  97.1 1.1 copy-start.7
  98.8 1.1 copy-start.5
  99.5 1.2 copy-start.22
  101.3 5.6 %copy-start.11 = (bf16[16,32,768]{2,1,0:T(8,128)(2,1)S(1)}, bf16[16,32,768]{2,1,0:T(8,128)(2,1)}, u32[]{:S(2)}) copy-start(bf16[16,32,768]{2,1,0:T(8,128)(2,1)} %copy-done.10) | copy-start | bytes 2359300
  101.3 5.6 %copy-start.15 = (bf16[1,16,48,384]{3,2,0,1:T(8,128)(2,1)S(1)}, bf16[1,16,48,384]{3,2,0,1:T(8,128)(2,1)}, u32[]{:S(2)}) copy-start(bf16[1,16,48,384]{3,2,0,1:T(8,128)(2,1)} %copy-done.14) | copy-start | bytes 1769476
  101.4 7.2 %collective-permute-start.3 = (f32[384,384]{1,0:T(8,128)S(1)}, f32[384,384]{1,0:T(8,128)S(1)}, u32[]{:S(2)}, u32[]{:S(2)}) collective-permute-start(f32[384,384]{1,0:T(8,128)S(1)} %slice_select_fusion), channel_id=1, source_target_pairs={{0,1},{1,0},{2,3},{3,2},{4,5},{5,4},{6,7},{7,6},{8,9},{9,8},{10,11... | collective-permute-start | bytes 1769480 | tf_op jit(solution)/shard_map/ppermute | solution.py:130
  104.7 4.1 %collective-permute-start.2 = (f32[384,384]{1,0:T(8,128)}, f32[384,384]{1,0:T(8,128)S(1)}, u32[]{:S(2)}, u32[]{:S(2)}) collective-permute-start(f32[384,384]{1,0:T(8,128)} %slice_select_fusion.1), channel_id=1, source_target_pairs={{0,1},{1,0},{2,3},{3,2},{4,5},{5,4},{6,7},{7,6},{8,9},{9,8},{10,11... | collective-permute-start | bytes 1769480 | tf_op jit(solution)/shard_map/ppermute | solution.py:130
  167.0 21.9 %all-to-all-start.4 = ((f32[32,1,1152]{2,1,0:T(1,128)}), f32[32,1,1152]{2,1,0:T(1,128)S(1)}, u32[]{:S(2)}, u32[]{:S(2)}) async-start(f32[32,1,1152]{2,1,0:T(1,128)} %broadcast_in_dim.2), calls=%async_computation.4 | async-start | bytes 294912 | tf_op jit(solution)/shard_map/all_to_all | solution.py:21

commit v10 on v9

--- a/solution.py
+++ b/solution.py
@@ -30,7 +30,7 @@
 
 def reduced_over_dp(value):
     dp_size = lax.axis_size("dp")
-    own_piece = summed_over(value.reshape(dp_size, -1), "dp")
+    own_piece = summed_over(value.reshape(dp_size, -1), "dp", jnp.bfloat16)
     return gathered(own_piece, "dp").reshape(value.shape)
 
 

time: 191 us -> 190 us (level)
    unnamed x74 -> x76, local copies, waits for them, and re-layouts: 5.53 us -> 5.81 us
where the time goes in v10:
time: 190 us; the launch traced here: 189 us
  blocking collectives  90.7 us (48%)
  local copies, waits for them, and re-layouts  35.1 us (18%)
  starting transfers between devices  18.8 us (10%)
  waiting for transfers between devices  15.5 us (8%)
  matrix products  14.3 us (8%)
  other arithmetic  11.8 us (6%)
  between operations  2.8 us (1%)
    all_to_all x2, blocking collectives, exchanged(): arrived = lax.all_to_all(joined, axis, 0, 0, tiled=True)  59.3 us
    all_to_all x1, blocking collectives, summed_over(): arrived = lax.all_to_all(pieces, axis, 0, 0, tiled=True)  31.4 us
    all_to_all x1, waiting for transfers between devices, gathered(): return lax.all_to_all(copies, axis, 0, 0, tiled=True)  15.5 us
    dot_general x8, matrix products, contract_last(): lax.dot_general(left, right, (((1,), (1,)), ((), ())), preferred_element_...  7.52 us
    unnamed x76, local copies, waits for them, and re-layouts  5.81 us
    all_to_all x1, starting transfers between devices, exchanged(): arrived = lax.all_to_all(joined, axis, 0, 0, tiled=True)  5.53 us
    ppermute x2, starting transfers between devices, whole_from_halves(): partner = lax.ppermute(own_halves, axis, [(i, i ^ 1) for i in range(peers)])  4.73 us
    ppermute x2, starting transfers between devices, chip_half(): partner = lax.ppermute(given, 'seq', [(i, i ^ 1) for i in range(peers)])  4.67 us
  transfers between devices with their start and end apart: 6, of which 1 were waited for; matrix products, arithmetic and copies ran while one was open for 18% of the time, Pallas kernels for 0%

profile of v10, /device:TPU:6, one launch (start us, length us, event | category | flops | bytes accessed | tf_op | source)
XLA Modules:
  0.0 189.0 jit_solution(1885822705911631083)
XLA Ops:
  0.6 1.0 fusion.101
  1.7 0.9 reshape.93
  3.4 36.4 %all_to_all.25 = bf16[16,92,768]{2,1,0:T(8,128)(2,1)S(1)} all-to-all(bf16[16,92,768]{2,1,0:T(8,128)(2,1)S(1)} %pad_maximum_fusion), channel_id=1, replica_groups=mesh['dp'=32,'seq'=16] {'seq'}, dimensions={0} | all-to-all | bytes 4521984 | tf_op jit(solution)/shard_map/all_to_all | solution.py:92
  39.9 2.0 %copy.69 = bf16[16,60,768]{2,0,1:T(8,128)(2,1)} copy(bf16[16,60,768]{2,1,0:T(8,128)(2,1)S(1)} %slice.187) | data formatting | bytes 2949120 | tf_op jit(solution)/shard_map/slice | solution.py:96
  41.9 2.4 %collective-permute-start = (bf16[16,60,768]{2,0,1:T(8,128)(2,1)}, bf16[16,60,768]{2,0,1:T(8,128)(2,1)}, u32[]{:S(2)}, u32[]{:S(2)}) collective-permute-start(bf16[16,60,768]{2,0,1:T(8,128)(2,1)} %copy.69), channel_id=1, source_target_pairs={{0,1},{1,0},{2,3},{3,2},{4,5},{5,4},{6,7},{7,6},{8,9},{9,8},{10,11... | collective-permute-start | bytes 4423688 | tf_op jit(solution)/shard_map/ppermute | solution.py:112
  44.3 0.6 fusion.102
  46.2 0.6 slice_reduce_fusion.4
  47.0 1.6 copy.72
  48.7 1.3 pad_maximum_fusion.2
  50.0 5.5 %all-to-all-start.1 = ((bf16[16,68,768]{2,1,0:T(8,128)(2,1)}), bf16[16,68,768]{2,1,0:T(8,128)(2,1)S(1)}, u32[]{:S(2)}, u32[]{:S(2)}) async-start(bf16[16,68,768]{2,1,0:T(8,128)(2,1)} %pad_maximum_fusion.2), calls=%async_computation.1 | async-start | bytes 3538944 | tf_op jit(solution)/shard_map/all_to_all | solution.py:92
  55.6 0.6 fusion.6
  56.2 1.2 fusion.98
  57.4 1.0 copy-done.2
  58.4 2.4 %broadcast_select_fusion.1 = (bf16[16,60,768]{2,1,0:T(8,128)(2,1)S(1)}, bf16[16,60,768]{2,1,0:T(8,128)(2,1)S(1)}) fusion(pred[]{:T(512)S(6)} %eq.11, bf16[16,60,768]{2,0,1:T(8,128)(2,1)} %collective-permute-done, bf16[16,92,768]{2,1,0:T(8,128)(2,1)S(1)} %copy-done.2), kind=kLoop, calls=%fused_computation.45 | loop fusion | flops 1474560 | bytes 5898241 | tf_op jit(solution)/shard_map/jit(_where)/select_n | solution.py:114
  60.8 1.4 pad_maximum_fusion.1
  62.2 1.4 slice.193
  63.6 3.6 %reshape.97 = bf16[384,2,768]{2,1,0:T(2,128)(2,1)} reshape(bf16[16,48,768]{2,1,0:T(8,128)(2,1)} %slice.193) | data formatting | bytes 2359296 | tf_op jit(solution)/shard_map/reshape | solution.py:180
  67.3 3.7 %reshape.95 = bf16[16,3,48,384]{3,2,1,0:T(8,128)(2,1)} reshape(bf16[16,72,768]{2,1,0:T(8,128)(2,1)} %pad_maximum_fusion.1) | data formatting | bytes 3538944 | tf_op jit(solution)/shard_map/reshape | solution.py:121
  71.0 1.7 fusion.94
  75.2 3.1 %fusion.96 = (bf16[384,1,768]{2,1,0:T(2,128)(2,1)}, bf16[384,1,768]{2,1,0:T(2,128)(2,1)}) fusion(bf16[384,2,768]{2,1,0:T(2,128)(2,1)S(1)} %copy-done.3), kind=kLoop, calls=%fused_computation.139 | loop fusion | bytes 2359296 | tf_op jit(solution)/shard_map/slice | solution.py:210
  78.6 2.4 %collective-permute-start.1 = (bf16[16,36,768]{2,0,1:T(8,128)(2,1)S(1)}, bf16[16,36,768]{2,0,1:T(8,128)(2,1)S(1)}, u32[]{:S(2)}, u32[]{:S(2)}) collective-permute-start(bf16[16,36,768]{2,0,1:T(8,128)(2,1)S(1)} %copy.73), channel_id=1, source_target_pairs={{0,1},{1,0},{2,3},{3,2},{4,5},{5,4},{6,7},{7,6},{8,9},{9,8},{10,11... | collective-permute-start | bytes 2654216 | tf_op jit(solution)/shard_map/ppermute | solution.py:112
  81.0 2.1 %multiply_convert_fusion = (bf16[512,768]{1,0:T(8,128)(2,1)S(1)}, bf16[512,768]{1,0:T(8,128)(2,1)}) fusion(f32[768]{0:T(1024)S(1)} %get-tuple-element.10, f32[768]{0:T(1024)S(1)} %get-tuple-element.45, bf16[384,1,768]{2,1,0:T(2,128)(2,1)S(1)} %copy-done.18, f32[512,384]{1,0:T(8,128)S(1)} %fusion.32, f32[]{:T(128)} %bitcast.10, bf16[512,768]{1,0:T(8,128)(2,1)S(1)} %bitcast.79), kind=kOutput, calls=%fused_computation.41 | convolution fusion | flops 310050816 | bytes 3741700 | tf_op jit(solution)/shard_map/dot_general | solution.py:61
  83.1 1.2 fusion.97
  84.4 1.0 fusion.25
  85.4 1.0 fusion.26
  87.1 0.6 reshape.98
  88.0 0.9 copy-done.17
  91.5 0.9 fusion.48
  92.5 0.6 fusion.103
  93.2 0.6 fusion.73
  94.5 1.6 fusion.24
  96.2 1.0 fusion.40
  97.2 1.0 copy-done.7
  98.2 0.6 fusion.104
  98.8 0.7 fusion.57
  99.9 0.6 fusion.70
  101.4 2.4 %collective-permute-start.3 = (f32[384,384]{1,0:T(8,128)S(1)}, f32[384,384]{1,0:T(8,128)S(1)}, u32[]{:S(2)}, u32[]{:S(2)}) collective-permute-start(f32[384,384]{1,0:T(8,128)S(1)} %slice_select_fusion), channel_id=1, source_target_pairs={{0,1},{1,0},{2,3},{3,2},{4,5},{5,4},{6,7},{7,6},{8,9},{9,8},{10,11... | collective-permute-start | bytes 1769480 | tf_op jit(solution)/shard_map/ppermute | solution.py:130
  103.8 0.9 slice_select_fusion.1
  104.7 2.3 %collective-permute-start.2 = (f32[384,384]{1,0:T(8,128)}, f32[384,384]{1,0:T(8,128)S(1)}, u32[]{:S(2)}, u32[]{:S(2)}) collective-permute-start(f32[384,384]{1,0:T(8,128)} %slice_select_fusion.1), channel_id=1, source_target_pairs={{0,1},{1,0},{2,3},{3,2},{4,5},{5,4},{6,7},{7,6},{8,9},{9,8},{10,11... | collective-permute-start | bytes 1769480 | tf_op jit(solution)/shard_map/ppermute | solution.py:130
  107.0 1.6 fusion.11
  109.2 23.0 %all_to_all.26 = bf16[16,56,768]{2,1,0:T(8,128)(2,1)S(1)} all-to-all(bf16[16,56,768]{2,1,0:T(8,128)(2,1)S(1)} %pad_maximum_fusion.4), channel_id=1, replica_groups=mesh['dp'=32,'seq'=16] {'seq'}, dimensions={0} | all-to-all | bytes 2752512 | tf_op jit(solution)/shard_map/all_to_all | solution.py:92
  133.5 1.1 reduce.21
  134.7 31.4 %all_to_all.27 = bf16[32,2,576]{2,1,0:T(2,128)(2,1)S(1)} all-to-all(bf16[32,2,576]{2,1,0:T(2,128)(2,1)S(1)} %reshape.113), channel_id=1, replica_groups=mesh['dp'=32,'seq'=16] {'dp'}, dimensions={0} | all-to-all | bytes 147456 | tf_op jit(solution)/shard_map/all_to_all | solution.py:27
  166.3 0.7 broadcast_in_dim.2
  167.1 3.9 %all-to-all-start.4 = ((f32[32,1,1152]{2,1,0:T(1,128)}), f32[32,1,1152]{2,1,0:T(1,128)S(1)}, u32[]{:S(2)}, u32[]{:S(2)}) async-start(f32[32,1,1152]{2,1,0:T(1,128)} %broadcast_in_dim.2), calls=%async_computation.4 | async-start | bytes 294912 | tf_op jit(solution)/shard_map/all_to_all | solution.py:21
  171.0 1.3 copy.80
  172.3 15.5 %all-to-all-done.4 = f32[32,1,1152]{2,1,0:T(1,128)S(1)} async-done(((f32[32,1,1152]{2,1,0:T(1,128)}), f32[32,1,1152]{2,1,0:T(1,128)S(1)}, u32[]{:S(2)}, u32[]{:S(2)}) %all-to-all-start.4) | async-done | bytes 147488 | tf_op jit(solution)/shard_map/all_to_all | solution.py:21
  188.3 0.8 mul.345
  (128 shorter events, 12.2 us)
Async XLA Ops:
  0.6 2.1 %copy-start.21 = (bf16[1,512,768]{2,1,0:T(8,128)(2,1)S(1)}, bf16[1,512,768]{2,1,0:T(8,128)(2,1)}, u32[]{:S(2)}) copy-start(bf16[1,512,768]{2,1,0:T(8,128)(2,1)} %param.9) | copy-start | bytes 2359300
  39.7 7.1 %copy-start.1 = (bf16[16,92,768]{2,1,0:T(8,128)(2,1)}, bf16[16,92,768]{2,1,0:T(8,128)(2,1)S(1)}, u32[]{:S(2)}) copy-start(bf16[16,92,768]{2,1,0:T(8,128)(2,1)S(1)} %all_to_all.25) | copy-start | bytes 6782980
  39.8 4.4 %copy-start.35 = (s32[1,2]{1,0:T(1,128)S(1)}, s32[1,2]{1,0:T(1,128)}, u32[]{:S(2)}) copy-start(s32[1,2]{1,0:T(1,128)} %param.11) | copy-start | bytes 28
  39.9 6.3 %copy-start.33 = (f32[2,384]{1,0:T(2,128)S(1)}, f32[2,384]{1,0:T(2,128)}, u32[]{:S(2)}) copy-start(f32[2,384]{1,0:T(2,128)} %param.15) | copy-start | bytes 9220
  39.9 6.9 %copy-start.34 = (f32[2,384]{1,0:T(2,128)S(1)}, f32[2,384]{1,0:T(2,128)}, u32[]{:S(2)}) copy-start(f32[2,384]{1,0:T(2,128)} %param.14) | copy-start | bytes 9220
  39.9 6.9 %copy-start.27 = (f32[2,768]{1,0:T(2,128)S(1)}, f32[2,768]{1,0:T(2,128)}, u32[]{:S(2)}) copy-start(f32[2,768]{1,0:T(2,128)} %param.13) | copy-start | bytes 18436
  39.9 6.9 %copy-start.28 = (f32[2,768]{1,0:T(2,128)S(1)}, f32[2,768]{1,0:T(2,128)}, u32[]{:S(2)}) copy-start(f32[2,768]{1,0:T(2,128)} %param.12) | copy-start | bytes 18436
  41.9 15.5 %collective-permute-start = (bf16[16,60,768]{2,0,1:T(8,128)(2,1)}, bf16[16,60,768]{2,0,1:T(8,128)(2,1)}, u32[]{:S(2)}, u32[]{:S(2)}) collective-permute-start(bf16[16,60,768]{2,0,1:T(8,128)(2,1)} %copy.69), channel_id=1, source_target_pairs={{0,1},{1,0},{2,3},{3,2},{4,5},{5,4},{6,7},{7,6},{8,9},{9,8},{10,11... | collective-permute-start | bytes 4423688 | tf_op jit(solution)/shard_map/ppermute | solution.py:112
  46.9 34.1 %copy-start.29 = (f32[768]{0:T(1024)}, f32[768]{0:T(1024)S(1)}, u32[]{:S(2)}) copy-start(f32[768]{0:T(1024)S(1)} %get-tuple-element.10) | copy-start | bytes 9220
  46.9 34.1 %copy-start.31 = (f32[768]{0:T(1024)}, f32[768]{0:T(1024)S(1)}, u32[]{:S(2)}) copy-start(f32[768]{0:T(1024)S(1)} %get-tuple-element.45) | copy-start | bytes 9220
  47.0 34.0 %copy-start.10 = (bf16[16,32,768]{2,1,0:T(8,128)(2,1)}, bf16[16,32,768]{2,1,0:T(8,128)(2,1)S(1)}, u32[]{:S(2)}) copy-start(bf16[16,32,768]{2,1,0:T(8,128)(2,1)S(1)} %slice.185) | copy-start | bytes 2359300
  50.0 28.3 %all-to-all-start.1 = ((bf16[16,68,768]{2,1,0:T(8,128)(2,1)}), bf16[16,68,768]{2,1,0:T(8,128)(2,1)S(1)}, u32[]{:S(2)}, u32[]{:S(2)}) async-start(bf16[16,68,768]{2,1,0:T(8,128)(2,1)} %pad_maximum_fusion.2), calls=%async_computation.1 | async-start | bytes 3538944 | tf_op jit(solution)/shard_map/all_to_all | solution.py:92
  56.2 2.2 %copy-start.2 = (bf16[16,92,768]{2,1,0:T(8,128)(2,1)S(1)}, bf16[16,92,768]{2,1,0:T(8,128)(2,1)}, u32[]{:S(2)}) copy-start(bf16[16,92,768]{2,1,0:T(8,128)(2,1)} %copy-done.1) | copy-start | bytes 6782980
  71.0 1.7 copy-start.13
  72.7 1.2 copy-start.4
  72.7 1.2 copy-start.6
  72.7 1.2 copy-start.14
  73.3 1.1 copy-start.12
  73.9 1.3 copy-start.3
  75.2 5.8 %copy-start.24 = (f32[512,384]{1,0:T(8,128)}, f32[512,384]{1,0:T(8,128)S(1)}, u32[]{:S(2)}) copy-start(f32[512,384]{1,0:T(8,128)S(1)} %fusion.32) | copy-start | bytes 2359300
  78.3 8.1 %copy-start = (bf16[16,68,768]{2,1,0:T(8,128)(2,1)}, bf16[16,68,768]{2,1,0:T(8,128)(2,1)S(1)}, u32[]{:S(2)}) copy-start(bf16[16,68,768]{2,1,0:T(8,128)(2,1)S(1)} %all-to-all-done.1) | copy-start | bytes 5013508
  78.3 2.7 %copy-start.18 = (bf16[384,1,768]{2,1,0:T(2,128)(2,1)S(1)}, bf16[384,1,768]{2,1,0:T(2,128)(2,1)}, u32[]{:S(2)}) copy-start(bf16[384,1,768]{2,1,0:T(2,128)(2,1)} %get-tuple-element.29) | copy-start | bytes 1769476
  78.6 7.9 %collective-permute-start.1 = (bf16[16,36,768]{2,0,1:T(8,128)(2,1)S(1)}, bf16[16,36,768]{2,0,1:T(8,128)(2,1)S(1)}, u32[]{:S(2)}, u32[]{:S(2)}) collective-permute-start(bf16[16,36,768]{2,0,1:T(8,128)(2,1)S(1)} %copy.73), channel_id=1, source_target_pairs={{0,1},{1,0},{2,3},{3,2},{4,5},{5,4},{6,7},{7,6},{8,9},{9,8},{10,11... | collective-permute-start | bytes 2654216 | tf_op jit(solution)/shard_map/ppermute | solution.py:112
  83.1 1.3 copy-start.8
  87.7 1.1 copy-start.17
  87.9 1.5 copy-start.9
  89.4 1.1 copy-start.16
  89.4 1.1 copy-start.26
  90.0 1.3 copy-start.20
  90.0 1.5 copy-start.23
  93.1 1.1 slice-start
  93.2 1.1 copy-start.30
  93.2 1.1 copy-start.32
  93.2 1.4 copy-start.36
  94.5 1.6 copy-start.19
  94.5 1.6 copy-start.25
  97.2 1.1 copy-start.7
  98.8 1.1 copy-start.5
  99.5 1.2 copy-start.22
  101.3 5.6 %copy-start.11 = (bf16[16,32,768]{2,1,0:T(8,128)(2,1)S(1)}, bf16[16,32,768]{2,1,0:T(8,128)(2,1)}, u32[]{:S(2)}) copy-start(bf16[16,32,768]{2,1,0:T(8,128)(2,1)} %copy-done.10) | copy-start | bytes 2359300
  101.3 5.6 %copy-start.15 = (bf16[1,16,48,384]{3,2,0,1:T(8,128)(2,1)S(1)}, bf16[1,16,48,384]{3,2,0,1:T(8,128)(2,1)}, u32[]{:S(2)}) copy-start(bf16[1,16,48,384]{3,2,0,1:T(8,128)(2,1)} %copy-done.14) | copy-start | bytes 1769476
  101.4 7.2 %collective-permute-start.3 = (f32[384,384]{1,0:T(8,128)S(1)}, f32[384,384]{1,0:T(8,128)S(1)}, u32[]{:S(2)}, u32[]{:S(2)}) collective-permute-start(f32[384,384]{1,0:T(8,128)S(1)} %slice_select_fusion), channel_id=1, source_target_pairs={{0,1},{1,0},{2,3},{3,2},{4,5},{5,4},{6,7},{7,6},{8,9},{9,8},{10,11... | collective-permute-start | bytes 1769480 | tf_op jit(solution)/shard_map/ppermute | solution.py:130
  104.7 4.1 %collective-permute-start.2 = (f32[384,384]{1,0:T(8,128)}, f32[384,384]{1,0:T(8,128)S(1)}, u32[]{:S(2)}, u32[]{:S(2)}) collective-permute-start(f32[384,384]{1,0:T(8,128)} %slice_select_fusion.1), channel_id=1, source_target_pairs={{0,1},{1,0},{2,3},{3,2},{4,5},{5,4},{6,7},{7,6},{8,9},{9,8},{10,11... | collective-permute-start | bytes 1769480 | tf_op jit(solution)/shard_map/ppermute | solution.py:130
  167.1 20.8 %all-to-all-start.4 = ((f32[32,1,1152]{2,1,0:T(1,128)}), f32[32,1,1152]{2,1,0:T(1,128)S(1)}, u32[]{:S(2)}, u32[]{:S(2)}) async-start(f32[32,1,1152]{2,1,0:T(1,128)} %broadcast_in_dim.2), calls=%async_computation.4 | async-start | bytes 294912 | tf_op jit(solution)/shard_map/all_to_all | solution.py:21

commit v11 on v10

--- a/solution.py
+++ b/solution.py
@@ -160,25 +160,29 @@
     channels = sequence_in.shape[2]
     block_shape = conv_weight.shape[1:]
     conv_rows = conv_weight[0].size // channels
-    first_weights = jnp.concatenate(
-        [conv_weight[0].reshape(-1, channels), point_weight.reshape(-1, channels)]
-    )
-    state_pieces, first_halves = exchanged(
+    point_rows = point_weight.size // channels
+    all_weights = jnp.concatenate(
+        [
+            conv_weight[0].reshape(-1, channels),
+            point_weight.reshape(-1, channels),
+            conv_weight[1].reshape(-1, channels),
+        ]
+    )
+    state_pieces, grad_pieces, weight_halves = exchanged(
         [
             strided_pieces(sequence_in[0], peers),
-            half_for_each(first_weights, peers, channels),
+            strided_pieces(output_grad[0], peers),
+            half_for_each(all_weights, peers, channels),
         ],
         "seq",
     )
     state = state_pieces.reshape(-1, channels)
-    grad_in, second_in, state = lax.optimization_barrier((output_grad[0], conv_weight[1], state))
-    grad_pieces, second_halves = exchanged(
-        [strided_pieces(grad_in, peers), half_for_each(second_in, peers, channels)], "seq"
-    )
-    first_whole = whole_from_halves(first_halves, "seq")
-    first_pieces = first_whole[:, :conv_rows]
-    point_full = first_whole[:, conv_rows:].reshape(-1, *point_weight.shape[1:])
-    second_pieces = whole_from_halves(second_halves, "seq")
+    weight_whole = whole_from_halves(weight_halves, "seq")
+    first_pieces = weight_whole[:, :conv_rows]
+    point_full = weight_whole[:, conv_rows : conv_rows + point_rows].reshape(
+        -1, *point_weight.shape[1:]
+    )
+    second_pieces = weight_whole[:, conv_rows + point_rows :]
     conv_full = [
         conv_from_pieces(first_pieces, block_shape),
         conv_from_pieces(second_pieces, block_shape),

time: 190 us -> 192 us (1.011)
  blocking collectives: 90.7 us -> 107 us
  starting transfers between devices: 18.8 us -> 10.7 us
  local copies, waits for them, and re-layouts: 35.1 us -> 29.9 us
    all_to_all x2, blocking collectives: 59.3 us -> 75.2 us  [exchanged(): arrived = lax.all_to_all(joined, axis, 0, 0, tiled=True)]
    all_to_all x1 -> x0, starting transfers between devices: 5.53 us -> none  [exchanged(): arrived = lax.all_to_all(joined, axis, 0, 0, tiled=True)]
    tanh x0 -> x1, other arithmetic: none -> 3.72 us  [gelu_tanh(): return jax.nn.gelu(values, approximate=True)]
    ppermute x2 -> x1, starting transfers between devices: 4.73 us -> 2.36 us  [whole_from_halves(): partner = lax.ppermute(own_halves, axis, [(i, i ^ 1) for i in range(peers)])]
    unnamed x76 -> x42, local copies, waits for them, and re-layouts: 5.81 us -> 4.65 us
  transfers between devices with their start and end apart: 6 -> 4, of which waited for: 1 -> 1; matrix products, arithmetic and copies ran while one was open for 18% -> 8% of each run, Pallas kernels for 0% -> 0%
where the time goes in v11:
time: 192 us; the launch traced here: 191 us
  blocking collectives  107 us (56%)
  local copies, waits for them, and re-layouts  29.9 us (16%)
  waiting for transfers between devices  15.5 us (8%)
  matrix products  13.3 us (7%)
  other arithmetic  12.3 us (6%)
  starting transfers between devices  10.7 us (6%)
  between operations  2.55 us (1%)
    all_to_all x2, blocking collectives, exchanged(): arrived = lax.all_to_all(joined, axis, 0, 0, tiled=True)  75.2 us
    all_to_all x1, blocking collectives, summed_over(): arrived = lax.all_to_all(pieces, axis, 0, 0, tiled=True)  31.4 us
    all_to_all x1, waiting for transfers between devices, gathered(): return lax.all_to_all(copies, axis, 0, 0, tiled=True)  15.5 us
    dot_general x8, matrix products, contract_last(): lax.dot_general(left, right, (((1,), (1,)), ((), ())), preferred_element_...  7.3 us
    unnamed x42, local copies, waits for them, and re-layouts  4.65 us
    reshape x2, local copies, waits for them, and re-layouts, conv_from_pieces(): parts = pieces.reshape(-1, taps, rows, hidden)  4.64 us
    ppermute x2, starting transfers between devices, chip_half(): partner = lax.ppermute(given, 'seq', [(i, i ^ 1) for i in range(peers)])  4.45 us
    all_to_all x1, starting transfers between devices, gathered(): return lax.all_to_all(copies, axis, 0, 0, tiled=True)  3.86 us
  transfers between devices with their start and end apart: 4, of which 1 were waited for; matrix products, arithmetic and copies ran while one was open for 8% of the time, Pallas kernels for 0%

profile of v11, /device:TPU:6, one launch (start us, length us, event | category | flops | bytes accessed | tf_op | source)
XLA Modules:
  0.0 190.8 jit_solution(9763497342367529776)
XLA Ops:
  0.6 1.0 reshape.97
  1.6 1.0 fusion.111
  2.7 1.6 copy_bitcast_fusion
  4.9 53.2 %all_to_all.20 = bf16[16,160,768]{2,1,0:T(8,128)(2,1)S(1)} all-to-all(bf16[16,160,768]{2,1,0:T(8,128)(2,1)S(1)} %pad_maximum_fusion), channel_id=1, replica_groups=mesh['dp'=32,'seq'=16] {'seq'}, dimensions={0} | all-to-all | bytes 7864320 | tf_op jit(solution)/shard_map/all_to_all | solution.py:92
  58.3 1.7 copy-done
  60.0 2.4 %collective-permute-start = (bf16[16,96,768]{2,1,0:T(8,128)(2,1)S(1)}, bf16[16,96,768]{2,1,0:T(8,128)(2,1)}, u32[]{:S(2)}, u32[]{:S(2)}) collective-permute-start(bf16[16,96,768]{2,1,0:T(8,128)(2,1)S(1)} %slice.187), channel_id=1, source_target_pairs={{0,1},{1,0},{2,3},{3,2},{4,5},{5,4},{6,7},{7,6},{8,9},{9,8},{10,11... | collective-permute-start | bytes 7077896 | tf_op jit(solution)/shard_map/ppermute | solution.py:112
  62.4 0.6 fusion.112
  64.3 0.6 slice_reduce_fusion.4
  65.0 0.6 slice_reduce_fusion
  65.6 3.7 %fusion.5 = (f32[512,768]{1,0:T(8,128)}, bf16[512,768]{1,0:T(8,128)(2,1)S(1)}, bf16[512,768]{1,0:T(8,128)(2,1)}) fusion(f32[768]{0:T(1024)S(1)} %get-tuple-element.5, f32[768]{0:T(1024)S(1)} %get-tuple-element.45, bf16[16,160,768]{2,1,0:T(8,128)(2,1)} %copy-done, f32[]{:T(128)} %bitcast.14), kind=kLoop, calls=%fused_computation.15 | loop fusion | flops 5898240 | bytes 4724740 | tf_op jit(solution)/shard_map/tanh | solution.py:38
  69.3 1.2 fusion.108
  70.5 1.3 fusion.102
  71.7 2.0 %fusion.26 = (bf16[16,32,768]{2,1,0:T(8,128)(2,1)}, bf16[16,32,768]{2,1,0:T(8,128)(2,1)}) fusion(f32[]{:T(128)} %bitcast.14, bf16[16,160,768]{2,1,0:T(8,128)(2,1)S(1)} %copy-done.1, f32[768]{0:T(1024)S(1)} %get-tuple-element.5, f32[768]{0:T(1024)S(1)} %get-tuple-element.45), kind=kLoop, calls=%fused_computation.38 | loop fusion | flops 5898240 | bytes 3151876 | tf_op jit(solution)/shard_map/convert_element_type | solution.py:67
  73.7 2.0 %broadcast_select_fusion.1 = (bf16[16,96,768]{2,1,0:T(8,128)(2,1)S(1)}, bf16[16,96,768]{2,1,0:T(8,128)(2,1)S(1)}) fusion(bf16[16,96,768]{2,1,0:T(8,128)(2,1)} %collective-permute-done, pred[]{:T(512)S(6)} %eq.9, bf16[16,160,768]{2,1,0:T(8,128)(2,1)S(1)} %copy-done.1), kind=kLoop, calls=%fused_computation.3 | loop fusion | flops 2359296 | bytes 9437185 | tf_op jit(solution)/shard_map/jit(_where)/select_n | solution.py:114
  75.8 1.1 pad_maximum_fusion.2
  76.9 1.4 slice.197
  78.3 2.6 %reshape.100 = bf16[16,3,48,384]{3,2,1,0:T(8,128)(2,1)S(1)} reshape(bf16[16,72,768]{2,1,0:T(8,128)(2,1)} %slice.197) | data formatting | bytes 3538944 | tf_op jit(solution)/shard_map/reshape | solution.py:121
  80.8 2.1 %reshape.98 = bf16[16,3,48,384]{3,2,1,0:T(8,128)(2,1)} reshape(bf16[16,72,768]{2,1,0:T(8,128)(2,1)S(1)} %slice.188) | data formatting | bytes 3538944 | tf_op jit(solution)/shard_map/reshape | solution.py:121
  82.9 3.0 %reshape.99 = bf16[384,2,768]{2,1,0:T(2,128)(2,1)S(1)} reshape(bf16[16,48,768]{2,1,0:T(8,128)(2,1)} %pad_maximum_fusion.2) | data formatting | bytes 2359296 | tf_op jit(solution)/shard_map/reshape | solution.py:182
  86.0 1.6 fusion.104
  87.8 1.6 fusion.106
  89.4 0.6 fusion.62
  90.6 0.6 convolution_add_fusion.3
  91.2 0.6 fusion.41
  92.3 1.2 multiply_convert_fusion
  94.2 0.6 convolution_add_fusion.1
  94.9 0.6 fusion.39
  95.9 0.9 fusion.57
  96.9 0.6 fusion.113
  97.5 0.6 fusion.82
  98.7 1.6 fusion.17
  100.3 1.0 fusion.49
  101.3 0.7 fusion.66
  102.1 0.6 fusion.114
  103.2 0.6 fusion.77
  104.1 2.0 %collective-permute-start.2 = (f32[384,384]{1,0:T(8,128)S(1)}, f32[384,384]{1,0:T(8,128)S(1)}, u32[]{:S(2)}, u32[]{:S(2)}) collective-permute-start(f32[384,384]{1,0:T(8,128)S(1)} %slice_select_fusion), channel_id=1, source_target_pairs={{0,1},{1,0},{2,3},{3,2},{4,5},{5,4},{6,7},{7,6},{8,9},{9,8},{10,11... | collective-permute-start | bytes 1769480 | tf_op jit(solution)/shard_map/ppermute | solution.py:130
  106.0 0.9 slice_select_fusion.1
  106.9 2.5 %collective-permute-start.1 = (f32[384,384]{1,0:T(8,128)}, f32[384,384]{1,0:T(8,128)S(1)}, u32[]{:S(2)}, u32[]{:S(2)}) collective-permute-start(f32[384,384]{1,0:T(8,128)} %slice_select_fusion.1), channel_id=1, source_target_pairs={{0,1},{1,0},{2,3},{3,2},{4,5},{5,4},{6,7},{7,6},{8,9},{9,8},{10,11... | collective-permute-start | bytes 1769480 | tf_op jit(solution)/shard_map/ppermute | solution.py:130
  109.4 0.6 fusion.79
  110.0 1.4 fusion.1
  112.1 21.9 %all_to_all.21 = bf16[16,56,768]{2,1,0:T(8,128)(2,1)S(1)} all-to-all(bf16[16,56,768]{2,1,0:T(8,128)(2,1)S(1)} %pad_maximum_fusion.1), channel_id=1, replica_groups=mesh['dp'=32,'seq'=16] {'seq'}, dimensions={0} | all-to-all | bytes 2752512 | tf_op jit(solution)/shard_map/all_to_all | solution.py:92
  135.3 1.1 reduce.21
  136.5 31.4 %all_to_all.22 = bf16[32,2,576]{2,1,0:T(2,128)(2,1)S(1)} all-to-all(bf16[32,2,576]{2,1,0:T(2,128)(2,1)S(1)} %reshape.116), channel_id=1, replica_groups=mesh['dp'=32,'seq'=16] {'dp'}, dimensions={0} | all-to-all | bytes 147456 | tf_op jit(solution)/shard_map/all_to_all | solution.py:27
  168.1 0.7 broadcast_in_dim.2
  168.9 3.9 %all-to-all-start.3 = ((f32[32,1,1152]{2,1,0:T(1,128)}), f32[32,1,1152]{2,1,0:T(1,128)S(1)}, u32[]{:S(2)}, u32[]{:S(2)}) async-start(f32[32,1,1152]{2,1,0:T(1,128)} %broadcast_in_dim.2), calls=%async_computation.3 | async-start | bytes 294912 | tf_op jit(solution)/shard_map/all_to_all | solution.py:21
  172.8 1.3 copy.27
  174.1 15.5 %all-to-all-done.3 = f32[32,1,1152]{2,1,0:T(1,128)S(1)} async-done(((f32[32,1,1152]{2,1,0:T(1,128)}), f32[32,1,1152]{2,1,0:T(1,128)S(1)}, u32[]{:S(2)}, u32[]{:S(2)}) %all-to-all-start.3) | async-done | bytes 147488 | tf_op jit(solution)/shard_map/all_to_all | solution.py:21
  190.0 0.8 mul.368
  (79 shorter events, 7.6 us)
Async XLA Ops:
  0.6 2.1 %copy-start.7 = (bf16[1,512,768]{2,1,0:T(8,128)(2,1)S(1)}, bf16[1,512,768]{2,1,0:T(8,128)(2,1)}, u32[]{:S(2)}) copy-start(bf16[1,512,768]{2,1,0:T(8,128)(2,1)} %param.10) | copy-start | bytes 2359300
  58.1 1.9 copy-start
  58.1 4.2 %copy-start.19 = (s32[1,2]{1,0:T(1,128)S(1)}, s32[1,2]{1,0:T(1,128)}, u32[]{:S(2)}) copy-start(s32[1,2]{1,0:T(1,128)} %param.11) | copy-start | bytes 28
  58.1 6.1 %copy-start.17 = (f32[2,384]{1,0:T(2,128)S(1)}, f32[2,384]{1,0:T(2,128)}, u32[]{:S(2)}) copy-start(f32[2,384]{1,0:T(2,128)} %param.14) | copy-start | bytes 9220
  58.2 6.2 %copy-start.18 = (f32[2,384]{1,0:T(2,128)S(1)}, f32[2,384]{1,0:T(2,128)}, u32[]{:S(2)}) copy-start(f32[2,384]{1,0:T(2,128)} %param.15) | copy-start | bytes 9220
  58.2 6.8 %copy-start.13 = (f32[2,768]{1,0:T(2,128)S(1)}, f32[2,768]{1,0:T(2,128)}, u32[]{:S(2)}) copy-start(f32[2,768]{1,0:T(2,128)} %param.13) | copy-start | bytes 18436
  58.2 6.8 %copy-start.14 = (f32[2,768]{1,0:T(2,128)S(1)}, f32[2,768]{1,0:T(2,128)}, u32[]{:S(2)}) copy-start(f32[2,768]{1,0:T(2,128)} %param.12) | copy-start | bytes 18436
  60.0 13.7 %collective-permute-start = (bf16[16,96,768]{2,1,0:T(8,128)(2,1)S(1)}, bf16[16,96,768]{2,1,0:T(8,128)(2,1)}, u32[]{:S(2)}, u32[]{:S(2)}) collective-permute-start(bf16[16,96,768]{2,1,0:T(8,128)(2,1)S(1)} %slice.187), channel_id=1, source_target_pairs={{0,1},{1,0},{2,3},{3,2},{4,5},{5,4},{6,7},{7,6},{8,9},{9,8},{10,11... | collective-permute-start | bytes 7077896 | tf_op jit(solution)/shard_map/ppermute | solution.py:112
  65.6 4.9 %copy-start.1 = (bf16[16,160,768]{2,1,0:T(8,128)(2,1)S(1)}, bf16[16,160,768]{2,1,0:T(8,128)(2,1)}, u32[]{:S(2)}) copy-start(bf16[16,160,768]{2,1,0:T(8,128)(2,1)} %copy-done) | copy-start | bytes 11796484
  87.8 1.7 copy-start.4
  89.4 1.1 copy-start.2
  90.0 1.2 copy-start.3
  90.0 1.2 copy-start.12
  91.1 1.1 copy-start.8
  91.2 1.1 copy-start.15
  91.2 1.1 copy-start.16
  94.2 0.7 copy-start.11
  94.8 1.1 copy-start.10
  97.5 1.1 copy-start.9
  102.1 1.1 copy-start.6
  104.1 7.4 %collective-permute-start.2 = (f32[384,384]{1,0:T(8,128)S(1)}, f32[384,384]{1,0:T(8,128)S(1)}, u32[]{:S(2)}, u32[]{:S(2)}) collective-permute-start(f32[384,384]{1,0:T(8,128)S(1)} %slice_select_fusion), channel_id=1, source_target_pairs={{0,1},{1,0},{2,3},{3,2},{4,5},{5,4},{6,7},{7,6},{8,9},{9,8},{10,11... | collective-permute-start | bytes 1769480 | tf_op jit(solution)/shard_map/ppermute | solution.py:130
  106.9 3.1 %copy-start.5 = (f32[512,768]{1,0:T(8,128)S(1)}, f32[512,768]{1,0:T(8,128)}, u32[]{:S(2)}) copy-start(f32[512,768]{1,0:T(8,128)} %get-tuple-element.12) | copy-start | bytes 4718596
  106.9 4.7 %collective-permute-start.1 = (f32[384,384]{1,0:T(8,128)}, f32[384,384]{1,0:T(8,128)S(1)}, u32[]{:S(2)}, u32[]{:S(2)}) collective-permute-start(f32[384,384]{1,0:T(8,128)} %slice_select_fusion.1), channel_id=1, source_target_pairs={{0,1},{1,0},{2,3},{3,2},{4,5},{5,4},{6,7},{7,6},{8,9},{9,8},{10,11... | collective-permute-start | bytes 1769480 | tf_op jit(solution)/shard_map/ppermute | solution.py:130
  168.9 20.8 %all-to-all-start.3 = ((f32[32,1,1152]{2,1,0:T(1,128)}), f32[32,1,1152]{2,1,0:T(1,128)S(1)}, u32[]{:S(2)}, u32[]{:S(2)}) async-start(f32[32,1,1152]{2,1,0:T(1,128)} %broadcast_in_dim.2), calls=%async_computation.3 | async-start | bytes 294912 | tf_op jit(solution)/shard_map/all_to_all | solution.py:21

commit v12 on v10

--- a/solution.py
+++ b/solution.py
@@ -210,7 +210,7 @@
         projection = point_full[:, block_index, :]
         first_operands = (gradient, middle, projection, mid_gain[block_index], kept_flag)
         conv_grad, branch_grad = backward_first(*first_operands)
-        terms[block_index] = grad_rows(hidden_act, branch_grad)
+        terms[block_index] = chip_half(grad_rows(hidden_act, branch_grad), peers, channels)
         earlier, later = row_shifted(conv_grad, row_reach[block_index])
         second_operands = (
             gradient,
@@ -222,9 +222,10 @@
             in_gain[block_index],
         )
         gradient = backward_second(*second_operands)
-    term_pieces = [chip_half(term, peers, channels) for term in terms]
+        if block_index == 1:
+            terms[1], gradient = lax.optimization_barrier((terms[1], gradient))
     first_term, second_term, back_pieces = exchanged(
-        term_pieces + [gradient.reshape(peers, -1, channels)], "seq"
+        terms + [gradient.reshape(peers, -1, channels)], "seq"
     )
     own_terms = [chip_sum(piece, peers, channels) for piece in (first_term, second_term)]
     summed = reduced_over_dp(jnp.stack(own_terms, axis=1))

time: 190 us -> 190 us (level)
  transfers between devices with their start and end apart: 6 -> 6, of which waited for: 1 -> 1; matrix products, arithmetic and copies ran while one was open for 18% -> 19% of each run, Pallas kernels for 0% -> 0%
where the time goes in v12:
time: 190 us; the launch traced here: 189 us
  blocking collectives  90.7 us (48%)
  local copies, waits for them, and re-layouts  35.6 us (19%)
  starting transfers between devices  18.9 us (10%)
  waiting for transfers between devices  15.5 us (8%)
  matrix products  14.4 us (8%)
  other arithmetic  10.9 us (6%)
  between operations  2.85 us (2%)
    all_to_all x2, blocking collectives, exchanged(): arrived = lax.all_to_all(joined, axis, 0, 0, tiled=True)  59.3 us
    all_to_all x1, blocking collectives, summed_over(): arrived = lax.all_to_all(pieces, axis, 0, 0, tiled=True)  31.4 us
    all_to_all x1, waiting for transfers between devices, gathered(): return lax.all_to_all(copies, axis, 0, 0, tiled=True)  15.5 us
    dot_general x8, matrix products, contract_last(): lax.dot_general(left, right, (((1,), (1,)), ((), ())), preferred_element_...  7.54 us
    unnamed x76, local copies, waits for them, and re-layouts  6.81 us
    all_to_all x1, starting transfers between devices, exchanged(): arrived = lax.all_to_all(joined, axis, 0, 0, tiled=True)  5.53 us
    ppermute x2, starting transfers between devices, chip_half(): partner = lax.ppermute(given, 'seq', [(i, i ^ 1) for i in range(peers)])  4.79 us
    ppermute x2, starting transfers between devices, whole_from_halves(): partner = lax.ppermute(own_halves, axis, [(i, i ^ 1) for i in range(peers)])  4.73 us
  transfers between devices with their start and end apart: 6, of which 1 were waited for; matrix products, arithmetic and copies ran while one was open for 19% of the time, Pallas kernels for 0%

profile of v12, /device:TPU:6, one launch (start us, length us, event | category | flops | bytes accessed | tf_op | source)
XLA Modules:
  0.0 188.9 jit_solution(3716789594604319958)
XLA Ops:
  0.6 1.0 fusion.101
  1.7 0.9 reshape.93
  3.4 36.4 %all_to_all.25 = bf16[16,92,768]{2,1,0:T(8,128)(2,1)S(1)} all-to-all(bf16[16,92,768]{2,1,0:T(8,128)(2,1)S(1)} %pad_maximum_fusion), channel_id=1, replica_groups=mesh['dp'=32,'seq'=16] {'seq'}, dimensions={0} | all-to-all | bytes 4521984 | tf_op jit(solution)/shard_map/all_to_all | solution.py:92
  39.9 2.0 %copy.69 = bf16[16,60,768]{2,0,1:T(8,128)(2,1)} copy(bf16[16,60,768]{2,1,0:T(8,128)(2,1)S(1)} %slice.187) | data formatting | bytes 2949120 | tf_op jit(solution)/shard_map/slice | solution.py:96
  41.9 2.4 %collective-permute-start = (bf16[16,60,768]{2,0,1:T(8,128)(2,1)}, bf16[16,60,768]{2,0,1:T(8,128)(2,1)}, u32[]{:S(2)}, u32[]{:S(2)}) collective-permute-start(bf16[16,60,768]{2,0,1:T(8,128)(2,1)} %copy.69), channel_id=1, source_target_pairs={{0,1},{1,0},{2,3},{3,2},{4,5},{5,4},{6,7},{7,6},{8,9},{9,8},{10,11... | collective-permute-start | bytes 4423688 | tf_op jit(solution)/shard_map/ppermute | solution.py:112
  44.3 0.6 fusion.102
  46.2 0.6 slice_reduce_fusion.4
  47.0 1.6 copy.72
  48.7 1.3 pad_maximum_fusion.2
  50.0 5.5 %all-to-all-start.1 = ((bf16[16,68,768]{2,1,0:T(8,128)(2,1)}), bf16[16,68,768]{2,1,0:T(8,128)(2,1)S(1)}, u32[]{:S(2)}, u32[]{:S(2)}) async-start(bf16[16,68,768]{2,1,0:T(8,128)(2,1)} %pad_maximum_fusion.2), calls=%async_computation.1 | async-start | bytes 3538944 | tf_op jit(solution)/shard_map/all_to_all | solution.py:92
  55.6 0.6 fusion.6
  56.2 1.2 fusion.98
  57.4 1.0 copy-done.2
  58.4 2.4 %broadcast_select_fusion.1 = (bf16[16,60,768]{2,1,0:T(8,128)(2,1)S(1)}, bf16[16,60,768]{2,1,0:T(8,128)(2,1)S(1)}) fusion(pred[]{:T(512)S(6)} %eq.11, bf16[16,60,768]{2,0,1:T(8,128)(2,1)} %collective-permute-done, bf16[16,92,768]{2,1,0:T(8,128)(2,1)S(1)} %copy-done.2), kind=kLoop, calls=%fused_computation.45 | loop fusion | flops 1474560 | bytes 5898241 | tf_op jit(solution)/shard_map/jit(_where)/select_n | solution.py:114
  60.8 1.4 pad_maximum_fusion.1
  62.2 1.4 slice.192
  63.6 3.6 %reshape.96 = bf16[384,2,768]{2,1,0:T(2,128)(2,1)} reshape(bf16[16,48,768]{2,1,0:T(8,128)(2,1)} %slice.192) | data formatting | bytes 2359296 | tf_op jit(solution)/shard_map/reshape | solution.py:180
  67.3 3.7 %reshape.95 = bf16[16,3,48,384]{3,2,1,0:T(8,128)(2,1)} reshape(bf16[16,72,768]{2,1,0:T(8,128)(2,1)} %pad_maximum_fusion.1) | data formatting | bytes 3538944 | tf_op jit(solution)/shard_map/reshape | solution.py:121
  71.0 1.7 fusion.94
  75.2 3.1 %fusion.96 = (bf16[384,1,768]{2,1,0:T(2,128)(2,1)}, bf16[384,1,768]{2,1,0:T(2,128)(2,1)}) fusion(bf16[384,2,768]{2,1,0:T(2,128)(2,1)S(1)} %copy-done.3), kind=kLoop, calls=%fused_computation.139 | loop fusion | bytes 2359296 | tf_op jit(solution)/shard_map/slice | solution.py:210
  78.6 2.4 %collective-permute-start.1 = (bf16[16,36,768]{2,0,1:T(8,128)(2,1)S(1)}, bf16[16,36,768]{2,0,1:T(8,128)(2,1)S(1)}, u32[]{:S(2)}, u32[]{:S(2)}) collective-permute-start(bf16[16,36,768]{2,0,1:T(8,128)(2,1)S(1)} %copy.73), channel_id=1, source_target_pairs={{0,1},{1,0},{2,3},{3,2},{4,5},{5,4},{6,7},{7,6},{8,9},{9,8},{10,11... | collective-permute-start | bytes 2654216 | tf_op jit(solution)/shard_map/ppermute | solution.py:112
  81.0 2.1 %multiply_convert_fusion = (bf16[512,768]{1,0:T(8,128)(2,1)S(1)}, bf16[512,768]{1,0:T(8,128)(2,1)}) fusion(f32[768]{0:T(1024)S(1)} %get-tuple-element.14, f32[768]{0:T(1024)S(1)} %get-tuple-element.49, bf16[384,1,768]{2,1,0:T(2,128)(2,1)S(1)} %copy-done.18, f32[512,384]{1,0:T(8,128)S(1)} %fusion.32, f32[]{:T(128)} %bitcast.10, bf16[512,768]{1,0:T(8,128)(2,1)S(1)} %bitcast.79), kind=kOutput, calls=%fused_computation.41 | convolution fusion | flops 310050816 | bytes 3741700 | tf_op jit(solution)/shard_map/dot_general | solution.py:61
  83.1 1.2 fusion.97
  84.4 1.0 fusion.26
  85.4 1.0 fusion.25
  87.2 0.6 reshape.98
  88.0 0.9 copy-done.17
  91.6 0.9 fusion.48
  92.6 0.6 fusion.103
  94.4 2.4 %collective-permute-start.2 = (f32[384,384]{1,0:T(8,128)S(1)}, f32[384,384]{1,0:T(8,128)S(1)}, u32[]{:S(2)}, u32[]{:S(2)}) collective-permute-start(f32[384,384]{1,0:T(8,128)S(1)} %slice_select_fusion.1), channel_id=1, source_target_pairs={{0,1},{1,0},{2,3},{3,2},{4,5},{5,4},{6,7},{7,6},{8,9},{9,8},{10,11... | collective-permute-start | bytes 1769480 | tf_op jit(solution)/shard_map/ppermute | solution.py:130
  96.8 0.6 fusion.73
  97.5 1.6 fusion.24
  99.3 1.0 copy-done.19
  100.6 0.9 fusion.40
  101.6 1.0 copy-done.7
  102.6 0.6 fusion.104
  103.2 0.7 fusion.57
  104.0 2.4 %collective-permute-start.3 = (f32[384,384]{1,0:T(8,128)S(1)}, f32[384,384]{1,0:T(8,128)S(1)}, u32[]{:S(2)}, u32[]{:S(2)}) collective-permute-start(f32[384,384]{1,0:T(8,128)S(1)} %slice_select_fusion), channel_id=1, source_target_pairs={{0,1},{1,0},{2,3},{3,2},{4,5},{5,4},{6,7},{7,6},{8,9},{9,8},{10,11... | collective-permute-start | bytes 1769480 | tf_op jit(solution)/shard_map/ppermute | solution.py:130
  106.5 0.6 fusion.70
  107.1 1.6 fusion.11
  109.1 23.0 %all_to_all.26 = bf16[16,56,768]{2,1,0:T(8,128)(2,1)S(1)} all-to-all(bf16[16,56,768]{2,1,0:T(8,128)(2,1)S(1)} %pad_maximum_fusion.4), channel_id=1, replica_groups=mesh['dp'=32,'seq'=16] {'seq'}, dimensions={0} | all-to-all | bytes 2752512 | tf_op jit(solution)/shard_map/all_to_all | solution.py:92
  133.4 1.1 reduce.21
  134.6 31.4 %all_to_all.27 = bf16[32,2,576]{2,1,0:T(2,128)(2,1)S(1)} all-to-all(bf16[32,2,576]{2,1,0:T(2,128)(2,1)S(1)} %reshape.113), channel_id=1, replica_groups=mesh['dp'=32,'seq'=16] {'dp'}, dimensions={0} | all-to-all | bytes 147456 | tf_op jit(solution)/shard_map/all_to_all | solution.py:27
  166.2 0.7 broadcast_in_dim.2
  167.0 3.9 %all-to-all-start.4 = ((f32[32,1,1152]{2,1,0:T(1,128)}), f32[32,1,1152]{2,1,0:T(1,128)S(1)}, u32[]{:S(2)}, u32[]{:S(2)}) async-start(f32[32,1,1152]{2,1,0:T(1,128)} %broadcast_in_dim.2), calls=%async_computation.4 | async-start | bytes 294912 | tf_op jit(solution)/shard_map/all_to_all | solution.py:21
  170.9 1.3 copy.80
  172.3 15.5 %all-to-all-done.4 = f32[32,1,1152]{2,1,0:T(1,128)S(1)} async-done(((f32[32,1,1152]{2,1,0:T(1,128)}), f32[32,1,1152]{2,1,0:T(1,128)S(1)}, u32[]{:S(2)}, u32[]{:S(2)}) %all-to-all-start.4) | async-done | bytes 147488 | tf_op jit(solution)/shard_map/all_to_all | solution.py:21
  188.2 0.8 mul.345
  (128 shorter events, 11.7 us)
Async XLA Ops:
  0.6 2.1 %copy-start.21 = (bf16[1,512,768]{2,1,0:T(8,128)(2,1)S(1)}, bf16[1,512,768]{2,1,0:T(8,128)(2,1)}, u32[]{:S(2)}) copy-start(bf16[1,512,768]{2,1,0:T(8,128)(2,1)} %param.9) | copy-start | bytes 2359300
  39.7 7.1 %copy-start.1 = (bf16[16,92,768]{2,1,0:T(8,128)(2,1)}, bf16[16,92,768]{2,1,0:T(8,128)(2,1)S(1)}, u32[]{:S(2)}) copy-start(bf16[16,92,768]{2,1,0:T(8,128)(2,1)S(1)} %all_to_all.25) | copy-start | bytes 6782980
  39.8 4.4 %copy-start.35 = (s32[1,2]{1,0:T(1,128)S(1)}, s32[1,2]{1,0:T(1,128)}, u32[]{:S(2)}) copy-start(s32[1,2]{1,0:T(1,128)} %param.11) | copy-start | bytes 28
  39.9 6.3 %copy-start.33 = (f32[2,384]{1,0:T(2,128)S(1)}, f32[2,384]{1,0:T(2,128)}, u32[]{:S(2)}) copy-start(f32[2,384]{1,0:T(2,128)} %param.15) | copy-start | bytes 9220
  39.9 6.9 %copy-start.34 = (f32[2,384]{1,0:T(2,128)S(1)}, f32[2,384]{1,0:T(2,128)}, u32[]{:S(2)}) copy-start(f32[2,384]{1,0:T(2,128)} %param.14) | copy-start | bytes 9220
  39.9 6.9 %copy-start.27 = (f32[2,768]{1,0:T(2,128)S(1)}, f32[2,768]{1,0:T(2,128)}, u32[]{:S(2)}) copy-start(f32[2,768]{1,0:T(2,128)} %param.13) | copy-start | bytes 18436
  39.9 6.9 %copy-start.28 = (f32[2,768]{1,0:T(2,128)S(1)}, f32[2,768]{1,0:T(2,128)}, u32[]{:S(2)}) copy-start(f32[2,768]{1,0:T(2,128)} %param.12) | copy-start | bytes 18436
  41.9 15.5 %collective-permute-start = (bf16[16,60,768]{2,0,1:T(8,128)(2,1)}, bf16[16,60,768]{2,0,1:T(8,128)(2,1)}, u32[]{:S(2)}, u32[]{:S(2)}) collective-permute-start(bf16[16,60,768]{2,0,1:T(8,128)(2,1)} %copy.69), channel_id=1, source_target_pairs={{0,1},{1,0},{2,3},{3,2},{4,5},{5,4},{6,7},{7,6},{8,9},{9,8},{10,11... | collective-permute-start | bytes 4423688 | tf_op jit(solution)/shard_map/ppermute | solution.py:112
  46.9 34.1 %copy-start.29 = (f32[768]{0:T(1024)}, f32[768]{0:T(1024)S(1)}, u32[]{:S(2)}) copy-start(f32[768]{0:T(1024)S(1)} %get-tuple-element.14) | copy-start | bytes 9220
  46.9 34.1 %copy-start.31 = (f32[768]{0:T(1024)}, f32[768]{0:T(1024)S(1)}, u32[]{:S(2)}) copy-start(f32[768]{0:T(1024)S(1)} %get-tuple-element.49) | copy-start | bytes 9220
  47.0 34.0 %copy-start.10 = (bf16[16,32,768]{2,1,0:T(8,128)(2,1)}, bf16[16,32,768]{2,1,0:T(8,128)(2,1)S(1)}, u32[]{:S(2)}) copy-start(bf16[16,32,768]{2,1,0:T(8,128)(2,1)S(1)} %slice.185) | copy-start | bytes 2359300
  50.0 28.3 %all-to-all-start.1 = ((bf16[16,68,768]{2,1,0:T(8,128)(2,1)}), bf16[16,68,768]{2,1,0:T(8,128)(2,1)S(1)}, u32[]{:S(2)}, u32[]{:S(2)}) async-start(bf16[16,68,768]{2,1,0:T(8,128)(2,1)} %pad_maximum_fusion.2), calls=%async_computation.1 | async-start | bytes 3538944 | tf_op jit(solution)/shard_map/all_to_all | solution.py:92
  56.2 2.2 %copy-start.2 = (bf16[16,92,768]{2,1,0:T(8,128)(2,1)S(1)}, bf16[16,92,768]{2,1,0:T(8,128)(2,1)}, u32[]{:S(2)}) copy-start(bf16[16,92,768]{2,1,0:T(8,128)(2,1)} %copy-done.1) | copy-start | bytes 6782980
  71.0 1.7 copy-start.13
  72.7 1.2 copy-start.4
  72.7 1.2 copy-start.6
  72.7 1.2 copy-start.14
  73.3 1.1 copy-start.12
  73.9 1.3 copy-start.3
  75.2 5.8 %copy-start.24 = (f32[512,384]{1,0:T(8,128)}, f32[512,384]{1,0:T(8,128)S(1)}, u32[]{:S(2)}) copy-start(f32[512,384]{1,0:T(8,128)S(1)} %fusion.32) | copy-start | bytes 2359300
  78.3 8.1 %copy-start = (bf16[16,68,768]{2,1,0:T(8,128)(2,1)}, bf16[16,68,768]{2,1,0:T(8,128)(2,1)S(1)}, u32[]{:S(2)}) copy-start(bf16[16,68,768]{2,1,0:T(8,128)(2,1)S(1)} %all-to-all-done.1) | copy-start | bytes 5013508
  78.3 2.7 %copy-start.18 = (bf16[384,1,768]{2,1,0:T(2,128)(2,1)S(1)}, bf16[384,1,768]{2,1,0:T(2,128)(2,1)}, u32[]{:S(2)}) copy-start(bf16[384,1,768]{2,1,0:T(2,128)(2,1)} %get-tuple-element.33) | copy-start | bytes 1769476
  78.6 7.9 %collective-permute-start.1 = (bf16[16,36,768]{2,0,1:T(8,128)(2,1)S(1)}, bf16[16,36,768]{2,0,1:T(8,128)(2,1)S(1)}, u32[]{:S(2)}, u32[]{:S(2)}) collective-permute-start(bf16[16,36,768]{2,0,1:T(8,128)(2,1)S(1)} %copy.73), channel_id=1, source_target_pairs={{0,1},{1,0},{2,3},{3,2},{4,5},{5,4},{6,7},{7,6},{8,9},{9,8},{10,11... | collective-permute-start | bytes 2654216 | tf_op jit(solution)/shard_map/ppermute | solution.py:112
  83.1 1.3 copy-start.8
  87.8 1.1 copy-start.17
  88.0 1.5 copy-start.9
  89.4 1.1 copy-start.16
  89.4 1.1 copy-start.26
  90.1 1.3 copy-start.20
  90.1 1.5 copy-start.23
  92.6 1.1 copy-start.22
  94.4 3.0 %slice-start = ((bf16[16,68,768]{2,1,0:T(8,128)(2,1)}), bf16[16,32,768]{2,1,0:T(8,128)(2,1)S(1)}, s32[]{:S(2)}) async-start(bf16[16,68,768]{2,1,0:T(8,128)(2,1)} %copy-done), calls=%async_computation.5 | async-start | bytes 1572864 | tf_op jit(solution)/shard_map/slice | solution.py:96
  94.4 3.0 %copy-start.30 = (f32[768]{0:T(1024)S(1)}, f32[768]{0:T(1024)}, u32[]{:S(2)}) copy-start(f32[768]{0:T(1024)} %copy-done.29) | copy-start | bytes 9220
  94.4 3.0 %copy-start.32 = (f32[768]{0:T(1024)S(1)}, f32[768]{0:T(1024)}, u32[]{:S(2)}) copy-start(f32[768]{0:T(1024)} %copy-done.31) | copy-start | bytes 9220
  94.4 3.0 %copy-start.36 = (bf16[512,768]{1,0:T(8,128)(2,1)S(1)}, bf16[512,768]{1,0:T(8,128)(2,1)}, u32[]{:S(2)}) copy-start(bf16[512,768]{1,0:T(8,128)(2,1)} %get-tuple-element.47) | copy-start | bytes 2359300
  94.4 4.7 %collective-permute-start.2 = (f32[384,384]{1,0:T(8,128)S(1)}, f32[384,384]{1,0:T(8,128)S(1)}, u32[]{:S(2)}, u32[]{:S(2)}) collective-permute-start(f32[384,384]{1,0:T(8,128)S(1)} %slice_select_fusion.1), channel_id=1, source_target_pairs={{0,1},{1,0},{2,3},{3,2},{4,5},{5,4},{6,7},{7,6},{8,9},{9,8},{10,11... | collective-permute-start | bytes 1769480 | tf_op jit(solution)/shard_map/ppermute | solution.py:130
  99.1 1.3 copy-start.19
  99.1 1.5 copy-start.25
  101.6 1.1 copy-start.7
  103.9 2.5 %copy-start.5 = (bf16[1,16,48,384]{3,2,0,1:T(8,128)(2,1)S(1)}, bf16[1,16,48,384]{3,2,0,1:T(8,128)(2,1)}, u32[]{:S(2)}) copy-start(bf16[1,16,48,384]{3,2,0,1:T(8,128)(2,1)} %copy-done.4) | copy-start | bytes 1769476
  104.0 3.0 %copy-start.11 = (bf16[16,32,768]{2,1,0:T(8,128)(2,1)S(1)}, bf16[16,32,768]{2,1,0:T(8,128)(2,1)}, u32[]{:S(2)}) copy-start(bf16[16,32,768]{2,1,0:T(8,128)(2,1)} %copy-done.10) | copy-start | bytes 2359300
  104.0 3.0 %copy-start.15 = (bf16[1,16,48,384]{3,2,0,1:T(8,128)(2,1)S(1)}, bf16[1,16,48,384]{3,2,0,1:T(8,128)(2,1)}, u32[]{:S(2)}) copy-start(bf16[1,16,48,384]{3,2,0,1:T(8,128)(2,1)} %copy-done.14) | copy-start | bytes 1769476
  104.0 4.7 %collective-permute-start.3 = (f32[384,384]{1,0:T(8,128)S(1)}, f32[384,384]{1,0:T(8,128)S(1)}, u32[]{:S(2)}, u32[]{:S(2)}) collective-permute-start(f32[384,384]{1,0:T(8,128)S(1)} %slice_select_fusion), channel_id=1, source_target_pairs={{0,1},{1,0},{2,3},{3,2},{4,5},{5,4},{6,7},{7,6},{8,9},{9,8},{10,11... | collective-permute-start | bytes 1769480 | tf_op jit(solution)/shard_map/ppermute | solution.py:130
  167.0 20.8 %all-to-all-start.4 = ((f32[32,1,1152]{2,1,0:T(1,128)}), f32[32,1,1152]{2,1,0:T(1,128)S(1)}, u32[]{:S(2)}, u32[]{:S(2)}) async-start(f32[32,1,1152]{2,1,0:T(1,128)} %broadcast_in_dim.2), calls=%async_computation.4 | async-start | bytes 294912 | tf_op jit(solution)/shard_map/all_to_all | solution.py:21

commit v13 on v12

--- a/solution.py
+++ b/solution.py
@@ -99,7 +99,7 @@
 
 
 def strided_pieces(block, peers):
-    return block.reshape(-1, peers, block.shape[-1]).swapaxes(0, 1)
+    return block.reshape(peers, -1, block.shape[-1])
 
 
 def half_for_each(shard, peers, lanes):
@@ -232,7 +232,7 @@
     sample_count = sequence_in.shape[0] * lax.axis_size("dp")
     full_length = sequence_in.shape[1] * peers
     point_grad = summed * (1.0 / math.sqrt(sample_count * full_length))
-    input_grad = back_pieces.swapaxes(0, 1).reshape(sequence_in.shape)
+    input_grad = back_pieces.reshape(sequence_in.shape)
     return (point_grad, input_grad)
 
 

time: 190 us -> 189 us (level)
  local copies, waits for them, and re-layouts: 35.6 us -> 33.3 us
    transpose x4 -> x0, local copies, waits for them, and re-layouts: 3.24 us -> none  [the longest x2 1.84 us: strided_pieces(): return block.reshape(-1, peers, block.shape[-1]).swapaxes(0, 1)]
where the time goes in v13:
time: 189 us; the launch traced here: 188 us
  blocking collectives  90.7 us (48%)
  local copies, waits for them, and re-layouts  33.3 us (18%)
  starting transfers between devices  18.9 us (10%)
  waiting for transfers between devices  16 us (8%)
  matrix products  14.4 us (8%)
  other arithmetic  12.2 us (6%)
  between operations  2.83 us (1%)
    all_to_all x2, blocking collectives, exchanged(): arrived = lax.all_to_all(joined, axis, 0, 0, tiled=True)  59.3 us
    all_to_all x1, blocking collectives, summed_over(): arrived = lax.all_to_all(pieces, axis, 0, 0, tiled=True)  31.4 us
    all_to_all x1, waiting for transfers between devices, gathered(): return lax.all_to_all(copies, axis, 0, 0, tiled=True)  16 us
    dot_general x8, matrix products, contract_last(): lax.dot_general(left, right, (((1,), (1,)), ((), ())), preferred_element_...  7.54 us
    unnamed x76, local copies, waits for them, and re-layouts  6.81 us
    all_to_all x1, starting transfers between devices, exchanged(): arrived = lax.all_to_all(joined, axis, 0, 0, tiled=True)  5.53 us
    ppermute x2, starting transfers between devices, chip_half(): partner = lax.ppermute(given, 'seq', [(i, i ^ 1) for i in range(peers)])  4.81 us
    ppermute x2, starting transfers between devices, whole_from_halves(): partner = lax.ppermute(own_halves, axis, [(i, i ^ 1) for i in range(peers)])  4.73 us
  transfers between devices with their start and end apart: 6, of which 1 were waited for; matrix products, arithmetic and copies ran while one was open for 19% of the time, Pallas kernels for 0%

profile of v13, /device:TPU:6, one launch (start us, length us, event | category | flops | bytes accessed | tf_op | source)
XLA Modules:
  0.0 188.4 jit_solution(17608645366342697728)
XLA Ops:
  0.6 1.0 fusion.101
  1.7 0.9 reshape.93
  3.1 36.4 %all_to_all.25 = bf16[16,92,768]{2,1,0:T(8,128)(2,1)S(1)} all-to-all(bf16[16,92,768]{2,1,0:T(8,128)(2,1)S(1)} %pad_maximum_fusion), channel_id=1, replica_groups=mesh['dp'=32,'seq'=16] {'seq'}, dimensions={0} | all-to-all | bytes 4521984 | tf_op jit(solution)/shard_map/all_to_all | solution.py:92
  39.7 2.0 %copy.33 = bf16[16,60,768]{2,0,1:T(8,128)(2,1)} copy(bf16[16,60,768]{2,1,0:T(8,128)(2,1)S(1)} %slice.187) | data formatting | bytes 2949120 | tf_op jit(solution)/shard_map/slice | solution.py:96
  41.6 2.4 %collective-permute-start = (bf16[16,60,768]{2,0,1:T(8,128)(2,1)}, bf16[16,60,768]{2,0,1:T(8,128)(2,1)}, u32[]{:S(2)}, u32[]{:S(2)}) collective-permute-start(bf16[16,60,768]{2,0,1:T(8,128)(2,1)} %copy.33), channel_id=1, source_target_pairs={{0,1},{1,0},{2,3},{3,2},{4,5},{5,4},{6,7},{7,6},{8,9},{9,8},{10,11... | collective-permute-start | bytes 4423688 | tf_op jit(solution)/shard_map/ppermute | solution.py:112
  44.0 0.6 fusion.102
  45.9 0.6 slice_reduce_fusion.4
  46.9 2.6 %pad_maximum_fusion.2 = bf16[16,68,768]{2,1,0:T(8,128)(2,1)} fusion(bf16[16,36,768]{2,1,0:T(8,128)(2,1)S(1)} %bitcast.71, bf16[16,32,768]{2,1,0:T(8,128)(2,1)} %bitcast.80), kind=kLoop, calls=%fused_computation.10 | loop fusion | flops 3342336 | bytes 3342336 | tf_op jit(solution)/shard_map/concatenate | solution.py:91
  49.5 5.5 %all-to-all-start.1 = ((bf16[16,68,768]{2,1,0:T(8,128)(2,1)}), bf16[16,68,768]{2,1,0:T(8,128)(2,1)S(1)}, u32[]{:S(2)}, u32[]{:S(2)}) async-start(bf16[16,68,768]{2,1,0:T(8,128)(2,1)} %pad_maximum_fusion.2), calls=%async_computation.1 | async-start | bytes 3538944 | tf_op jit(solution)/shard_map/all_to_all | solution.py:92
  55.0 0.6 fusion.6
  55.7 1.2 fusion.98
  56.8 1.0 copy-done.2
  57.8 2.4 %broadcast_select_fusion.1 = (bf16[16,60,768]{2,1,0:T(8,128)(2,1)S(1)}, bf16[16,60,768]{2,1,0:T(8,128)(2,1)S(1)}) fusion(pred[]{:T(512)S(6)} %eq.11, bf16[16,60,768]{2,0,1:T(8,128)(2,1)} %collective-permute-done, bf16[16,92,768]{2,1,0:T(8,128)(2,1)S(1)} %copy-done.2), kind=kLoop, calls=%fused_computation.45 | loop fusion | flops 1474560 | bytes 5898241 | tf_op jit(solution)/shard_map/jit(_where)/select_n | solution.py:114
  60.2 1.4 pad_maximum_fusion.1
  61.6 1.4 slice.192
  63.1 3.6 %reshape.96 = bf16[384,2,768]{2,1,0:T(2,128)(2,1)} reshape(bf16[16,48,768]{2,1,0:T(8,128)(2,1)} %slice.192) | data formatting | bytes 2359296 | tf_op jit(solution)/shard_map/reshape | solution.py:180
  66.7 3.7 %reshape.95 = bf16[16,3,48,384]{3,2,1,0:T(8,128)(2,1)} reshape(bf16[16,72,768]{2,1,0:T(8,128)(2,1)} %pad_maximum_fusion.1) | data formatting | bytes 3538944 | tf_op jit(solution)/shard_map/reshape | solution.py:121
  70.5 1.7 fusion.94
  74.7 3.1 %fusion.96 = (bf16[384,1,768]{2,1,0:T(2,128)(2,1)}, bf16[384,1,768]{2,1,0:T(2,128)(2,1)}) fusion(bf16[384,2,768]{2,1,0:T(2,128)(2,1)S(1)} %copy-done.3), kind=kLoop, calls=%fused_computation.138 | loop fusion | bytes 2359296 | tf_op jit(solution)/shard_map/slice | solution.py:210
  78.0 2.4 %collective-permute-start.1 = (bf16[16,36,768]{2,0,1:T(8,128)(2,1)S(1)}, bf16[16,36,768]{2,0,1:T(8,128)(2,1)S(1)}, u32[]{:S(2)}, u32[]{:S(2)}) collective-permute-start(bf16[16,36,768]{2,0,1:T(8,128)(2,1)S(1)} %copy.36), channel_id=1, source_target_pairs={{0,1},{1,0},{2,3},{3,2},{4,5},{5,4},{6,7},{7,6},{8,9},{9,8},{10,11... | collective-permute-start | bytes 2654216 | tf_op jit(solution)/shard_map/ppermute | solution.py:112
  80.5 2.1 %multiply_convert_fusion = (bf16[512,768]{1,0:T(8,128)(2,1)S(1)}, bf16[512,768]{1,0:T(8,128)(2,1)}) fusion(f32[768]{0:T(1024)S(1)} %get-tuple-element.14, f32[768]{0:T(1024)S(1)} %get-tuple-element.49, bf16[384,1,768]{2,1,0:T(2,128)(2,1)S(1)} %copy-done.18, f32[512,384]{1,0:T(8,128)S(1)} %fusion.32, f32[]{:T(128)} %bitcast.9, bf16[512,768]{1,0:T(8,128)(2,1)S(1)} %bitcast.73), kind=kOutput, calls=%fused_computation.41 | convolution fusion | flops 310050816 | bytes 3741700 | tf_op jit(solution)/shard_map/dot_general | solution.py:61
  82.6 1.2 fusion.97
  83.9 1.0 fusion.26
  84.9 1.0 fusion.25
  86.6 0.6 reshape.98
  87.5 0.9 copy-done.17
  88.9 0.6 convolution_add_fusion.1
  91.0 0.9 fusion.48
  92.0 0.6 fusion.103
  93.9 2.4 %collective-permute-start.2 = (f32[384,384]{1,0:T(8,128)S(1)}, f32[384,384]{1,0:T(8,128)S(1)}, u32[]{:S(2)}, u32[]{:S(2)}) collective-permute-start(f32[384,384]{1,0:T(8,128)S(1)} %slice_select_fusion.1), channel_id=1, source_target_pairs={{0,1},{1,0},{2,3},{3,2},{4,5},{5,4},{6,7},{7,6},{8,9},{9,8},{10,11... | collective-permute-start | bytes 1769480 | tf_op jit(solution)/shard_map/ppermute | solution.py:130
  96.3 0.6 fusion.73
  96.9 1.6 fusion.24
  98.8 1.0 copy-done.19
  100.0 0.9 fusion.40
  101.1 1.0 copy-done.7
  102.1 0.6 fusion.104
  102.7 0.7 fusion.57
  103.5 2.4 %collective-permute-start.3 = (f32[384,384]{1,0:T(8,128)S(1)}, f32[384,384]{1,0:T(8,128)S(1)}, u32[]{:S(2)}, u32[]{:S(2)}) collective-permute-start(f32[384,384]{1,0:T(8,128)S(1)} %slice_select_fusion), channel_id=1, source_target_pairs={{0,1},{1,0},{2,3},{3,2},{4,5},{5,4},{6,7},{7,6},{8,9},{9,8},{10,11... | collective-permute-start | bytes 1769480 | tf_op jit(solution)/shard_map/ppermute | solution.py:130
  105.9 0.6 fusion.70
  106.5 1.6 fusion.11
  108.6 22.9 %all_to_all.26 = bf16[16,56,768]{2,1,0:T(8,128)(2,1)S(1)} all-to-all(bf16[16,56,768]{2,1,0:T(8,128)(2,1)S(1)} %pad_maximum_fusion.4), channel_id=1, replica_groups=mesh['dp'=32,'seq'=16] {'seq'}, dimensions={0} | all-to-all | bytes 2752512 | tf_op jit(solution)/shard_map/all_to_all | solution.py:92
  132.8 1.1 reduce.21
  134.0 31.4 %all_to_all.27 = bf16[32,2,576]{2,1,0:T(2,128)(2,1)S(1)} all-to-all(bf16[32,2,576]{2,1,0:T(2,128)(2,1)S(1)} %reshape.113), channel_id=1, replica_groups=mesh['dp'=32,'seq'=16] {'dp'}, dimensions={0} | all-to-all | bytes 147456 | tf_op jit(solution)/shard_map/all_to_all | solution.py:27
  165.7 0.7 broadcast_in_dim.2
  166.4 3.9 %all-to-all-start.4 = ((f32[32,1,1152]{2,1,0:T(1,128)}), f32[32,1,1152]{2,1,0:T(1,128)S(1)}, u32[]{:S(2)}, u32[]{:S(2)}) async-start(f32[32,1,1152]{2,1,0:T(1,128)} %broadcast_in_dim.2), calls=%async_computation.4 | async-start | bytes 294912 | tf_op jit(solution)/shard_map/all_to_all | solution.py:21
  170.3 1.0 slice.212
  171.3 16.0 %all-to-all-done.4 = f32[32,1,1152]{2,1,0:T(1,128)S(1)} async-done(((f32[32,1,1152]{2,1,0:T(1,128)}), f32[32,1,1152]{2,1,0:T(1,128)S(1)}, u32[]{:S(2)}, u32[]{:S(2)}) %all-to-all-start.4) | async-done | bytes 147488 | tf_op jit(solution)/shard_map/all_to_all | solution.py:21
  187.6 0.8 mul.345
  (125 shorter events, 10.8 us)
Async XLA Ops:
  0.6 2.3 %copy-start.21 = (bf16[1,512,768]{2,1,0:T(8,128)(2,1)S(1)}, bf16[1,512,768]{2,1,0:T(8,128)(2,1)}, u32[]{:S(2)}) copy-start(bf16[1,512,768]{2,1,0:T(8,128)(2,1)} %param.9) | copy-start | bytes 2359300
  39.5 7.1 %copy-start.1 = (bf16[16,92,768]{2,1,0:T(8,128)(2,1)}, bf16[16,92,768]{2,1,0:T(8,128)(2,1)S(1)}, u32[]{:S(2)}) copy-start(bf16[16,92,768]{2,1,0:T(8,128)(2,1)S(1)} %all_to_all.25) | copy-start | bytes 6782980
  39.6 4.4 %copy-start.35 = (s32[1,2]{1,0:T(1,128)S(1)}, s32[1,2]{1,0:T(1,128)}, u32[]{:S(2)}) copy-start(s32[1,2]{1,0:T(1,128)} %param.11) | copy-start | bytes 28
  39.6 6.3 %copy-start.33 = (f32[2,384]{1,0:T(2,128)S(1)}, f32[2,384]{1,0:T(2,128)}, u32[]{:S(2)}) copy-start(f32[2,384]{1,0:T(2,128)} %param.15) | copy-start | bytes 9220
  39.6 6.9 %copy-start.34 = (f32[2,384]{1,0:T(2,128)S(1)}, f32[2,384]{1,0:T(2,128)}, u32[]{:S(2)}) copy-start(f32[2,384]{1,0:T(2,128)} %param.14) | copy-start | bytes 9220
  39.6 6.9 %copy-start.27 = (f32[2,768]{1,0:T(2,128)S(1)}, f32[2,768]{1,0:T(2,128)}, u32[]{:S(2)}) copy-start(f32[2,768]{1,0:T(2,128)} %param.13) | copy-start | bytes 18436
  39.7 6.9 %copy-start.28 = (f32[2,768]{1,0:T(2,128)S(1)}, f32[2,768]{1,0:T(2,128)}, u32[]{:S(2)}) copy-start(f32[2,768]{1,0:T(2,128)} %param.12) | copy-start | bytes 18436
  41.6 15.2 %collective-permute-start = (bf16[16,60,768]{2,0,1:T(8,128)(2,1)}, bf16[16,60,768]{2,0,1:T(8,128)(2,1)}, u32[]{:S(2)}, u32[]{:S(2)}) collective-permute-start(bf16[16,60,768]{2,0,1:T(8,128)(2,1)} %copy.33), channel_id=1, source_target_pairs={{0,1},{1,0},{2,3},{3,2},{4,5},{5,4},{6,7},{7,6},{8,9},{9,8},{10,11... | collective-permute-start | bytes 4423688 | tf_op jit(solution)/shard_map/ppermute | solution.py:112
  46.6 33.8 %copy-start.29 = (f32[768]{0:T(1024)}, f32[768]{0:T(1024)S(1)}, u32[]{:S(2)}) copy-start(f32[768]{0:T(1024)S(1)} %get-tuple-element.14) | copy-start | bytes 9220
  46.6 33.8 %copy-start.31 = (f32[768]{0:T(1024)}, f32[768]{0:T(1024)S(1)}, u32[]{:S(2)}) copy-start(f32[768]{0:T(1024)S(1)} %get-tuple-element.49) | copy-start | bytes 9220
  46.7 33.7 %copy-start.10 = (bf16[16,32,768]{2,1,0:T(8,128)(2,1)}, bf16[16,32,768]{2,1,0:T(8,128)(2,1)S(1)}, u32[]{:S(2)}) copy-start(bf16[16,32,768]{2,1,0:T(8,128)(2,1)S(1)} %slice.185) | copy-start | bytes 2359300
  49.5 28.3 %all-to-all-start.1 = ((bf16[16,68,768]{2,1,0:T(8,128)(2,1)}), bf16[16,68,768]{2,1,0:T(8,128)(2,1)S(1)}, u32[]{:S(2)}, u32[]{:S(2)}) async-start(bf16[16,68,768]{2,1,0:T(8,128)(2,1)} %pad_maximum_fusion.2), calls=%async_computation.1 | async-start | bytes 3538944 | tf_op jit(solution)/shard_map/all_to_all | solution.py:92
  55.7 2.2 %copy-start.2 = (bf16[16,92,768]{2,1,0:T(8,128)(2,1)S(1)}, bf16[16,92,768]{2,1,0:T(8,128)(2,1)}, u32[]{:S(2)}) copy-start(bf16[16,92,768]{2,1,0:T(8,128)(2,1)} %copy-done.1) | copy-start | bytes 6782980
  70.5 1.7 copy-start.13
  72.1 1.2 copy-start.4
  72.1 1.2 copy-start.6
  72.1 1.2 copy-start.14
  72.7 1.1 copy-start.12
  73.4 1.3 copy-start.3
  74.7 5.8 %copy-start.24 = (f32[512,384]{1,0:T(8,128)}, f32[512,384]{1,0:T(8,128)S(1)}, u32[]{:S(2)}) copy-start(f32[512,384]{1,0:T(8,128)S(1)} %fusion.32) | copy-start | bytes 2359300
  77.8 8.1 %copy-start = (bf16[16,68,768]{2,1,0:T(8,128)(2,1)}, bf16[16,68,768]{2,1,0:T(8,128)(2,1)S(1)}, u32[]{:S(2)}) copy-start(bf16[16,68,768]{2,1,0:T(8,128)(2,1)S(1)} %all-to-all-done.1) | copy-start | bytes 5013508
  77.8 2.7 %copy-start.18 = (bf16[384,1,768]{2,1,0:T(2,128)(2,1)S(1)}, bf16[384,1,768]{2,1,0:T(2,128)(2,1)}, u32[]{:S(2)}) copy-start(bf16[384,1,768]{2,1,0:T(2,128)(2,1)} %get-tuple-element.33) | copy-start | bytes 1769476
  78.0 7.9 %collective-permute-start.1 = (bf16[16,36,768]{2,0,1:T(8,128)(2,1)S(1)}, bf16[16,36,768]{2,0,1:T(8,128)(2,1)S(1)}, u32[]{:S(2)}, u32[]{:S(2)}) collective-permute-start(bf16[16,36,768]{2,0,1:T(8,128)(2,1)S(1)} %copy.36), channel_id=1, source_target_pairs={{0,1},{1,0},{2,3},{3,2},{4,5},{5,4},{6,7},{7,6},{8,9},{9,8},{10,11... | collective-permute-start | bytes 2654216 | tf_op jit(solution)/shard_map/ppermute | solution.py:112
  82.6 1.3 copy-start.8
  87.2 1.1 copy-start.17
  87.4 1.5 copy-start.9
  88.9 1.1 copy-start.16
  88.9 1.1 copy-start.26
  89.5 1.3 copy-start.20
  89.5 1.5 copy-start.23
  92.0 1.1 copy-start.22
  93.8 3.0 %slice-start = ((bf16[16,68,768]{2,1,0:T(8,128)(2,1)}), bf16[16,32,768]{2,1,0:T(8,128)(2,1)S(1)}, s32[]{:S(2)}) async-start(bf16[16,68,768]{2,1,0:T(8,128)(2,1)} %copy-done), calls=%async_computation.5 | async-start | bytes 1572864 | tf_op jit(solution)/shard_map/slice | solution.py:96
  93.8 3.0 %copy-start.30 = (f32[768]{0:T(1024)S(1)}, f32[768]{0:T(1024)}, u32[]{:S(2)}) copy-start(f32[768]{0:T(1024)} %copy-done.29) | copy-start | bytes 9220
  93.8 3.0 %copy-start.32 = (f32[768]{0:T(1024)S(1)}, f32[768]{0:T(1024)}, u32[]{:S(2)}) copy-start(f32[768]{0:T(1024)} %copy-done.31) | copy-start | bytes 9220
  93.9 3.0 %copy-start.36 = (bf16[512,768]{1,0:T(8,128)(2,1)S(1)}, bf16[512,768]{1,0:T(8,128)(2,1)}, u32[]{:S(2)}) copy-start(bf16[512,768]{1,0:T(8,128)(2,1)} %get-tuple-element.47) | copy-start | bytes 2359300
  93.9 4.7 %collective-permute-start.2 = (f32[384,384]{1,0:T(8,128)S(1)}, f32[384,384]{1,0:T(8,128)S(1)}, u32[]{:S(2)}, u32[]{:S(2)}) collective-permute-start(f32[384,384]{1,0:T(8,128)S(1)} %slice_select_fusion.1), channel_id=1, source_target_pairs={{0,1},{1,0},{2,3},{3,2},{4,5},{5,4},{6,7},{7,6},{8,9},{9,8},{10,11... | collective-permute-start | bytes 1769480 | tf_op jit(solution)/shard_map/ppermute | solution.py:130
  98.6 1.3 copy-start.19
  98.6 1.5 copy-start.25
  101.0 1.1 copy-start.7
  103.4 2.5 %copy-start.5 = (bf16[1,16,48,384]{3,2,0,1:T(8,128)(2,1)S(1)}, bf16[1,16,48,384]{3,2,0,1:T(8,128)(2,1)}, u32[]{:S(2)}) copy-start(bf16[1,16,48,384]{3,2,0,1:T(8,128)(2,1)} %copy-done.4) | copy-start | bytes 1769476
  103.5 3.0 %copy-start.11 = (bf16[16,32,768]{2,1,0:T(8,128)(2,1)S(1)}, bf16[16,32,768]{2,1,0:T(8,128)(2,1)}, u32[]{:S(2)}) copy-start(bf16[16,32,768]{2,1,0:T(8,128)(2,1)} %copy-done.10) | copy-start | bytes 2359300
  103.5 3.0 %copy-start.15 = (bf16[1,16,48,384]{3,2,0,1:T(8,128)(2,1)S(1)}, bf16[1,16,48,384]{3,2,0,1:T(8,128)(2,1)}, u32[]{:S(2)}) copy-start(bf16[1,16,48,384]{3,2,0,1:T(8,128)(2,1)} %copy-done.14) | copy-start | bytes 1769476
  103.5 4.7 %collective-permute-start.3 = (f32[384,384]{1,0:T(8,128)S(1)}, f32[384,384]{1,0:T(8,128)S(1)}, u32[]{:S(2)}, u32[]{:S(2)}) collective-permute-start(f32[384,384]{1,0:T(8,128)S(1)} %slice_select_fusion), channel_id=1, source_target_pairs={{0,1},{1,0},{2,3},{3,2},{4,5},{5,4},{6,7},{7,6},{8,9},{9,8},{10,11... | collective-permute-start | bytes 1769480 | tf_op jit(solution)/shard_map/ppermute | solution.py:130
  166.4 20.8 %all-to-all-start.4 = ((f32[32,1,1152]{2,1,0:T(1,128)}), f32[32,1,1152]{2,1,0:T(1,128)S(1)}, u32[]{:S(2)}, u32[]{:S(2)}) async-start(f32[32,1,1152]{2,1,0:T(1,128)} %broadcast_in_dim.2), calls=%async_computation.4 | async-start | bytes 294912 | tf_op jit(solution)/shard_map/all_to_all | solution.py:21

commit v14 on v13

--- a/solution.py
+++ b/solution.py
@@ -171,10 +171,14 @@
         "seq",
     )
     state = state_pieces.reshape(-1, channels)
-    grad_in, second_in, state = lax.optimization_barrier((output_grad[0], conv_weight[1], state))
-    grad_pieces, second_halves = exchanged(
-        [strided_pieces(grad_in, peers), half_for_each(second_in, peers, channels)], "seq"
-    )
+    grad_rows_sent = strided_pieces(output_grad[0], peers)
+    second_joined = jnp.concatenate(
+        [grad_rows_sent, half_for_each(conv_weight[1], peers, channels)], axis=1
+    )
+    second_joined, state = lax.optimization_barrier((second_joined, state))
+    second_arrived = lax.all_to_all(second_joined, "seq", 0, 0, tiled=True)
+    grad_pieces = second_arrived[:, : grad_rows_sent.shape[1]]
+    second_halves = second_arrived[:, grad_rows_sent.shape[1] :]
     first_whole = whole_from_halves(first_halves, "seq")
     first_pieces = first_whole[:, :conv_rows]
     point_full = first_whole[:, conv_rows:].reshape(-1, *point_weight.shape[1:])

time: 189 us -> 188 us (level)
    concatenate x3 -> x2, other arithmetic: 3.06 us -> 0.43 us  [exchanged(): joined = jnp.concatenate(parts, axis=1)]
    unnamed x76 -> x78, local copies, waits for them, and re-layouts: 6.81 us -> 6.84 us
  transfers between devices with their start and end apart: 6 -> 6, of which waited for: 1 -> 1; matrix products, arithmetic and copies ran while one was open for 19% -> 18% of each run, Pallas kernels for 0% -> 0%
where the time goes in v14:
time: 188 us; the launch traced here: 187 us
  blocking collectives  90.7 us (48%)
  local copies, waits for them, and re-layouts  33.3 us (18%)
  starting transfers between devices  18.9 us (10%)
  waiting for transfers between devices  16 us (9%)
  matrix products  14.4 us (8%)
  other arithmetic  10.9 us (6%)
  between operations  2.84 us (2%)
    all_to_all x2, blocking collectives, exchanged(): arrived = lax.all_to_all(joined, axis, 0, 0, tiled=True)  59.3 us
    all_to_all x1, blocking collectives, summed_over(): arrived = lax.all_to_all(pieces, axis, 0, 0, tiled=True)  31.4 us
    all_to_all x1, waiting for transfers between devices, gathered(): return lax.all_to_all(copies, axis, 0, 0, tiled=True)  16 us
    dot_general x8, matrix products, contract_last(): lax.dot_general(left, right, (((1,), (1,)), ((), ())), preferred_element_...  7.54 us
    unnamed x78, local copies, waits for them, and re-layouts  6.84 us
    all_to_all x1, starting transfers between devices, shards(): second_arrived = lax.all_to_all(second_joined, 'seq', 0, 0, tiled=True)  5.54 us
    ppermute x2, starting transfers between devices, chip_half(): partner = lax.ppermute(given, 'seq', [(i, i ^ 1) for i in range(peers)])  4.81 us
    ppermute x2, starting transfers between devices, whole_from_halves(): partner = lax.ppermute(own_halves, axis, [(i, i ^ 1) for i in range(peers)])  4.73 us
  transfers between devices with their start and end apart: 6, of which 1 were waited for; matrix products, arithmetic and copies ran while one was open for 18% of the time, Pallas kernels for 0%

profile of v14, /device:TPU:6, one launch (start us, length us, event | category | flops | bytes accessed | tf_op | source)
XLA Modules:
  0.0 187.1 jit_solution(4776139404737587964)
XLA Ops:
  0.6 1.0 fusion.101
  1.7 0.9 reshape.90
  3.1 36.4 %all_to_all.25 = bf16[16,92,768]{2,1,0:T(8,128)(2,1)S(1)} all-to-all(bf16[16,92,768]{2,1,0:T(8,128)(2,1)S(1)} %pad_maximum_fusion), channel_id=1, replica_groups=mesh['dp'=32,'seq'=16] {'seq'}, dimensions={0} | all-to-all | bytes 4521984 | tf_op jit(solution)/shard_map/all_to_all | solution.py:92
  39.7 2.0 %copy.33 = bf16[16,60,768]{2,0,1:T(8,128)(2,1)} copy(bf16[16,60,768]{2,1,0:T(8,128)(2,1)S(1)} %slice.187) | data formatting | bytes 2949120 | tf_op jit(solution)/shard_map/slice | solution.py:96
  41.6 2.4 %collective-permute-start = (bf16[16,60,768]{2,0,1:T(8,128)(2,1)}, bf16[16,60,768]{2,0,1:T(8,128)(2,1)}, u32[]{:S(2)}, u32[]{:S(2)}) collective-permute-start(bf16[16,60,768]{2,0,1:T(8,128)(2,1)} %copy.33), channel_id=1, source_target_pairs={{0,1},{1,0},{2,3},{3,2},{4,5},{5,4},{6,7},{7,6},{8,9},{9,8},{10,11... | collective-permute-start | bytes 4423688 | tf_op jit(solution)/shard_map/ppermute | solution.py:112
  44.0 0.6 fusion.102
  46.0 0.6 slice_reduce_fusion.4
  46.8 1.3 pad_maximum_fusion.2
  48.2 5.5 %all-to-all-start.1 = ((bf16[16,68,768]{2,1,0:T(8,128)(2,1)}), bf16[16,68,768]{2,1,0:T(8,128)(2,1)S(1)}, u32[]{:S(2)}, u32[]{:S(2)}) async-start(bf16[16,68,768]{2,1,0:T(8,128)(2,1)} %pad_maximum_fusion.2), calls=%async_computation.1 | async-start | bytes 3538944 | tf_op jit(solution)/shard_map/all_to_all | solution.py:179
  53.7 0.6 fusion.6
  54.4 1.2 fusion.98
  55.5 1.0 copy-done.2
  56.5 2.4 %broadcast_select_fusion.1 = (bf16[16,60,768]{2,1,0:T(8,128)(2,1)S(1)}, bf16[16,60,768]{2,1,0:T(8,128)(2,1)S(1)}) fusion(pred[]{:T(512)S(6)} %eq.11, bf16[16,60,768]{2,0,1:T(8,128)(2,1)} %collective-permute-done, bf16[16,92,768]{2,1,0:T(8,128)(2,1)S(1)} %copy-done.2), kind=kLoop, calls=%fused_computation.45 | loop fusion | flops 1474560 | bytes 5898241 | tf_op jit(solution)/shard_map/jit(_where)/select_n | solution.py:114
  59.0 1.4 pad_maximum_fusion.1
  60.4 1.4 slice.192
  61.8 3.7 %reshape.93 = bf16[384,2,768]{2,1,0:T(2,128)(2,1)} reshape(bf16[16,48,768]{2,1,0:T(8,128)(2,1)} %slice.192) | data formatting | bytes 2359296 | tf_op jit(solution)/shard_map/reshape | solution.py:184
  65.4 3.7 %reshape.92 = bf16[16,3,48,384]{3,2,1,0:T(8,128)(2,1)} reshape(bf16[16,72,768]{2,1,0:T(8,128)(2,1)} %pad_maximum_fusion.1) | data formatting | bytes 3538944 | tf_op jit(solution)/shard_map/reshape | solution.py:121
  69.2 1.7 fusion.94
  73.4 3.1 %fusion.96 = (bf16[384,1,768]{2,1,0:T(2,128)(2,1)}, bf16[384,1,768]{2,1,0:T(2,128)(2,1)}) fusion(bf16[384,2,768]{2,1,0:T(2,128)(2,1)S(1)} %copy-done.3), kind=kLoop, calls=%fused_computation.137 | loop fusion | bytes 2359296 | tf_op jit(solution)/shard_map/slice | solution.py:214
  76.7 2.4 %collective-permute-start.1 = (bf16[16,36,768]{2,0,1:T(8,128)(2,1)S(1)}, bf16[16,36,768]{2,0,1:T(8,128)(2,1)S(1)}, u32[]{:S(2)}, u32[]{:S(2)}) collective-permute-start(bf16[16,36,768]{2,0,1:T(8,128)(2,1)S(1)} %copy.36), channel_id=1, source_target_pairs={{0,1},{1,0},{2,3},{3,2},{4,5},{5,4},{6,7},{7,6},{8,9},{9,8},{10,11... | collective-permute-start | bytes 2654216 | tf_op jit(solution)/shard_map/ppermute | solution.py:112
  79.2 2.1 %multiply_convert_fusion = (bf16[512,768]{1,0:T(8,128)(2,1)S(1)}, bf16[512,768]{1,0:T(8,128)(2,1)}) fusion(f32[768]{0:T(1024)S(1)} %get-tuple-element.12, f32[768]{0:T(1024)S(1)} %get-tuple-element.47, bf16[384,1,768]{2,1,0:T(2,128)(2,1)S(1)} %copy-done.18, f32[512,384]{1,0:T(8,128)S(1)} %fusion.32, f32[]{:T(128)} %bitcast.9, bf16[512,768]{1,0:T(8,128)(2,1)S(1)} %bitcast.72), kind=kOutput, calls=%fused_computation.41 | convolution fusion | flops 310050816 | bytes 3741700 | tf_op jit(solution)/shard_map/dot_general | solution.py:61
  81.3 1.2 fusion.97
  82.6 1.0 fusion.26
  83.6 1.0 fusion.25
  85.3 0.6 reshape.94
  86.2 0.9 copy-done.17
  88.7 0.6 fusion.30
  89.7 0.9 fusion.48
  90.7 0.6 fusion.103
  92.6 2.4 %collective-permute-start.2 = (f32[384,384]{1,0:T(8,128)S(1)}, f32[384,384]{1,0:T(8,128)S(1)}, u32[]{:S(2)}, u32[]{:S(2)}) collective-permute-start(f32[384,384]{1,0:T(8,128)S(1)} %slice_select_fusion.1), channel_id=1, source_target_pairs={{0,1},{1,0},{2,3},{3,2},{4,5},{5,4},{6,7},{7,6},{8,9},{9,8},{10,11... | collective-permute-start | bytes 1769480 | tf_op jit(solution)/shard_map/ppermute | solution.py:130
  95.0 0.6 fusion.73
  95.6 1.6 fusion.24
  97.5 1.0 copy-done.19
  98.8 0.9 fusion.40
  99.8 1.0 copy-done.7
  100.8 0.6 fusion.104
  101.4 0.7 fusion.57
  102.2 2.4 %collective-permute-start.3 = (f32[384,384]{1,0:T(8,128)S(1)}, f32[384,384]{1,0:T(8,128)S(1)}, u32[]{:S(2)}, u32[]{:S(2)}) collective-permute-start(f32[384,384]{1,0:T(8,128)S(1)} %slice_select_fusion), channel_id=1, source_target_pairs={{0,1},{1,0},{2,3},{3,2},{4,5},{5,4},{6,7},{7,6},{8,9},{9,8},{10,11... | collective-permute-start | bytes 1769480 | tf_op jit(solution)/shard_map/ppermute | solution.py:130
  104.6 0.6 fusion.70
  105.2 1.6 fusion.11
  107.3 23.0 %all_to_all.26 = bf16[16,56,768]{2,1,0:T(8,128)(2,1)S(1)} all-to-all(bf16[16,56,768]{2,1,0:T(8,128)(2,1)S(1)} %pad_maximum_fusion.4), channel_id=1, replica_groups=mesh['dp'=32,'seq'=16] {'seq'}, dimensions={0} | all-to-all | bytes 2752512 | tf_op jit(solution)/shard_map/all_to_all | solution.py:92
  131.5 1.1 reduce.21
  132.7 31.4 %all_to_all.27 = bf16[32,2,576]{2,1,0:T(2,128)(2,1)S(1)} all-to-all(bf16[32,2,576]{2,1,0:T(2,128)(2,1)S(1)} %reshape.109), channel_id=1, replica_groups=mesh['dp'=32,'seq'=16] {'dp'}, dimensions={0} | all-to-all | bytes 147456 | tf_op jit(solution)/shard_map/all_to_all | solution.py:27
  164.4 0.7 broadcast_in_dim.2
  165.1 3.9 %all-to-all-start.4 = ((f32[32,1,1152]{2,1,0:T(1,128)}), f32[32,1,1152]{2,1,0:T(1,128)S(1)}, u32[]{:S(2)}, u32[]{:S(2)}) async-start(f32[32,1,1152]{2,1,0:T(1,128)} %broadcast_in_dim.2), calls=%async_computation.4 | async-start | bytes 294912 | tf_op jit(solution)/shard_map/all_to_all | solution.py:21
  169.0 1.0 slice.212
  170.0 16.0 %all-to-all-done.4 = f32[32,1,1152]{2,1,0:T(1,128)S(1)} async-done(((f32[32,1,1152]{2,1,0:T(1,128)}), f32[32,1,1152]{2,1,0:T(1,128)S(1)}, u32[]{:S(2)}, u32[]{:S(2)}) %all-to-all-start.4) | async-done | bytes 147488 | tf_op jit(solution)/shard_map/all_to_all | solution.py:21
  186.3 0.8 mul.345
  (127 shorter events, 10.8 us)
Async XLA Ops:
  0.6 2.3 %copy-start.21 = (bf16[1,512,768]{2,1,0:T(8,128)(2,1)S(1)}, bf16[1,512,768]{2,1,0:T(8,128)(2,1)}, u32[]{:S(2)}) copy-start(bf16[1,512,768]{2,1,0:T(8,128)(2,1)} %param.9) | copy-start | bytes 2359300
  39.5 8.6 %copy-start.1 = (bf16[16,92,768]{2,1,0:T(8,128)(2,1)}, bf16[16,92,768]{2,1,0:T(8,128)(2,1)S(1)}, u32[]{:S(2)}) copy-start(bf16[16,92,768]{2,1,0:T(8,128)(2,1)S(1)} %all_to_all.25) | copy-start | bytes 6782980
  39.6 4.4 %copy-start.36 = (s32[1,2]{1,0:T(1,128)S(1)}, s32[1,2]{1,0:T(1,128)}, u32[]{:S(2)}) copy-start(s32[1,2]{1,0:T(1,128)} %param.11) | copy-start | bytes 28
  39.6 6.4 %copy-start.34 = (f32[2,384]{1,0:T(2,128)S(1)}, f32[2,384]{1,0:T(2,128)}, u32[]{:S(2)}) copy-start(f32[2,384]{1,0:T(2,128)} %param.15) | copy-start | bytes 9220
  39.6 7.0 %copy-start.35 = (f32[2,384]{1,0:T(2,128)S(1)}, f32[2,384]{1,0:T(2,128)}, u32[]{:S(2)}) copy-start(f32[2,384]{1,0:T(2,128)} %param.14) | copy-start | bytes 9220
  39.6 7.0 %copy-start.28 = (f32[2,768]{1,0:T(2,128)S(1)}, f32[2,768]{1,0:T(2,128)}, u32[]{:S(2)}) copy-start(f32[2,768]{1,0:T(2,128)} %param.13) | copy-start | bytes 18436
  39.7 7.0 %copy-start.29 = (f32[2,768]{1,0:T(2,128)S(1)}, f32[2,768]{1,0:T(2,128)}, u32[]{:S(2)}) copy-start(f32[2,768]{1,0:T(2,128)} %param.12) | copy-start | bytes 18436
  39.7 7.1 %copy-start.22 = (bf16[1,512,768]{2,1,0:T(8,128)(2,1)S(1)}, bf16[1,512,768]{2,1,0:T(8,128)(2,1)}, u32[]{:S(2)}) copy-start(bf16[1,512,768]{2,1,0:T(8,128)(2,1)} %param.10) | copy-start | bytes 2359300
  41.6 13.9 %collective-permute-start = (bf16[16,60,768]{2,0,1:T(8,128)(2,1)}, bf16[16,60,768]{2,0,1:T(8,128)(2,1)}, u32[]{:S(2)}, u32[]{:S(2)}) collective-permute-start(bf16[16,60,768]{2,0,1:T(8,128)(2,1)} %copy.33), channel_id=1, source_target_pairs={{0,1},{1,0},{2,3},{3,2},{4,5},{5,4},{6,7},{7,6},{8,9},{9,8},{10,11... | collective-permute-start | bytes 4423688 | tf_op jit(solution)/shard_map/ppermute | solution.py:112
  46.7 32.4 %copy-start.30 = (f32[768]{0:T(1024)}, f32[768]{0:T(1024)S(1)}, u32[]{:S(2)}) copy-start(f32[768]{0:T(1024)S(1)} %get-tuple-element.12) | copy-start | bytes 9220
  46.7 32.4 %copy-start.32 = (f32[768]{0:T(1024)}, f32[768]{0:T(1024)S(1)}, u32[]{:S(2)}) copy-start(f32[768]{0:T(1024)S(1)} %get-tuple-element.47) | copy-start | bytes 9220
  48.2 31.0 %copy-start.10 = (bf16[16,32,768]{2,1,0:T(8,128)(2,1)}, bf16[16,32,768]{2,1,0:T(8,128)(2,1)S(1)}, u32[]{:S(2)}) copy-start(bf16[16,32,768]{2,1,0:T(8,128)(2,1)S(1)} %slice.185) | copy-start | bytes 2359300
  48.2 28.3 %all-to-all-start.1 = ((bf16[16,68,768]{2,1,0:T(8,128)(2,1)}), bf16[16,68,768]{2,1,0:T(8,128)(2,1)S(1)}, u32[]{:S(2)}, u32[]{:S(2)}) async-start(bf16[16,68,768]{2,1,0:T(8,128)(2,1)} %pad_maximum_fusion.2), calls=%async_computation.1 | async-start | bytes 3538944 | tf_op jit(solution)/shard_map/all_to_all | solution.py:179
  54.4 2.2 %copy-start.2 = (bf16[16,92,768]{2,1,0:T(8,128)(2,1)S(1)}, bf16[16,92,768]{2,1,0:T(8,128)(2,1)}, u32[]{:S(2)}) copy-start(bf16[16,92,768]{2,1,0:T(8,128)(2,1)} %copy-done.1) | copy-start | bytes 6782980
  69.2 1.7 copy-start.13
  70.8 1.2 copy-start.4
  70.9 1.2 copy-start.6
  70.9 1.2 copy-start.14
  71.5 1.1 copy-start.12
  72.1 1.3 copy-start.3
  73.4 5.7 %copy-start.25 = (f32[512,384]{1,0:T(8,128)}, f32[512,384]{1,0:T(8,128)S(1)}, u32[]{:S(2)}) copy-start(f32[512,384]{1,0:T(8,128)S(1)} %fusion.32) | copy-start | bytes 2359300
  76.5 8.1 %copy-start = (bf16[16,68,768]{2,1,0:T(8,128)(2,1)}, bf16[16,68,768]{2,1,0:T(8,128)(2,1)S(1)}, u32[]{:S(2)}) copy-start(bf16[16,68,768]{2,1,0:T(8,128)(2,1)S(1)} %all-to-all-done.1) | copy-start | bytes 5013508
  76.5 2.7 %copy-start.18 = (bf16[384,1,768]{2,1,0:T(2,128)(2,1)S(1)}, bf16[384,1,768]{2,1,0:T(2,128)(2,1)}, u32[]{:S(2)}) copy-start(bf16[384,1,768]{2,1,0:T(2,128)(2,1)} %get-tuple-element.31) | copy-start | bytes 1769476
  76.7 7.9 %collective-permute-start.1 = (bf16[16,36,768]{2,0,1:T(8,128)(2,1)S(1)}, bf16[16,36,768]{2,0,1:T(8,128)(2,1)S(1)}, u32[]{:S(2)}, u32[]{:S(2)}) collective-permute-start(bf16[16,36,768]{2,0,1:T(8,128)(2,1)S(1)} %copy.36), channel_id=1, source_target_pairs={{0,1},{1,0},{2,3},{3,2},{4,5},{5,4},{6,7},{7,6},{8,9},{9,8},{10,11... | collective-permute-start | bytes 2654216 | tf_op jit(solution)/shard_map/ppermute | solution.py:112
  81.3 1.3 copy-start.8
  85.9 1.1 copy-start.17
  86.1 1.5 copy-start.9
  87.6 1.1 copy-start.16
  87.6 1.1 copy-start.27
  88.2 1.3 copy-start.20
  88.2 1.5 copy-start.24
  90.7 1.1 copy-start.23
  92.5 3.1 %slice-start = ((bf16[16,68,768]{2,1,0:T(8,128)(2,1)}), bf16[16,32,768]{2,1,0:T(8,128)(2,1)S(1)}, s32[]{:S(2)}) async-start(bf16[16,68,768]{2,1,0:T(8,128)(2,1)} %copy-done), calls=%async_computation.5 | async-start | bytes 1572864 | tf_op jit(solution)/shard_map/slice | solution.py:180
  92.5 3.1 %copy-start.31 = (f32[768]{0:T(1024)S(1)}, f32[768]{0:T(1024)}, u32[]{:S(2)}) copy-start(f32[768]{0:T(1024)} %copy-done.30) | copy-start | bytes 9220
  92.5 3.0 %copy-start.33 = (f32[768]{0:T(1024)S(1)}, f32[768]{0:T(1024)}, u32[]{:S(2)}) copy-start(f32[768]{0:T(1024)} %copy-done.32) | copy-start | bytes 9220
  92.5 3.0 %copy-start.37 = (bf16[512,768]{1,0:T(8,128)(2,1)S(1)}, bf16[512,768]{1,0:T(8,128)(2,1)}, u32[]{:S(2)}) copy-start(bf16[512,768]{1,0:T(8,128)(2,1)} %get-tuple-element.45) | copy-start | bytes 2359300
  92.6 4.7 %collective-permute-start.2 = (f32[384,384]{1,0:T(8,128)S(1)}, f32[384,384]{1,0:T(8,128)S(1)}, u32[]{:S(2)}, u32[]{:S(2)}) collective-permute-start(f32[384,384]{1,0:T(8,128)S(1)} %slice_select_fusion.1), channel_id=1, source_target_pairs={{0,1},{1,0},{2,3},{3,2},{4,5},{5,4},{6,7},{7,6},{8,9},{9,8},{10,11... | collective-permute-start | bytes 1769480 | tf_op jit(solution)/shard_map/ppermute | solution.py:130
  97.3 1.3 copy-start.19
  97.3 1.5 copy-start.26
  99.7 1.1 copy-start.7
  102.1 2.5 %copy-start.5 = (bf16[1,16,48,384]{3,2,0,1:T(8,128)(2,1)S(1)}, bf16[1,16,48,384]{3,2,0,1:T(8,128)(2,1)}, u32[]{:S(2)}) copy-start(bf16[1,16,48,384]{3,2,0,1:T(8,128)(2,1)} %copy-done.4) | copy-start | bytes 1769476
  102.2 3.0 %copy-start.11 = (bf16[16,32,768]{2,1,0:T(8,128)(2,1)S(1)}, bf16[16,32,768]{2,1,0:T(8,128)(2,1)}, u32[]{:S(2)}) copy-start(bf16[16,32,768]{2,1,0:T(8,128)(2,1)} %copy-done.10) | copy-start | bytes 2359300
  102.2 3.0 %copy-start.15 = (bf16[1,16,48,384]{3,2,0,1:T(8,128)(2,1)S(1)}, bf16[1,16,48,384]{3,2,0,1:T(8,128)(2,1)}, u32[]{:S(2)}) copy-start(bf16[1,16,48,384]{3,2,0,1:T(8,128)(2,1)} %copy-done.14) | copy-start | bytes 1769476
  102.2 4.7 %collective-permute-start.3 = (f32[384,384]{1,0:T(8,128)S(1)}, f32[384,384]{1,0:T(8,128)S(1)}, u32[]{:S(2)}, u32[]{:S(2)}) collective-permute-start(f32[384,384]{1,0:T(8,128)S(1)} %slice_select_fusion), channel_id=1, source_target_pairs={{0,1},{1,0},{2,3},{3,2},{4,5},{5,4},{6,7},{7,6},{8,9},{9,8},{10,11... | collective-permute-start | bytes 1769480 | tf_op jit(solution)/shard_map/ppermute | solution.py:130
  165.1 20.8 %all-to-all-start.4 = ((f32[32,1,1152]{2,1,0:T(1,128)}), f32[32,1,1152]{2,1,0:T(1,128)S(1)}, u32[]{:S(2)}, u32[]{:S(2)}) async-start(f32[32,1,1152]{2,1,0:T(1,128)} %broadcast_in_dim.2), calls=%async_computation.4 | async-start | bytes 294912 | tf_op jit(solution)/shard_map/all_to_all | solution.py:21

commit v15 on v14

--- a/solution.py
+++ b/solution.py
@@ -161,7 +161,7 @@
     block_shape = conv_weight.shape[1:]
     conv_rows = conv_weight[0].size // channels
     first_weights = jnp.concatenate(
-        [conv_weight[0].reshape(-1, channels), point_weight.reshape(-1, channels)]
+        [conv_weight[0].reshape(-1, channels), point_weight[:, 0, :]]
     )
     state_pieces, first_halves = exchanged(
         [
@@ -172,21 +172,19 @@
     )
     state = state_pieces.reshape(-1, channels)
     grad_rows_sent = strided_pieces(output_grad[0], peers)
+    second_weights = jnp.concatenate(
+        [conv_weight[1].reshape(-1, channels), point_weight[:, 1, :]]
+    )
     second_joined = jnp.concatenate(
-        [grad_rows_sent, half_for_each(conv_weight[1], peers, channels)], axis=1
+        [grad_rows_sent, half_for_each(second_weights, peers, channels)], axis=1
     )
     second_joined, state = lax.optimization_barrier((second_joined, state))
     second_arrived = lax.all_to_all(second_joined, "seq", 0, 0, tiled=True)
     grad_pieces = second_arrived[:, : grad_rows_sent.shape[1]]
     second_halves = second_arrived[:, grad_rows_sent.shape[1] :]
-    first_whole = whole_from_halves(first_halves, "seq")
-    first_pieces = first_whole[:, :conv_rows]
-    point_full = first_whole[:, conv_rows:].reshape(-1, *point_weight.shape[1:])
-    second_pieces = whole_from_halves(second_halves, "seq")
-    conv_full = [
-        conv_from_pieces(first_pieces, block_shape),
-        conv_from_pieces(second_pieces, block_shape),
-    ]
+    wholes = [whole_from_halves(first_halves, "seq"), whole_from_halves(second_halves, "seq")]
+    conv_full = [conv_from_pieces(whole[:, :conv_rows], block_shape) for whole in wholes]
+    point_blocks = [whole[:, conv_rows:].reshape(-1, channels) for whole in wholes]
     row_reach = (FIRST_DILATION // peers, SECOND_DILATION // peers)
     saved = []
     for block_index in range(2):
@@ -202,7 +200,7 @@
             conv_full[block_index],
             mid_gain[block_index],
             mid_offset[block_index],
-            point_full[:, block_index, :],
+            point_blocks[block_index],
             kept_flag,
         )
         middle, hidden_act, state = forward_local(*operands)
@@ -211,7 +209,7 @@
     terms = [None, None]
     for block_index in (1, 0):
         normed, middle, hidden_act, kept_flag = saved[block_index]
-        projection = point_full[:, block_index, :]
+        projection = point_blocks[block_index]
         first_operands = (gradient, middle, projection, mid_gain[block_index], kept_flag)
         conv_grad, branch_grad = backward_first(*first_operands)
         terms[block_index] = chip_half(grad_rows(hidden_act, branch_grad), peers, channels)

time: 188 us -> 186 us (0.989)
  waiting for transfers between devices: 16 us -> 24.5 us
  local copies, waits for them, and re-layouts: 33.3 us -> 26 us
  blocking collectives: 90.7 us -> 87.4 us
    all_to_all x1, waiting for transfers between devices: 0.01 us -> 8.56 us  [shards(): second_arrived = lax.all_to_all(second_joined, 'seq', 0, 0, tiled=True)]
    reshape x2 -> x0, local copies, waits for them, and re-layouts: 4.57 us -> none  [the longest x1 3.65 us: shards(): point_full = first_whole[:, conv_rows:].reshape(-1, *point_weight.shape[1:])]
    all_to_all x2, blocking collectives: 59.3 us -> 56.1 us  [exchanged(): arrived = lax.all_to_all(joined, axis, 0, 0, tiled=True)]
    slice x2 -> x3, local copies, waits for them, and re-layouts: 4.52 us -> 2 us  [the longest x1 1.12 us: shards(): point_weight[:, 0, :]]
    unnamed x78 -> x84, local copies, waits for them, and re-layouts: 6.84 us -> 6.2 us
  transfers between devices with their start and end apart: 6 -> 6, of which waited for: 1 -> 2; matrix products, arithmetic and copies ran while one was open for 18% -> 15% of each run, Pallas kernels for 0% -> 0%
where the time goes in v15:
time: 186 us; the launch traced here: 185 us
  blocking collectives  87.4 us (47%)
  local copies, waits for them, and re-layouts  26 us (14%)
  waiting for transfers between devices  24.5 us (13%)
  starting transfers between devices  19 us (10%)
  matrix products  15.2 us (8%)
  other arithmetic  9.66 us (5%)
  between operations  2.75 us (1%)
    all_to_all x2, blocking collectives, exchanged(): arrived = lax.all_to_all(joined, axis, 0, 0, tiled=True)  56.1 us
    all_to_all x1, blocking collectives, summed_over(): arrived = lax.all_to_all(pieces, axis, 0, 0, tiled=True)  31.3 us
    all_to_all x1, waiting for transfers between devices, gathered(): return lax.all_to_all(copies, axis, 0, 0, tiled=True)  16 us
    all_to_all x1, waiting for transfers between devices, shards(): second_arrived = lax.all_to_all(second_joined, 'seq', 0, 0, tiled=True)  8.56 us
    dot_general x8, matrix products, contract_last(): lax.dot_general(left, right, (((1,), (1,)), ((), ())), preferred_element_...  7.53 us
    unnamed x84, local copies, waits for them, and re-layouts  6.2 us
    all_to_all x1, starting transfers between devices, shards(): second_arrived = lax.all_to_all(second_joined, 'seq', 0, 0, tiled=True)  5.58 us
    ppermute x2, starting transfers between devices, whole_from_halves(): partner = lax.ppermute(own_halves, axis, [(i, i ^ 1) for i in range(peers)])  4.8 us
  transfers between devices with their start and end apart: 6, of which 2 were waited for; matrix products, arithmetic and copies ran while one was open for 15% of the time, Pallas kernels for 0%

profile of v15, /device:TPU:6, one launch (start us, length us, event | category | flops | bytes accessed | tf_op | source)
XLA Modules:
  0.0 184.5 jit_solution(16693318237529412210)
XLA Ops:
  0.6 1.1 fusion.92
  1.8 1.0 fusion.91
  3.1 32.0 %all_to_all.25 = bf16[16,80,768]{2,1,0:T(8,128)(2,1)S(1)} all-to-all(bf16[16,80,768]{2,1,0:T(8,128)(2,1)S(1)} %pad_maximum_fusion.1), channel_id=1, replica_groups=mesh['dp'=32,'seq'=16] {'seq'}, dimensions={0} | all-to-all | bytes 3932160 | tf_op jit(solution)/shard_map/all_to_all | solution.py:92
  35.1 1.2 slice.194
  36.3 2.5 %collective-permute-start = (bf16[16,48,768]{2,1,0:T(8,128)(2,1)}, bf16[16,48,768]{2,1,0:T(8,128)(2,1)}, u32[]{:S(2)}, u32[]{:S(2)}) collective-permute-start(bf16[16,48,768]{2,1,0:T(8,128)(2,1)} %slice.194), channel_id=1, source_target_pairs={{0,1},{1,0},{2,3},{3,2},{4,5},{5,4},{6,7},{7,6},{8,9},{9,8},{10,11... | collective-permute-start | bytes 3538952 | tf_op jit(solution)/shard_map/ppermute | solution.py:112
  38.8 0.6 fusion.93
  40.7 0.6 slice_reduce_fusion.4
  41.4 0.6 slice_reduce_fusion
  42.1 1.4 pad_maximum_fusion
  43.6 5.6 %all-to-all-start.1 = ((bf16[16,80,768]{2,1,0:T(8,128)(2,1)}), bf16[16,80,768]{2,1,0:T(8,128)(2,1)S(1)}, u32[]{:S(2)}, u32[]{:S(2)}) async-start(bf16[16,80,768]{2,1,0:T(8,128)(2,1)} %pad_maximum_fusion), calls=%async_computation.1 | async-start | bytes 3932160 | tf_op jit(solution)/shard_map/all_to_all | solution.py:182
  49.2 0.6 fusion.6
  49.8 1.2 fusion.88
  51.0 0.9 copy-done.2
  51.9 1.4 broadcast_select_fusion.3
  53.3 1.0 copy-done.3
  54.4 1.4 pad_maximum_fusion.3
  55.7 3.8 %reshape.91 = bf16[16,3,48,384]{3,2,1,0:T(8,128)(2,1)} reshape(bf16[16,72,768]{2,1,0:T(8,128)(2,1)} %pad_maximum_fusion.3) | data formatting | bytes 3538944 | tf_op jit(solution)/shard_map/reshape | solution.py:121
  59.5 2.5 %fusion.85 = (bf16[1,16,48,384]{3,2,0,1:T(8,128)(2,1)}, bf16[1,16,48,384]{3,2,0,1:T(8,128)(2,1)S(1)}, bf16[1,16,48,384]{3,2,0,1:T(8,128)(2,1)S(1)}) fusion(bf16[3,16,48,384]{3,2,0,1:T(8,128)(2,1)} %bitcast.58), kind=kLoop, calls=%fused_computation.131 | loop fusion | bytes 3538944 | tf_op jit(solution)/shard_map/slice | solution.py:58
  63.1 1.5 convolution_add_fusion.3
  64.5 8.6 %all-to-all-done.1 = bf16[16,80,768]{2,1,0:T(8,128)(2,1)S(1)} async-done(((bf16[16,80,768]{2,1,0:T(8,128)(2,1)}), bf16[16,80,768]{2,1,0:T(8,128)(2,1)S(1)}, u32[]{:S(2)}, u32[]{:S(2)}) %all-to-all-start.1) | async-done | bytes 1966112 | tf_op jit(solution)/shard_map/all_to_all | solution.py:182
  73.2 2.3 %collective-permute-start.1 = (bf16[16,48,768]{2,1,0:T(8,128)(2,1)S(1)}, bf16[16,48,768]{2,1,0:T(8,128)(2,1)S(1)}, u32[]{:S(2)}, u32[]{:S(2)}) collective-permute-start(bf16[16,48,768]{2,1,0:T(8,128)(2,1)S(1)} %slice.201), channel_id=1, source_target_pairs={{0,1},{1,0},{2,3},{3,2},{4,5},{5,4},{6,7},{7,6},{8,9},{9,8},{10,11... | collective-permute-start | bytes 3538952 | tf_op jit(solution)/shard_map/ppermute | solution.py:112
  76.3 2.0 %multiply_convert_fusion = (bf16[512,768]{1,0:T(8,128)(2,1)S(1)}, bf16[512,768]{1,0:T(8,128)(2,1)}) fusion(f32[768]{0:T(1024)S(1)} %copy-done.33, f32[768]{0:T(1024)S(1)} %copy-done.35, bf16[384,768]{1,0:T(8,128)(2,1)S(1)} %bitcast.82, f32[512,384]{1,0:T(8,128)S(1)} %fusion.32, f32[]{:T(128)} %bitcast.13, bf16[512,768]{1,0:T(8,128)(2,1)S(1)} %bitcast.71), kind=kOutput, calls=%fused_computation.41 | convolution fusion | flops 310050816 | bytes 3741700 | tf_op jit(solution)/shard_map/dot_general | solution.py:61
  78.3 1.2 fusion.87
  79.6 1.0 fusion.26
  80.6 1.1 fusion.25
  81.9 0.8 slice.209
  82.9 0.6 reshape.93
  83.7 0.9 copy-done.19
  87.1 0.9 fusion.48
  88.1 0.6 fusion.94
  89.9 2.6 %collective-permute-start.2 = (f32[384,384]{1,0:T(8,128)S(1)}, f32[384,384]{1,0:T(8,128)S(1)}, u32[]{:S(2)}, u32[]{:S(2)}) collective-permute-start(f32[384,384]{1,0:T(8,128)S(1)} %slice_select_fusion.1), channel_id=1, source_target_pairs={{0,1},{1,0},{2,3},{3,2},{4,5},{5,4},{6,7},{7,6},{8,9},{9,8},{10,11... | collective-permute-start | bytes 1769480 | tf_op jit(solution)/shard_map/ppermute | solution.py:130
  92.4 0.6 fusion.66
  93.1 1.6 fusion.24
  94.9 0.9 copy-done.23
  96.0 0.9 fusion.40
  97.0 0.7 fusion.57
  98.0 0.6 fusion.95
  98.7 2.2 %collective-permute-start.3 = (f32[384,384]{1,0:T(8,128)S(1)}, f32[384,384]{1,0:T(8,128)S(1)}, u32[]{:S(2)}, u32[]{:S(2)}) collective-permute-start(f32[384,384]{1,0:T(8,128)S(1)} %slice_select_fusion), channel_id=1, source_target_pairs={{0,1},{1,0},{2,3},{3,2},{4,5},{5,4},{6,7},{7,6},{8,9},{9,8},{10,11... | collective-permute-start | bytes 1769480 | tf_op jit(solution)/shard_map/ppermute | solution.py:130
  100.9 0.6 fusion.63
  101.6 1.6 fusion.11
  103.6 24.1 %all_to_all.26 = bf16[16,56,768]{2,1,0:T(8,128)(2,1)S(1)} all-to-all(bf16[16,56,768]{2,1,0:T(8,128)(2,1)S(1)} %pad_maximum_fusion.4), channel_id=1, replica_groups=mesh['dp'=32,'seq'=16] {'seq'}, dimensions={0} | all-to-all | bytes 2752512 | tf_op jit(solution)/shard_map/all_to_all | solution.py:92
  129.0 1.1 reduce.21
  130.2 31.3 %all_to_all.27 = bf16[32,2,576]{2,1,0:T(2,128)(2,1)S(1)} all-to-all(bf16[32,2,576]{2,1,0:T(2,128)(2,1)S(1)} %reshape.109), channel_id=1, replica_groups=mesh['dp'=32,'seq'=16] {'dp'}, dimensions={0} | all-to-all | bytes 147456 | tf_op jit(solution)/shard_map/all_to_all | solution.py:27
  161.9 0.7 broadcast_in_dim.2
  162.6 3.9 %all-to-all-start.4 = ((f32[32,1,1152]{2,1,0:T(1,128)}), f32[32,1,1152]{2,1,0:T(1,128)S(1)}, u32[]{:S(2)}, u32[]{:S(2)}) async-start(f32[32,1,1152]{2,1,0:T(1,128)} %broadcast_in_dim.2), calls=%async_computation.4 | async-start | bytes 294912 | tf_op jit(solution)/shard_map/all_to_all | solution.py:21
  166.5 1.0 slice.218
  167.4 16.0 %all-to-all-done.4 = f32[32,1,1152]{2,1,0:T(1,128)S(1)} async-done(((f32[32,1,1152]{2,1,0:T(1,128)}), f32[32,1,1152]{2,1,0:T(1,128)S(1)}, u32[]{:S(2)}, u32[]{:S(2)}) %all-to-all-start.4) | async-done | bytes 147488 | tf_op jit(solution)/shard_map/all_to_all | solution.py:21
  183.8 0.8 mul.345
  (131 shorter events, 9.6 us)
Async XLA Ops:
  0.6 2.3 %copy-start.24 = (bf16[1,512,768]{2,1,0:T(8,128)(2,1)S(1)}, bf16[1,512,768]{2,1,0:T(8,128)(2,1)}, u32[]{:S(2)}) copy-start(bf16[1,512,768]{2,1,0:T(8,128)(2,1)} %param.9) | copy-start | bytes 2359300
  35.0 8.5 %copy-start.1 = (bf16[16,80,768]{2,1,0:T(8,128)(2,1)}, bf16[16,80,768]{2,1,0:T(8,128)(2,1)S(1)}, u32[]{:S(2)}) copy-start(bf16[16,80,768]{2,1,0:T(8,128)(2,1)S(1)} %all_to_all.25) | copy-start | bytes 5898244
  35.0 3.7 %copy-start.39 = (s32[1,2]{1,0:T(1,128)S(1)}, s32[1,2]{1,0:T(1,128)}, u32[]{:S(2)}) copy-start(s32[1,2]{1,0:T(1,128)} %param.11) | copy-start | bytes 28
  35.0 5.6 %copy-start.37 = (f32[2,384]{1,0:T(2,128)S(1)}, f32[2,384]{1,0:T(2,128)}, u32[]{:S(2)}) copy-start(f32[2,384]{1,0:T(2,128)} %param.14) | copy-start | bytes 9220
  35.1 5.7 %copy-start.38 = (f32[2,384]{1,0:T(2,128)S(1)}, f32[2,384]{1,0:T(2,128)}, u32[]{:S(2)}) copy-start(f32[2,384]{1,0:T(2,128)} %param.15) | copy-start | bytes 9220
  35.1 6.3 %copy-start.31 = (f32[2,768]{1,0:T(2,128)S(1)}, f32[2,768]{1,0:T(2,128)}, u32[]{:S(2)}) copy-start(f32[2,768]{1,0:T(2,128)} %param.13) | copy-start | bytes 18436
  35.1 6.3 %copy-start.32 = (f32[2,768]{1,0:T(2,128)S(1)}, f32[2,768]{1,0:T(2,128)}, u32[]{:S(2)}) copy-start(f32[2,768]{1,0:T(2,128)} %param.12) | copy-start | bytes 18436
  35.1 7.0 %copy-start.25 = (bf16[1,512,768]{2,1,0:T(8,128)(2,1)S(1)}, bf16[1,512,768]{2,1,0:T(8,128)(2,1)}, u32[]{:S(2)}) copy-start(bf16[1,512,768]{2,1,0:T(8,128)(2,1)} %param.10) | copy-start | bytes 2359300
  36.3 14.8 %collective-permute-start = (bf16[16,48,768]{2,1,0:T(8,128)(2,1)}, bf16[16,48,768]{2,1,0:T(8,128)(2,1)}, u32[]{:S(2)}, u32[]{:S(2)}) collective-permute-start(bf16[16,48,768]{2,1,0:T(8,128)(2,1)} %slice.194), channel_id=1, source_target_pairs={{0,1},{1,0},{2,3},{3,2},{4,5},{5,4},{6,7},{7,6},{8,9},{9,8},{10,11... | collective-permute-start | bytes 3538952 | tf_op jit(solution)/shard_map/ppermute | solution.py:112
  43.6 32.7 %copy-start.11 = (bf16[16,32,768]{2,1,0:T(8,128)(2,1)}, bf16[16,32,768]{2,1,0:T(8,128)(2,1)S(1)}, u32[]{:S(2)}) copy-start(bf16[16,32,768]{2,1,0:T(8,128)(2,1)S(1)} %slice.192) | copy-start | bytes 2359300
  43.6 29.5 %all-to-all-start.1 = ((bf16[16,80,768]{2,1,0:T(8,128)(2,1)}), bf16[16,80,768]{2,1,0:T(8,128)(2,1)S(1)}, u32[]{:S(2)}, u32[]{:S(2)}) async-start(bf16[16,80,768]{2,1,0:T(8,128)(2,1)} %pad_maximum_fusion), calls=%async_computation.1 | async-start | bytes 3932160 | tf_op jit(solution)/shard_map/all_to_all | solution.py:182
  49.8 2.0 %copy-start.2 = (bf16[16,80,768]{2,1,0:T(8,128)(2,1)S(1)}, bf16[16,80,768]{2,1,0:T(8,128)(2,1)}, u32[]{:S(2)}) copy-start(bf16[16,80,768]{2,1,0:T(8,128)(2,1)} %copy-done.1) | copy-start | bytes 5898244
  53.3 1.0 copy-start.3
  59.5 2.5 %copy-start.15 = (bf16[448,768]{1,0:T(8,128)(2,1)S(1)}, bf16[448,768]{1,0:T(8,128)(2,1)}, u32[]{:S(2)}) copy-start(bf16[448,768]{1,0:T(8,128)(2,1)} %get-tuple-element.33) | copy-start | bytes 2064388
  62.0 0.8 copy-start.5
  62.0 1.0 copy-start.7
  64.5 11.0 %copy-start.13 = (f32[512,384]{1,0:T(8,128)S(1)}, f32[512,384]{1,0:T(8,128)}, u32[]{:S(2)}) copy-start(f32[512,384]{1,0:T(8,128)} %convolution_add_fusion.3) | copy-start | bytes 2359300
  73.1 8.6 %copy-start = (bf16[16,80,768]{2,1,0:T(8,128)(2,1)}, bf16[16,80,768]{2,1,0:T(8,128)(2,1)S(1)}, u32[]{:S(2)}) copy-start(bf16[16,80,768]{2,1,0:T(8,128)(2,1)S(1)} %all-to-all-done.1) | copy-start | bytes 5898244
  73.1 2.5 %copy-start.14 = (bf16[448,768]{1,0:T(8,128)(2,1)S(1)}, bf16[448,768]{1,0:T(8,128)(2,1)}, u32[]{:S(2)}) copy-start(bf16[448,768]{1,0:T(8,128)(2,1)} %get-tuple-element.32) | copy-start | bytes 2064388
  73.1 2.5 %copy-start.16 = (bf16[1,16,48,384]{3,2,0,1:T(8,128)(2,1)S(1)}, bf16[1,16,48,384]{3,2,0,1:T(8,128)(2,1)}, u32[]{:S(2)}) copy-start(bf16[1,16,48,384]{3,2,0,1:T(8,128)(2,1)} %get-tuple-element.25) | copy-start | bytes 1769476
  73.1 2.5 %copy-start.30 = (f32[384]{0:T(512)S(1)}, f32[384]{0:T(512)}, u32[]{:S(2)}) copy-start(f32[384]{0:T(512)} %get-tuple-element.17) | copy-start | bytes 4612
  73.2 3.0 %copy-start.4 = (bf16[16,48,768]{2,1,0:T(8,128)(2,1)S(1)}, bf16[16,48,768]{2,1,0:T(8,128)(2,1)}, u32[]{:S(2)}) copy-start(bf16[16,48,768]{2,1,0:T(8,128)(2,1)} %copy-done.3) | copy-start | bytes 3538948
  73.2 8.5 %collective-permute-start.1 = (bf16[16,48,768]{2,1,0:T(8,128)(2,1)S(1)}, bf16[16,48,768]{2,1,0:T(8,128)(2,1)S(1)}, u32[]{:S(2)}, u32[]{:S(2)}) collective-permute-start(bf16[16,48,768]{2,1,0:T(8,128)(2,1)S(1)} %slice.201), channel_id=1, source_target_pairs={{0,1},{1,0},{2,3},{3,2},{4,5},{5,4},{6,7},{7,6},{8,9},{9,8},{10,11... | collective-permute-start | bytes 3538952 | tf_op jit(solution)/shard_map/ppermute | solution.py:112
  75.6 0.7 copy-start.33
  75.6 0.7 copy-start.35
  76.2 2.1 %copy-start.22 = (f32[512,384]{1,0:T(8,128)}, f32[512,384]{1,0:T(8,128)S(1)}, u32[]{:S(2)}) copy-start(f32[512,384]{1,0:T(8,128)S(1)} %fusion.32) | copy-start | bytes 2359300
  76.3 2.0 %copy-start.26 = (bf16[16,24,768]{2,1,0:T(8,128)(2,1)}, bf16[16,24,768]{2,1,0:T(8,128)(2,1)S(1)}, u32[]{:S(2)}) copy-start(bf16[16,24,768]{2,1,0:T(8,128)(2,1)S(1)} %slice.199) | copy-start | bytes 1769476
  78.3 1.3 copy-start.9
  83.5 1.1 copy-start.19
  83.7 1.5 copy-start.10
  85.1 1.1 copy-start.18
  85.1 1.1 copy-start.29
  85.8 1.2 copy-start.21
  85.8 1.3 copy-start.28
  88.0 1.1 copy-start.20
  89.8 3.2 %slice-start = ((bf16[16,80,768]{2,1,0:T(8,128)(2,1)}), bf16[16,32,768]{2,1,0:T(8,128)(2,1)S(1)}, s32[]{:S(2)}) async-start(bf16[16,80,768]{2,1,0:T(8,128)(2,1)} %copy-done), calls=%async_computation.5 | async-start | bytes 1572864 | tf_op jit(solution)/shard_map/slice | solution.py:183
  89.8 3.2 %copy-start.34 = (f32[768]{0:T(1024)S(1)}, f32[768]{0:T(1024)}, u32[]{:S(2)}) copy-start(f32[768]{0:T(1024)} %get-tuple-element.12) | copy-start | bytes 9220
  89.8 3.2 %copy-start.36 = (f32[768]{0:T(1024)S(1)}, f32[768]{0:T(1024)}, u32[]{:S(2)}) copy-start(f32[768]{0:T(1024)} %get-tuple-element.49) | copy-start | bytes 9220
  89.9 3.2 %copy-start.40 = (bf16[512,768]{1,0:T(8,128)(2,1)S(1)}, bf16[512,768]{1,0:T(8,128)(2,1)}, u32[]{:S(2)}) copy-start(bf16[512,768]{1,0:T(8,128)(2,1)} %get-tuple-element.45) | copy-start | bytes 2359300
  89.9 4.9 %collective-permute-start.2 = (f32[384,384]{1,0:T(8,128)S(1)}, f32[384,384]{1,0:T(8,128)S(1)}, u32[]{:S(2)}, u32[]{:S(2)}) collective-permute-start(f32[384,384]{1,0:T(8,128)S(1)} %slice_select_fusion.1), channel_id=1, source_target_pairs={{0,1},{1,0},{2,3},{3,2},{4,5},{5,4},{6,7},{7,6},{8,9},{9,8},{10,11... | collective-permute-start | bytes 1769480 | tf_op jit(solution)/shard_map/ppermute | solution.py:130
  94.7 1.1 copy-start.23
  94.7 1.3 copy-start.27
  97.0 1.1 copy-start.8
  98.0 2.9 %copy-start.6 = (bf16[1,16,48,384]{3,2,0,1:T(8,128)(2,1)S(1)}, bf16[1,16,48,384]{3,2,0,1:T(8,128)(2,1)}, u32[]{:S(2)}) copy-start(bf16[1,16,48,384]{3,2,0,1:T(8,128)(2,1)} %copy-done.5) | copy-start | bytes 1769476
  98.7 2.8 %copy-start.12 = (bf16[16,32,768]{2,1,0:T(8,128)(2,1)S(1)}, bf16[16,32,768]{2,1,0:T(8,128)(2,1)}, u32[]{:S(2)}) copy-start(bf16[16,32,768]{2,1,0:T(8,128)(2,1)} %copy-done.11) | copy-start | bytes 2359300
  98.7 2.8 %copy-start.17 = (bf16[1,16,48,384]{3,2,0,1:T(8,128)(2,1)S(1)}, bf16[1,16,48,384]{3,2,0,1:T(8,128)(2,1)}, u32[]{:S(2)}) copy-start(bf16[1,16,48,384]{3,2,0,1:T(8,128)(2,1)} %get-tuple-element.25) | copy-start | bytes 1769476
  98.7 4.5 %collective-permute-start.3 = (f32[384,384]{1,0:T(8,128)S(1)}, f32[384,384]{1,0:T(8,128)S(1)}, u32[]{:S(2)}, u32[]{:S(2)}) collective-permute-start(f32[384,384]{1,0:T(8,128)S(1)} %slice_select_fusion), channel_id=1, source_target_pairs={{0,1},{1,0},{2,3},{3,2},{4,5},{5,4},{6,7},{7,6},{8,9},{9,8},{10,11... | collective-permute-start | bytes 1769480 | tf_op jit(solution)/shard_map/ppermute | solution.py:130
  162.6 20.8 %all-to-all-start.4 = ((f32[32,1,1152]{2,1,0:T(1,128)}), f32[32,1,1152]{2,1,0:T(1,128)S(1)}, u32[]{:S(2)}, u32[]{:S(2)}) async-start(f32[32,1,1152]{2,1,0:T(1,128)} %broadcast_in_dim.2), calls=%async_computation.4 | async-start | bytes 294912 | tf_op jit(solution)/shard_map/all_to_all | solution.py:21

commit v16 on v15

--- a/solution.py
+++ b/solution.py
@@ -212,7 +212,11 @@
         projection = point_blocks[block_index]
         first_operands = (gradient, middle, projection, mid_gain[block_index], kept_flag)
         conv_grad, branch_grad = backward_first(*first_operands)
-        terms[block_index] = chip_half(grad_rows(hidden_act, branch_grad), peers, channels)
+        term = grad_rows(hidden_act, branch_grad)
+        if block_index == 1:
+            terms[1] = chip_half(term, peers, channels)
+        else:
+            terms[0] = term.astype(jnp.bfloat16).reshape(peers, -1, channels)
         earlier, later = row_shifted(conv_grad, row_reach[block_index])
         second_operands = (
             gradient,
@@ -229,7 +233,7 @@
     first_term, second_term, back_pieces = exchanged(
         terms + [gradient.reshape(peers, -1, channels)], "seq"
     )
-    own_terms = [chip_sum(piece, peers, channels) for piece in (first_term, second_term)]
+    own_terms = [first_term.astype(jnp.float32).sum(axis=0), chip_sum(second_term, peers, channels)]
     summed = reduced_over_dp(jnp.stack(own_terms, axis=1))
     sample_count = sequence_in.shape[0] * lax.axis_size("dp")
     full_length = sequence_in.shape[1] * peers

time: 186 us -> 189 us (1.016)
  blocking collectives: 87.4 us -> 91.8 us
  starting transfers between devices: 19 us -> 16.8 us
    all_to_all x2, blocking collectives: 56.1 us -> 60.7 us  [exchanged(): arrived = lax.all_to_all(joined, axis, 0, 0, tiled=True)]
    ppermute x2 -> x1, starting transfers between devices: 4.77 us -> 2.56 us  [chip_half(): partner = lax.ppermute(given, 'seq', [(i, i ^ 1) for i in range(peers)])]
  transfers between devices with their start and end apart: 6 -> 5, of which waited for: 2 -> 2; matrix products, arithmetic and copies ran while one was open for 15% -> 14% of each run, Pallas kernels for 0% -> 0%
where the time goes in v16:
time: 189 us; the launch traced here: 188 us
  blocking collectives  91.8 us (49%)
  local copies, waits for them, and re-layouts  27.2 us (14%)
  waiting for transfers between devices  24.3 us (13%)
  starting transfers between devices  16.8 us (9%)
  matrix products  15.1 us (8%)
  other arithmetic  9.66 us (5%)
  between operations  2.67 us (1%)
    all_to_all x2, blocking collectives, exchanged(): arrived = lax.all_to_all(joined, axis, 0, 0, tiled=True)  60.7 us
    all_to_all x1, blocking collectives, summed_over(): arrived = lax.all_to_all(pieces, axis, 0, 0, tiled=True)  31.1 us
    all_to_all x1, waiting for transfers between devices, gathered(): return lax.all_to_all(copies, axis, 0, 0, tiled=True)  15.8 us
    all_to_all x1, waiting for transfers between devices, shards(): second_arrived = lax.all_to_all(second_joined, 'seq', 0, 0, tiled=True)  8.56 us
    unnamed x84, local copies, waits for them, and re-layouts  7.64 us
    dot_general x8, matrix products, contract_last(): lax.dot_general(left, right, (((1,), (1,)), ((), ())), preferred_element_...  7.52 us
    all_to_all x1, starting transfers between devices, shards(): second_arrived = lax.all_to_all(second_joined, 'seq', 0, 0, tiled=True)  5.58 us
    ppermute x2, starting transfers between devices, whole_from_halves(): partner = lax.ppermute(own_halves, axis, [(i, i ^ 1) for i in range(peers)])  4.8 us
  transfers between devices with their start and end apart: 5, of which 2 were waited for; matrix products, arithmetic and copies ran while one was open for 14% of the time, Pallas kernels for 0%

profile of v16, /device:TPU:6, one launch (start us, length us, event | category | flops | bytes accessed | tf_op | source)
XLA Modules:
  0.0 187.6 jit_solution(12692106099984711685)
XLA Ops:
  0.6 1.1 fusion.90
  1.8 1.0 fusion.89
  3.1 32.0 %all_to_all.25 = bf16[16,80,768]{2,1,0:T(8,128)(2,1)S(1)} all-to-all(bf16[16,80,768]{2,1,0:T(8,128)(2,1)S(1)} %pad_maximum_fusion.1), channel_id=1, replica_groups=mesh['dp'=32,'seq'=16] {'seq'}, dimensions={0} | all-to-all | bytes 3932160 | tf_op jit(solution)/shard_map/all_to_all | solution.py:92
  35.1 1.2 slice.184
  36.3 2.5 %collective-permute-start = (bf16[16,48,768]{2,1,0:T(8,128)(2,1)}, bf16[16,48,768]{2,1,0:T(8,128)(2,1)}, u32[]{:S(2)}, u32[]{:S(2)}) collective-permute-start(bf16[16,48,768]{2,1,0:T(8,128)(2,1)} %slice.184), channel_id=1, source_target_pairs={{0,1},{1,0},{2,3},{3,2},{4,5},{5,4},{6,7},{7,6},{8,9},{9,8},{10,11... | collective-permute-start | bytes 3538952 | tf_op jit(solution)/shard_map/ppermute | solution.py:112
  38.8 0.6 fusion.91
  40.8 0.6 slice_reduce_fusion.5
  41.4 0.6 slice_reduce_fusion.1
  42.1 1.4 pad_maximum_fusion
  43.6 5.6 %all-to-all-start.1 = ((bf16[16,80,768]{2,1,0:T(8,128)(2,1)}), bf16[16,80,768]{2,1,0:T(8,128)(2,1)S(1)}, u32[]{:S(2)}, u32[]{:S(2)}) async-start(bf16[16,80,768]{2,1,0:T(8,128)(2,1)} %pad_maximum_fusion), calls=%async_computation.1 | async-start | bytes 3932160 | tf_op jit(solution)/shard_map/all_to_all | solution.py:182
  49.2 0.6 fusion.6
  49.9 1.2 fusion.86
  51.1 0.8 copy-done.2
  51.9 1.4 broadcast_select_fusion.3
  53.3 1.0 copy-done.3
  54.4 1.4 pad_maximum_fusion.3
  55.8 3.8 %reshape.88 = bf16[16,3,48,384]{3,2,1,0:T(8,128)(2,1)} reshape(bf16[16,72,768]{2,1,0:T(8,128)(2,1)} %pad_maximum_fusion.3) | data formatting | bytes 3538944 | tf_op jit(solution)/shard_map/reshape | solution.py:121
  59.5 2.5 %fusion.84 = (bf16[1,16,48,384]{3,2,0,1:T(8,128)(2,1)}, bf16[1,16,48,384]{3,2,0,1:T(8,128)(2,1)S(1)}, bf16[1,16,48,384]{3,2,0,1:T(8,128)(2,1)S(1)}) fusion(bf16[3,16,48,384]{3,2,0,1:T(8,128)(2,1)} %bitcast.59), kind=kLoop, calls=%fused_computation.130 | loop fusion | bytes 3538944 | tf_op jit(solution)/shard_map/slice | solution.py:58
  63.1 1.5 convolution_add_fusion.3
  64.5 8.6 %all-to-all-done.1 = bf16[16,80,768]{2,1,0:T(8,128)(2,1)S(1)} async-done(((bf16[16,80,768]{2,1,0:T(8,128)(2,1)}), bf16[16,80,768]{2,1,0:T(8,128)(2,1)S(1)}, u32[]{:S(2)}, u32[]{:S(2)}) %all-to-all-start.1) | async-done | bytes 1966112 | tf_op jit(solution)/shard_map/all_to_all | solution.py:182
  73.2 2.3 %collective-permute-start.1 = (bf16[16,48,768]{2,1,0:T(8,128)(2,1)S(1)}, bf16[16,48,768]{2,1,0:T(8,128)(2,1)S(1)}, u32[]{:S(2)}, u32[]{:S(2)}) collective-permute-start(bf16[16,48,768]{2,1,0:T(8,128)(2,1)S(1)} %slice.191), channel_id=1, source_target_pairs={{0,1},{1,0},{2,3},{3,2},{4,5},{5,4},{6,7},{7,6},{8,9},{9,8},{10,11... | collective-permute-start | bytes 3538952 | tf_op jit(solution)/shard_map/ppermute | solution.py:112
  76.3 2.0 %multiply_convert_fusion = (bf16[512,768]{1,0:T(8,128)(2,1)S(1)}, bf16[512,768]{1,0:T(8,128)(2,1)}) fusion(f32[768]{0:T(1024)S(1)} %copy-done.33, f32[768]{0:T(1024)S(1)} %copy-done.35, bf16[384,768]{1,0:T(8,128)(2,1)S(1)} %bitcast.84, f32[512,384]{1,0:T(8,128)S(1)} %fusion.32, f32[]{:T(128)} %bitcast.13, bf16[512,768]{1,0:T(8,128)(2,1)S(1)} %bitcast.72), kind=kOutput, calls=%fused_computation.42 | convolution fusion | flops 310050816 | bytes 3741700 | tf_op jit(solution)/shard_map/dot_general | solution.py:61
  78.3 1.3 fusion.85
  79.6 1.0 fusion.26
  80.6 1.1 fusion.25
  81.9 0.8 slice.199
  82.9 0.6 reshape.90
  83.7 0.9 copy-done.19
  87.1 0.9 fusion.48
  88.1 0.6 fusion.92
  89.9 2.6 %collective-permute-start.2 = (f32[384,384]{1,0:T(8,128)S(1)}, f32[384,384]{1,0:T(8,128)S(1)}, u32[]{:S(2)}, u32[]{:S(2)}) collective-permute-start(f32[384,384]{1,0:T(8,128)S(1)} %slice_select_fusion), channel_id=1, source_target_pairs={{0,1},{1,0},{2,3},{3,2},{4,5},{5,4},{6,7},{7,6},{8,9},{9,8},{10,11... | collective-permute-start | bytes 1769480 | tf_op jit(solution)/shard_map/ppermute | solution.py:130
  92.4 0.6 fusion.65
  93.1 1.6 fusion.24
  94.9 0.9 copy-done.23
  96.0 0.9 fusion.40
  97.0 0.7 convolution_convert_fusion
  97.8 1.0 copy-done.8
  98.8 0.6 fusion.93
  99.8 0.6 fusion.62
  100.7 1.6 fusion.11
  102.7 28.7 %all_to_all.26 = bf16[16,68,768]{2,1,0:T(8,128)(2,1)S(1)} all-to-all(bf16[16,68,768]{2,1,0:T(8,128)(2,1)S(1)} %pad_maximum_fusion.4), channel_id=1, replica_groups=mesh['dp'=32,'seq'=16] {'seq'}, dimensions={0} | all-to-all | bytes 3342336 | tf_op jit(solution)/shard_map/all_to_all | solution.py:92
  132.4 1.1 reduce.22
  133.6 31.1 %all_to_all.27 = bf16[32,2,576]{2,1,0:T(2,128)(2,1)S(1)} all-to-all(bf16[32,2,576]{2,1,0:T(2,128)(2,1)S(1)} %reshape.106), channel_id=1, replica_groups=mesh['dp'=32,'seq'=16] {'dp'}, dimensions={0} | all-to-all | bytes 147456 | tf_op jit(solution)/shard_map/all_to_all | solution.py:27
  165.0 0.7 broadcast_in_dim.2
  165.7 3.9 %all-to-all-start.4 = ((f32[32,1,1152]{2,1,0:T(1,128)}), f32[32,1,1152]{2,1,0:T(1,128)S(1)}, u32[]{:S(2)}, u32[]{:S(2)}) async-start(f32[32,1,1152]{2,1,0:T(1,128)} %broadcast_in_dim.2), calls=%async_computation.4 | async-start | bytes 294912 | tf_op jit(solution)/shard_map/all_to_all | solution.py:21
  169.6 1.1 slice.206
  170.7 15.8 %all-to-all-done.4 = f32[32,1,1152]{2,1,0:T(1,128)S(1)} async-done(((f32[32,1,1152]{2,1,0:T(1,128)}), f32[32,1,1152]{2,1,0:T(1,128)S(1)}, u32[]{:S(2)}, u32[]{:S(2)}) %all-to-all-start.4) | async-done | bytes 147488 | tf_op jit(solution)/shard_map/all_to_all | solution.py:21
  186.9 0.8 mul.345
  (123 shorter events, 9.7 us)
Async XLA Ops:
  0.6 2.3 %copy-start.24 = (bf16[1,512,768]{2,1,0:T(8,128)(2,1)S(1)}, bf16[1,512,768]{2,1,0:T(8,128)(2,1)}, u32[]{:S(2)}) copy-start(bf16[1,512,768]{2,1,0:T(8,128)(2,1)} %param.9) | copy-start | bytes 2359300
  35.0 8.5 %copy-start.1 = (bf16[16,80,768]{2,1,0:T(8,128)(2,1)}, bf16[16,80,768]{2,1,0:T(8,128)(2,1)S(1)}, u32[]{:S(2)}) copy-start(bf16[16,80,768]{2,1,0:T(8,128)(2,1)S(1)} %all_to_all.25) | copy-start | bytes 5898244
  35.0 3.7 %copy-start.39 = (s32[1,2]{1,0:T(1,128)S(1)}, s32[1,2]{1,0:T(1,128)}, u32[]{:S(2)}) copy-start(s32[1,2]{1,0:T(1,128)} %param.11) | copy-start | bytes 28
  35.0 5.7 %copy-start.37 = (f32[2,384]{1,0:T(2,128)S(1)}, f32[2,384]{1,0:T(2,128)}, u32[]{:S(2)}) copy-start(f32[2,384]{1,0:T(2,128)} %param.14) | copy-start | bytes 9220
  35.1 5.7 %copy-start.38 = (f32[2,384]{1,0:T(2,128)S(1)}, f32[2,384]{1,0:T(2,128)}, u32[]{:S(2)}) copy-start(f32[2,384]{1,0:T(2,128)} %param.15) | copy-start | bytes 9220
  35.1 6.3 %copy-start.31 = (f32[2,768]{1,0:T(2,128)S(1)}, f32[2,768]{1,0:T(2,128)}, u32[]{:S(2)}) copy-start(f32[2,768]{1,0:T(2,128)} %param.13) | copy-start | bytes 18436
  35.1 6.3 %copy-start.32 = (f32[2,768]{1,0:T(2,128)S(1)}, f32[2,768]{1,0:T(2,128)}, u32[]{:S(2)}) copy-start(f32[2,768]{1,0:T(2,128)} %param.12) | copy-start | bytes 18436
  35.1 7.0 %copy-start.25 = (bf16[1,512,768]{2,1,0:T(8,128)(2,1)S(1)}, bf16[1,512,768]{2,1,0:T(8,128)(2,1)}, u32[]{:S(2)}) copy-start(bf16[1,512,768]{2,1,0:T(8,128)(2,1)} %param.10) | copy-start | bytes 2359300
  36.3 14.8 %collective-permute-start = (bf16[16,48,768]{2,1,0:T(8,128)(2,1)}, bf16[16,48,768]{2,1,0:T(8,128)(2,1)}, u32[]{:S(2)}, u32[]{:S(2)}) collective-permute-start(bf16[16,48,768]{2,1,0:T(8,128)(2,1)} %slice.184), channel_id=1, source_target_pairs={{0,1},{1,0},{2,3},{3,2},{4,5},{5,4},{6,7},{7,6},{8,9},{9,8},{10,11... | collective-permute-start | bytes 3538952 | tf_op jit(solution)/shard_map/ppermute | solution.py:112
  43.6 32.7 %copy-start.11 = (bf16[16,32,768]{2,1,0:T(8,128)(2,1)}, bf16[16,32,768]{2,1,0:T(8,128)(2,1)S(1)}, u32[]{:S(2)}) copy-start(bf16[16,32,768]{2,1,0:T(8,128)(2,1)S(1)} %slice.182) | copy-start | bytes 2359300
  43.6 29.5 %all-to-all-start.1 = ((bf16[16,80,768]{2,1,0:T(8,128)(2,1)}), bf16[16,80,768]{2,1,0:T(8,128)(2,1)S(1)}, u32[]{:S(2)}, u32[]{:S(2)}) async-start(bf16[16,80,768]{2,1,0:T(8,128)(2,1)} %pad_maximum_fusion), calls=%async_computation.1 | async-start | bytes 3932160 | tf_op jit(solution)/shard_map/all_to_all | solution.py:182
  49.9 2.0 %copy-start.2 = (bf16[16,80,768]{2,1,0:T(8,128)(2,1)S(1)}, bf16[16,80,768]{2,1,0:T(8,128)(2,1)}, u32[]{:S(2)}) copy-start(bf16[16,80,768]{2,1,0:T(8,128)(2,1)} %copy-done.1) | copy-start | bytes 5898244
  53.3 1.0 copy-start.3
  59.5 2.5 %copy-start.15 = (bf16[448,768]{1,0:T(8,128)(2,1)S(1)}, bf16[448,768]{1,0:T(8,128)(2,1)}, u32[]{:S(2)}) copy-start(bf16[448,768]{1,0:T(8,128)(2,1)} %get-tuple-element.31) | copy-start | bytes 2064388
  62.0 0.8 copy-start.5
  62.1 1.0 copy-start.7
  64.5 11.0 %copy-start.13 = (f32[512,384]{1,0:T(8,128)S(1)}, f32[512,384]{1,0:T(8,128)}, u32[]{:S(2)}) copy-start(f32[512,384]{1,0:T(8,128)} %convolution_add_fusion.3) | copy-start | bytes 2359300
  73.1 8.6 %copy-start = (bf16[16,80,768]{2,1,0:T(8,128)(2,1)}, bf16[16,80,768]{2,1,0:T(8,128)(2,1)S(1)}, u32[]{:S(2)}) copy-start(bf16[16,80,768]{2,1,0:T(8,128)(2,1)S(1)} %all-to-all-done.1) | copy-start | bytes 5898244
  73.1 2.5 %copy-start.14 = (bf16[448,768]{1,0:T(8,128)(2,1)S(1)}, bf16[448,768]{1,0:T(8,128)(2,1)}, u32[]{:S(2)}) copy-start(bf16[448,768]{1,0:T(8,128)(2,1)} %get-tuple-element.30) | copy-start | bytes 2064388
  73.1 2.5 %copy-start.16 = (bf16[1,16,48,384]{3,2,0,1:T(8,128)(2,1)S(1)}, bf16[1,16,48,384]{3,2,0,1:T(8,128)(2,1)}, u32[]{:S(2)}) copy-start(bf16[1,16,48,384]{3,2,0,1:T(8,128)(2,1)} %get-tuple-element.25) | copy-start | bytes 1769476
  73.1 2.5 %copy-start.30 = (f32[384]{0:T(512)S(1)}, f32[384]{0:T(512)}, u32[]{:S(2)}) copy-start(f32[384]{0:T(512)} %get-tuple-element.17) | copy-start | bytes 4612
  73.2 3.0 %copy-start.4 = (bf16[16,48,768]{2,1,0:T(8,128)(2,1)S(1)}, bf16[16,48,768]{2,1,0:T(8,128)(2,1)}, u32[]{:S(2)}) copy-start(bf16[16,48,768]{2,1,0:T(8,128)(2,1)} %copy-done.3) | copy-start | bytes 3538948
  73.2 8.5 %collective-permute-start.1 = (bf16[16,48,768]{2,1,0:T(8,128)(2,1)S(1)}, bf16[16,48,768]{2,1,0:T(8,128)(2,1)S(1)}, u32[]{:S(2)}, u32[]{:S(2)}) collective-permute-start(bf16[16,48,768]{2,1,0:T(8,128)(2,1)S(1)} %slice.191), channel_id=1, source_target_pairs={{0,1},{1,0},{2,3},{3,2},{4,5},{5,4},{6,7},{7,6},{8,9},{9,8},{10,11... | collective-permute-start | bytes 3538952 | tf_op jit(solution)/shard_map/ppermute | solution.py:112
  75.6 0.7 copy-start.33
  75.6 0.7 copy-start.35
  76.2 2.1 %copy-start.22 = (f32[512,384]{1,0:T(8,128)}, f32[512,384]{1,0:T(8,128)S(1)}, u32[]{:S(2)}) copy-start(f32[512,384]{1,0:T(8,128)S(1)} %fusion.32) | copy-start | bytes 2359300
  76.3 2.0 %copy-start.26 = (bf16[16,24,768]{2,1,0:T(8,128)(2,1)}, bf16[16,24,768]{2,1,0:T(8,128)(2,1)S(1)}, u32[]{:S(2)}) copy-start(bf16[16,24,768]{2,1,0:T(8,128)(2,1)S(1)} %slice.189) | copy-start | bytes 1769476
  78.3 1.3 copy-start.9
  83.5 1.1 copy-start.19
  83.7 1.5 copy-start.10
  85.1 1.1 copy-start.18
  85.1 1.1 copy-start.29
  85.7 1.2 copy-start.21
  85.8 1.3 copy-start.28
  88.0 1.1 copy-start.20
  89.8 3.2 %slice-start = ((bf16[16,80,768]{2,1,0:T(8,128)(2,1)}), bf16[16,32,768]{2,1,0:T(8,128)(2,1)S(1)}, s32[]{:S(2)}) async-start(bf16[16,80,768]{2,1,0:T(8,128)(2,1)} %copy-done), calls=%async_computation.5 | async-start | bytes 1572864 | tf_op jit(solution)/shard_map/slice | solution.py:183
  89.8 3.2 %copy-start.34 = (f32[768]{0:T(1024)S(1)}, f32[768]{0:T(1024)}, u32[]{:S(2)}) copy-start(f32[768]{0:T(1024)} %get-tuple-element.12) | copy-start | bytes 9220
  89.8 3.2 %copy-start.36 = (f32[768]{0:T(1024)S(1)}, f32[768]{0:T(1024)}, u32[]{:S(2)}) copy-start(f32[768]{0:T(1024)} %get-tuple-element.47) | copy-start | bytes 9220
  89.9 3.2 %copy-start.40 = (bf16[512,768]{1,0:T(8,128)(2,1)S(1)}, bf16[512,768]{1,0:T(8,128)(2,1)}, u32[]{:S(2)}) copy-start(bf16[512,768]{1,0:T(8,128)(2,1)} %get-tuple-element.43) | copy-start | bytes 2359300
  89.9 4.9 %collective-permute-start.2 = (f32[384,384]{1,0:T(8,128)S(1)}, f32[384,384]{1,0:T(8,128)S(1)}, u32[]{:S(2)}, u32[]{:S(2)}) collective-permute-start(f32[384,384]{1,0:T(8,128)S(1)} %slice_select_fusion), channel_id=1, source_target_pairs={{0,1},{1,0},{2,3},{3,2},{4,5},{5,4},{6,7},{7,6},{8,9},{9,8},{10,11... | collective-permute-start | bytes 1769480 | tf_op jit(solution)/shard_map/ppermute | solution.py:130
  94.7 1.1 copy-start.23
  94.7 1.3 copy-start.27
  97.7 1.1 copy-start.8
  98.7 1.1 copy-start.6
  99.3 1.2 copy-start.12
  99.3 1.3 copy-start.17
  165.7 20.7 %all-to-all-start.4 = ((f32[32,1,1152]{2,1,0:T(1,128)}), f32[32,1,1152]{2,1,0:T(1,128)S(1)}, u32[]{:S(2)}, u32[]{:S(2)}) async-start(f32[32,1,1152]{2,1,0:T(1,128)} %broadcast_in_dim.2), calls=%async_computation.4 | async-start | bytes 294912 | tf_op jit(solution)/shard_map/all_to_all | solution.py:21

commit v17 on v15

--- a/solution.py
+++ b/solution.py
@@ -178,7 +178,6 @@
     second_joined = jnp.concatenate(
         [grad_rows_sent, half_for_each(second_weights, peers, channels)], axis=1
     )
-    second_joined, state = lax.optimization_barrier((second_joined, state))
     second_arrived = lax.all_to_all(second_joined, "seq", 0, 0, tiled=True)
     grad_pieces = second_arrived[:, : grad_rows_sent.shape[1]]
     second_halves = second_arrived[:, grad_rows_sent.shape[1] :]

time: 186 us -> 198 us (1.065)
  blocking collectives: 87.4 us -> 54.6 us
  waiting for transfers between devices: 24.5 us -> 54.8 us
  starting transfers between devices: 19 us -> 29.2 us
  other arithmetic: 9.66 us -> 15 us
    all_to_all x2 -> x1, blocking collectives: 56.1 us -> 24.1 us  [exchanged(): arrived = lax.all_to_all(joined, axis, 0, 0, tiled=True)]
    all_to_all x0 -> x1, waiting for transfers between devices: none -> 17.6 us  [exchanged(): arrived = lax.all_to_all(joined, axis, 0, 0, tiled=True)]
    all_to_all x1, waiting for transfers between devices: 8.56 us -> 21.3 us  [shards(): second_arrived = lax.all_to_all(second_joined, 'seq', 0, 0, tiled=True)]
    all_to_all x0 -> x1, starting transfers between devices: none -> 7 us  [exchanged(): arrived = lax.all_to_all(joined, axis, 0, 0, tiled=True)]
    all_to_all x1, starting transfers between devices: 5.58 us -> 9.39 us  [shards(): second_arrived = lax.all_to_all(second_joined, 'seq', 0, 0, tiled=True)]
    slice x4, local copies, waits for them, and re-layouts: 2.36 us -> 5.65 us  [exchanged(): pieces.append(arrived[:, offset:offset + part.shape[1]])]
    reshape x2, local copies, waits for them, and re-layouts: 4.41 us -> 1.28 us  [conv_from_pieces(): parts = pieces.reshape(-1, taps, rows, hidden)]
    tanh x0 -> x1, other arithmetic: none -> 2.94 us  [gelu_tanh(): return jax.nn.gelu(values, approximate=True)]
  transfers between devices with their start and end apart: 6 -> 7, of which waited for: 2 -> 3; matrix products, arithmetic and copies ran while one was open for 15% -> 14% of each run, Pallas kernels for 0% -> 0%
where the time goes in v17:
time: 198 us; the launch traced here: 197 us
  waiting for transfers between devices  54.8 us (28%)
  blocking collectives  54.6 us (28%)
  starting transfers between devices  29.2 us (15%)
  local copies, waits for them, and re-layouts  24.6 us (12%)
  matrix products  15.7 us (8%)
  other arithmetic  15 us (8%)
  between operations  2.61 us (1%)
    all_to_all x1, blocking collectives, summed_over(): arrived = lax.all_to_all(pieces, axis, 0, 0, tiled=True)  30.5 us
    all_to_all x1, blocking collectives, exchanged(): arrived = lax.all_to_all(joined, axis, 0, 0, tiled=True)  24.1 us
    all_to_all x1, waiting for transfers between devices, shards(): second_arrived = lax.all_to_all(second_joined, 'seq', 0, 0, tiled=True)  21.3 us
    all_to_all x1, waiting for transfers between devices, exchanged(): arrived = lax.all_to_all(joined, axis, 0, 0, tiled=True)  17.6 us
    all_to_all x1, waiting for transfers between devices, gathered(): return lax.all_to_all(copies, axis, 0, 0, tiled=True)  16 us
    dot_general x8, matrix products, contract_last(): lax.dot_general(left, right, (((1,), (1,)), ((), ())), preferred_element_...  9.83 us
    all_to_all x1, starting transfers between devices, shards(): second_arrived = lax.all_to_all(second_joined, 'seq', 0, 0, tiled=True)  9.39 us
    all_to_all x1, starting transfers between devices, exchanged(): arrived = lax.all_to_all(joined, axis, 0, 0, tiled=True)  7 us
  transfers between devices with their start and end apart: 7, of which 3 were waited for; matrix products, arithmetic and copies ran while one was open for 14% of the time, Pallas kernels for 0%

profile of v17, /device:TPU:6, one launch (start us, length us, event | category | flops | bytes accessed | tf_op | source)
XLA Modules:
  0.0 196.5 jit_solution(9728133261848545871)
XLA Ops:
  0.6 1.1 fusion.101
  1.8 1.0 fusion.100
  2.9 1.4 pad_maximum_fusion.1
  4.4 9.4 %all-to-all-start.1 = ((bf16[16,80,768]{2,1,0:T(8,128)(2,1)}), bf16[16,80,768]{2,1,0:T(8,128)(2,1)S(1)}, u32[]{:S(2)}, u32[]{:S(2)}) async-start(bf16[16,80,768]{2,1,0:T(8,128)(2,1)} %pad_maximum_fusion.1), calls=%async_computation.1 | async-start | bytes 3932160 | tf_op jit(solution)/shard_map/all_to_all | solution.py:181
  13.9 1.0 copy-done.14
  14.9 1.5 pad_maximum_fusion
  16.4 21.3 %all-to-all-done.1 = bf16[16,80,768]{2,1,0:T(8,128)(2,1)S(1)} async-done(((bf16[16,80,768]{2,1,0:T(8,128)(2,1)}), bf16[16,80,768]{2,1,0:T(8,128)(2,1)S(1)}, u32[]{:S(2)}, u32[]{:S(2)}) %all-to-all-start.1) | async-done | bytes 1966112 | tf_op jit(solution)/shard_map/all_to_all | solution.py:181
  37.6 7.0 %all-to-all-start = ((bf16[16,80,768]{2,1,0:T(8,128)(2,1)}), bf16[16,80,768]{2,1,0:T(8,128)(2,1)}, u32[]{:S(2)}, u32[]{:S(2)}) async-start(bf16[16,80,768]{2,1,0:T(8,128)(2,1)} %pad_maximum_fusion), calls=%async_computation | async-start | bytes 3932160 | tf_op jit(solution)/shard_map/all_to_all | solution.py:92
  46.6 0.6 slice_reduce_fusion.4
  47.2 0.6 slice_reduce_fusion
  47.8 1.1 slice.201
  48.9 2.0 %collective-permute-start.1 = (bf16[16,48,768]{2,1,0:T(8,128)(2,1)}, bf16[16,48,768]{2,1,0:T(8,128)(2,1)S(1)}, u32[]{:S(2)}, u32[]{:S(2)}) collective-permute-start(bf16[16,48,768]{2,1,0:T(8,128)(2,1)} %slice.201), channel_id=1, source_target_pairs={{0,1},{1,0},{2,3},{3,2},{4,5},{5,4},{6,7},{7,6},{8,9},{9,8},{10,11... | collective-permute-start | bytes 3538952 | tf_op jit(solution)/shard_map/ppermute | solution.py:112
  51.0 17.6 %all-to-all-done = bf16[16,80,768]{2,1,0:T(8,128)(2,1)} async-done(((bf16[16,80,768]{2,1,0:T(8,128)(2,1)}), bf16[16,80,768]{2,1,0:T(8,128)(2,1)}, u32[]{:S(2)}, u32[]{:S(2)}) %all-to-all-start) | async-done | bytes 1966112 | tf_op jit(solution)/shard_map/all_to_all | solution.py:92
  68.6 2.4 %slice.194 = bf16[16,48,768]{2,1,0:T(8,128)(2,1)} slice(bf16[16,80,768]{2,1,0:T(8,128)(2,1)} %all-to-all-done), slice={[0:16], [32:80], [0:768]} | slice | bytes 2359296 | tf_op jit(solution)/shard_map/slice | solution.py:96
  70.9 2.1 %collective-permute-start = (bf16[16,48,768]{2,1,0:T(8,128)(2,1)}, bf16[16,48,768]{2,1,0:T(8,128)(2,1)}, u32[]{:S(2)}, u32[]{:S(2)}) collective-permute-start(bf16[16,48,768]{2,1,0:T(8,128)(2,1)} %slice.194), channel_id=1, source_target_pairs={{0,1},{1,0},{2,3},{3,2},{4,5},{5,4},{6,7},{7,6},{8,9},{9,8},{10,11... | collective-permute-start | bytes 3538952 | tf_op jit(solution)/shard_map/ppermute | solution.py:112
  73.1 1.0 fusion.27
  74.0 2.7 %fusion.25 = bf16[16,32,768]{2,1,0:T(8,128)(2,1)} fusion(f32[768]{0:T(1024)S(1)} %get-tuple-element.9, f32[768]{0:T(1024)S(1)} %get-tuple-element.46, bf16[16,80,768]{2,1,0:T(8,128)(2,1)} %all-to-all-done), kind=kLoop, calls=%fused_computation.36 | loop fusion | flops 4718592 | bytes 1579008 | tf_op jit(solution)/shard_map/convert_element_type | solution.py:192
  76.7 2.9 %fusion.5 = (f32[512,768]{1,0:T(8,128)}, bf16[512,768]{1,0:T(8,128)(2,1)S(1)}) fusion(f32[768]{0:T(1024)S(1)} %get-tuple-element.9, f32[768]{0:T(1024)S(1)} %get-tuple-element.46, bf16[16,80,768]{2,1,0:T(8,128)(2,1)} %all-to-all-done), kind=kLoop, calls=%fused_computation.16 | loop fusion | flops 4718592 | bytes 3151872 | tf_op jit(solution)/shard_map/tanh | solution.py:38
  79.6 1.0 fusion.26
  80.7 2.2 %slice.192 = bf16[16,32,768]{2,1,0:T(8,128)(2,1)} slice(bf16[16,80,768]{2,1,0:T(8,128)(2,1)} %all-to-all-done), slice={[0:16], [0:32], [0:768]} | slice | bytes 1572864 | tf_op jit(solution)/shard_map/slice | solution.py:96
  82.9 1.2 fusion.97
  84.2 0.9 slice.209
  85.2 0.6 reshape.103
  85.9 1.3 fusion.93
  87.1 1.8 broadcast_select_fusion.3
  88.9 0.9 slice.199
  89.9 0.6 reshape.101
  90.8 0.9 copy-done.5
  94.2 1.1 multiply_convert_fusion
  95.5 1.0 copy-done.2
  99.0 0.9 fusion.57
  101.7 2.5 %collective-permute-start.2 = (f32[384,384]{1,0:T(8,128)S(1)}, f32[384,384]{1,0:T(8,128)S(1)}, u32[]{:S(2)}, u32[]{:S(2)}) collective-permute-start(f32[384,384]{1,0:T(8,128)S(1)} %slice_select_fusion.1), channel_id=1, source_target_pairs={{0,1},{1,0},{2,3},{3,2},{4,5},{5,4},{6,7},{7,6},{8,9},{9,8},{10,11... | collective-permute-start | bytes 1769480 | tf_op jit(solution)/shard_map/ppermute | solution.py:130
  104.2 0.6 fusion.75
  104.8 2.5 %fusion.17 = bf16[512,768]{1,0:T(8,128)(2,1)} fusion(bf16[16,32,768]{2,1,0:T(8,128)(2,1)S(1)} %slice-done, f32[512,768]{1,0:T(8,128)S(1)} %fusion.75, f32[512,768]{1,0:T(8,128)S(1)} %fusion.103, bf16[512,768]{1,0:T(8,128)(2,1)S(1)} %get-tuple-element.43, bf16[768,384]{1,0:T(8,128)(2,1)S(1)} %bitcast.99, f32[768]{0:T(1024)S(1)} %copy-done.21, ...), kind=kOutput, calls=%fused_computation.28 | convolution fusion | flops 312999936 | bytes 6395904 | tf_op jit(solution)/shard_map/dot_general | solution.py:42
  107.6 2.6 %fusion.49 = bf16[512,384]{1,0:T(8,128)(2,1)S(1)} fusion(f32[512,384]{1,0:T(8,128)} %copy-done.11, bf16[384,768]{1,0:T(8,128)(2,1)} %bitcast.105, bf16[512,768]{1,0:T(8,128)(2,1)} %fusion.17, f32[]{:T(128)} %bitcast.10, f32[384]{0:T(512)S(1)} %get-tuple-element.11), kind=kOutput, calls=%fused_computation.80 | convolution fusion | flops 307298304 | bytes 2557444 | tf_op jit(solution)/shard_map/dot_general | solution.py:42
  110.2 0.7 fusion.66
  111.0 0.6 fusion.104
  111.6 2.3 %collective-permute-start.3 = (f32[384,384]{1,0:T(8,128)S(1)}, f32[384,384]{1,0:T(8,128)S(1)}, u32[]{:S(2)}, u32[]{:S(2)}) collective-permute-start(f32[384,384]{1,0:T(8,128)S(1)} %slice_select_fusion), channel_id=1, source_target_pairs={{0,1},{1,0},{2,3},{3,2},{4,5},{5,4},{6,7},{7,6},{8,9},{9,8},{10,11... | collective-permute-start | bytes 1769480 | tf_op jit(solution)/shard_map/ppermute | solution.py:130
  113.9 0.6 fusion.72
  114.5 1.4 fusion.1
  116.4 24.1 %all_to_all.25 = bf16[16,56,768]{2,1,0:T(8,128)(2,1)S(1)} all-to-all(bf16[16,56,768]{2,1,0:T(8,128)(2,1)S(1)} %pad_maximum_fusion.4), channel_id=1, replica_groups=mesh['dp'=32,'seq'=16] {'seq'}, dimensions={0} | all-to-all | bytes 2752512 | tf_op jit(solution)/shard_map/all_to_all | solution.py:92
  141.8 1.1 reduce.21
  143.0 30.5 %all_to_all.26 = bf16[32,2,576]{2,1,0:T(2,128)(2,1)S(1)} all-to-all(bf16[32,2,576]{2,1,0:T(2,128)(2,1)S(1)} %reshape.120), channel_id=1, replica_groups=mesh['dp'=32,'seq'=16] {'dp'}, dimensions={0} | all-to-all | bytes 147456 | tf_op jit(solution)/shard_map/all_to_all | solution.py:27
  173.8 0.7 broadcast_in_dim.2
  174.6 3.9 %all-to-all-start.4 = ((f32[32,1,1152]{2,1,0:T(1,128)}), f32[32,1,1152]{2,1,0:T(1,128)S(1)}, u32[]{:S(2)}, u32[]{:S(2)}) async-start(f32[32,1,1152]{2,1,0:T(1,128)} %broadcast_in_dim.2), calls=%async_computation.4 | async-start | bytes 294912 | tf_op jit(solution)/shard_map/all_to_all | solution.py:21
  178.4 1.0 slice.218
  179.4 16.0 %all-to-all-done.4 = f32[32,1,1152]{2,1,0:T(1,128)S(1)} async-done(((f32[32,1,1152]{2,1,0:T(1,128)}), f32[32,1,1152]{2,1,0:T(1,128)S(1)}, u32[]{:S(2)}, u32[]{:S(2)}) %all-to-all-start.4) | async-done | bytes 147488 | tf_op jit(solution)/shard_map/all_to_all | solution.py:21
  195.8 0.8 mul.368
  (105 shorter events, 11.1 us)
Async XLA Ops:
  0.6 2.3 %copy-start.13 = (bf16[1,512,768]{2,1,0:T(8,128)(2,1)S(1)}, bf16[1,512,768]{2,1,0:T(8,128)(2,1)}, u32[]{:S(2)}) copy-start(bf16[1,512,768]{2,1,0:T(8,128)(2,1)} %param.10) | copy-start | bytes 2359300
  4.4 33.3 %all-to-all-start.1 = ((bf16[16,80,768]{2,1,0:T(8,128)(2,1)}), bf16[16,80,768]{2,1,0:T(8,128)(2,1)S(1)}, u32[]{:S(2)}, u32[]{:S(2)}) async-start(bf16[16,80,768]{2,1,0:T(8,128)(2,1)} %pad_maximum_fusion.1), calls=%async_computation.1 | async-start | bytes 3932160 | tf_op jit(solution)/shard_map/all_to_all | solution.py:181
  13.7 1.1 copy-start.14
  16.4 28.3 %copy-start.25 = (s32[1,2]{1,0:T(1,128)S(1)}, s32[1,2]{1,0:T(1,128)}, u32[]{:S(2)}) copy-start(s32[1,2]{1,0:T(1,128)} %param.11) | copy-start | bytes 28
  16.4 30.2 %copy-start.23 = (f32[2,384]{1,0:T(2,128)S(1)}, f32[2,384]{1,0:T(2,128)}, u32[]{:S(2)}) copy-start(f32[2,384]{1,0:T(2,128)} %param.14) | copy-start | bytes 9220
  16.4 30.2 %copy-start.24 = (f32[2,384]{1,0:T(2,128)S(1)}, f32[2,384]{1,0:T(2,128)}, u32[]{:S(2)}) copy-start(f32[2,384]{1,0:T(2,128)} %param.15) | copy-start | bytes 9220
  16.4 30.8 %copy-start.19 = (f32[2,768]{1,0:T(2,128)S(1)}, f32[2,768]{1,0:T(2,128)}, u32[]{:S(2)}) copy-start(f32[2,768]{1,0:T(2,128)} %param.13) | copy-start | bytes 18436
  16.4 30.8 %copy-start.20 = (f32[2,768]{1,0:T(2,128)S(1)}, f32[2,768]{1,0:T(2,128)}, u32[]{:S(2)}) copy-start(f32[2,768]{1,0:T(2,128)} %param.12) | copy-start | bytes 18436
  37.6 46.4 %copy-start = (bf16[16,80,768]{2,1,0:T(8,128)(2,1)}, bf16[16,80,768]{2,1,0:T(8,128)(2,1)S(1)}, u32[]{:S(2)}) copy-start(bf16[16,80,768]{2,1,0:T(8,128)(2,1)S(1)} %all-to-all-done.1) | copy-start | bytes 5898244
  37.6 30.9 %all-to-all-start = ((bf16[16,80,768]{2,1,0:T(8,128)(2,1)}), bf16[16,80,768]{2,1,0:T(8,128)(2,1)}, u32[]{:S(2)}, u32[]{:S(2)}) async-start(bf16[16,80,768]{2,1,0:T(8,128)(2,1)} %pad_maximum_fusion), calls=%async_computation | async-start | bytes 3932160 | tf_op jit(solution)/shard_map/all_to_all | solution.py:92
  48.9 35.2 %collective-permute-start.1 = (bf16[16,48,768]{2,1,0:T(8,128)(2,1)}, bf16[16,48,768]{2,1,0:T(8,128)(2,1)S(1)}, u32[]{:S(2)}, u32[]{:S(2)}) collective-permute-start(bf16[16,48,768]{2,1,0:T(8,128)(2,1)} %slice.201), channel_id=1, source_target_pairs={{0,1},{1,0},{2,3},{3,2},{4,5},{5,4},{6,7},{7,6},{8,9},{9,8},{10,11... | collective-permute-start | bytes 3538952 | tf_op jit(solution)/shard_map/ppermute | solution.py:112
  70.9 16.2 %collective-permute-start = (bf16[16,48,768]{2,1,0:T(8,128)(2,1)}, bf16[16,48,768]{2,1,0:T(8,128)(2,1)}, u32[]{:S(2)}, u32[]{:S(2)}) collective-permute-start(bf16[16,48,768]{2,1,0:T(8,128)(2,1)} %slice.194), channel_id=1, source_target_pairs={{0,1},{1,0},{2,3},{3,2},{4,5},{5,4},{6,7},{7,6},{8,9},{9,8},{10,11... | collective-permute-start | bytes 3538952 | tf_op jit(solution)/shard_map/ppermute | solution.py:112
  90.6 1.1 copy-start.5
  90.8 1.5 copy-start.3
  92.3 1.1 copy-start.4
  92.3 1.1 copy-start.18
  92.9 1.2 copy-start.8
  92.9 1.3 copy-start.15
  92.9 1.3 copy-start.21
  92.9 1.3 copy-start.22
  93.9 1.4 copy-start.11
  95.4 1.1 copy-start.2
  95.5 1.6 copy-start.1
  97.0 1.1 copy-start.6
  97.0 1.1 copy-start.17
  97.6 1.2 copy-start.10
  97.6 1.3 copy-start.16
  99.9 1.1 copy-start.9
  101.7 3.1 %slice-start = ((bf16[16,80,768]{2,1,0:T(8,128)(2,1)}), bf16[16,32,768]{2,1,0:T(8,128)(2,1)S(1)}, s32[]{:S(2)}) async-start(bf16[16,80,768]{2,1,0:T(8,128)(2,1)} %copy-done), calls=%async_computation.5 | async-start | bytes 1572864 | tf_op jit(solution)/shard_map/slice | solution.py:182
  101.7 5.7 %collective-permute-start.2 = (f32[384,384]{1,0:T(8,128)S(1)}, f32[384,384]{1,0:T(8,128)S(1)}, u32[]{:S(2)}, u32[]{:S(2)}) collective-permute-start(f32[384,384]{1,0:T(8,128)S(1)} %slice_select_fusion.1), channel_id=1, source_target_pairs={{0,1},{1,0},{2,3},{3,2},{4,5},{5,4},{6,7},{7,6},{8,9},{9,8},{10,11... | collective-permute-start | bytes 1769480 | tf_op jit(solution)/shard_map/ppermute | solution.py:130
  107.5 2.6 %copy-start.12 = (f32[512,384]{1,0:T(8,128)S(1)}, f32[512,384]{1,0:T(8,128)}, u32[]{:S(2)}) copy-start(f32[512,384]{1,0:T(8,128)} %copy-done.11) | copy-start | bytes 2359300
  107.5 2.6 %copy-start.26 = (bf16[512,768]{1,0:T(8,128)(2,1)S(1)}, bf16[512,768]{1,0:T(8,128)(2,1)}, u32[]{:S(2)}) copy-start(bf16[512,768]{1,0:T(8,128)(2,1)} %fusion.17) | copy-start | bytes 2359300
  111.6 2.9 %copy-start.7 = (f32[512,768]{1,0:T(8,128)S(1)}, f32[512,768]{1,0:T(8,128)}, u32[]{:S(2)}) copy-start(f32[512,768]{1,0:T(8,128)} %get-tuple-element.18) | copy-start | bytes 4718596
  111.6 4.3 %collective-permute-start.3 = (f32[384,384]{1,0:T(8,128)S(1)}, f32[384,384]{1,0:T(8,128)S(1)}, u32[]{:S(2)}, u32[]{:S(2)}) collective-permute-start(f32[384,384]{1,0:T(8,128)S(1)} %slice_select_fusion), channel_id=1, source_target_pairs={{0,1},{1,0},{2,3},{3,2},{4,5},{5,4},{6,7},{7,6},{8,9},{9,8},{10,11... | collective-permute-start | bytes 1769480 | tf_op jit(solution)/shard_map/ppermute | solution.py:130
  174.6 20.8 %all-to-all-start.4 = ((f32[32,1,1152]{2,1,0:T(1,128)}), f32[32,1,1152]{2,1,0:T(1,128)S(1)}, u32[]{:S(2)}, u32[]{:S(2)}) async-start(f32[32,1,1152]{2,1,0:T(1,128)} %broadcast_in_dim.2), calls=%async_computation.4 | async-start | bytes 294912 | tf_op jit(solution)/shard_map/all_to_all | solution.py:21

commit v18 on v15

--- a/solution.py
+++ b/solution.py
@@ -163,25 +163,21 @@
     first_weights = jnp.concatenate(
         [conv_weight[0].reshape(-1, channels), point_weight[:, 0, :]]
     )
-    state_pieces, first_halves = exchanged(
+    state_pieces, grad_pieces, first_halves = exchanged(
         [
             strided_pieces(sequence_in[0], peers),
+            strided_pieces(output_grad[0], peers),
             half_for_each(first_weights, peers, channels),
         ],
         "seq",
     )
     state = state_pieces.reshape(-1, channels)
-    grad_rows_sent = strided_pieces(output_grad[0], peers)
     second_weights = jnp.concatenate(
         [conv_weight[1].reshape(-1, channels), point_weight[:, 1, :]]
     )
-    second_joined = jnp.concatenate(
-        [grad_rows_sent, half_for_each(second_weights, peers, channels)], axis=1
-    )
+    second_joined = half_for_each(second_weights, peers, channels)
     second_joined, state = lax.optimization_barrier((second_joined, state))
-    second_arrived = lax.all_to_all(second_joined, "seq", 0, 0, tiled=True)
-    grad_pieces = second_arrived[:, : grad_rows_sent.shape[1]]
-    second_halves = second_arrived[:, grad_rows_sent.shape[1] :]
+    second_halves = lax.all_to_all(second_joined, "seq", 0, 0, tiled=True)
     wholes = [whole_from_halves(first_halves, "seq"), whole_from_halves(second_halves, "seq")]
     conv_full = [conv_from_pieces(whole[:, :conv_rows], block_shape) for whole in wholes]
     point_blocks = [whole[:, conv_rows:].reshape(-1, channels) for whole in wholes]

time: 186 us -> 195 us (1.048)
  blocking collectives: 87.4 us -> 52.9 us
  waiting for transfers between devices: 24.5 us -> 58.7 us
  starting transfers between devices: 19 us -> 29.4 us
    all_to_all x1 -> x2, waiting for transfers between devices: 8.56 us -> 42.7 us  [the longest x1 33.2 us: exchanged(): arrived = lax.all_to_all(joined, axis, 0, 0, tiled=True)]
    all_to_all x2 -> x1, blocking collectives: 56.1 us -> 22.4 us  [exchanged(): arrived = lax.all_to_all(joined, axis, 0, 0, tiled=True)]
    all_to_all x1 -> x2, starting transfers between devices: 5.58 us -> 16.7 us  [the longest x1 9.55 us: exchanged(): arrived = lax.all_to_all(joined, axis, 0, 0, tiled=True)]
    slice x2, local copies, waits for them, and re-layouts: 2.69 us -> 0.36 us  [forward_local(): weight[2]]
    unnamed x84 -> x76, local copies, waits for them, and re-layouts: 6.2 us -> 5.5 us
  transfers between devices with their start and end apart: 6 -> 7, of which waited for: 2 -> 3; matrix products, arithmetic and copies ran while one was open for 15% -> 13% of each run, Pallas kernels for 0% -> 0%
where the time goes in v18:
time: 195 us; the launch traced here: 194 us
  waiting for transfers between devices  58.7 us (30%)
  blocking collectives  52.9 us (27%)
  starting transfers between devices  29.4 us (15%)
  local copies, waits for them, and re-layouts  24.8 us (13%)
  matrix products  14.3 us (7%)
  other arithmetic  11.3 us (6%)
  between operations  2.54 us (1%)
    all_to_all x1, waiting for transfers between devices, exchanged(): arrived = lax.all_to_all(joined, axis, 0, 0, tiled=True)  33.2 us
    all_to_all x1, blocking collectives, summed_over(): arrived = lax.all_to_all(pieces, axis, 0, 0, tiled=True)  30.5 us
    all_to_all x1, blocking collectives, exchanged(): arrived = lax.all_to_all(joined, axis, 0, 0, tiled=True)  22.4 us
    all_to_all x1, waiting for transfers between devices, gathered(): return lax.all_to_all(copies, axis, 0, 0, tiled=True)  16 us
    all_to_all x1, waiting for transfers between devices, shards(): second_halves = lax.all_to_all(second_joined, 'seq', 0, 0, tiled=True)  9.58 us
    all_to_all x1, starting transfers between devices, exchanged(): arrived = lax.all_to_all(joined, axis, 0, 0, tiled=True)  9.55 us
    dot_general x8, matrix products, contract_last(): lax.dot_general(left, right, (((1,), (1,)), ((), ())), preferred_element_...  7.53 us
    all_to_all x1, starting transfers between devices, shards(): second_halves = lax.all_to_all(second_joined, 'seq', 0, 0, tiled=True)  7.18 us
  transfers between devices with their start and end apart: 7, of which 3 were waited for; matrix products, arithmetic and copies ran while one was open for 13% of the time, Pallas kernels for 0%

profile of v18, /device:TPU:6, one launch (start us, length us, event | category | flops | bytes accessed | tf_op | source)
XLA Modules:
  0.0 194.0 jit_solution(3343961523689369140)
XLA Ops:
  0.6 1.2 fusion.93
  1.8 1.0 fusion.92
  3.0 1.7 pad_maximum_fusion
  4.7 9.6 %all-to-all-start = ((bf16[16,112,768]{2,1,0:T(8,128)(2,1)}), bf16[16,112,768]{2,1,0:T(8,128)(2,1)S(1)}, u32[]{:S(2)}, u32[]{:S(2)}) async-start(bf16[16,112,768]{2,1,0:T(8,128)(2,1)} %pad_maximum_fusion), calls=%async_computation | async-start | bytes 5505024 | tf_op jit(solution)/shard_map/all_to_all | solution.py:92
  14.4 0.6 slice_reduce_fusion.4
  15.0 0.6 slice_reduce_fusion
  15.6 33.2 %all-to-all-done = bf16[16,112,768]{2,1,0:T(8,128)(2,1)S(1)} async-done(((bf16[16,112,768]{2,1,0:T(8,128)(2,1)}), bf16[16,112,768]{2,1,0:T(8,128)(2,1)S(1)}, u32[]{:S(2)}, u32[]{:S(2)}) %all-to-all-start) | async-done | bytes 2752544 | tf_op jit(solution)/shard_map/all_to_all | solution.py:92
  48.8 1.1 slice.190
  49.9 1.9 collective-permute-start
  51.8 1.4 fusion.84
  53.2 1.1 tile.21
  54.3 7.2 %all-to-all-start.1 = ((bf16[16,48,768]{2,1,0:T(8,128)(2,1)}), bf16[16,48,768]{2,1,0:T(8,128)(2,1)}, u32[]{:S(2)}, u32[]{:S(2)}) async-start(bf16[16,48,768]{2,1,0:T(8,128)(2,1)} %bitcast.68), calls=%async_computation.1 | async-start | bytes 2359296 | tf_op jit(solution)/shard_map/all_to_all | solution.py:180
  63.2 1.1 fusion.26
  64.3 1.0 fusion.25
  65.3 0.6 fusion.6
  66.0 1.2 fusion.89
  67.2 9.6 %all-to-all-done.1 = bf16[16,48,768]{2,1,0:T(8,128)(2,1)} async-done(((bf16[16,48,768]{2,1,0:T(8,128)(2,1)}), bf16[16,48,768]{2,1,0:T(8,128)(2,1)}, u32[]{:S(2)}, u32[]{:S(2)}) %all-to-all-start.1) | async-done | bytes 1179680 | tf_op jit(solution)/shard_map/all_to_all | solution.py:180
  76.8 2.2 %collective-permute-start.1 = (bf16[16,48,768]{2,1,0:T(8,128)(2,1)}, bf16[16,48,768]{2,1,0:T(8,128)(2,1)}, u32[]{:S(2)}, u32[]{:S(2)}) collective-permute-start(bf16[16,48,768]{2,1,0:T(8,128)(2,1)} %all-to-all-done.1), channel_id=1, source_target_pairs={{0,1},{1,0},{2,3},{3,2},{4,5},{5,4},{6,7},{7,6},{8,9},{9,8},{10,11... | collective-permute-start | bytes 3538952 | tf_op jit(solution)/shard_map/ppermute | solution.py:112
  79.0 1.4 broadcast_select_fusion.3
  80.4 0.8 slice.195
  81.2 1.3 pad_maximum_fusion.2
  82.6 2.6 %reshape.91 = bf16[16,3,48,384]{3,2,1,0:T(8,128)(2,1)S(1)} reshape(bf16[16,72,768]{2,1,0:T(8,128)(2,1)} %pad_maximum_fusion.2) | data formatting | bytes 3538944 | tf_op jit(solution)/shard_map/reshape | solution.py:121
  85.4 0.9 copy-done.10
  88.8 2.0 %multiply_convert_fusion = (bf16[512,768]{1,0:T(8,128)(2,1)S(1)}, bf16[512,768]{1,0:T(8,128)(2,1)}) fusion(f32[768]{0:T(1024)S(1)} %copy-done.29, f32[768]{0:T(1024)S(1)} %copy-done.31, bf16[384,768]{1,0:T(8,128)(2,1)S(1)} %bitcast.82, f32[512,384]{1,0:T(8,128)S(1)} %fusion.32, f32[]{:T(128)} %bitcast.13, bf16[512,768]{1,0:T(8,128)(2,1)S(1)} %bitcast.71), kind=kOutput, calls=%fused_computation.40 | convolution fusion | flops 310050816 | bytes 3741700 | tf_op jit(solution)/shard_map/dot_general | solution.py:61
  90.8 1.2 fusion.88
  92.1 1.8 broadcast_select_fusion.1
  93.9 0.9 slice.204
  94.9 0.6 reshape.93
  95.8 0.9 copy-done.14
  99.2 0.9 fusion.48
  100.2 0.6 fusion.95
  101.9 2.5 %collective-permute-start.2 = (f32[384,384]{1,0:T(8,128)S(1)}, f32[384,384]{1,0:T(8,128)S(1)}, u32[]{:S(2)}, u32[]{:S(2)}) collective-permute-start(f32[384,384]{1,0:T(8,128)S(1)} %slice_select_fusion.1), channel_id=1, source_target_pairs={{0,1},{1,0},{2,3},{3,2},{4,5},{5,4},{6,7},{7,6},{8,9},{9,8},{10,11... | collective-permute-start | bytes 1769480 | tf_op jit(solution)/shard_map/ppermute | solution.py:130
  104.4 0.6 fusion.66
  105.0 1.6 fusion.24
  106.9 0.9 copy-done.19
  108.0 0.9 fusion.40
  108.9 0.7 fusion.57
  110.7 2.3 %collective-permute-start.3 = (f32[384,384]{1,0:T(8,128)S(1)}, f32[384,384]{1,0:T(8,128)S(1)}, u32[]{:S(2)}, u32[]{:S(2)}) collective-permute-start(f32[384,384]{1,0:T(8,128)S(1)} %slice_select_fusion), channel_id=1, source_target_pairs={{0,1},{1,0},{2,3},{3,2},{4,5},{5,4},{6,7},{7,6},{8,9},{9,8},{10,11... | collective-permute-start | bytes 1769480 | tf_op jit(solution)/shard_map/ppermute | solution.py:130
  113.0 0.6 fusion.63
  113.6 1.6 fusion.11
  115.7 22.4 %all_to_all.25 = bf16[16,56,768]{2,1,0:T(8,128)(2,1)S(1)} all-to-all(bf16[16,56,768]{2,1,0:T(8,128)(2,1)S(1)} %pad_maximum_fusion.3), channel_id=1, replica_groups=mesh['dp'=32,'seq'=16] {'seq'}, dimensions={0} | all-to-all | bytes 2752512 | tf_op jit(solution)/shard_map/all_to_all | solution.py:92
  139.4 1.1 reduce.21
  140.6 30.5 %all_to_all.26 = bf16[32,2,576]{2,1,0:T(2,128)(2,1)S(1)} all-to-all(bf16[32,2,576]{2,1,0:T(2,128)(2,1)S(1)} %reshape.109), channel_id=1, replica_groups=mesh['dp'=32,'seq'=16] {'dp'}, dimensions={0} | all-to-all | bytes 147456 | tf_op jit(solution)/shard_map/all_to_all | solution.py:27
  171.3 0.7 broadcast_in_dim.2
  172.1 3.9 %all-to-all-start.4 = ((f32[32,1,1152]{2,1,0:T(1,128)}), f32[32,1,1152]{2,1,0:T(1,128)S(1)}, u32[]{:S(2)}, u32[]{:S(2)}) async-start(f32[32,1,1152]{2,1,0:T(1,128)} %broadcast_in_dim.2), calls=%async_computation.4 | async-start | bytes 294912 | tf_op jit(solution)/shard_map/all_to_all | solution.py:21
  175.9 1.0 slice.213
  176.9 16.0 %all-to-all-done.4 = f32[32,1,1152]{2,1,0:T(1,128)S(1)} async-done(((f32[32,1,1152]{2,1,0:T(1,128)}), f32[32,1,1152]{2,1,0:T(1,128)S(1)}, u32[]{:S(2)}, u32[]{:S(2)}) %all-to-all-start.4) | async-done | bytes 147488 | tf_op jit(solution)/shard_map/all_to_all | solution.py:21
  193.3 0.8 mul.345
  (120 shorter events, 11.3 us)
Async XLA Ops:
  0.6 2.3 %copy-start.20 = (bf16[1,512,768]{2,1,0:T(8,128)(2,1)S(1)}, bf16[1,512,768]{2,1,0:T(8,128)(2,1)}, u32[]{:S(2)}) copy-start(bf16[1,512,768]{2,1,0:T(8,128)(2,1)} %param.10) | copy-start | bytes 2359300
  0.6 2.3 %copy-start.21 = (bf16[1,512,768]{2,1,0:T(8,128)(2,1)S(1)}, bf16[1,512,768]{2,1,0:T(8,128)(2,1)}, u32[]{:S(2)}) copy-start(bf16[1,512,768]{2,1,0:T(8,128)(2,1)} %param.9) | copy-start | bytes 2359300
  4.7 9.6 %copy-start.33 = (f32[2,384]{1,0:T(2,128)S(1)}, f32[2,384]{1,0:T(2,128)}, u32[]{:S(2)}) copy-start(f32[2,384]{1,0:T(2,128)} %param.14) | copy-start | bytes 9220
  4.7 9.6 %copy-start.34 = (f32[2,384]{1,0:T(2,128)S(1)}, f32[2,384]{1,0:T(2,128)}, u32[]{:S(2)}) copy-start(f32[2,384]{1,0:T(2,128)} %param.15) | copy-start | bytes 9220
  4.7 10.3 %copy-start.27 = (f32[2,768]{1,0:T(2,128)S(1)}, f32[2,768]{1,0:T(2,128)}, u32[]{:S(2)}) copy-start(f32[2,768]{1,0:T(2,128)} %param.13) | copy-start | bytes 18436
  4.7 10.3 %copy-start.28 = (f32[2,768]{1,0:T(2,128)S(1)}, f32[2,768]{1,0:T(2,128)}, u32[]{:S(2)}) copy-start(f32[2,768]{1,0:T(2,128)} %param.12) | copy-start | bytes 18436
  4.7 44.1 %all-to-all-start = ((bf16[16,112,768]{2,1,0:T(8,128)(2,1)}), bf16[16,112,768]{2,1,0:T(8,128)(2,1)S(1)}, u32[]{:S(2)}, u32[]{:S(2)}) async-start(bf16[16,112,768]{2,1,0:T(8,128)(2,1)} %pad_maximum_fusion), calls=%async_computation | async-start | bytes 5505024 | tf_op jit(solution)/shard_map/all_to_all | solution.py:92
  49.9 29.1 %collective-permute-start = (bf16[16,48,768]{2,1,0:T(8,128)(2,1)}, bf16[16,48,768]{2,1,0:T(8,128)(2,1)}, u32[]{:S(2)}, u32[]{:S(2)}) collective-permute-start(bf16[16,48,768]{2,1,0:T(8,128)(2,1)} %slice.190), channel_id=1, source_target_pairs={{0,1},{1,0},{2,3},{3,2},{4,5},{5,4},{6,7},{7,6},{8,9},{9,8},{10,11... | collective-permute-start | bytes 3538952 | tf_op jit(solution)/shard_map/ppermute | solution.py:112
  53.2 8.3 %copy-start.35 = (s32[1,2]{1,0:T(1,128)S(1)}, s32[1,2]{1,0:T(1,128)}, u32[]{:S(2)}) copy-start(s32[1,2]{1,0:T(1,128)} %param.11) | copy-start | bytes 28
  54.3 22.5 %all-to-all-start.1 = ((bf16[16,48,768]{2,1,0:T(8,128)(2,1)}), bf16[16,48,768]{2,1,0:T(8,128)(2,1)}, u32[]{:S(2)}, u32[]{:S(2)}) async-start(bf16[16,48,768]{2,1,0:T(8,128)(2,1)} %bitcast.68), calls=%async_computation.1 | async-start | bytes 2359296 | tf_op jit(solution)/shard_map/all_to_all | solution.py:180
  63.2 2.1 %copy-start.6 = (bf16[16,32,768]{2,1,0:T(8,128)(2,1)S(1)}, bf16[16,32,768]{2,1,0:T(8,128)(2,1)}, u32[]{:S(2)}) copy-start(bf16[16,32,768]{2,1,0:T(8,128)(2,1)} %get-tuple-element.21) | copy-start | bytes 2359300
  76.8 15.4 %collective-permute-start.1 = (bf16[16,48,768]{2,1,0:T(8,128)(2,1)}, bf16[16,48,768]{2,1,0:T(8,128)(2,1)}, u32[]{:S(2)}, u32[]{:S(2)}) collective-permute-start(bf16[16,48,768]{2,1,0:T(8,128)(2,1)} %all-to-all-done.1), channel_id=1, source_target_pairs={{0,1},{1,0},{2,3},{3,2},{4,5},{5,4},{6,7},{7,6},{8,9},{9,8},{10,11... | collective-permute-start | bytes 3538952 | tf_op jit(solution)/shard_map/ppermute | solution.py:112
  85.1 1.1 copy-start.10
  85.3 2.1 %copy-start = (bf16[1,16,48,384]{3,2,0,1:T(8,128)(2,1)}, bf16[1,16,48,384]{3,2,0,1:T(8,128)(2,1)S(1)}, u32[]{:S(2)}) copy-start(bf16[1,16,48,384]{3,2,0,1:T(8,128)(2,1)S(1)} %get-tuple-element.29) | copy-start | bytes 1769476
  85.3 2.1 %copy-start.2 = (bf16[1,16,48,384]{3,2,0,1:T(8,128)(2,1)}, bf16[1,16,48,384]{3,2,0,1:T(8,128)(2,1)S(1)}, u32[]{:S(2)}) copy-start(bf16[1,16,48,384]{3,2,0,1:T(8,128)(2,1)S(1)} %get-tuple-element.28) | copy-start | bytes 1769476
  85.4 2.1 %copy-start.11 = (bf16[1,16,48,384]{3,2,0,1:T(8,128)(2,1)}, bf16[1,16,48,384]{3,2,0,1:T(8,128)(2,1)S(1)}, u32[]{:S(2)}) copy-start(bf16[1,16,48,384]{3,2,0,1:T(8,128)(2,1)S(1)} %get-tuple-element.27) | copy-start | bytes 1769476
  86.8 1.1 copy-start.9
  86.8 1.1 copy-start.26
  87.4 1.2 copy-start.7
  87.4 1.3 copy-start.22
  87.5 1.3 copy-start.29
  87.5 1.3 copy-start.31
  88.5 2.3 %copy-start.18 = (f32[512,384]{1,0:T(8,128)}, f32[512,384]{1,0:T(8,128)S(1)}, u32[]{:S(2)}) copy-start(f32[512,384]{1,0:T(8,128)S(1)} %fusion.32) | copy-start | bytes 2359300
  90.8 1.3 copy-start.4
  95.6 1.1 copy-start.14
  95.8 1.5 copy-start.5
  97.2 1.1 copy-start.13
  97.2 1.1 copy-start.25
  97.8 1.2 copy-start.16
  97.8 1.3 copy-start.24
  100.1 1.1 copy-start.15
  101.9 3.1 %copy-start.17 = (bf16[16,32,768]{2,1,0:T(8,128)(2,1)S(1)}, bf16[16,32,768]{2,1,0:T(8,128)(2,1)}, u32[]{:S(2)}) copy-start(bf16[16,32,768]{2,1,0:T(8,128)(2,1)} %get-tuple-element.20) | copy-start | bytes 2359300
  101.9 3.1 %copy-start.30 = (f32[768]{0:T(1024)S(1)}, f32[768]{0:T(1024)}, u32[]{:S(2)}) copy-start(f32[768]{0:T(1024)} %get-tuple-element.12) | copy-start | bytes 9220
  101.9 3.1 %copy-start.32 = (f32[768]{0:T(1024)S(1)}, f32[768]{0:T(1024)}, u32[]{:S(2)}) copy-start(f32[768]{0:T(1024)} %get-tuple-element.51) | copy-start | bytes 9220
  101.9 3.1 %copy-start.36 = (bf16[512,768]{1,0:T(8,128)(2,1)S(1)}, bf16[512,768]{1,0:T(8,128)(2,1)}, u32[]{:S(2)}) copy-start(bf16[512,768]{1,0:T(8,128)(2,1)} %get-tuple-element.47) | copy-start | bytes 2359300
  101.9 4.8 %collective-permute-start.2 = (f32[384,384]{1,0:T(8,128)S(1)}, f32[384,384]{1,0:T(8,128)S(1)}, u32[]{:S(2)}, u32[]{:S(2)}) collective-permute-start(f32[384,384]{1,0:T(8,128)S(1)} %slice_select_fusion.1), channel_id=1, source_target_pairs={{0,1},{1,0},{2,3},{3,2},{4,5},{5,4},{6,7},{7,6},{8,9},{9,8},{10,11... | collective-permute-start | bytes 1769480 | tf_op jit(solution)/shard_map/ppermute | solution.py:130
  106.7 1.1 copy-start.19
  106.7 1.3 copy-start.23
  108.9 1.1 copy-start.3
  110.0 3.0 %copy-start.1 = (bf16[1,16,48,384]{3,2,0,1:T(8,128)(2,1)S(1)}, bf16[1,16,48,384]{3,2,0,1:T(8,128)(2,1)}, u32[]{:S(2)}) copy-start(bf16[1,16,48,384]{3,2,0,1:T(8,128)(2,1)} %copy-done) | copy-start | bytes 1769476
  110.7 2.9 %copy-start.8 = (bf16[16,32,768]{2,1,0:T(8,128)(2,1)S(1)}, bf16[16,32,768]{2,1,0:T(8,128)(2,1)}, u32[]{:S(2)}) copy-start(bf16[16,32,768]{2,1,0:T(8,128)(2,1)} %get-tuple-element.21) | copy-start | bytes 2359300
  110.7 2.9 %copy-start.12 = (bf16[1,16,48,384]{3,2,0,1:T(8,128)(2,1)S(1)}, bf16[1,16,48,384]{3,2,0,1:T(8,128)(2,1)}, u32[]{:S(2)}) copy-start(bf16[1,16,48,384]{3,2,0,1:T(8,128)(2,1)} %copy-done.11) | copy-start | bytes 1769476
  110.7 4.6 %collective-permute-start.3 = (f32[384,384]{1,0:T(8,128)S(1)}, f32[384,384]{1,0:T(8,128)S(1)}, u32[]{:S(2)}, u32[]{:S(2)}) collective-permute-start(f32[384,384]{1,0:T(8,128)S(1)} %slice_select_fusion), channel_id=1, source_target_pairs={{0,1},{1,0},{2,3},{3,2},{4,5},{5,4},{6,7},{7,6},{8,9},{9,8},{10,11... | collective-permute-start | bytes 1769480 | tf_op jit(solution)/shard_map/ppermute | solution.py:130
  172.1 20.8 %all-to-all-start.4 = ((f32[32,1,1152]{2,1,0:T(1,128)}), f32[32,1,1152]{2,1,0:T(1,128)S(1)}, u32[]{:S(2)}, u32[]{:S(2)}) async-start(f32[32,1,1152]{2,1,0:T(1,128)} %broadcast_in_dim.2), calls=%async_computation.4 | async-start | bytes 294912 | tf_op jit(solution)/shard_map/all_to_all | solution.py:21

commit v19 on v15

--- a/solution.py
+++ b/solution.py
@@ -230,10 +230,10 @@
         terms + [gradient.reshape(peers, -1, channels)], "seq"
     )
     own_terms = [chip_sum(piece, peers, channels) for piece in (first_term, second_term)]
-    summed = reduced_over_dp(jnp.stack(own_terms, axis=1))
     sample_count = sequence_in.shape[0] * lax.axis_size("dp")
     full_length = sequence_in.shape[1] * peers
-    point_grad = summed * (1.0 / math.sqrt(sample_count * full_length))
+    scale = 1.0 / math.sqrt(sample_count * full_length)
+    point_grad = reduced_over_dp(jnp.stack(own_terms, axis=1) * scale)
     input_grad = back_pieces.reshape(sequence_in.shape)
     return (point_grad, input_grad)
 

time: 186 us -> 186 us (level)
  no operation moved by 1% of the time
where the time goes in v19:
time: 186 us; the launch traced here: 185 us
  blocking collectives  87.4 us (47%)
  local copies, waits for them, and re-layouts  26 us (14%)
  waiting for transfers between devices  24.5 us (13%)
  starting transfers between devices  19 us (10%)
  matrix products  15.2 us (8%)
  other arithmetic  9.72 us (5%)
  between operations  2.76 us (1%)
    all_to_all x2, blocking collectives, exchanged(): arrived = lax.all_to_all(joined, axis, 0, 0, tiled=True)  56.1 us
    all_to_all x1, blocking collectives, summed_over(): arrived = lax.all_to_all(pieces, axis, 0, 0, tiled=True)  31.3 us
    all_to_all x1, waiting for transfers between devices, gathered(): return lax.all_to_all(copies, axis, 0, 0, tiled=True)  16 us
    all_to_all x1, waiting for transfers between devices, shards(): second_arrived = lax.all_to_all(second_joined, 'seq', 0, 0, tiled=True)  8.56 us
    dot_general x8, matrix products, contract_last(): lax.dot_general(left, right, (((1,), (1,)), ((), ())), preferred_element_...  7.53 us
    unnamed x84, local copies, waits for them, and re-layouts  6.2 us
    all_to_all x1, starting transfers between devices, shards(): second_arrived = lax.all_to_all(second_joined, 'seq', 0, 0, tiled=True)  5.58 us
    ppermute x2, starting transfers between devices, whole_from_halves(): partner = lax.ppermute(own_halves, axis, [(i, i ^ 1) for i in range(peers)])  4.8 us
  transfers between devices with their start and end apart: 6, of which 2 were waited for; matrix products, arithmetic and copies ran while one was open for 15% of the time, Pallas kernels for 0%

profile of v19, /device:TPU:6, one launch (start us, length us, event | category | flops | bytes accessed | tf_op | source)
XLA Modules:
  0.0 184.6 jit_solution(12588706204831225533)
XLA Ops:
  0.6 1.1 fusion.92
  1.8 1.0 fusion.91
  3.1 32.0 %all_to_all.25 = bf16[16,80,768]{2,1,0:T(8,128)(2,1)S(1)} all-to-all(bf16[16,80,768]{2,1,0:T(8,128)(2,1)S(1)} %pad_maximum_fusion.1), channel_id=1, replica_groups=mesh['dp'=32,'seq'=16] {'seq'}, dimensions={0} | all-to-all | bytes 3932160 | tf_op jit(solution)/shard_map/all_to_all | solution.py:92
  35.1 1.2 slice.194
  36.3 2.5 %collective-permute-start = (bf16[16,48,768]{2,1,0:T(8,128)(2,1)}, bf16[16,48,768]{2,1,0:T(8,128)(2,1)}, u32[]{:S(2)}, u32[]{:S(2)}) collective-permute-start(bf16[16,48,768]{2,1,0:T(8,128)(2,1)} %slice.194), channel_id=1, source_target_pairs={{0,1},{1,0},{2,3},{3,2},{4,5},{5,4},{6,7},{7,6},{8,9},{9,8},{10,11... | collective-permute-start | bytes 3538952 | tf_op jit(solution)/shard_map/ppermute | solution.py:112
  38.8 0.6 fusion.93
  40.7 0.6 slice_reduce_fusion.4
  41.4 0.6 slice_reduce_fusion
  42.1 1.4 pad_maximum_fusion
  43.6 5.6 %all-to-all-start.1 = ((bf16[16,80,768]{2,1,0:T(8,128)(2,1)}), bf16[16,80,768]{2,1,0:T(8,128)(2,1)S(1)}, u32[]{:S(2)}, u32[]{:S(2)}) async-start(bf16[16,80,768]{2,1,0:T(8,128)(2,1)} %pad_maximum_fusion), calls=%async_computation.1 | async-start | bytes 3932160 | tf_op jit(solution)/shard_map/all_to_all | solution.py:182
  49.2 0.6 fusion.6
  49.8 1.2 fusion.88
  51.0 0.9 copy-done.2
  51.9 1.4 broadcast_select_fusion.3
  53.3 1.0 copy-done.3
  54.4 1.4 pad_maximum_fusion.3
  55.7 3.8 %reshape.97 = bf16[16,3,48,384]{3,2,1,0:T(8,128)(2,1)} reshape(bf16[16,72,768]{2,1,0:T(8,128)(2,1)} %pad_maximum_fusion.3) | data formatting | bytes 3538944 | tf_op jit(solution)/shard_map/reshape | solution.py:121
  59.5 2.5 %fusion.86 = (bf16[1,16,48,384]{3,2,0,1:T(8,128)(2,1)}, bf16[1,16,48,384]{3,2,0,1:T(8,128)(2,1)S(1)}, bf16[1,16,48,384]{3,2,0,1:T(8,128)(2,1)S(1)}) fusion(bf16[3,16,48,384]{3,2,0,1:T(8,128)(2,1)} %bitcast.58), kind=kLoop, calls=%fused_computation.133 | loop fusion | bytes 3538944 | tf_op jit(solution)/shard_map/slice | solution.py:58
  63.1 1.5 convolution_add_fusion.3
  64.5 8.6 %all-to-all-done.1 = bf16[16,80,768]{2,1,0:T(8,128)(2,1)S(1)} async-done(((bf16[16,80,768]{2,1,0:T(8,128)(2,1)}), bf16[16,80,768]{2,1,0:T(8,128)(2,1)S(1)}, u32[]{:S(2)}, u32[]{:S(2)}) %all-to-all-start.1) | async-done | bytes 1966112 | tf_op jit(solution)/shard_map/all_to_all | solution.py:182
  73.2 2.3 %collective-permute-start.1 = (bf16[16,48,768]{2,1,0:T(8,128)(2,1)S(1)}, bf16[16,48,768]{2,1,0:T(8,128)(2,1)S(1)}, u32[]{:S(2)}, u32[]{:S(2)}) collective-permute-start(bf16[16,48,768]{2,1,0:T(8,128)(2,1)S(1)} %slice.201), channel_id=1, source_target_pairs={{0,1},{1,0},{2,3},{3,2},{4,5},{5,4},{6,7},{7,6},{8,9},{9,8},{10,11... | collective-permute-start | bytes 3538952 | tf_op jit(solution)/shard_map/ppermute | solution.py:112
  76.3 2.0 %multiply_convert_fusion = (bf16[512,768]{1,0:T(8,128)(2,1)S(1)}, bf16[512,768]{1,0:T(8,128)(2,1)}) fusion(f32[768]{0:T(1024)S(1)} %copy-done.33, f32[768]{0:T(1024)S(1)} %copy-done.35, bf16[384,768]{1,0:T(8,128)(2,1)S(1)} %bitcast.82, f32[512,384]{1,0:T(8,128)S(1)} %fusion.32, f32[]{:T(128)} %bitcast.13, bf16[512,768]{1,0:T(8,128)(2,1)S(1)} %bitcast.71), kind=kOutput, calls=%fused_computation.41 | convolution fusion | flops 310050816 | bytes 3741700 | tf_op jit(solution)/shard_map/dot_general | solution.py:61
  78.3 1.2 fusion.87
  79.6 1.0 fusion.26
  80.6 1.1 fusion.25
  81.9 0.8 slice.209
  82.9 0.6 reshape.99
  83.7 0.9 copy-done.19
  87.1 0.9 fusion.48
  88.1 0.6 fusion.94
  89.9 2.6 %collective-permute-start.2 = (f32[384,384]{1,0:T(8,128)S(1)}, f32[384,384]{1,0:T(8,128)S(1)}, u32[]{:S(2)}, u32[]{:S(2)}) collective-permute-start(f32[384,384]{1,0:T(8,128)S(1)} %slice_select_fusion.1), channel_id=1, source_target_pairs={{0,1},{1,0},{2,3},{3,2},{4,5},{5,4},{6,7},{7,6},{8,9},{9,8},{10,11... | collective-permute-start | bytes 1769480 | tf_op jit(solution)/shard_map/ppermute | solution.py:130
  92.4 0.6 fusion.66
  93.1 1.6 fusion.24
  94.9 0.9 copy-done.23
  96.0 0.9 fusion.40
  97.0 0.7 fusion.57
  98.0 0.6 fusion.95
  98.7 2.2 %collective-permute-start.3 = (f32[384,384]{1,0:T(8,128)S(1)}, f32[384,384]{1,0:T(8,128)S(1)}, u32[]{:S(2)}, u32[]{:S(2)}) collective-permute-start(f32[384,384]{1,0:T(8,128)S(1)} %slice_select_fusion), channel_id=1, source_target_pairs={{0,1},{1,0},{2,3},{3,2},{4,5},{5,4},{6,7},{7,6},{8,9},{9,8},{10,11... | collective-permute-start | bytes 1769480 | tf_op jit(solution)/shard_map/ppermute | solution.py:130
  100.9 0.6 fusion.63
  101.6 1.6 fusion.11
  103.6 24.1 %all_to_all.26 = bf16[16,56,768]{2,1,0:T(8,128)(2,1)S(1)} all-to-all(bf16[16,56,768]{2,1,0:T(8,128)(2,1)S(1)} %pad_maximum_fusion.4), channel_id=1, replica_groups=mesh['dp'=32,'seq'=16] {'seq'}, dimensions={0} | all-to-all | bytes 2752512 | tf_op jit(solution)/shard_map/all_to_all | solution.py:92
  129.1 1.1 reduce.18
  130.3 31.3 %all_to_all.27 = bf16[32,2,576]{2,1,0:T(2,128)(2,1)S(1)} all-to-all(bf16[32,2,576]{2,1,0:T(2,128)(2,1)S(1)} %reshape.118), channel_id=1, replica_groups=mesh['dp'=32,'seq'=16] {'dp'}, dimensions={0} | all-to-all | bytes 147456 | tf_op jit(solution)/shard_map/all_to_all | solution.py:27
  161.9 0.7 broadcast_in_dim.2
  162.7 3.9 %all-to-all-start.4 = ((f32[32,1,1152]{2,1,0:T(1,128)}), f32[32,1,1152]{2,1,0:T(1,128)S(1)}, u32[]{:S(2)}, u32[]{:S(2)}) async-start(f32[32,1,1152]{2,1,0:T(1,128)} %broadcast_in_dim.2), calls=%async_computation.4 | async-start | bytes 294912 | tf_op jit(solution)/shard_map/all_to_all | solution.py:21
  166.5 1.0 slice.218
  167.5 16.0 %all-to-all-done.4 = f32[32,1,1152]{2,1,0:T(1,128)S(1)} async-done(((f32[32,1,1152]{2,1,0:T(1,128)}), f32[32,1,1152]{2,1,0:T(1,128)S(1)}, u32[]{:S(2)}, u32[]{:S(2)}) %all-to-all-start.4) | async-done | bytes 147488 | tf_op jit(solution)/shard_map/all_to_all | solution.py:21
  183.8 0.8 reshape.104
  (131 shorter events, 9.6 us)
Async XLA Ops:
  0.6 2.3 %copy-start.24 = (bf16[1,512,768]{2,1,0:T(8,128)(2,1)S(1)}, bf16[1,512,768]{2,1,0:T(8,128)(2,1)}, u32[]{:S(2)}) copy-start(bf16[1,512,768]{2,1,0:T(8,128)(2,1)} %param.9) | copy-start | bytes 2359300
  35.0 8.5 %copy-start.1 = (bf16[16,80,768]{2,1,0:T(8,128)(2,1)}, bf16[16,80,768]{2,1,0:T(8,128)(2,1)S(1)}, u32[]{:S(2)}) copy-start(bf16[16,80,768]{2,1,0:T(8,128)(2,1)S(1)} %all_to_all.25) | copy-start | bytes 5898244
  35.0 3.7 %copy-start.39 = (s32[1,2]{1,0:T(1,128)S(1)}, s32[1,2]{1,0:T(1,128)}, u32[]{:S(2)}) copy-start(s32[1,2]{1,0:T(1,128)} %param.11) | copy-start | bytes 28
  35.0 5.6 %copy-start.37 = (f32[2,384]{1,0:T(2,128)S(1)}, f32[2,384]{1,0:T(2,128)}, u32[]{:S(2)}) copy-start(f32[2,384]{1,0:T(2,128)} %param.14) | copy-start | bytes 9220
  35.1 5.7 %copy-start.38 = (f32[2,384]{1,0:T(2,128)S(1)}, f32[2,384]{1,0:T(2,128)}, u32[]{:S(2)}) copy-start(f32[2,384]{1,0:T(2,128)} %param.15) | copy-start | bytes 9220
  35.1 6.3 %copy-start.31 = (f32[2,768]{1,0:T(2,128)S(1)}, f32[2,768]{1,0:T(2,128)}, u32[]{:S(2)}) copy-start(f32[2,768]{1,0:T(2,128)} %param.13) | copy-start | bytes 18436
  35.1 6.3 %copy-start.32 = (f32[2,768]{1,0:T(2,128)S(1)}, f32[2,768]{1,0:T(2,128)}, u32[]{:S(2)}) copy-start(f32[2,768]{1,0:T(2,128)} %param.12) | copy-start | bytes 18436
  35.1 7.0 %copy-start.25 = (bf16[1,512,768]{2,1,0:T(8,128)(2,1)S(1)}, bf16[1,512,768]{2,1,0:T(8,128)(2,1)}, u32[]{:S(2)}) copy-start(bf16[1,512,768]{2,1,0:T(8,128)(2,1)} %param.10) | copy-start | bytes 2359300
  36.3 14.8 %collective-permute-start = (bf16[16,48,768]{2,1,0:T(8,128)(2,1)}, bf16[16,48,768]{2,1,0:T(8,128)(2,1)}, u32[]{:S(2)}, u32[]{:S(2)}) collective-permute-start(bf16[16,48,768]{2,1,0:T(8,128)(2,1)} %slice.194), channel_id=1, source_target_pairs={{0,1},{1,0},{2,3},{3,2},{4,5},{5,4},{6,7},{7,6},{8,9},{9,8},{10,11... | collective-permute-start | bytes 3538952 | tf_op jit(solution)/shard_map/ppermute | solution.py:112
  43.6 32.7 %copy-start.11 = (bf16[16,32,768]{2,1,0:T(8,128)(2,1)}, bf16[16,32,768]{2,1,0:T(8,128)(2,1)S(1)}, u32[]{:S(2)}) copy-start(bf16[16,32,768]{2,1,0:T(8,128)(2,1)S(1)} %slice.192) | copy-start | bytes 2359300
  43.6 29.5 %all-to-all-start.1 = ((bf16[16,80,768]{2,1,0:T(8,128)(2,1)}), bf16[16,80,768]{2,1,0:T(8,128)(2,1)S(1)}, u32[]{:S(2)}, u32[]{:S(2)}) async-start(bf16[16,80,768]{2,1,0:T(8,128)(2,1)} %pad_maximum_fusion), calls=%async_computation.1 | async-start | bytes 3932160 | tf_op jit(solution)/shard_map/all_to_all | solution.py:182
  49.8 2.0 %copy-start.2 = (bf16[16,80,768]{2,1,0:T(8,128)(2,1)S(1)}, bf16[16,80,768]{2,1,0:T(8,128)(2,1)}, u32[]{:S(2)}) copy-start(bf16[16,80,768]{2,1,0:T(8,128)(2,1)} %copy-done.1) | copy-start | bytes 5898244
  53.3 1.0 copy-start.3
  59.5 2.5 %copy-start.15 = (bf16[448,768]{1,0:T(8,128)(2,1)S(1)}, bf16[448,768]{1,0:T(8,128)(2,1)}, u32[]{:S(2)}) copy-start(bf16[448,768]{1,0:T(8,128)(2,1)} %get-tuple-element.33) | copy-start | bytes 2064388
  62.0 0.8 copy-start.5
  62.0 1.0 copy-start.7
  64.5 11.0 %copy-start.13 = (f32[512,384]{1,0:T(8,128)S(1)}, f32[512,384]{1,0:T(8,128)}, u32[]{:S(2)}) copy-start(f32[512,384]{1,0:T(8,128)} %convolution_add_fusion.3) | copy-start | bytes 2359300
  73.1 8.6 %copy-start = (bf16[16,80,768]{2,1,0:T(8,128)(2,1)}, bf16[16,80,768]{2,1,0:T(8,128)(2,1)S(1)}, u32[]{:S(2)}) copy-start(bf16[16,80,768]{2,1,0:T(8,128)(2,1)S(1)} %all-to-all-done.1) | copy-start | bytes 5898244
  73.1 2.5 %copy-start.14 = (bf16[448,768]{1,0:T(8,128)(2,1)S(1)}, bf16[448,768]{1,0:T(8,128)(2,1)}, u32[]{:S(2)}) copy-start(bf16[448,768]{1,0:T(8,128)(2,1)} %get-tuple-element.32) | copy-start | bytes 2064388
  73.1 2.5 %copy-start.16 = (bf16[1,16,48,384]{3,2,0,1:T(8,128)(2,1)S(1)}, bf16[1,16,48,384]{3,2,0,1:T(8,128)(2,1)}, u32[]{:S(2)}) copy-start(bf16[1,16,48,384]{3,2,0,1:T(8,128)(2,1)} %get-tuple-element.25) | copy-start | bytes 1769476
  73.1 2.5 %copy-start.30 = (f32[384]{0:T(512)S(1)}, f32[384]{0:T(512)}, u32[]{:S(2)}) copy-start(f32[384]{0:T(512)} %get-tuple-element.17) | copy-start | bytes 4612
  73.2 3.0 %copy-start.4 = (bf16[16,48,768]{2,1,0:T(8,128)(2,1)S(1)}, bf16[16,48,768]{2,1,0:T(8,128)(2,1)}, u32[]{:S(2)}) copy-start(bf16[16,48,768]{2,1,0:T(8,128)(2,1)} %copy-done.3) | copy-start | bytes 3538948
  73.2 8.5 %collective-permute-start.1 = (bf16[16,48,768]{2,1,0:T(8,128)(2,1)S(1)}, bf16[16,48,768]{2,1,0:T(8,128)(2,1)S(1)}, u32[]{:S(2)}, u32[]{:S(2)}) collective-permute-start(bf16[16,48,768]{2,1,0:T(8,128)(2,1)S(1)} %slice.201), channel_id=1, source_target_pairs={{0,1},{1,0},{2,3},{3,2},{4,5},{5,4},{6,7},{7,6},{8,9},{9,8},{10,11... | collective-permute-start | bytes 3538952 | tf_op jit(solution)/shard_map/ppermute | solution.py:112
  75.6 0.7 copy-start.33
  75.6 0.7 copy-start.35
  76.2 2.1 %copy-start.22 = (f32[512,384]{1,0:T(8,128)}, f32[512,384]{1,0:T(8,128)S(1)}, u32[]{:S(2)}) copy-start(f32[512,384]{1,0:T(8,128)S(1)} %fusion.32) | copy-start | bytes 2359300
  76.3 2.0 %copy-start.26 = (bf16[16,24,768]{2,1,0:T(8,128)(2,1)}, bf16[16,24,768]{2,1,0:T(8,128)(2,1)S(1)}, u32[]{:S(2)}) copy-start(bf16[16,24,768]{2,1,0:T(8,128)(2,1)S(1)} %slice.199) | copy-start | bytes 1769476
  78.3 1.3 copy-start.9
  83.5 1.1 copy-start.19
  83.7 1.5 copy-start.10
  85.1 1.1 copy-start.18
  85.1 1.1 copy-start.29
  85.8 1.2 copy-start.21
  85.8 1.3 copy-start.28
  88.0 1.1 copy-start.20
  89.8 3.2 %slice-start = ((bf16[16,80,768]{2,1,0:T(8,128)(2,1)}), bf16[16,32,768]{2,1,0:T(8,128)(2,1)S(1)}, s32[]{:S(2)}) async-start(bf16[16,80,768]{2,1,0:T(8,128)(2,1)} %copy-done), calls=%async_computation.5 | async-start | bytes 1572864 | tf_op jit(solution)/shard_map/slice | solution.py:183
  89.8 3.2 %copy-start.34 = (f32[768]{0:T(1024)S(1)}, f32[768]{0:T(1024)}, u32[]{:S(2)}) copy-start(f32[768]{0:T(1024)} %get-tuple-element.12) | copy-start | bytes 9220
  89.8 3.2 %copy-start.36 = (f32[768]{0:T(1024)S(1)}, f32[768]{0:T(1024)}, u32[]{:S(2)}) copy-start(f32[768]{0:T(1024)} %get-tuple-element.49) | copy-start | bytes 9220
  89.9 3.2 %copy-start.40 = (bf16[512,768]{1,0:T(8,128)(2,1)S(1)}, bf16[512,768]{1,0:T(8,128)(2,1)}, u32[]{:S(2)}) copy-start(bf16[512,768]{1,0:T(8,128)(2,1)} %get-tuple-element.45) | copy-start | bytes 2359300
  89.9 4.9 %collective-permute-start.2 = (f32[384,384]{1,0:T(8,128)S(1)}, f32[384,384]{1,0:T(8,128)S(1)}, u32[]{:S(2)}, u32[]{:S(2)}) collective-permute-start(f32[384,384]{1,0:T(8,128)S(1)} %slice_select_fusion.1), channel_id=1, source_target_pairs={{0,1},{1,0},{2,3},{3,2},{4,5},{5,4},{6,7},{7,6},{8,9},{9,8},{10,11... | collective-permute-start | bytes 1769480 | tf_op jit(solution)/shard_map/ppermute | solution.py:130
  94.7 1.1 copy-start.23
  94.7 1.3 copy-start.27
  97.0 1.1 copy-start.8
  98.0 2.9 %copy-start.6 = (bf16[1,16,48,384]{3,2,0,1:T(8,128)(2,1)S(1)}, bf16[1,16,48,384]{3,2,0,1:T(8,128)(2,1)}, u32[]{:S(2)}) copy-start(bf16[1,16,48,384]{3,2,0,1:T(8,128)(2,1)} %copy-done.5) | copy-start | bytes 1769476
  98.7 2.8 %copy-start.12 = (bf16[16,32,768]{2,1,0:T(8,128)(2,1)S(1)}, bf16[16,32,768]{2,1,0:T(8,128)(2,1)}, u32[]{:S(2)}) copy-start(bf16[16,32,768]{2,1,0:T(8,128)(2,1)} %copy-done.11) | copy-start | bytes 2359300
  98.7 2.8 %copy-start.17 = (bf16[1,16,48,384]{3,2,0,1:T(8,128)(2,1)S(1)}, bf16[1,16,48,384]{3,2,0,1:T(8,128)(2,1)}, u32[]{:S(2)}) copy-start(bf16[1,16,48,384]{3,2,0,1:T(8,128)(2,1)} %get-tuple-element.25) | copy-start | bytes 1769476
  98.7 4.5 %collective-permute-start.3 = (f32[384,384]{1,0:T(8,128)S(1)}, f32[384,384]{1,0:T(8,128)S(1)}, u32[]{:S(2)}, u32[]{:S(2)}) collective-permute-start(f32[384,384]{1,0:T(8,128)S(1)} %slice_select_fusion), channel_id=1, source_target_pairs={{0,1},{1,0},{2,3},{3,2},{4,5},{5,4},{6,7},{7,6},{8,9},{9,8},{10,11... | collective-permute-start | bytes 1769480 | tf_op jit(solution)/shard_map/ppermute | solution.py:130
  162.7 20.8 %all-to-all-start.4 = ((f32[32,1,1152]{2,1,0:T(1,128)}), f32[32,1,1152]{2,1,0:T(1,128)S(1)}, u32[]{:S(2)}, u32[]{:S(2)}) async-start(f32[32,1,1152]{2,1,0:T(1,128)} %broadcast_in_dim.2), calls=%async_computation.4 | async-start | bytes 294912 | tf_op jit(solution)/shard_map/all_to_all | solution.py:21

commit v20 on v19

--- a/solution.py
+++ b/solution.py
@@ -163,14 +163,10 @@
     first_weights = jnp.concatenate(
         [conv_weight[0].reshape(-1, channels), point_weight[:, 0, :]]
     )
-    state_pieces, first_halves = exchanged(
-        [
-            strided_pieces(sequence_in[0], peers),
-            half_for_each(first_weights, peers, channels),
-        ],
-        "seq",
-    )
-    state = state_pieces.reshape(-1, channels)
+    state_sent = strided_pieces(sequence_in[0], peers)
+    first_joined = jnp.concatenate(
+        [state_sent, half_for_each(first_weights, peers, channels)], axis=1
+    )
     grad_rows_sent = strided_pieces(output_grad[0], peers)
     second_weights = jnp.concatenate(
         [conv_weight[1].reshape(-1, channels), point_weight[:, 1, :]]
@@ -178,6 +174,10 @@
     second_joined = jnp.concatenate(
         [grad_rows_sent, half_for_each(second_weights, peers, channels)], axis=1
     )
+    first_joined, second_joined = lax.optimization_barrier((first_joined, second_joined))
+    first_arrived = lax.all_to_all(first_joined, "seq", 0, 0, tiled=True)
+    state = first_arrived[:, : state_sent.shape[1]].reshape(-1, channels)
+    first_halves = first_arrived[:, state_sent.shape[1] :]
     second_joined, state = lax.optimization_barrier((second_joined, state))
     second_arrived = lax.all_to_all(second_joined, "seq", 0, 0, tiled=True)
     grad_pieces = second_arrived[:, : grad_rows_sent.shape[1]]

time: 186 us -> 187 us (level)
    all_to_all x2 -> x1, blocking collectives: 56.1 us -> 24.1 us  [exchanged(): arrived = lax.all_to_all(joined, axis, 0, 0, tiled=True)]
    all_to_all x0 -> x1, blocking collectives: none -> 32 us  [shards(): first_arrived = lax.all_to_all(first_joined, 'seq', 0, 0, tiled=True)]
  transfers between devices with their start and end apart: 6 -> 6, of which waited for: 2 -> 2; matrix products, arithmetic and copies ran while one was open for 15% -> 14% of each run, Pallas kernels for 0% -> 0%
where the time goes in v20:
time: 187 us; the launch traced here: 186 us
  blocking collectives  87.4 us (47%)
  local copies, waits for them, and re-layouts  27 us (14%)
  waiting for transfers between devices  24.5 us (13%)
  starting transfers between devices  19 us (10%)
  matrix products  15.2 us (8%)
  other arithmetic  9.72 us (5%)
  between operations  2.78 us (1%)
    all_to_all x1, blocking collectives, shards(): first_arrived = lax.all_to_all(first_joined, 'seq', 0, 0, tiled=True)  32 us
    all_to_all x1, blocking collectives, summed_over(): arrived = lax.all_to_all(pieces, axis, 0, 0, tiled=True)  31.3 us
    all_to_all x1, blocking collectives, exchanged(): arrived = lax.all_to_all(joined, axis, 0, 0, tiled=True)  24.1 us
    all_to_all x1, waiting for transfers between devices, gathered(): return lax.all_to_all(copies, axis, 0, 0, tiled=True)  16 us
    all_to_all x1, waiting for transfers between devices, shards(): second_arrived = lax.all_to_all(second_joined, 'seq', 0, 0, tiled=True)  8.56 us
    dot_general x8, matrix products, contract_last(): lax.dot_general(left, right, (((1,), (1,)), ((), ())), preferred_element_...  7.53 us
    unnamed x84, local copies, waits for them, and re-layouts  7.24 us
    all_to_all x1, starting transfers between devices, shards(): second_arrived = lax.all_to_all(second_joined, 'seq', 0, 0, tiled=True)  5.58 us
  transfers between devices with their start and end apart: 6, of which 2 were waited for; matrix products, arithmetic and copies ran while one was open for 14% of the time, Pallas kernels for 0%

profile of v20, /device:TPU:6, one launch (start us, length us, event | category | flops | bytes accessed | tf_op | source)
XLA Modules:
  0.0 185.6 jit_solution(14883938904171646112)
XLA Ops:
  0.6 1.1 fusion.92
  1.7 1.0 fusion.91
  3.3 1.0 copy-done.25
  4.3 1.4 pad_maximum_fusion.1
  5.7 32.0 %all_to_all.25 = bf16[16,80,768]{2,1,0:T(8,128)(2,1)S(1)} all-to-all(bf16[16,80,768]{2,1,0:T(8,128)(2,1)S(1)} %pad_maximum_fusion), channel_id=1, replica_groups=mesh['dp'=32,'seq'=16] {'seq'}, dimensions={0} | all-to-all | bytes 3932160 | tf_op jit(solution)/shard_map/all_to_all | solution.py:178
  37.7 1.2 slice.194
  38.9 2.5 %collective-permute-start = (bf16[16,48,768]{2,1,0:T(8,128)(2,1)}, bf16[16,48,768]{2,1,0:T(8,128)(2,1)}, u32[]{:S(2)}, u32[]{:S(2)}) collective-permute-start(bf16[16,48,768]{2,1,0:T(8,128)(2,1)} %slice.194), channel_id=1, source_target_pairs={{0,1},{1,0},{2,3},{3,2},{4,5},{5,4},{6,7},{7,6},{8,9},{9,8},{10,11... | collective-permute-start | bytes 3538952 | tf_op jit(solution)/shard_map/ppermute | solution.py:112
  43.3 0.6 slice_reduce_fusion.4
  44.0 0.6 slice_reduce_fusion
  44.7 5.6 %all-to-all-start.1 = ((bf16[16,80,768]{2,1,0:T(8,128)(2,1)}), bf16[16,80,768]{2,1,0:T(8,128)(2,1)S(1)}, u32[]{:S(2)}, u32[]{:S(2)}) async-start(bf16[16,80,768]{2,1,0:T(8,128)(2,1)} %pad_maximum_fusion.1), calls=%async_computation.1 | async-start | bytes 3932160 | tf_op jit(solution)/shard_map/all_to_all | solution.py:182
  50.3 0.6 fusion.6
  50.9 1.2 fusion.88
  52.1 0.9 copy-done.2
  53.0 1.4 broadcast_select_fusion.3
  54.4 1.0 copy-done.3
  55.4 1.4 pad_maximum_fusion.3
  56.8 3.8 %reshape.97 = bf16[16,3,48,384]{3,2,1,0:T(8,128)(2,1)} reshape(bf16[16,72,768]{2,1,0:T(8,128)(2,1)} %pad_maximum_fusion.3) | data formatting | bytes 3538944 | tf_op jit(solution)/shard_map/reshape | solution.py:121
  60.6 2.5 %fusion.86 = (bf16[1,16,48,384]{3,2,0,1:T(8,128)(2,1)}, bf16[1,16,48,384]{3,2,0,1:T(8,128)(2,1)S(1)}, bf16[1,16,48,384]{3,2,0,1:T(8,128)(2,1)S(1)}) fusion(bf16[3,16,48,384]{3,2,0,1:T(8,128)(2,1)} %bitcast.58), kind=kLoop, calls=%fused_computation.133 | loop fusion | bytes 3538944 | tf_op jit(solution)/shard_map/slice | solution.py:58
  64.1 1.5 convolution_add_fusion.3
  65.6 8.6 %all-to-all-done.1 = bf16[16,80,768]{2,1,0:T(8,128)(2,1)S(1)} async-done(((bf16[16,80,768]{2,1,0:T(8,128)(2,1)}), bf16[16,80,768]{2,1,0:T(8,128)(2,1)S(1)}, u32[]{:S(2)}, u32[]{:S(2)}) %all-to-all-start.1) | async-done | bytes 1966112 | tf_op jit(solution)/shard_map/all_to_all | solution.py:182
  74.3 2.3 %collective-permute-start.1 = (bf16[16,48,768]{2,1,0:T(8,128)(2,1)S(1)}, bf16[16,48,768]{2,1,0:T(8,128)(2,1)S(1)}, u32[]{:S(2)}, u32[]{:S(2)}) collective-permute-start(bf16[16,48,768]{2,1,0:T(8,128)(2,1)S(1)} %slice.201), channel_id=1, source_target_pairs={{0,1},{1,0},{2,3},{3,2},{4,5},{5,4},{6,7},{7,6},{8,9},{9,8},{10,11... | collective-permute-start | bytes 3538952 | tf_op jit(solution)/shard_map/ppermute | solution.py:112
  77.4 2.0 %multiply_convert_fusion = (bf16[512,768]{1,0:T(8,128)(2,1)S(1)}, bf16[512,768]{1,0:T(8,128)(2,1)}) fusion(f32[768]{0:T(1024)S(1)} %copy-done.33, f32[768]{0:T(1024)S(1)} %copy-done.35, bf16[384,768]{1,0:T(8,128)(2,1)S(1)} %bitcast.82, f32[512,384]{1,0:T(8,128)S(1)} %fusion.32, f32[]{:T(128)} %bitcast.13, bf16[512,768]{1,0:T(8,128)(2,1)S(1)} %bitcast.71), kind=kOutput, calls=%fused_computation.41 | convolution fusion | flops 310050816 | bytes 3741700 | tf_op jit(solution)/shard_map/dot_general | solution.py:61
  79.4 1.2 fusion.87
  80.7 1.0 fusion.26
  81.7 1.1 fusion.25
  83.0 0.8 slice.209
  83.9 0.6 reshape.99
  84.8 0.9 copy-done.19
  88.2 0.9 fusion.48
  89.2 0.6 fusion.94
  90.9 2.6 %collective-permute-start.2 = (f32[384,384]{1,0:T(8,128)S(1)}, f32[384,384]{1,0:T(8,128)S(1)}, u32[]{:S(2)}, u32[]{:S(2)}) collective-permute-start(f32[384,384]{1,0:T(8,128)S(1)} %slice_select_fusion.1), channel_id=1, source_target_pairs={{0,1},{1,0},{2,3},{3,2},{4,5},{5,4},{6,7},{7,6},{8,9},{9,8},{10,11... | collective-permute-start | bytes 1769480 | tf_op jit(solution)/shard_map/ppermute | solution.py:130
  93.5 0.6 fusion.66
  94.1 1.6 fusion.24
  96.0 0.9 copy-done.23
  97.1 0.9 fusion.40
  98.0 0.7 fusion.57
  99.1 0.6 fusion.95
  99.8 2.2 %collective-permute-start.3 = (f32[384,384]{1,0:T(8,128)S(1)}, f32[384,384]{1,0:T(8,128)S(1)}, u32[]{:S(2)}, u32[]{:S(2)}) collective-permute-start(f32[384,384]{1,0:T(8,128)S(1)} %slice_select_fusion), channel_id=1, source_target_pairs={{0,1},{1,0},{2,3},{3,2},{4,5},{5,4},{6,7},{7,6},{8,9},{9,8},{10,11... | collective-permute-start | bytes 1769480 | tf_op jit(solution)/shard_map/ppermute | solution.py:130
  102.0 0.6 fusion.63
  102.6 1.6 fusion.11
  104.7 24.1 %all_to_all.26 = bf16[16,56,768]{2,1,0:T(8,128)(2,1)S(1)} all-to-all(bf16[16,56,768]{2,1,0:T(8,128)(2,1)S(1)} %pad_maximum_fusion.4), channel_id=1, replica_groups=mesh['dp'=32,'seq'=16] {'seq'}, dimensions={0} | all-to-all | bytes 2752512 | tf_op jit(solution)/shard_map/all_to_all | solution.py:92
  130.2 1.1 reduce.18
  131.4 31.3 %all_to_all.27 = bf16[32,2,576]{2,1,0:T(2,128)(2,1)S(1)} all-to-all(bf16[32,2,576]{2,1,0:T(2,128)(2,1)S(1)} %reshape.118), channel_id=1, replica_groups=mesh['dp'=32,'seq'=16] {'dp'}, dimensions={0} | all-to-all | bytes 147456 | tf_op jit(solution)/shard_map/all_to_all | solution.py:27
  163.0 0.7 broadcast_in_dim.2
  163.7 3.9 %all-to-all-start.4 = ((f32[32,1,1152]{2,1,0:T(1,128)}), f32[32,1,1152]{2,1,0:T(1,128)S(1)}, u32[]{:S(2)}, u32[]{:S(2)}) async-start(f32[32,1,1152]{2,1,0:T(1,128)} %broadcast_in_dim.2), calls=%async_computation.4 | async-start | bytes 294912 | tf_op jit(solution)/shard_map/all_to_all | solution.py:21
  167.6 1.0 slice.218
  168.6 16.0 %all-to-all-done.4 = f32[32,1,1152]{2,1,0:T(1,128)S(1)} async-done(((f32[32,1,1152]{2,1,0:T(1,128)}), f32[32,1,1152]{2,1,0:T(1,128)S(1)}, u32[]{:S(2)}, u32[]{:S(2)}) %all-to-all-start.4) | async-done | bytes 147488 | tf_op jit(solution)/shard_map/all_to_all | solution.py:21
  184.9 0.8 reshape.104
  (131 shorter events, 10.2 us)
Async XLA Ops:
  1.7 1.3 copy-start.24
  3.2 1.1 copy-start.25
  37.7 7.0 %copy-start.1 = (bf16[16,80,768]{2,1,0:T(8,128)(2,1)}, bf16[16,80,768]{2,1,0:T(8,128)(2,1)S(1)}, u32[]{:S(2)}) copy-start(bf16[16,80,768]{2,1,0:T(8,128)(2,1)S(1)} %all_to_all.25) | copy-start | bytes 5898244
  37.7 3.7 %copy-start.39 = (s32[1,2]{1,0:T(1,128)S(1)}, s32[1,2]{1,0:T(1,128)}, u32[]{:S(2)}) copy-start(s32[1,2]{1,0:T(1,128)} %param.11) | copy-start | bytes 28
  37.7 5.6 %copy-start.37 = (f32[2,384]{1,0:T(2,128)S(1)}, f32[2,384]{1,0:T(2,128)}, u32[]{:S(2)}) copy-start(f32[2,384]{1,0:T(2,128)} %param.14) | copy-start | bytes 9220
  37.7 5.6 %copy-start.38 = (f32[2,384]{1,0:T(2,128)S(1)}, f32[2,384]{1,0:T(2,128)}, u32[]{:S(2)}) copy-start(f32[2,384]{1,0:T(2,128)} %param.15) | copy-start | bytes 9220
  37.7 6.2 %copy-start.31 = (f32[2,768]{1,0:T(2,128)S(1)}, f32[2,768]{1,0:T(2,128)}, u32[]{:S(2)}) copy-start(f32[2,768]{1,0:T(2,128)} %param.13) | copy-start | bytes 18436
  37.7 6.2 %copy-start.32 = (f32[2,768]{1,0:T(2,128)S(1)}, f32[2,768]{1,0:T(2,128)}, u32[]{:S(2)}) copy-start(f32[2,768]{1,0:T(2,128)} %param.12) | copy-start | bytes 18436
  38.9 13.2 %collective-permute-start = (bf16[16,48,768]{2,1,0:T(8,128)(2,1)}, bf16[16,48,768]{2,1,0:T(8,128)(2,1)}, u32[]{:S(2)}, u32[]{:S(2)}) collective-permute-start(bf16[16,48,768]{2,1,0:T(8,128)(2,1)} %slice.194), channel_id=1, source_target_pairs={{0,1},{1,0},{2,3},{3,2},{4,5},{5,4},{6,7},{7,6},{8,9},{9,8},{10,11... | collective-permute-start | bytes 3538952 | tf_op jit(solution)/shard_map/ppermute | solution.py:112
  44.7 32.7 %copy-start.11 = (bf16[16,32,768]{2,1,0:T(8,128)(2,1)}, bf16[16,32,768]{2,1,0:T(8,128)(2,1)S(1)}, u32[]{:S(2)}) copy-start(bf16[16,32,768]{2,1,0:T(8,128)(2,1)S(1)} %slice.192) | copy-start | bytes 2359300
  44.7 29.5 %all-to-all-start.1 = ((bf16[16,80,768]{2,1,0:T(8,128)(2,1)}), bf16[16,80,768]{2,1,0:T(8,128)(2,1)S(1)}, u32[]{:S(2)}, u32[]{:S(2)}) async-start(bf16[16,80,768]{2,1,0:T(8,128)(2,1)} %pad_maximum_fusion.1), calls=%async_computation.1 | async-start | bytes 3932160 | tf_op jit(solution)/shard_map/all_to_all | solution.py:182
  50.9 2.0 %copy-start.2 = (bf16[16,80,768]{2,1,0:T(8,128)(2,1)S(1)}, bf16[16,80,768]{2,1,0:T(8,128)(2,1)}, u32[]{:S(2)}) copy-start(bf16[16,80,768]{2,1,0:T(8,128)(2,1)} %copy-done.1) | copy-start | bytes 5898244
  54.4 1.0 copy-start.3
  60.6 2.5 %copy-start.15 = (bf16[448,768]{1,0:T(8,128)(2,1)S(1)}, bf16[448,768]{1,0:T(8,128)(2,1)}, u32[]{:S(2)}) copy-start(bf16[448,768]{1,0:T(8,128)(2,1)} %get-tuple-element.37) | copy-start | bytes 2064388
  63.1 0.8 copy-start.5
  63.1 1.0 copy-start.7
  65.6 11.0 %copy-start.13 = (f32[512,384]{1,0:T(8,128)S(1)}, f32[512,384]{1,0:T(8,128)}, u32[]{:S(2)}) copy-start(f32[512,384]{1,0:T(8,128)} %convolution_add_fusion.3) | copy-start | bytes 2359300
  74.2 8.6 %copy-start = (bf16[16,80,768]{2,1,0:T(8,128)(2,1)}, bf16[16,80,768]{2,1,0:T(8,128)(2,1)S(1)}, u32[]{:S(2)}) copy-start(bf16[16,80,768]{2,1,0:T(8,128)(2,1)S(1)} %all-to-all-done.1) | copy-start | bytes 5898244
  74.2 2.5 %copy-start.14 = (bf16[448,768]{1,0:T(8,128)(2,1)S(1)}, bf16[448,768]{1,0:T(8,128)(2,1)}, u32[]{:S(2)}) copy-start(bf16[448,768]{1,0:T(8,128)(2,1)} %get-tuple-element.36) | copy-start | bytes 2064388
  74.2 2.5 %copy-start.16 = (bf16[1,16,48,384]{3,2,0,1:T(8,128)(2,1)S(1)}, bf16[1,16,48,384]{3,2,0,1:T(8,128)(2,1)}, u32[]{:S(2)}) copy-start(bf16[1,16,48,384]{3,2,0,1:T(8,128)(2,1)} %get-tuple-element.29) | copy-start | bytes 1769476
  74.2 2.5 %copy-start.30 = (f32[384]{0:T(512)S(1)}, f32[384]{0:T(512)}, u32[]{:S(2)}) copy-start(f32[384]{0:T(512)} %get-tuple-element.21) | copy-start | bytes 4612
  74.3 3.0 %copy-start.4 = (bf16[16,48,768]{2,1,0:T(8,128)(2,1)S(1)}, bf16[16,48,768]{2,1,0:T(8,128)(2,1)}, u32[]{:S(2)}) copy-start(bf16[16,48,768]{2,1,0:T(8,128)(2,1)} %copy-done.3) | copy-start | bytes 3538948
  74.3 8.5 %collective-permute-start.1 = (bf16[16,48,768]{2,1,0:T(8,128)(2,1)S(1)}, bf16[16,48,768]{2,1,0:T(8,128)(2,1)S(1)}, u32[]{:S(2)}, u32[]{:S(2)}) collective-permute-start(bf16[16,48,768]{2,1,0:T(8,128)(2,1)S(1)} %slice.201), channel_id=1, source_target_pairs={{0,1},{1,0},{2,3},{3,2},{4,5},{5,4},{6,7},{7,6},{8,9},{9,8},{10,11... | collective-permute-start | bytes 3538952 | tf_op jit(solution)/shard_map/ppermute | solution.py:112
  76.7 0.7 copy-start.33
  76.7 0.7 copy-start.35
  77.3 2.1 %copy-start.22 = (f32[512,384]{1,0:T(8,128)}, f32[512,384]{1,0:T(8,128)S(1)}, u32[]{:S(2)}) copy-start(f32[512,384]{1,0:T(8,128)S(1)} %fusion.32) | copy-start | bytes 2359300
  77.3 2.0 %copy-start.26 = (bf16[16,24,768]{2,1,0:T(8,128)(2,1)}, bf16[16,24,768]{2,1,0:T(8,128)(2,1)S(1)}, u32[]{:S(2)}) copy-start(bf16[16,24,768]{2,1,0:T(8,128)(2,1)S(1)} %slice.199) | copy-start | bytes 1769476
  79.4 1.3 copy-start.9
  84.6 1.1 copy-start.19
  84.8 1.5 copy-start.10
  86.2 1.1 copy-start.18
  86.2 1.1 copy-start.29
  86.8 1.2 copy-start.21
  86.8 1.3 copy-start.28
  89.1 1.1 copy-start.20
  90.9 3.2 %slice-start = ((bf16[16,80,768]{2,1,0:T(8,128)(2,1)}), bf16[16,32,768]{2,1,0:T(8,128)(2,1)S(1)}, s32[]{:S(2)}) async-start(bf16[16,80,768]{2,1,0:T(8,128)(2,1)} %copy-done), calls=%async_computation.5 | async-start | bytes 1572864 | tf_op jit(solution)/shard_map/slice | solution.py:183
  90.9 3.2 %copy-start.34 = (f32[768]{0:T(1024)S(1)}, f32[768]{0:T(1024)}, u32[]{:S(2)}) copy-start(f32[768]{0:T(1024)} %get-tuple-element.16) | copy-start | bytes 9220
  90.9 3.2 %copy-start.36 = (f32[768]{0:T(1024)S(1)}, f32[768]{0:T(1024)}, u32[]{:S(2)}) copy-start(f32[768]{0:T(1024)} %get-tuple-element.53) | copy-start | bytes 9220
  90.9 3.2 %copy-start.40 = (bf16[512,768]{1,0:T(8,128)(2,1)S(1)}, bf16[512,768]{1,0:T(8,128)(2,1)}, u32[]{:S(2)}) copy-start(bf16[512,768]{1,0:T(8,128)(2,1)} %get-tuple-element.49) | copy-start | bytes 2359300
  90.9 4.9 %collective-permute-start.2 = (f32[384,384]{1,0:T(8,128)S(1)}, f32[384,384]{1,0:T(8,128)S(1)}, u32[]{:S(2)}, u32[]{:S(2)}) collective-permute-start(f32[384,384]{1,0:T(8,128)S(1)} %slice_select_fusion.1), channel_id=1, source_target_pairs={{0,1},{1,0},{2,3},{3,2},{4,5},{5,4},{6,7},{7,6},{8,9},{9,8},{10,11... | collective-permute-start | bytes 1769480 | tf_op jit(solution)/shard_map/ppermute | solution.py:130
  95.8 1.1 copy-start.23
  95.8 1.3 copy-start.27
  98.0 1.1 copy-start.8
  99.1 2.9 %copy-start.6 = (bf16[1,16,48,384]{3,2,0,1:T(8,128)(2,1)S(1)}, bf16[1,16,48,384]{3,2,0,1:T(8,128)(2,1)}, u32[]{:S(2)}) copy-start(bf16[1,16,48,384]{3,2,0,1:T(8,128)(2,1)} %copy-done.5) | copy-start | bytes 1769476
  99.8 2.8 %copy-start.12 = (bf16[16,32,768]{2,1,0:T(8,128)(2,1)S(1)}, bf16[16,32,768]{2,1,0:T(8,128)(2,1)}, u32[]{:S(2)}) copy-start(bf16[16,32,768]{2,1,0:T(8,128)(2,1)} %copy-done.11) | copy-start | bytes 2359300
  99.8 2.8 %copy-start.17 = (bf16[1,16,48,384]{3,2,0,1:T(8,128)(2,1)S(1)}, bf16[1,16,48,384]{3,2,0,1:T(8,128)(2,1)}, u32[]{:S(2)}) copy-start(bf16[1,16,48,384]{3,2,0,1:T(8,128)(2,1)} %get-tuple-element.29) | copy-start | bytes 1769476
  99.8 4.5 %collective-permute-start.3 = (f32[384,384]{1,0:T(8,128)S(1)}, f32[384,384]{1,0:T(8,128)S(1)}, u32[]{:S(2)}, u32[]{:S(2)}) collective-permute-start(f32[384,384]{1,0:T(8,128)S(1)} %slice_select_fusion), channel_id=1, source_target_pairs={{0,1},{1,0},{2,3},{3,2},{4,5},{5,4},{6,7},{7,6},{8,9},{9,8},{10,11... | collective-permute-start | bytes 1769480 | tf_op jit(solution)/shard_map/ppermute | solution.py:130
  163.7 20.8 %all-to-all-start.4 = ((f32[32,1,1152]{2,1,0:T(1,128)}), f32[32,1,1152]{2,1,0:T(1,128)S(1)}, u32[]{:S(2)}, u32[]{:S(2)}) async-start(f32[32,1,1152]{2,1,0:T(1,128)} %broadcast_in_dim.2), calls=%async_computation.4 | async-start | bytes 294912 | tf_op jit(solution)/shard_map/all_to_all | solution.py:21
